TPU v7x, 32 devices: a whole 2x2x4 slice. The times are simulated.
32 devices in a mesh: row: 2 (over y), col: 8 (over z, x), leaf: 2 (over core).
Axes of the slice: x: 2, y: 2, z: 4, core: 2. Of those that a mesh axis runs over, the one named last changes fastest.
Arguments:
- leaf_rhs: float32 [2, 2, 2, 256, 512], P('leaf', None, None, 'col'), may hold values from -6 to 6
- root_rhs: float32 [2, 2, 256, 512], P(None, None, 'col'), may hold values from -6 to 6
- leaf_inverses: float32 [2, 2, 2, 256, 512], P('leaf', None, None, 'col', 'row'), may hold values from -0.02 to 2, as said below
- root_inverses: float32 [2, 2, 256, 512], P(None, None, 'col', 'row'), may hold values from -0.02 to 2, as said below
- leaf_blocks: float32 [2, 5, 2, 256, 512], P('leaf', None, None, 'col', 'row'), may hold values from -0.375 to 0.375
- root_block: float32 [2, 256, 512], P(None, 'col', 'row'), may hold values from -0.25 to 0.25
- pattern: int32 [2, 5, 4, 8], P('leaf', None, 'row', 'col'), may hold values 0 or 1
Outputs:
- leaf_solution: float32 [2, 2, 2, 256, 512], P('leaf', None, None, 'col')
- root_solution: float32 [2, 2, 256, 512], P(None, None, 'col')
Inputs may be any that keep to these rules, and one draw needn't show every extreme that they name: `leaf_inverses`: lower triangular as a 512 x 512 matrix, diagonal entries between 1 and 2. `root_inverses`: lower triangular as a 512 x 512 matrix, diagonal entries between 1 and 2.
All inputs are finite; a program needn't handle non-finite values. No bound on the sum of `pattern` on one device may be relied on, other than what follows from the above.
Results may differ from a plain program's by a relative error of at most 0.00017.
Values sent between devices are 32-bit elements; how exact they have to be, the bound alone decides.
No kernel may reach another device: no remote copies, remote signals or barrier semaphores. Data moves between devices by JAX's collectives and lax.ppermute only.
A program may use at most 64 MiB of HBM per device.

v0:
```python
import jax
import jax.numpy as jnp
from jax import lax
from jax.sharding import PartitionSpec as P

BLK = 128


def apply_rows(pairs):
    flats = [
        (block.reshape(-1, block.shape[-1]), vector.reshape(-1, vector.shape[-1]))
        for block, vector in pairs
    ]
    block, vector = flats[0]
    term = lax.dot_general(
        block,
        vector,
        (((0,), (0,)), ((), ())),
        precision=lax.Precision.HIGHEST,
        preferred_element_type=jnp.float32,
    )
    owned = lax.psum_scatter(term, "col", scatter_dimension=0, tiled=True)
    return lax.all_gather(owned[None], "row", axis=0, tiled=True)


def shards(leaf_rhs, root_rhs, leaf_inverses, root_inverses, leaf_blocks, root_block, pattern):
    local_blocks = leaf_blocks[0]
    shaped = local_blocks.reshape(
        5, local_blocks.shape[1], local_blocks.shape[2], local_blocks.shape[3] // BLK, BLK
    )
    weights = pattern[0].astype(jnp.float32).transpose(0, 2, 1)[:, None, :, :, None]
    blocks = (shaped * weights).reshape(local_blocks.shape)
    first = apply_rows([(leaf_inverses[0, 0], leaf_rhs[0, 0])])
    upper_two = apply_rows([(blocks[1], first)])
    upper_three = apply_rows([(blocks[3], first)])
    second = apply_rows([(leaf_inverses[0, 1], leaf_rhs[0, 1] - apply_rows([(blocks[0], first)]))])
    upper_two = upper_two + apply_rows([(blocks[2], second)])
    upper_three = upper_three + apply_rows([(blocks[4], second)])
    upper_two, upper_three = lax.psum((upper_two, upper_three), "leaf")
    third = apply_rows([(root_inverses[0], root_rhs[0] - upper_two)])
    fourth = apply_rows(
        [(root_inverses[1], root_rhs[1] - upper_three - apply_rows([(root_block, third)]))]
    )
    return (jnp.stack([first, second])[None], jnp.stack([third, fourth]))


def solution(mesh):
    placed = (
        P("leaf", None, None, "col", None),
        P(None, None, "col", None),
        P("leaf", None, None, "col", "row"),
        P(None, None, "col", "row"),
        P("leaf", None, None, "col", "row"),
        P(None, "col", "row"),
        P("leaf", None, "row", "col"),
    )
    return jax.shard_map(
        shards,
        mesh=mesh,
        in_specs=placed,
        out_specs=(P("leaf", None, None, "col", None), P(None, None, "col", None)),
        check_vma=False,
    )
```

profile of v0, /device:TPU:0, one launch (start us, length us, event | category | flops | bytes accessed | tf_op | source)
XLA Modules:
  0.0 714.1 jit_solution(7544418516872488972)
XLA Ops:
  7.2 2.4 convolution_bitcast_fusion.4
  9.7 0.7 copy-done.6
  10.3 0.1 copy.21
  10.4 0.2 copy-done.1
  10.6 0.2 reshape_squeeze.29
  10.8 0.2 broadcast_multiply_fusion
  11.0 65.7 %reduce-scatter.19.cloned.1.call-done = f32[32,512]{1,0:T(8,128)} async-done(((f32[256,512]{1,0:T(8,128)}), f32[32,512]{1,0:T(8,128)}) %reduce-scatter.19.cloned.1.call-update) | async-done | bytes 65552 | tf_op jit(solution)/shard_map/reduce_scatter | solution.py:22
  76.7 5.1 all-gather
  81.8 1.4 fusion.15
  83.3 61.7 %reduce-scatter.21.cloned.1.call-done = f32[32,512]{1,0:T(8,128)} async-done(((f32[256,512]{1,0:T(8,128)}), f32[32,512]{1,0:T(8,128)}) %reduce-scatter.21.cloned.1.call-update) | async-done | bytes 65552 | tf_op jit(solution)/shard_map/reduce_scatter | solution.py:22
  145.0 5.1 all-gather.1
  150.2 0.8 slice-done
  151.0 0.6 convolution_bitcast_fusion.3
  151.6 1.0 copy.26
  152.7 1.4 fusion.12
  154.2 0.0 reduce-scatter.27.cloned.1.call-start
  154.2 1.4 fusion.6
  155.7 58.7 %reduce-scatter.31.cloned.1.call-done = f32[32,512]{1,0:T(8,128)} async-done(((f32[256,512]{1,0:T(8,128)}), f32[32,512]{1,0:T(8,128)}) %reduce-scatter.31.cloned.1.call-update) | async-done | bytes 65552 | tf_op jit(solution)/shard_map/reduce_scatter | solution.py:22
  214.4 5.1 all-gather.2
  219.6 1.4 fusion.9
  221.1 1.4 fusion.3
  222.6 56.7 %reduce-scatter.23.cloned.1.call-done = f32[32,512]{1,0:T(8,128)} async-done(((f32[256,512]{1,0:T(8,128)}), f32[32,512]{1,0:T(8,128)}) %reduce-scatter.23.cloned.1.call-update) | async-done | bytes 65552 | tf_op jit(solution)/shard_map/reduce_scatter | solution.py:22
  279.3 5.1 all-gather.3
  284.4 59.7 %reduce-scatter.27.cloned.1.call-done = f32[32,512]{1,0:T(8,128)} async-done(((f32[256,512]{1,0:T(8,128)}), f32[32,512]{1,0:T(8,128)}) %reduce-scatter.27.cloned.1.call-update) | async-done | bytes 65552 | tf_op jit(solution)/shard_map/reduce_scatter | solution.py:22
  344.1 5.1 all-gather.6
  349.3 59.7 %reduce-scatter.25.cloned.1.call-done = f32[32,512]{1,0:T(8,128)} async-done(((f32[256,512]{1,0:T(8,128)}), f32[32,512]{1,0:T(8,128)}) %reduce-scatter.25.cloned.1.call-update) | async-done | bytes 65552 | tf_op jit(solution)/shard_map/reduce_scatter | solution.py:22
  409.0 5.1 all-gather.4
  414.1 0.7 add.32
  414.8 59.2 %reduce-scatter.29.cloned.1.call-done = f32[32,512]{1,0:T(8,128)} async-done(((f32[256,512]{1,0:T(8,128)}), f32[32,512]{1,0:T(8,128)}) %reduce-scatter.29.cloned.1.call-update) | async-done | bytes 65552 | tf_op jit(solution)/shard_map/reduce_scatter | solution.py:22
  474.0 5.1 all-gather.7
  479.2 0.7 add.33
  479.9 0.2 copy-done.4
  480.1 17.2 %all-reduce.3.cloned.1.call-done = (f32[2,32,512]{2,1,0:T(8,128)}, f32[2,32,512]{2,1,0:T(8,128)}) async-done(((f32[2,32,512]{2,1,0:T(8,128)}, f32[2,32,512]{2,1,0:T(8,128)}), (f32[2,32,512]{2,1,0:T(8,128)}, f32[2,32,512]{2,1,0:T(8,128)})) %all-reduce.3.cloned.1.call-update) | async-done | bytes 262160 | tf_op jit(solution)/shard_map/psum | solution.py:39
  497.3 0.9 bitcast_subtract_fusion.1
  498.3 0.6 convolution_bitcast_fusion.2
  498.9 1.0 copy.28
  500.0 64.6 %reduce-scatter.33.cloned.1.call-done = f32[32,512]{1,0:T(8,128)} async-done(((f32[256,512]{1,0:T(8,128)}), f32[32,512]{1,0:T(8,128)}) %reduce-scatter.33.cloned.1.call-update) | async-done | bytes 65552 | tf_op jit(solution)/shard_map/reduce_scatter | solution.py:22
  564.5 5.1 all-gather.5
  569.7 0.6 convolution_bitcast_fusion.1
  570.3 1.0 copy.30
  571.4 61.7 %reduce-scatter.35.cloned.1.call-done = f32[32,512]{1,0:T(8,128)} async-done(((f32[256,512]{1,0:T(8,128)}), f32[32,512]{1,0:T(8,128)}) %reduce-scatter.35.cloned.1.call-update) | async-done | bytes 65552 | tf_op jit(solution)/shard_map/reduce_scatter | solution.py:22
  633.1 5.1 all-gather.8
  638.3 0.6 convolution_bitcast_fusion
  638.9 1.0 copy.32
  639.9 0.7 maximum_bitcast_fusion
  640.7 61.1 %reduce-scatter.37.cloned.1.call-done = f32[32,512]{1,0:T(8,128)} async-done(((f32[256,512]{1,0:T(8,128)}), f32[32,512]{1,0:T(8,128)}) %reduce-scatter.37.cloned.1.call-update) | async-done | bytes 65552 | tf_op jit(solution)/shard_map/reduce_scatter | solution.py:22
  701.7 5.1 all-gather.9
  706.9 0.7 pad_maximum_fusion
  (38 shorter events, 0.7 us)
Async XLA Ops:
  7.2 562.5 %copy-start = (f32[2,32,256]{2,1,0:T(8,128)S(1)}, f32[2,32,256]{2,1,0:T(8,128)}, u32[]{:S(2)}) copy-start(f32[2,32,256]{2,1,0:T(8,128)} %param.12) | copy-start | bytes 196612
  7.2 69.5 %reduce-scatter.19.cloned.1.call-start = ((), (), s32[]{:S(2)}) async-start(), calls=%async_computation.10 | async-start | bytes 589824 | tf_op jit(solution)/shard_map/reduce_scatter | solution.py:22
  9.6 1.0 copy-start.1
  9.6 0.7 copy-start.6
  9.6 135.4 %reduce-scatter.21.cloned.1.call-start = ((), (), s32[]{:S(2)}) async-start(), calls=%async_computation.11 | async-start | bytes 589824 | tf_op jit(solution)/shard_map/reduce_scatter | solution.py:22
  83.3 66.9 %copy-start.2 = (f32[1,2,2,32,512]{4,3,2,1,0:T(8,128)S(1)}, f32[1,2,2,32,512]{4,3,2,1,0:T(8,128)}, u32[]{:S(2)}) copy-start(f32[1,2,2,32,512]{4,3,2,1,0:T(8,128)} %param.7) | copy-start | bytes 786436
  83.3 131.2 %reduce-scatter.31.cloned.1.call-start = ((), (), s32[]{:S(2)}) async-start(), calls=%async_computation.16 | async-start | bytes 589824 | tf_op jit(solution)/shard_map/reduce_scatter | solution.py:22
  150.2 0.8 slice-start
  152.7 126.6 %reduce-scatter.23.cloned.1.call-start = ((), (), s32[]{:S(2)}) async-start(), calls=%async_computation.12 | async-start | bytes 589824 | tf_op jit(solution)/shard_map/reduce_scatter | solution.py:22
  154.2 190.0 %reduce-scatter.27.cloned.1.call-start = ((), (), s32[]{:S(2)}) async-start(), calls=%async_computation.14 | async-start | bytes 589824 | tf_op jit(solution)/shard_map/reduce_scatter | solution.py:22
  155.7 253.3 %reduce-scatter.25.cloned.1.call-start = ((), (), s32[]{:S(2)}) async-start(), calls=%async_computation.13 | async-start | bytes 589824 | tf_op jit(solution)/shard_map/reduce_scatter | solution.py:22
  221.1 253.0 %reduce-scatter.29.cloned.1.call-start = ((), (), s32[]{:S(2)}) async-start(), calls=%async_computation.15 | async-start | bytes 589824 | tf_op jit(solution)/shard_map/reduce_scatter | solution.py:22
  222.6 274.8 %all-reduce.3.cloned.1.call-start = ((), (), s32[]{:S(2)}) async-start(), calls=%async_computation.20 | async-start | bytes 524288 | tf_op jit(solution)/shard_map/psum | solution.py:39
  479.2 1.0 copy-start.4
  479.8 17.5 %copy-start.3 = (f32[2,2,32,512]{3,2,1,0:T(8,128)S(1)}, f32[2,2,32,512]{3,2,1,0:T(8,128)}, u32[]{:S(2)}) copy-start(f32[2,2,32,512]{3,2,1,0:T(8,128)} %param.8) | copy-start | bytes 786436
  479.9 84.7 %reduce-scatter.33.cloned.1.call-start = ((), (), s32[]{:S(2)}) async-start(), calls=%async_computation.17 | async-start | bytes 589824 | tf_op jit(solution)/shard_map/reduce_scatter | solution.py:22
  499.9 133.2 %reduce-scatter.35.cloned.1.call-start = ((), (), s32[]{:S(2)}) async-start(), calls=%async_computation.18 | async-start | bytes 589824 | tf_op jit(solution)/shard_map/reduce_scatter | solution.py:22
  571.3 66.9 %copy-start.5 = (f32[2,32,512]{2,1,0:T(8,128)S(1)}, f32[2,32,512]{2,1,0:T(8,128)}, u32[]{:S(2)}) copy-start(f32[2,32,512]{2,1,0:T(8,128)} %get-tuple-element.3) | copy-start | bytes 393220
  571.3 130.4 %reduce-scatter.37.cloned.1.call-start = ((), (), s32[]{:S(2)}) async-start(), calls=%async_computation.19 | async-start | bytes 589824 | tf_op jit(solution)/shard_map/reduce_scatter | solution.py:22
Sparse Core Ops, SparseCore 0:
  11.3 65.3 reduce-scatter.18
  83.4 61.6 reduce-scatter.20
  152.8 61.5 reduce-scatter.30
  217.6 61.6 reduce-scatter.22
  282.5 61.6 reduce-scatter.26
  347.3 61.6 reduce-scatter.24
  412.3 61.6 reduce-scatter.28
  480.0 17.3 all-reduce.2
  500.7 63.8 reduce-scatter.32
  571.5 61.6 reduce-scatter.34
  640.0 61.6 reduce-scatter.36
where the time goes:
time: 714 us
  waiting for transfers between devices  626 us (88%)
  blocking collectives  51.3 us (7%)
  between operations  14 us (2%)
  matrix products  12 us (2%)
    reduce_scatter x10, waiting for transfers between devices, apply_rows(): owned = lax.psum_scatter(term, 'col', scatter_dimension=0, tiled=True)  609 us
    all_gather x10, blocking collectives, apply_rows(): return lax.all_gather(owned[None], 'row', axis=0, tiled=True)  51.3 us
    psum x1, waiting for transfers between devices, shards(): upper_two, upper_three = lax.psum((upper_two, upper_three), 'leaf')  17.2 us
  transfers between devices with their start and end apart: 11, of which 11 were waited for; matrix products, arithmetic and copies ran while one was open for 1% of the time, Pallas kernels for 0%

commit v1 on v0

v1 whole, which is shorter than its diff:
```python
import functools

import jax
import jax.numpy as jnp
from jax import lax
from jax.experimental import pallas as pl
from jax.experimental.pallas import tpu as pltpu
from jax.sharding import PartitionSpec as P

BLK = 128
AXES = ("row", "col", "leaf")
F32 = jnp.float32
BF16 = jnp.bfloat16


def apply_rows(block, vector):
    block = block.reshape(-1, block.shape[-1])
    vector = vector.reshape(-1, vector.shape[-1])
    term = lax.dot_general(
        block,
        vector,
        (((0,), (0,)), ((), ())),
        precision=lax.Precision.HIGHEST,
        preferred_element_type=F32,
    )
    owned = lax.psum_scatter(term, "col", scatter_dimension=0, tiled=True)
    return lax.all_gather(owned[None], "row", axis=0, tiled=True)


def masked(leaf_blocks, pattern):
    local = leaf_blocks[0]
    shaped = local.reshape(local.shape[:3] + (local.shape[3] // BLK, BLK))
    weights = pattern[0].astype(F32).transpose(0, 2, 1)[:, None, :, :, None]
    return (shaped * weights).reshape(local.shape)


def general(leaf_rhs, root_rhs, leaf_inverses, root_inverses, leaf_blocks, root_block, pattern):
    blocks = masked(leaf_blocks, pattern)
    first = apply_rows(leaf_inverses[0, 0], leaf_rhs[0, 0])
    second = apply_rows(leaf_inverses[0, 1], leaf_rhs[0, 1] - apply_rows(blocks[0], first))
    upper_two = apply_rows(blocks[1], first) + apply_rows(blocks[2], second)
    upper_three = apply_rows(blocks[3], first) + apply_rows(blocks[4], second)
    upper_two, upper_three = lax.psum((upper_two, upper_three), "leaf")
    third = apply_rows(root_inverses[0], root_rhs[0] - upper_two)
    fourth = apply_rows(root_inverses[1], root_rhs[1] - upper_three - apply_rows(root_block, third))
    return (jnp.stack([first, second])[None], jnp.stack([third, fourth]))


def pairs(dest):
    out = []
    for r in range(2):
        for zh in range(2):
            for zl in range(2):
                for x in range(2):
                    for l in range(2):
                        d = dest(r, zh, zl, x, l)
                        if d is None:
                            continue
                        s = (r * 8 + zh * 4 + zl * 2 + x) * 2 + l
                        e = (d[0] * 8 + d[1] * 4 + d[2] * 2 + d[3]) * 2 + d[4]
                        out.append((s, e))
    return out


def send(value, dest):
    return lax.ppermute(value, AXES, pairs(dest))


def to_far(r, zh, zl, x, l):
    return r, zh ^ 1, zl, x, l


def to_second(r, zh, zl, x, l):
    return (r, zh, zl, x ^ 1, l) if l == 0 else (r ^ 1, zh, zl, x, l)


def to_third(r, zh, zl, x, l):
    return (r ^ 1, zh, zl, x, l) if l == 0 else (r, zh, zl, x ^ 1, l)


def to_pair(r, zh, zl, x, l):
    return r, zh, zl ^ 1, x, l


def to_core(r, zh, zl, x, l):
    return r, zh, zl, x, l ^ 1


def to_row(r, zh, zl, x, l):
    return r ^ 1, zh, zl, x, l


def to_group(b1, b2):
    return lambda r, zh, zl, x, l: (r, zh ^ b1, zl, x ^ b2, l)


def to_group_by_core(b1, b2):
    return lambda r, zh, zl, x, l: (r ^ l, zh ^ b1, zl, x ^ b2, l)


def gather_begin(local):
    return send(local, to_far)


def gather_rest(local, far):
    two = jnp.stack([local, far])
    four = jnp.concatenate([two, send(two, to_second)])
    return four, send(four, to_third)


def vmem():
    return pl.BlockSpec(memory_space=pltpu.VMEM)


def anywhere():
    return pl.BlockSpec(memory_space=pl.ANY)


def smem():
    return pl.BlockSpec(memory_space=pltpu.SMEM)


def lanes_low():
    return lax.broadcasted_iota(jnp.int32, (1, 128), 1) < 64


def split(value):
    high = value.astype(BF16)
    return high, (value - high.astype(F32)).astype(BF16)


def dot3(left, right):
    lh, ll = left
    rh, rl = right
    whole = jnp.dot(lh, rl, preferred_element_type=F32)
    whole += jnp.dot(ll, rh, preferred_element_type=F32)
    return whole + jnp.dot(lh, rh, preferred_element_type=F32)


def step_kernel(vec_fn, terms, nvec, nchunk, nextra, where_ref, *refs):
    vecs = refs[:nvec]
    chunks = refs[nvec : nvec + 2 * nchunk]
    outs = refs[nvec + 2 * nchunk : nvec + 2 * nchunk + 2 + nextra]
    held, sems = refs[nvec + 2 * nchunk + 2 + nextra :]
    r, zh, zl, x, l = (where_ref[k] for k in range(5))
    copies = []
    for t, (chunk, m, _) in enumerate(terms):
        row = []
        for b3 in range(2):
            for b2 in range(2):
                for b1 in range(2):
                    rr = r ^ jnp.where(l == 0, b3, b2)
                    xx = x ^ jnp.where(l == 0, b2, b3)
                    copy = pltpu.make_async_copy(
                        chunks[2 * chunk + b3].at[b2 * 2 + b1, m],
                        held.at[t, rr, :, zh ^ b1, xx],
                        sems.at[t, b3 * 4 + b2 * 2 + b1],
                    )
                    copy.start()
                    row.append(copy)
        copies.append(row)
    sources, extras = vec_fn([v[...] for v in vecs])
    for k, value in enumerate(extras):
        outs[2 + k][...] = value
    halves = [
        split(jnp.concatenate([s[:64], s[64:]], axis=1)) for s in sources
    ]
    sums = [None, None]
    for t, (_, _, which) in enumerate(terms):
        for copy in copies[t]:
            copy.wait()
        for a in range(2):
            matrix = split(held[t, a].reshape(256, 256))
            part = dot3(halves[which], matrix)
            sums[a] = part if sums[a] is None else sums[a] + part
    whole = jnp.concatenate(sums, axis=0)
    one, two = whole[:, :128], whole[:, 128:]
    low = lanes_low()
    even = jnp.where(low, one, pltpu.roll(two, 64, 1))
    odd = jnp.where(low, pltpu.roll(one, 64, 1), two)
    outs[0][...] = jnp.where(zl == 0, even, odd)
    outs[1][...] = jnp.where(zl == 0, odd, even)


def step(name, where, vec_fn, vecs, chunks, terms, nextra=0):
    flat = [array for pair in chunks for array in pair]
    kernel = functools.partial(step_kernel, vec_fn, terms, len(vecs), len(chunks), nextra)
    shape = jax.ShapeDtypeStruct((128, 128), F32)
    return pl.pallas_call(
        kernel,
        out_shape=[shape] * (2 + nextra),
        in_specs=[smem()] + [vmem()] * len(vecs) + [anywhere()] * len(flat),
        out_specs=[vmem()] * (2 + nextra),
        scratch_shapes=[
            pltpu.VMEM((len(terms), 2, 2, 2, 2, 32, 256), F32),
            pltpu.SemaphoreType.DMA((len(terms), 8)),
        ],
        name=name,
    )(where, *vecs, *flat)


def cut_kernel(where_ref, leaf_ref, root_ref, *refs):
    outs, held = refs[:4], refs[4]
    r, zh, x = where_ref[0], where_ref[1], where_ref[3]
    low = lanes_low()
    for p in range(4):
        source = leaf_ref if p < 2 else root_ref
        for z in range(2):
            start = pl.multiple_of((2 * r + z) * 128, 128)
            one = source[p % 2, 0, :, pl.ds(start, 128)]
            two = source[p % 2, 1, :, pl.ds(start, 128)]
            held[2 * z, p] = jnp.where(low, one, pltpu.roll(two, 64, 1))
            held[2 * z + 1, p] = jnp.where(low, pltpu.roll(one, 64, 1), two)
    for b1 in range(2):
        for b2 in range(2):
            outs[b1 * 2 + b2][...] = held[(zh ^ b1) * 2 + (x ^ b2)]


def cut(where, leaf_rhs, root_rhs):
    shape = jax.ShapeDtypeStruct((4, 32, 128), F32)
    return pl.pallas_call(
        cut_kernel,
        out_shape=[shape] * 4,
        in_specs=[smem(), vmem(), vmem()],
        out_specs=[vmem()] * 4,
        scratch_shapes=[pltpu.VMEM((4, 4, 32, 128), F32)],
        name="cut_columns",
    )(where, leaf_rhs, root_rhs)


def stand_kernel(where_ref, *refs):
    pieces, outs, held = refs[:4], refs[4:8], refs[8]
    zh, x = where_ref[1], where_ref[3]
    for b1 in range(2):
        for b2 in range(2):
            held[(zh ^ b1) * 2 + (x ^ b2)] = pieces[b1 * 2 + b2][...]
    for p in range(4):
        outs[p][...] = held[:, p].reshape(128, 128).T


def stand(where, pieces):
    shape = jax.ShapeDtypeStruct((128, 128), F32)
    return pl.pallas_call(
        stand_kernel,
        out_shape=[shape] * 4,
        in_specs=[smem()] + [vmem()] * 4,
        out_specs=[vmem()] * 4,
        scratch_shapes=[pltpu.VMEM((4, 4, 32, 128), F32)],
        name="stand_columns",
    )(where, *pieces)


def lay_kernel(where_ref, *refs):
    first, keep, got = refs[:3]
    outs, held = refs[3:7], refs[7]
    zh, x = where_ref[1], where_ref[3]
    for p, value in enumerate((first[...], keep[...] + got[...])):
        held[:, p] = value.T.reshape(4, 32, 128)
    for b1 in range(2):
        for b2 in range(2):
            outs[b1 * 2 + b2][...] = held[(zh ^ b1) * 2 + (x ^ b2)]


def lay(name, where, first, keep, got):
    shape = jax.ShapeDtypeStruct((2, 32, 128), F32)
    return pl.pallas_call(
        lay_kernel,
        out_shape=[shape] * 4,
        in_specs=[smem()] + [vmem()] * 3,
        out_specs=[vmem()] * 4,
        scratch_shapes=[pltpu.VMEM((4, 2, 32, 128), F32)],
        name=name,
    )(where, first, keep, got)


def join_kernel(where_ref, near_ref, other_ref, out_ref, held):
    r, zh, x = where_ref[0], where_ref[1], where_ref[3]
    for b1 in range(2):
        for b2 in range(2):
            place = (zh ^ b1) * 2 + (x ^ b2)
            held[r * 4 + place] = near_ref[b1 * 2 + b2]
            held[(r ^ 1) * 4 + place] = other_ref[b1 * 2 + b2]
    low = lanes_low()
    for p in range(2):
        for u in range(4):
            one, two = held[2 * u, p], held[2 * u + 1, p]
            out_ref[p, 0, :, u * 128 : u * 128 + 128] = jnp.where(low, one, pltpu.roll(two, 64, 1))
            out_ref[p, 1, :, u * 128 : u * 128 + 128] = jnp.where(low, pltpu.roll(one, 64, 1), two)


def join(name, where, near, other):
    return pl.pallas_call(
        join_kernel,
        out_shape=jax.ShapeDtypeStruct((2, 2, 32, 512), F32),
        in_specs=[smem()] + [vmem()] * 2,
        out_specs=vmem(),
        scratch_shapes=[pltpu.VMEM((8, 2, 32, 128), F32)],
        name=name,
    )(where, near, other)


def total(keep, got):
    return keep + got


def grouped(leaf_rhs, root_rhs, leaf_inverses, root_inverses, leaf_blocks, root_block, pattern):
    row, col, core = (lax.axis_index(name) for name in AXES)
    where = jnp.stack([row, col // 4, (col // 2) % 2, col % 2, core]).astype(jnp.int32)
    blocks = masked(leaf_blocks, pattern)
    inverses = leaf_inverses[0]
    chunk_a = jnp.stack([inverses[0], blocks[0]])
    chunk_b = jnp.stack([inverses[1], blocks[1], blocks[2]])
    chunk_c = jnp.concatenate([blocks[3:5], root_inverses, root_block[None]])

    far_a = gather_begin(chunk_a)
    mine = cut(where, leaf_rhs[0], root_rhs)
    pieces = [mine[0]] + [send(mine[k], to_group(k // 2, k % 2)) for k in (1, 2, 3)]
    chunk_b, far_a = lax.optimization_barrier((chunk_b, far_a))
    far_b = gather_begin(chunk_b)
    pair_a = gather_rest(chunk_a, far_a)
    b0, b1, r2, r3 = stand(where, pieces)

    keep, out = step("solve_0", where, lambda v: ([v[0]], []), [b0], [pair_a], [(0, 0, 0)])
    got = send(out, to_pair)
    chunk_c, far_b = lax.optimization_barrier((chunk_c, far_b))
    far_c = gather_begin(chunk_c)
    pair_b = gather_rest(chunk_b, far_b)
    keep, out, y0 = step(
        "update_10", where, lambda v: ([v[0] + v[1]], [v[0] + v[1]]), [keep, got], [pair_a], [(0, 1, 0)], 1
    )
    got = send(out, to_pair)
    keep1, out = step(
        "solve_1", where, lambda v: ([v[0] - (v[1] + v[2])], []), [b1, keep, got], [pair_b], [(0, 0, 0)]
    )
    got1 = send(out, to_pair)
    pair_c = gather_rest(chunk_c, far_c)
    keep, out, y1 = step(
        "update_2",
        where,
        lambda v: ([v[0], v[1] + v[2]], [v[1] + v[2]]),
        [y0, keep1, got1],
        [pair_b],
        [(0, 1, 0), (0, 2, 1)],
        1,
    )
    got = send(out, to_pair)
    own2 = keep + got
    other2 = send(own2, to_core)
    keep3, out3 = step(
        "update_3", where, lambda v: (v, []), [y0, y1], [pair_c], [(0, 0, 0), (0, 1, 1)]
    )
    got3 = send(out3, to_pair)
    keep, out = step(
        "solve_2", where, lambda v: ([v[0] - (v[1] + v[2])], []), [r2, own2, other2], [pair_c], [(0, 2, 0)]
    )
    got = send(out, to_pair)
    own3 = keep3 + got3
    other3 = send(own3, to_core)
    keep, out, y2 = step(
        "update_32", where, lambda v: ([v[0] + v[1]], [v[0] + v[1]]), [keep, got], [pair_c], [(0, 4, 0)], 1
    )
    got = send(out, to_pair)

    leaf_parts = lay("lay_leaf", where, y0, keep1, got1)
    leaf_near = jnp.stack(
        [leaf_parts[0]] + [send(leaf_parts[k], to_group(k // 2, k % 2)) for k in (1, 2, 3)]
    )
    leaf_other = send(leaf_near, to_row)
    leaf_solution = join("join_leaf", where, leaf_near, leaf_other)

    keep, out = step(
        "solve_3",
        where,
        lambda v: ([v[0] - (v[1] + v[2]) - (v[3] + v[4])], []),
        [r3, own3, other3, keep, got],
        [pair_c],
        [(0, 3, 0)],
    )
    got = send(out, to_pair)
    root_parts = lay("lay_root", where, y2, keep, got)
    moved = jnp.stack([send(root_parts[k], to_group_by_core(k // 2, k % 2)) for k in range(4)])
    swapped = send(moved, to_core)
    near = jnp.where(core == 0, moved, swapped)
    other = jnp.where(core == 0, swapped, moved)
    root_solution = join("join_root", where, near, other)
    return leaf_solution[None], root_solution


def solution(mesh):
    placed = (
        P("leaf", None, None, "col", None),
        P(None, None, "col", None),
        P("leaf", None, None, "col", "row"),
        P(None, None, "col", "row"),
        P("leaf", None, None, "col", "row"),
        P(None, "col", "row"),
        P("leaf", None, "row", "col"),
    )
    small = (mesh.shape["row"], mesh.shape["col"], mesh.shape["leaf"]) == (2, 8, 2)
    return jax.shard_map(
        grouped if small else general,
        mesh=mesh,
        in_specs=placed,
        out_specs=(P("leaf", None, None, "col", None), P(None, None, "col", None)),
        check_vma=False,
    )
```

time: 714 us -> 178 us (0.25)
  waiting for transfers between devices: 626 us -> 91.7 us
  blocking collectives: 51.3 us -> 0 us
  Pallas kernels: 0 us -> 35.6 us
  starting transfers between devices: 0.46 us -> 35.6 us
  between operations: 14 us -> 1.04 us
  matrix products: 12 us -> 0 us
    reduce_scatter x10 -> x0, waiting for transfers between devices: 609 us -> none  [apply_rows(): owned = lax.psum_scatter(term, 'col', scatter_dimension=0, tiled=True)]
    ppermute x0 -> x31, waiting for transfers between devices: none -> 91.7 us  [send(): return lax.ppermute(value, AXES, pairs(dest))]
    all_gather x10 -> x0, blocking collectives: 51.3 us -> none  [apply_rows(): return lax.all_gather(owned[None], 'row', axis=0, tiled=True)]
    ppermute x0 -> x31, starting transfers between devices: none -> 35.6 us  [send(): return lax.ppermute(value, AXES, pairs(dest))]
    pallas_call x0 -> x14, Pallas kernels: none -> 35.6 us  [the longest x8 24.9 us: step(): pl.pallas_call(kernel, out_shape=[shape] * (2 + nextra), in_specs=[smem()...]
    psum x1 -> x0, waiting for transfers between devices: 17.2 us -> none  [shards(): upper_two, upper_three = lax.psum((upper_two, upper_three), 'leaf')]
    dot_general x10 -> x0, matrix products: 12 us -> none  [apply_rows(): lax.dot_general(block, vector, (((0,), (0,)), ((), ())), precision=lax.Pr...]
  transfers between devices with their start and end apart: 11 -> 31, of which waited for: 11 -> 18; matrix products, arithmetic and copies ran while one was open for 1% -> 2% of each run, Pallas kernels for 0% -> 17%
where the time goes in v1:
time: 178 us; the launch traced here: 177 us
  waiting for transfers between devices  91.7 us (52%)
  starting transfers between devices  35.6 us (20%)
  Pallas kernels  35.6 us (20%)
  local copies, waits for them, and re-layouts  8.37 us (5%)
  other arithmetic  4.39 us (2%)
    ppermute x31, waiting for transfers between devices, send(): return lax.ppermute(value, AXES, pairs(dest))  91.7 us
    ppermute x31, starting transfers between devices, send(): return lax.ppermute(value, AXES, pairs(dest))  35.6 us
    pallas_call x8, Pallas kernels, step(): pl.pallas_call(kernel, out_shape=[shape] * (2 + nextra), in_specs=[smem()...  24.9 us
    unnamed x54, local copies, waits for them, and re-layouts  6.19 us
    pallas_call x2, Pallas kernels, join(): pl.pallas_call(join_kernel, out_shape=jax.ShapeDtypeStruct((2, 2, 32, 512...  3.67 us
  transfers between devices with their start and end apart: 31, of which 18 were waited for; matrix products, arithmetic and copies ran while one was open for 2% of the time, Pallas kernels for 17%

profile of v1, /device:TPU:0, one launch (start us, length us, event | category | flops | bytes accessed | tf_op | source)
XLA Modules:
  0.0 176.7 jit_solution(10467689651183899560)
XLA Ops:
  0.6 1.2 reshape_squeeze.3
  3.0 4.1 %collective-permute-start.3 = (f32[2,2,32,256]{3,2,1,0:T(8,128)S(1)}, f32[2,2,32,256]{3,2,1,0:T(8,128)S(1)}, u32[]{:S(2)}, u32[]{:S(2)}) collective-permute-start(f32[2,2,32,256]{3,2,1,0:T(8,128)S(1)} %get-tuple-element.86), channel_id=1, source_target_pairs={{0,8},{1,9},{2,10},{3,11},{4,12},{5,13},{6,14},{7,15},{8,0},{9,1},... | collective-permute-start | bytes 393224 | tf_op jit(solution)/shard_map/ppermute | solution.py:66
  7.2 6.2 %collective-permute-done.3 = f32[2,2,32,256]{3,2,1,0:T(8,128)S(1)} collective-permute-done((f32[2,2,32,256]{3,2,1,0:T(8,128)S(1)}, f32[2,2,32,256]{3,2,1,0:T(8,128)S(1)}, u32[]{:S(2)}, u32[]{:S(2)}) %collective-permute-start.3) | collective-permute-done | bytes 131104 | tf_op jit(solution)/shard_map/ppermute | solution.py:66
  13.6 11.0 %collective-permute-done.8 = f32[3,2,32,256]{3,2,1,0:T(8,128)S(1)} collective-permute-done((f32[3,2,32,256]{3,2,1,0:T(8,128)S(1)}, f32[3,2,32,256]{3,2,1,0:T(8,128)S(1)}, u32[]{:S(2)}, u32[]{:S(2)}) %collective-permute-start.8) | collective-permute-done | bytes 196640 | tf_op jit(solution)/shard_map/ppermute | solution.py:66
  24.6 15.9 %collective-permute-done.18 = f32[5,2,32,256]{3,2,1,0:T(8,128)S(1)} collective-permute-done((f32[5,2,32,256]{3,2,1,0:T(8,128)S(1)}, f32[5,2,32,256]{3,2,1,0:T(8,128)S(1)}, u32[]{:S(2)}, u32[]{:S(2)}) %collective-permute-start.18) | collective-permute-done | bytes 327712 | tf_op jit(solution)/shard_map/ppermute | solution.py:66
  40.6 1.1 collective-permute-start.19
  42.8 8.4 %collective-permute-done.19 = f32[2,5,2,32,256]{4,3,2,1,0:T(8,128)S(1)} collective-permute-done((f32[2,5,2,32,256]{4,3,2,1,0:T(8,128)S(1)}, f32[2,5,2,32,256]{4,3,2,1,0:T(8,128)S(1)}, u32[]{:S(2)}, u32[]{:S(2)}) %collective-permute-start.19) | collective-permute-done | bytes 655392 | tf_op jit(solution)/shard_map/ppermute | solution.py:66
  51.4 1.1 collective-permute-start.20
  52.5 1.6 collective-permute-start.4
  54.1 3.8 %collective-permute-done.9 = f32[2,3,2,32,256]{4,3,2,1,0:T(8,128)S(1)} collective-permute-done((f32[2,3,2,32,256]{4,3,2,1,0:T(8,128)S(1)}, f32[2,3,2,32,256]{4,3,2,1,0:T(8,128)S(1)}, u32[]{:S(2)}, u32[]{:S(2)}) %collective-permute-start.9) | collective-permute-done | bytes 393248 | tf_op jit(solution)/shard_map/ppermute | solution.py:66
  57.9 1.4 collective-permute-start.10
  59.3 4.2 %collective-permute-done.4 = f32[2,2,2,32,256]{4,3,2,1,0:T(8,128)S(1)} collective-permute-done((f32[2,2,2,32,256]{4,3,2,1,0:T(8,128)S(1)}, f32[2,2,2,32,256]{4,3,2,1,0:T(8,128)S(1)}, u32[]{:S(2)}, u32[]{:S(2)}) %collective-permute-start.4) | collective-permute-done | bytes 262176 | tf_op jit(solution)/shard_map/ppermute | solution.py:66
  64.3 1.3 collective-permute-start.5
  66.2 1.9 %cut_columns.1 = (f32[4,32,128]{2,1,0:T(8,128)}, f32[4,32,128]{2,1,0:T(8,128)}, f32[4,32,128]{2,1,0:T(8,128)}, f32[4,32,128]{2,1,0:T(8,128)}) custom-call(s32[5]{0:T(128)} %stack.86.where_ref, f32[2,2,32,512]{3,2,1,0:T(8,128)} %bitcast.40, f32[2,2,32,512]{3,2,1,0:T(8,128)} %root_ref.1), custom_call_target="tpu_custom_call" | custom-call | tf_op jit(solution)/shard_map/cut_columns/pallas_call | solution.py:221
  68.1 1.5 collective-permute-start
  69.6 3.7 %collective-permute-done.refs_1_ = f32[4,32,128]{2,1,0:T(8,128)S(1)} collective-permute-done((f32[4,32,128]{2,1,0:T(8,128)}, f32[4,32,128]{2,1,0:T(8,128)S(1)}, u32[]{:S(2)}, u32[]{:S(2)}) %collective-permute-start) | collective-permute-done | bytes 65568 | tf_op jit(solution)/shard_map/ppermute | solution.py:66
  73.8 1.2 collective-permute-done.1.refs_2_
  75.0 4.8 %collective-permute-done.2.refs_3_ = f32[4,32,128]{2,1,0:T(8,128)} collective-permute-done((f32[4,32,128]{2,1,0:T(8,128)}, f32[4,32,128]{2,1,0:T(8,128)}, u32[]{:S(2)}, u32[]{:S(2)}) %collective-permute-start.2) | collective-permute-done | bytes 65568 | tf_op jit(solution)/shard_map/ppermute | solution.py:66
  79.8 1.8 %stand_columns.1 = (f32[128,128]{1,0:T(8,128)}, f32[128,128]{1,0:T(8,128)}, f32[128,128]{1,0:T(8,128)}, f32[128,128]{1,0:T(8,128)}) custom-call(s32[5]{0:T(128)} %stack.86.where_ref, f32[4,32,128]{2,1,0:T(8,128)} %get-tuple-element.41.refs_0_, f32[4,32,128]{2,1,0:T(8,128)} %copy-done.24, f32[4,32,128]{2,1,0:T(8,128)} %copy-done.25, ...), custom_call_target="tpu_custom_call" | custom-call | tf_op jit(solution)/shard_map/stand_columns/pallas_call | solution.py:243
  81.6 3.8 %collective-permute-done.5.refs_2_.refs_3_ = f32[4,2,2,32,256]{4,3,2,1,0:T(8,128)} collective-permute-done((f32[4,2,2,32,256]{4,3,2,1,0:T(8,128)}, f32[4,2,2,32,256]{4,3,2,1,0:T(8,128)}, u32[]{:S(2)}, u32[]{:S(2)}) %collective-permute-start.5) | collective-permute-done | bytes 524320 | tf_op jit(solution)/shard_map/ppermute | solution.py:66
  85.4 3.0 %solve_0.1 = (f32[128,128]{1,0:T(8,128)}, f32[128,128]{1,0:T(8,128)}) custom-call(s32[5]{0:T(128)} %stack.86.where_ref, f32[128,128]{1,0:T(8,128)} %get-tuple-element.45.refs_0_, f32[4,2,2,32,256]{4,3,2,1,0:T(8,128)} %pad_maximum_fusion.3.refs_1_.refs_2_, f32[4,2,2,32,256]{4,3,2,1,0:T(8,128)} %collective-permute-done.5.refs_2_.refs_3_), custom_call_target="tpu_custom_call" | custom-call | tf_op jit(solution)/shard_map/solve_0/pallas_call | solution.py:189
  88.4 5.2 %collective-permute-done.6.refs_1_ = f32[128,128]{1,0:T(8,128)S(1)} collective-permute-done((f32[128,128]{1,0:T(8,128)}, f32[128,128]{1,0:T(8,128)S(1)}, u32[]{:S(2)}, u32[]{:S(2)}) %collective-permute-start.6) | collective-permute-done | bytes 65568 | tf_op jit(solution)/shard_map/ppermute | solution.py:66
  94.2 3.0 %update_10.1 = (f32[128,128]{1,0:T(8,128)}, f32[128,128]{1,0:T(8,128)}, f32[128,128]{1,0:T(8,128)}) custom-call(s32[5]{0:T(128)} %stack.86.where_ref, f32[128,128]{1,0:T(8,128)} %get-tuple-element.47.refs_0_, f32[128,128]{1,0:T(8,128)} %copy-done.23, f32[4,2,2,32,256]{4,3,2,1,0:T(8,128)} %pad_maximum_fusion.3.refs_1_.refs_2_, ...), custom_call_target="tpu_custom_call" | custom-call | tf_op jit(solution)/shard_map/update_10/pallas_call | solution.py:189
  97.4 5.0 %collective-permute-done.7.refs_2_ = f32[128,128]{1,0:T(8,128)S(1)} collective-permute-done((f32[128,128]{1,0:T(8,128)}, f32[128,128]{1,0:T(8,128)S(1)}, u32[]{:S(2)}, u32[]{:S(2)}) %collective-permute-start.7) | collective-permute-done | bytes 65568 | tf_op jit(solution)/shard_map/ppermute | solution.py:66
  103.0 3.0 %solve_1.1 = (f32[128,128]{1,0:T(8,128)}, f32[128,128]{1,0:T(8,128)}) custom-call(s32[5]{0:T(128)} %stack.86.where_ref, f32[128,128]{1,0:T(8,128)} %get-tuple-element.50.refs_0_, f32[128,128]{1,0:T(8,128)} %get-tuple-element.51.refs_1_, f32[128,128]{1,0:T(8,128)} %copy-done.26, f32[4,3,2,32,256]{4,3,2,1,0:T(8,128)} %copy-done.2, ...), custom_call_target="tpu_custom_call" | custom-call | tf_op jit(solution)/shard_map/solve_1/pallas_call | solution.py:189
  106.1 4.5 %collective-permute-done.11.refs_2_ = f32[128,128]{1,0:T(8,128)S(1)} collective-permute-done((f32[128,128]{1,0:T(8,128)}, f32[128,128]{1,0:T(8,128)S(1)}, u32[]{:S(2)}, u32[]{:S(2)}) %collective-permute-start.11) | collective-permute-done | bytes 65568 | tf_op jit(solution)/shard_map/ppermute | solution.py:66
  111.2 3.3 %update_2.1 = (f32[128,128]{1,0:T(8,128)}, f32[128,128]{1,0:T(8,128)}, f32[128,128]{1,0:T(8,128)}) custom-call(s32[5]{0:T(128)} %stack.86.where_ref, f32[128,128]{1,0:T(8,128)} %get-tuple-element.49.refs_0_, f32[128,128]{1,0:T(8,128)} %get-tuple-element.55.refs_1_, f32[128,128]{1,0:T(8,128)} %copy-done.12, f32[4,3,2,32,256]{4,3,2,1,0:T(8,128)} %copy-done.2, ...), custom_call_target="tpu_custom_call" | custom-call | tf_op jit(solution)/shard_map/update_2/pallas_call | solution.py:189
  114.7 4.3 %collective-permute-done.16 = f32[128,128]{1,0:T(8,128)S(1)} collective-permute-done((f32[128,128]{1,0:T(8,128)}, f32[128,128]{1,0:T(8,128)S(1)}, u32[]{:S(2)}, u32[]{:S(2)}) %collective-permute-start.16) | collective-permute-done | bytes 65568 | tf_op jit(solution)/shard_map/ppermute | solution.py:66
  119.9 5.0 %collective-permute-start.17 = (f32[128,128]{1,0:T(8,128)S(1)}, f32[128,128]{1,0:T(8,128)S(1)}, u32[]{:S(2)}, u32[]{:S(2)}) collective-permute-start(f32[128,128]{1,0:T(8,128)S(1)} %add.17.refs_1_), channel_id=1, source_target_pairs={{0,1},{1,0},{2,3},{3,2},{4,5},{5,4},{6,7},{7,6},{8,9},{9,8},{10,11... | collective-permute-start | bytes 196616 | tf_op jit(solution)/shard_map/ppermute | solution.py:66
  124.9 1.1 copy-done.1
  126.0 3.3 %update_3.1 = (f32[128,128]{1,0:T(8,128)}, f32[128,128]{1,0:T(8,128)}) custom-call(s32[5]{0:T(128)} %stack.86.where_ref, f32[128,128]{1,0:T(8,128)} %get-tuple-element.49.refs_0_, f32[128,128]{1,0:T(8,128)} %get-tuple-element.69.refs_1_, f32[4,5,2,32,256]{4,3,2,1,0:T(8,128)} %copy-done, f32[4,5,2,32,256]{4,3,2,1,0:T(8,128)} %copy-done.1), custom_call_target="tpu_custom_call" | custom-call | tf_op jit(solution)/shard_map/update_3/pallas_call | solution.py:189
  130.6 3.1 %solve_2.1 = (f32[128,128]{1,0:T(8,128)}, f32[128,128]{1,0:T(8,128)}) custom-call(s32[5]{0:T(128)} %stack.86.where_ref, f32[128,128]{1,0:T(8,128)} %get-tuple-element.61.refs_0_, f32[128,128]{1,0:T(8,128)} %copy-done.11, f32[128,128]{1,0:T(8,128)} %copy-done.21, f32[4,5,2,32,256]{4,3,2,1,0:T(8,128)} %copy-done, f32[4,5,2,32,256]{4,3,2,1,0:T(8,128)} %copy-done.1), custom_call_target="tpu_custom_call" | custom-call | tf_op jit(solution)/shard_map/solve_2/pallas_call | solution.py:189
  133.7 1.4 collective-permute-start.21
  135.2 3.1 %collective-permute-done.21.refs_1_ = f32[128,128]{1,0:T(8,128)S(1)} collective-permute-done((f32[128,128]{1,0:T(8,128)}, f32[128,128]{1,0:T(8,128)S(1)}, u32[]{:S(2)}, u32[]{:S(2)}) %collective-permute-start.21) | collective-permute-done | bytes 65568 | tf_op jit(solution)/shard_map/ppermute | solution.py:66
  138.9 3.1 %update_32.1 = (f32[128,128]{1,0:T(8,128)}, f32[128,128]{1,0:T(8,128)}, f32[128,128]{1,0:T(8,128)}) custom-call(s32[5]{0:T(128)} %stack.86.where_ref, f32[128,128]{1,0:T(8,128)} %get-tuple-element.65.refs_0_, f32[128,128]{1,0:T(8,128)} %copy-done.20, f32[4,5,2,32,256]{4,3,2,1,0:T(8,128)} %copy-done, f32[4,5,2,32,256]{4,3,2,1,0:T(8,128)} %copy-done.1), custom_call_target="tpu_custom_call" | custom-call | tf_op jit(solution)/shard_map/update_32/pallas_call | solution.py:189
  142.0 1.4 collective-permute-start.24
  143.4 3.2 %collective-permute-done.24.refs_4_ = f32[128,128]{1,0:T(8,128)S(1)} collective-permute-done((f32[128,128]{1,0:T(8,128)}, f32[128,128]{1,0:T(8,128)S(1)}, u32[]{:S(2)}, u32[]{:S(2)}) %collective-permute-start.24) | collective-permute-done | bytes 65568 | tf_op jit(solution)/shard_map/ppermute | solution.py:66
  147.2 3.1 %solve_3.1 = (f32[128,128]{1,0:T(8,128)}, f32[128,128]{1,0:T(8,128)}) custom-call(s32[5]{0:T(128)} %stack.86.where_ref, f32[128,128]{1,0:T(8,128)} %get-tuple-element.68.refs_0_, f32[128,128]{1,0:T(8,128)} %copy-done.10, f32[128,128]{1,0:T(8,128)} %copy-done.18, f32[128,128]{1,0:T(8,128)} %get-tuple-element.72.refs_3_, f32[128,128]{1,0:T(8,128)} %copy-done.22, ...), custom_call_target="tpu_custom_call" | custom-call | tf_op jit(solution)/shard_map/solve_3/pallas_call | solution.py:189
  150.3 1.4 collective-permute-start.25
  151.7 1.7 lay_leaf.1
  154.8 2.9 %collective-permute-start.14 = (f32[2,32,128]{2,1,0:T(8,128)}, f32[2,32,128]{2,1,0:T(8,128)S(1)}, u32[]{:S(2)}, u32[]{:S(2)}) collective-permute-start(f32[2,32,128]{2,1,0:T(8,128)} %get-tuple-element.60), channel_id=1, source_target_pairs={{0,10},{1,11},{2,8},{3,9},{4,14},{5,15},{6,12},{7,13},{8,2},{9,3},... | collective-permute-start | bytes 98312 | tf_op jit(solution)/shard_map/ppermute | solution.py:66
  158.3 1.7 lay_root.1
  160.0 1.4 collective-permute-start.26
  162.9 2.9 %collective-permute-start.29 = (f32[2,32,128]{2,1,0:T(8,128)}, f32[2,32,128]{2,1,0:T(8,128)S(1)}, u32[]{:S(2)}, u32[]{:S(2)}) collective-permute-start(f32[2,32,128]{2,1,0:T(8,128)} %get-tuple-element.79), channel_id=1, source_target_pairs={{0,10},{1,27},{2,8},{3,25},{4,14},{5,31},{6,12},{7,29},{8,2},{9,19... | collective-permute-start | bytes 98312 | tf_op jit(solution)/shard_map/ppermute | solution.py:66
  166.6 1.4 collective-permute-start.15
  169.0 2.7 %collective-permute-done.15.other_ref = f32[4,2,32,128]{3,2,1,0:T(8,128)S(1)} collective-permute-done((f32[4,2,32,128]{3,2,1,0:T(8,128)S(1)}, f32[4,2,32,128]{3,2,1,0:T(8,128)S(1)}, u32[]{:S(2)}, u32[]{:S(2)}) %collective-permute-start.15) | collective-permute-done | bytes 131104 | tf_op jit(solution)/shard_map/ppermute | solution.py:66
  172.3 1.8 %join_leaf.1 = f32[2,2,32,512]{3,2,1,0:T(8,128)} custom-call(s32[5]{0:T(128)} %stack.86.where_ref, f32[4,2,32,128]{3,2,1,0:T(8,128)} %copy-done.7, f32[4,2,32,128]{3,2,1,0:T(8,128)} %copy-done.14), custom_call_target="tpu_custom_call" | custom-call | tf_op jit(solution)/shard_map/join_leaf/pallas_call | solution.py:292
  174.9 1.8 %join_root.1 = f32[2,2,32,512]{3,2,1,0:T(8,128)} custom-call(s32[5]{0:T(128)} %stack.86.where_ref, f32[4,2,32,128]{3,2,1,0:T(8,128)} %get-tuple-element.84.near_ref, f32[4,2,32,128]{3,2,1,0:T(8,128)} %get-tuple-element.83.other_ref), custom_call_target="tpu_custom_call" | custom-call | tf_op jit(solution)/shard_map/join_root/pallas_call | solution.py:292
  (108 shorter events, 17.3 us)
Async XLA Ops:
  2.8 10.7 %copy-start.13 = (f32[2,2,32,256]{3,2,1,0:T(8,128)S(1)}, f32[2,2,32,256]{3,2,1,0:T(8,128)}, u32[]{:S(2)}) copy-start(f32[2,2,32,256]{3,2,1,0:T(8,128)} %param.10) | copy-start | bytes 393220
  2.8 10.7 %copy-start.16 = (f32[2,32,256]{2,1,0:T(8,128)S(1)}, f32[2,32,256]{2,1,0:T(8,128)}, u32[]{:S(2)}) copy-start(f32[2,32,256]{2,1,0:T(8,128)} %param.12) | copy-start | bytes 196612
  3.0 10.4 %collective-permute-start.3 = (f32[2,2,32,256]{3,2,1,0:T(8,128)S(1)}, f32[2,2,32,256]{3,2,1,0:T(8,128)S(1)}, u32[]{:S(2)}, u32[]{:S(2)}) collective-permute-start(f32[2,2,32,256]{3,2,1,0:T(8,128)S(1)} %get-tuple-element.86), channel_id=1, source_target_pairs={{0,8},{1,9},{2,10},{3,11},{4,12},{5,13},{6,14},{7,15},{8,0},{9,1},... | collective-permute-start | bytes 393224 | tf_op jit(solution)/shard_map/ppermute | solution.py:66
  7.2 34.5 %copy-start.3 = (f32[3,2,32,256]{3,2,1,0:T(8,128)}, f32[3,2,32,256]{3,2,1,0:T(8,128)S(1)}, u32[]{:S(2)}) copy-start(f32[3,2,32,256]{3,2,1,0:T(8,128)S(1)} %pad_maximum_fusion.7) | copy-start | bytes 589828
  13.4 39.1 %copy-start.8 = (f32[2,2,32,256]{3,2,1,0:T(8,128)}, f32[2,2,32,256]{3,2,1,0:T(8,128)S(1)}, u32[]{:S(2)}) copy-start(f32[2,2,32,256]{3,2,1,0:T(8,128)S(1)} %collective-permute-done.3) | copy-start | bytes 393220
  13.4 11.2 %collective-permute-start.8 = (f32[3,2,32,256]{3,2,1,0:T(8,128)S(1)}, f32[3,2,32,256]{3,2,1,0:T(8,128)S(1)}, u32[]{:S(2)}, u32[]{:S(2)}) collective-permute-start(f32[3,2,32,256]{3,2,1,0:T(8,128)S(1)} %pad_maximum_fusion.7), channel_id=1, source_target_pairs={{0,8},{1,9},{2,10},{3,11},{4,12},{5,13},{6,14},{7,15},{8,0},{9,1},... | collective-permute-start | bytes 589832 | tf_op jit(solution)/shard_map/ppermute | solution.py:66
  24.6 18.2 %copy-start.5 = (f32[3,2,32,256]{3,2,1,0:T(8,128)}, f32[3,2,32,256]{3,2,1,0:T(8,128)S(1)}, u32[]{:S(2)}) copy-start(f32[3,2,32,256]{3,2,1,0:T(8,128)S(1)} %collective-permute-done.8) | copy-start | bytes 589828
  24.6 16.0 %collective-permute-start.18 = (f32[5,2,32,256]{3,2,1,0:T(8,128)S(1)}, f32[5,2,32,256]{3,2,1,0:T(8,128)S(1)}, u32[]{:S(2)}, u32[]{:S(2)}) collective-permute-start(f32[5,2,32,256]{3,2,1,0:T(8,128)S(1)} %pad_maximum_fusion.5), channel_id=1, source_target_pairs={{0,8},{1,9},{2,10},{3,11},{4,12},{5,13},{6,14},{7,15},{8,0},{9,1},... | collective-permute-start | bytes 983048 | tf_op jit(solution)/shard_map/ppermute | solution.py:66
  40.6 10.7 %collective-permute-start.19 = (f32[2,5,2,32,256]{4,3,2,1,0:T(8,128)S(1)}, f32[2,5,2,32,256]{4,3,2,1,0:T(8,128)S(1)}, u32[]{:S(2)}, u32[]{:S(2)}) collective-permute-start(f32[2,5,2,32,256]{4,3,2,1,0:T(8,128)S(1)} %pad_maximum_fusion.2), channel_id=1, source_target_pairs={{0,2},{1,17},{2,0},{3,19},{4,6},{5,21},{6,4},{7,23},{8,10},{9,25},... | collective-permute-start | bytes 1966088 | tf_op jit(solution)/shard_map/ppermute | solution.py:66
  41.7 16.1 %collective-permute-start.9 = (f32[2,3,2,32,256]{4,3,2,1,0:T(8,128)S(1)}, f32[2,3,2,32,256]{4,3,2,1,0:T(8,128)S(1)}, u32[]{:S(2)}, u32[]{:S(2)}) collective-permute-start(f32[2,3,2,32,256]{4,3,2,1,0:T(8,128)S(1)} %pad_maximum_fusion.4), channel_id=1, source_target_pairs={{0,2},{1,17},{2,0},{3,19},{4,6},{5,21},{6,4},{7,23},{8,10},{9,25},... | collective-permute-start | bytes 1179656 | tf_op jit(solution)/shard_map/ppermute | solution.py:66
  42.8 15.1 %copy-start.4 = (f32[3,2,32,256]{3,2,1,0:T(8,128)S(1)}, f32[3,2,32,256]{3,2,1,0:T(8,128)}, u32[]{:S(2)}) copy-start(f32[3,2,32,256]{3,2,1,0:T(8,128)} %copy-done.3) | copy-start | bytes 589828
  51.2 6.6 %copy-start.6 = (f32[3,2,32,256]{3,2,1,0:T(8,128)S(1)}, f32[3,2,32,256]{3,2,1,0:T(8,128)}, u32[]{:S(2)}) copy-start(f32[3,2,32,256]{3,2,1,0:T(8,128)} %copy-done.5) | copy-start | bytes 589828
  51.4 13.0 %copy-start = (f32[4,5,2,32,256]{4,3,2,1,0:T(8,128)}, f32[4,5,2,32,256]{4,3,2,1,0:T(8,128)S(1)}, u32[]{:S(2)}) copy-start(f32[4,5,2,32,256]{4,3,2,1,0:T(8,128)S(1)} %pad_maximum_fusion.refs_3_.refs_2_.refs_5_) | copy-start | bytes 3932164
  51.4 73.5 %collective-permute-start.20 = (f32[4,5,2,32,256]{4,3,2,1,0:T(8,128)S(1)}, f32[4,5,2,32,256]{4,3,2,1,0:T(8,128)S(1)}, u32[]{:S(2)}, u32[]{:S(2)}) collective-permute-start(f32[4,5,2,32,256]{4,3,2,1,0:T(8,128)S(1)} %pad_maximum_fusion.refs_3_.refs_2_.refs_5_), channel_id=1, source_target_pairs={{0,16},{1,3},{2,18},{3,1},{4,20},{5,7},{6,22},{7,5},{8,24},{9,11},... | collective-permute-start | bytes 3932168 | tf_op jit(solution)/shard_map/ppermute | solution.py:66
  52.5 11.0 %copy-start.9 = (f32[2,2,32,256]{3,2,1,0:T(8,128)S(1)}, f32[2,2,32,256]{3,2,1,0:T(8,128)}, u32[]{:S(2)}) copy-start(f32[2,2,32,256]{3,2,1,0:T(8,128)} %copy-done.8) | copy-start | bytes 393220
  52.5 11.0 %collective-permute-start.4 = (f32[2,2,2,32,256]{4,3,2,1,0:T(8,128)S(1)}, f32[2,2,2,32,256]{4,3,2,1,0:T(8,128)S(1)}, u32[]{:S(2)}, u32[]{:S(2)}) collective-permute-start(f32[2,2,2,32,256]{4,3,2,1,0:T(8,128)S(1)} %pad_maximum_fusion.6), channel_id=1, source_target_pairs={{0,2},{1,17},{2,0},{3,19},{4,6},{5,21},{6,4},{7,23},{8,10},{9,25},... | collective-permute-start | bytes 786440 | tf_op jit(solution)/shard_map/ppermute | solution.py:66
  57.9 30.4 %copy-start.2 = (f32[4,3,2,32,256]{4,3,2,1,0:T(8,128)}, f32[4,3,2,32,256]{4,3,2,1,0:T(8,128)S(1)}, u32[]{:S(2)}) copy-start(f32[4,3,2,32,256]{4,3,2,1,0:T(8,128)S(1)} %pad_maximum_fusion.1.refs_3_) | copy-start | bytes 2359300
  57.9 44.4 %collective-permute-start.10 = (f32[4,3,2,32,256]{4,3,2,1,0:T(8,128)S(1)}, f32[4,3,2,32,256]{4,3,2,1,0:T(8,128)}, u32[]{:S(2)}, u32[]{:S(2)}) collective-permute-start(f32[4,3,2,32,256]{4,3,2,1,0:T(8,128)S(1)} %pad_maximum_fusion.1.refs_3_), channel_id=1, source_target_pairs={{0,16},{1,3},{2,18},{3,1},{4,20},{5,7},{6,22},{7,5},{8,24},{9,11},... | collective-permute-start | bytes 2359304 | tf_op jit(solution)/shard_map/ppermute | solution.py:66
  64.3 21.0 %collective-permute-start.5 = (f32[4,2,2,32,256]{4,3,2,1,0:T(8,128)}, f32[4,2,2,32,256]{4,3,2,1,0:T(8,128)}, u32[]{:S(2)}, u32[]{:S(2)}) collective-permute-start(f32[4,2,2,32,256]{4,3,2,1,0:T(8,128)} %pad_maximum_fusion.3.refs_1_.refs_2_), channel_id=1, source_target_pairs={{0,16},{1,3},{2,18},{3,1},{4,20},{5,7},{6,22},{7,5},{8,24},{9,11},... | collective-permute-start | bytes 1572872 | tf_op jit(solution)/shard_map/ppermute | solution.py:66
  68.1 5.2 %collective-permute-start = (f32[4,32,128]{2,1,0:T(8,128)}, f32[4,32,128]{2,1,0:T(8,128)S(1)}, u32[]{:S(2)}, u32[]{:S(2)}) collective-permute-start(f32[4,32,128]{2,1,0:T(8,128)} %get-tuple-element.42), channel_id=1, source_target_pairs={{0,2},{1,3},{2,0},{3,1},{4,6},{5,7},{6,4},{7,5},{8,10},{9,11},{10,... | collective-permute-start | bytes 196616 | tf_op jit(solution)/shard_map/ppermute | solution.py:66
  69.6 5.4 %collective-permute-start.1 = (f32[4,32,128]{2,1,0:T(8,128)}, f32[4,32,128]{2,1,0:T(8,128)S(1)}, u32[]{:S(2)}, u32[]{:S(2)}) collective-permute-start(f32[4,32,128]{2,1,0:T(8,128)} %get-tuple-element.43), channel_id=1, source_target_pairs={{0,8},{1,9},{2,10},{3,11},{4,12},{5,13},{6,14},{7,15},{8,0},{9,1},... | collective-permute-start | bytes 196616 | tf_op jit(solution)/shard_map/ppermute | solution.py:66
  73.3 6.5 %copy-start.24 = (f32[4,32,128]{2,1,0:T(8,128)}, f32[4,32,128]{2,1,0:T(8,128)S(1)}, u32[]{:S(2)}) copy-start(f32[4,32,128]{2,1,0:T(8,128)S(1)} %collective-permute-done.refs_1_) | copy-start | bytes 196612
  73.3 6.5 %collective-permute-start.2 = (f32[4,32,128]{2,1,0:T(8,128)}, f32[4,32,128]{2,1,0:T(8,128)}, u32[]{:S(2)}, u32[]{:S(2)}) collective-permute-start(f32[4,32,128]{2,1,0:T(8,128)} %get-tuple-element.44), channel_id=1, source_target_pairs={{0,10},{1,11},{2,8},{3,9},{4,14},{5,15},{6,12},{7,13},{8,2},{9,3},... | collective-permute-start | bytes 196616 | tf_op jit(solution)/shard_map/ppermute | solution.py:66
  75.0 4.8 %copy-start.25 = (f32[4,32,128]{2,1,0:T(8,128)}, f32[4,32,128]{2,1,0:T(8,128)S(1)}, u32[]{:S(2)}) copy-start(f32[4,32,128]{2,1,0:T(8,128)S(1)} %collective-permute-done.1.refs_2_) | copy-start | bytes 196612
  88.4 5.2 %collective-permute-start.6 = (f32[128,128]{1,0:T(8,128)}, f32[128,128]{1,0:T(8,128)S(1)}, u32[]{:S(2)}, u32[]{:S(2)}) collective-permute-start(f32[128,128]{1,0:T(8,128)} %get-tuple-element.48), channel_id=1, source_target_pairs={{0,4},{1,5},{2,6},{3,7},{4,0},{5,1},{6,2},{7,3},{8,12},{9,13},{10,... | collective-permute-start | bytes 196616 | tf_op jit(solution)/shard_map/ppermute | solution.py:66
  97.3 5.1 %collective-permute-start.7 = (f32[128,128]{1,0:T(8,128)}, f32[128,128]{1,0:T(8,128)S(1)}, u32[]{:S(2)}, u32[]{:S(2)}) collective-permute-start(f32[128,128]{1,0:T(8,128)} %get-tuple-element.52), channel_id=1, source_target_pairs={{0,4},{1,5},{2,6},{3,7},{4,0},{5,1},{6,2},{7,3},{8,12},{9,13},{10,... | collective-permute-start | bytes 196616 | tf_op jit(solution)/shard_map/ppermute | solution.py:66
  106.0 4.5 %collective-permute-start.11 = (f32[128,128]{1,0:T(8,128)}, f32[128,128]{1,0:T(8,128)S(1)}, u32[]{:S(2)}, u32[]{:S(2)}) collective-permute-start(f32[128,128]{1,0:T(8,128)} %get-tuple-element.56), channel_id=1, source_target_pairs={{0,4},{1,5},{2,6},{3,7},{4,0},{5,1},{6,2},{7,3},{8,12},{9,13},{10,... | collective-permute-start | bytes 196616 | tf_op jit(solution)/shard_map/ppermute | solution.py:66
  114.5 4.5 %collective-permute-start.16 = (f32[128,128]{1,0:T(8,128)}, f32[128,128]{1,0:T(8,128)S(1)}, u32[]{:S(2)}, u32[]{:S(2)}) collective-permute-start(f32[128,128]{1,0:T(8,128)} %get-tuple-element.63), channel_id=1, source_target_pairs={{0,4},{1,5},{2,6},{3,7},{4,0},{5,1},{6,2},{7,3},{8,12},{9,13},{10,... | collective-permute-start | bytes 196616 | tf_op jit(solution)/shard_map/ppermute | solution.py:66
  119.9 10.1 %copy-start.11 = (f32[128,128]{1,0:T(8,128)}, f32[128,128]{1,0:T(8,128)S(1)}, u32[]{:S(2)}) copy-start(f32[128,128]{1,0:T(8,128)S(1)} %add.17.refs_1_) | copy-start | bytes 196612
  119.9 10.1 %collective-permute-start.17 = (f32[128,128]{1,0:T(8,128)S(1)}, f32[128,128]{1,0:T(8,128)S(1)}, u32[]{:S(2)}, u32[]{:S(2)}) collective-permute-start(f32[128,128]{1,0:T(8,128)S(1)} %add.17.refs_1_), channel_id=1, source_target_pairs={{0,1},{1,0},{2,3},{3,2},{4,5},{5,4},{6,7},{7,6},{8,9},{9,8},{10,11... | collective-permute-start | bytes 196616 | tf_op jit(solution)/shard_map/ppermute | solution.py:66
  129.2 5.9 %collective-permute-start.22 = (f32[128,128]{1,0:T(8,128)}, f32[128,128]{1,0:T(8,128)S(1)}, u32[]{:S(2)}, u32[]{:S(2)}) collective-permute-start(f32[128,128]{1,0:T(8,128)} %get-tuple-element.71), channel_id=1, source_target_pairs={{0,4},{1,5},{2,6},{3,7},{4,0},{5,1},{6,2},{7,3},{8,12},{9,13},{10,... | collective-permute-start | bytes 196616 | tf_op jit(solution)/shard_map/ppermute | solution.py:66
  130.6 4.5 %copy-start.19 = (f32[128,128]{1,0:T(8,128)S(1)}, f32[128,128]{1,0:T(8,128)}, u32[]{:S(2)}) copy-start(f32[128,128]{1,0:T(8,128)} %get-tuple-element.70) | copy-start | bytes 196612
  133.7 4.5 %collective-permute-start.21 = (f32[128,128]{1,0:T(8,128)}, f32[128,128]{1,0:T(8,128)S(1)}, u32[]{:S(2)}, u32[]{:S(2)}) collective-permute-start(f32[128,128]{1,0:T(8,128)} %get-tuple-element.66), channel_id=1, source_target_pairs={{0,4},{1,5},{2,6},{3,7},{4,0},{5,1},{6,2},{7,3},{8,12},{9,13},{10,... | collective-permute-start | bytes 196616 | tf_op jit(solution)/shard_map/ppermute | solution.py:66
  135.1 6.8 %copy-start.10 = (f32[128,128]{1,0:T(8,128)}, f32[128,128]{1,0:T(8,128)S(1)}, u32[]{:S(2)}) copy-start(f32[128,128]{1,0:T(8,128)S(1)} %add.18.refs_1_) | copy-start | bytes 196612
  135.1 8.2 %collective-permute-start.23 = (f32[128,128]{1,0:T(8,128)S(1)}, f32[128,128]{1,0:T(8,128)S(1)}, u32[]{:S(2)}, u32[]{:S(2)}) collective-permute-start(f32[128,128]{1,0:T(8,128)S(1)} %add.18.refs_1_), channel_id=1, source_target_pairs={{0,1},{1,0},{2,3},{3,2},{4,5},{5,4},{6,7},{7,6},{8,9},{9,8},{10,11... | collective-permute-start | bytes 196616 | tf_op jit(solution)/shard_map/ppermute | solution.py:66
  142.0 4.5 %collective-permute-start.24 = (f32[128,128]{1,0:T(8,128)}, f32[128,128]{1,0:T(8,128)S(1)}, u32[]{:S(2)}, u32[]{:S(2)}) collective-permute-start(f32[128,128]{1,0:T(8,128)} %get-tuple-element.73), channel_id=1, source_target_pairs={{0,4},{1,5},{2,6},{3,7},{4,0},{5,1},{6,2},{7,3},{8,12},{9,13},{10,... | collective-permute-start | bytes 196616 | tf_op jit(solution)/shard_map/ppermute | solution.py:66
  143.4 3.2 %copy-start.18 = (f32[128,128]{1,0:T(8,128)}, f32[128,128]{1,0:T(8,128)S(1)}, u32[]{:S(2)}) copy-start(f32[128,128]{1,0:T(8,128)S(1)} %collective-permute-done.23.refs_2_) | copy-start | bytes 196612
  150.3 7.4 %collective-permute-start.25 = (f32[128,128]{1,0:T(8,128)}, f32[128,128]{1,0:T(8,128)S(1)}, u32[]{:S(2)}, u32[]{:S(2)}) collective-permute-start(f32[128,128]{1,0:T(8,128)} %get-tuple-element.75), channel_id=1, source_target_pairs={{0,4},{1,5},{2,6},{3,7},{4,0},{5,1},{6,2},{7,3},{8,12},{9,13},{10,... | collective-permute-start | bytes 196616 | tf_op jit(solution)/shard_map/ppermute | solution.py:66
  153.3 8.7 %collective-permute-start.12 = (f32[2,32,128]{2,1,0:T(8,128)}, f32[2,32,128]{2,1,0:T(8,128)S(1)}, u32[]{:S(2)}, u32[]{:S(2)}) collective-permute-start(f32[2,32,128]{2,1,0:T(8,128)} %get-tuple-element.58), channel_id=1, source_target_pairs={{0,2},{1,3},{2,0},{3,1},{4,6},{5,7},{6,4},{7,5},{8,10},{9,11},{10,... | collective-permute-start | bytes 98312 | tf_op jit(solution)/shard_map/ppermute | solution.py:66
  154.0 9.0 %collective-permute-start.13 = (f32[2,32,128]{2,1,0:T(8,128)}, f32[2,32,128]{2,1,0:T(8,128)S(1)}, u32[]{:S(2)}, u32[]{:S(2)}) collective-permute-start(f32[2,32,128]{2,1,0:T(8,128)} %get-tuple-element.59), channel_id=1, source_target_pairs={{0,8},{1,9},{2,10},{3,11},{4,12},{5,13},{6,14},{7,15},{8,0},{9,1},... | collective-permute-start | bytes 98312 | tf_op jit(solution)/shard_map/ppermute | solution.py:66
  154.8 11.0 %collective-permute-start.14 = (f32[2,32,128]{2,1,0:T(8,128)}, f32[2,32,128]{2,1,0:T(8,128)S(1)}, u32[]{:S(2)}, u32[]{:S(2)}) collective-permute-start(f32[2,32,128]{2,1,0:T(8,128)} %get-tuple-element.60), channel_id=1, source_target_pairs={{0,10},{1,11},{2,8},{3,9},{4,14},{5,15},{6,12},{7,13},{8,2},{9,3},... | collective-permute-start | bytes 98312 | tf_op jit(solution)/shard_map/ppermute | solution.py:66
  160.0 8.0 %collective-permute-start.26 = (f32[2,32,128]{2,1,0:T(8,128)}, f32[2,32,128]{2,1,0:T(8,128)S(1)}, u32[]{:S(2)}, u32[]{:S(2)}) collective-permute-start(f32[2,32,128]{2,1,0:T(8,128)} %get-tuple-element.76), channel_id=1, source_target_pairs={{0,0},{1,17},{2,2},{3,19},{4,4},{5,21},{6,6},{7,23},{8,8},{9,25},{... | collective-permute-start | bytes 98312 | tf_op jit(solution)/shard_map/ppermute | solution.py:66
  161.4 6.6 %collective-permute-start.27 = (f32[2,32,128]{2,1,0:T(8,128)}, f32[2,32,128]{2,1,0:T(8,128)S(1)}, u32[]{:S(2)}, u32[]{:S(2)}) collective-permute-start(f32[2,32,128]{2,1,0:T(8,128)} %get-tuple-element.77), channel_id=1, source_target_pairs={{0,2},{1,19},{2,0},{3,17},{4,6},{5,23},{6,4},{7,21},{8,10},{9,27},... | collective-permute-start | bytes 98312 | tf_op jit(solution)/shard_map/ppermute | solution.py:66
  162.0 6.0 %collective-permute-start.28 = (f32[2,32,128]{2,1,0:T(8,128)}, f32[2,32,128]{2,1,0:T(8,128)S(1)}, u32[]{:S(2)}, u32[]{:S(2)}) collective-permute-start(f32[2,32,128]{2,1,0:T(8,128)} %get-tuple-element.78), channel_id=1, source_target_pairs={{0,8},{1,25},{2,10},{3,27},{4,12},{5,29},{6,14},{7,31},{8,0},{9,17... | collective-permute-start | bytes 98312 | tf_op jit(solution)/shard_map/ppermute | solution.py:66
  162.9 5.9 %collective-permute-start.29 = (f32[2,32,128]{2,1,0:T(8,128)}, f32[2,32,128]{2,1,0:T(8,128)S(1)}, u32[]{:S(2)}, u32[]{:S(2)}) collective-permute-start(f32[2,32,128]{2,1,0:T(8,128)} %get-tuple-element.79), channel_id=1, source_target_pairs={{0,10},{1,27},{2,8},{3,25},{4,14},{5,31},{6,12},{7,29},{8,2},{9,19... | collective-permute-start | bytes 98312 | tf_op jit(solution)/shard_map/ppermute | solution.py:66
  166.6 5.0 %copy-start.7 = (f32[4,2,32,128]{3,2,1,0:T(8,128)}, f32[4,2,32,128]{3,2,1,0:T(8,128)S(1)}, u32[]{:S(2)}) copy-start(f32[4,2,32,128]{3,2,1,0:T(8,128)S(1)} %pad_maximum_fusion.9.near_ref) | copy-start | bytes 393220
  166.6 5.0 %collective-permute-start.15 = (f32[4,2,32,128]{3,2,1,0:T(8,128)S(1)}, f32[4,2,32,128]{3,2,1,0:T(8,128)S(1)}, u32[]{:S(2)}, u32[]{:S(2)}) collective-permute-start(f32[4,2,32,128]{3,2,1,0:T(8,128)S(1)} %pad_maximum_fusion.9.near_ref), channel_id=1, source_target_pairs={{0,16},{1,17},{2,18},{3,19},{4,20},{5,21},{6,22},{7,23},{8,24},{9,... | collective-permute-start | bytes 393224 | tf_op jit(solution)/shard_map/ppermute | solution.py:66
  168.9 5.2 %collective-permute-start.30 = (f32[4,2,32,128]{3,2,1,0:T(8,128)S(1)}, f32[4,2,32,128]{3,2,1,0:T(8,128)S(1)}, u32[]{:S(2)}, u32[]{:S(2)}) collective-permute-start(f32[4,2,32,128]{3,2,1,0:T(8,128)S(1)} %pad_maximum_fusion.10), channel_id=1, source_target_pairs={{0,1},{1,0},{2,3},{3,2},{4,5},{5,4},{6,7},{7,6},{8,9},{9,8},{10,11... | collective-permute-start | bytes 393224 | tf_op jit(solution)/shard_map/ppermute | solution.py:66
  (10 other events, 8.3 us)

commit v2 on v0

v2 whole, which is shorter than its diff:
```python
import functools

import jax
import jax.numpy as jnp
from jax import lax
from jax.experimental import pallas as pl
from jax.experimental.pallas import tpu as pltpu
from jax.sharding import PartitionSpec as P

BLK = 128
AXES = ("row", "col", "leaf")
F32 = jnp.float32
BF16 = jnp.bfloat16


def apply_rows(block, vector):
    block = block.reshape(-1, block.shape[-1])
    vector = vector.reshape(-1, vector.shape[-1])
    term = lax.dot_general(
        block,
        vector,
        (((0,), (0,)), ((), ())),
        precision=lax.Precision.HIGHEST,
        preferred_element_type=F32,
    )
    owned = lax.psum_scatter(term, "col", scatter_dimension=0, tiled=True)
    return lax.all_gather(owned[None], "row", axis=0, tiled=True)


def masked(leaf_blocks, pattern):
    local = leaf_blocks[0]
    shaped = local.reshape(local.shape[:3] + (local.shape[3] // BLK, BLK))
    weights = pattern[0].astype(F32).transpose(0, 2, 1)[:, None, :, :, None]
    return (shaped * weights).reshape(local.shape)


def general(leaf_rhs, root_rhs, leaf_inverses, root_inverses, leaf_blocks, root_block, pattern):
    blocks = masked(leaf_blocks, pattern)
    first = apply_rows(leaf_inverses[0, 0], leaf_rhs[0, 0])
    second = apply_rows(leaf_inverses[0, 1], leaf_rhs[0, 1] - apply_rows(blocks[0], first))
    upper_two = apply_rows(blocks[1], first) + apply_rows(blocks[2], second)
    upper_three = apply_rows(blocks[3], first) + apply_rows(blocks[4], second)
    upper_two, upper_three = lax.psum((upper_two, upper_three), "leaf")
    third = apply_rows(root_inverses[0], root_rhs[0] - upper_two)
    fourth = apply_rows(root_inverses[1], root_rhs[1] - upper_three - apply_rows(root_block, third))
    return (jnp.stack([first, second])[None], jnp.stack([third, fourth]))


def pairs(dest):
    out = []
    for r in range(2):
        for zh in range(2):
            for zl in range(2):
                for x in range(2):
                    for l in range(2):
                        d = dest(r, zh, zl, x, l)
                        if d is None:
                            continue
                        s = (r * 8 + zh * 4 + zl * 2 + x) * 2 + l
                        e = (d[0] * 8 + d[1] * 4 + d[2] * 2 + d[3]) * 2 + d[4]
                        out.append((s, e))
    return out


def send(value, dest):
    return lax.ppermute(value, AXES, pairs(dest))


def to_far(r, zh, zl, x, l):
    return r, zh ^ 1, zl, x, l


def to_second(r, zh, zl, x, l):
    return (r, zh, zl, x ^ 1, l) if l == 0 else (r ^ 1, zh, zl, x, l)


def to_third(r, zh, zl, x, l):
    return (r ^ 1, zh, zl, x, l) if l == 0 else (r, zh, zl, x ^ 1, l)


def to_pair(r, zh, zl, x, l):
    return r, zh, zl ^ 1, x, l


def to_core(r, zh, zl, x, l):
    return r, zh, zl, x, l ^ 1


def to_pair_core(r, zh, zl, x, l):
    return r, zh, zl ^ 1, x, l ^ 1


def to_row(r, zh, zl, x, l):
    return r ^ 1, zh, zl, x, l


def to_group(b1, b2):
    return lambda r, zh, zl, x, l: (r, zh ^ b1, zl, x ^ b2, l)


def to_group_by_core(b1, b2):
    return lambda r, zh, zl, x, l: (r ^ l, zh ^ b1, zl, x ^ b2, l)


def after(value, *others):
    return lax.optimization_barrier((value,) + others)[0]


def vmem():
    return pl.BlockSpec(memory_space=pltpu.VMEM)


def anywhere():
    return pl.BlockSpec(memory_space=pl.ANY)


def smem():
    return pl.BlockSpec(memory_space=pltpu.SMEM)


def shaped(*dims):
    return jax.ShapeDtypeStruct(dims, F32)


def lanes_low():
    return lax.broadcasted_iota(jnp.int32, (1, 128), 1) < 64


def swap_lanes(one, two):
    low = lanes_low()
    even = jnp.where(low, one, pltpu.roll(two, 64, one.ndim - 1))
    odd = jnp.where(low, pltpu.roll(one, 64, one.ndim - 1), two)
    return even, odd


def split(value):
    high = value.astype(BF16)
    return high, (value - high.astype(F32)).astype(BF16)


def dot3(left, right):
    lh, ll = left
    rh, rl = right
    whole = jnp.dot(lh, rl, preferred_element_type=F32)
    whole += jnp.dot(ll, rh, preferred_element_type=F32)
    return whole + jnp.dot(lh, rh, preferred_element_type=F32)


def flat(value):
    return jnp.concatenate([value[:64], value[64:]], axis=1)


def rows_kernel(where_ref, leaf_ref, root_ref, first_ref, keep_ref, out_ref):
    zl = where_ref[2]
    for m in range(4):
        source = leaf_ref if m < 2 else root_ref
        for a in range(2):
            even, odd = swap_lanes(source[m % 2, a, :, :128], source[m % 2, a, :, 128:])
            mine = jnp.where(zl == 0, even, odd)
            theirs = jnp.where(zl == 0, odd, even)
            keep_ref[m, a] = mine
            if m == 0:
                first_ref[a] = theirs
            else:
                out_ref[m - 1, a] = theirs


def rows(where, leaf, root):
    return pl.pallas_call(
        rows_kernel,
        out_shape=[shaped(2, 32, 128), shaped(4, 2, 32, 128), shaped(3, 2, 32, 128)],
        in_specs=[smem(), vmem(), vmem()],
        out_specs=[vmem()] * 3,
        name="split_rows",
    )(where, leaf, root)


def mask_kernel(tiles_ref, blocks_ref, out_ref):
    for m in range(5):
        for t in range(2):
            weight = tiles_ref[m, t].astype(F32)
            for a in range(2):
                out_ref[m, t, a] = blocks_ref[m, a, :, t * 128 : t * 128 + 128] * weight


def mask(tiles, blocks):
    return pl.pallas_call(
        mask_kernel,
        out_shape=shaped(5, 2, 2, 32, 128),
        in_specs=[smem(), vmem()],
        out_specs=vmem(),
        name="mask_blocks",
    )(tiles, blocks)


def fetch(where_ref, near, far, m, dest, sems):
    r, zh, x, l = where_ref[0], where_ref[1], where_ref[3], where_ref[4]
    copies = []
    for b3, source in enumerate((near, far)):
        for b2 in range(2):
            for b1 in range(2):
                rr = r ^ jnp.where(l == 0, b3, b2)
                xx = x ^ jnp.where(l == 0, b2, b3)
                copy = pltpu.make_async_copy(
                    source.at[b2 * 2 + b1, m],
                    dest(rr, zh ^ b1, xx),
                    sems.at[b3 * 4 + b2 * 2 + b1],
                )
                copy.start()
                copies.append(copy)
    return copies


def solve(inverse, vector, copies):
    for copy in copies:
        copy.wait()
    left = split(flat(vector))
    parts = [dot3(left, split(inverse[a].reshape(512, 128))) for a in range(2)]
    return jnp.concatenate(parts, axis=0)


def update(held, terms, copies):
    sums = [None, None]
    for t, vector in enumerate(terms):
        for copy in copies[t]:
            copy.wait()
        left = split(flat(vector))
        for a in range(2):
            right = jnp.concatenate(
                [held[t, a, 0].reshape(256, 128), held[t, a, 1].reshape(256, 128)], axis=1
            )
            part = dot3(left, split(right))
            sums[a] = part if sums[a] is None else sums[a] + part
    return jnp.concatenate(sums, axis=0)


def link_kernel(plan, where_ref, *refs):
    nvec, nchunk = plan["nvec"], plan["nchunk"]
    vecs = refs[:nvec]
    chunks = refs[nvec : nvec + 2 * nchunk]
    rest = refs[nvec + 2 * nchunk :]
    outs, (inverse, held, sems) = rest[:2], rest[2:]
    chunk, m = plan["inverse"]
    solving = fetch(
        where_ref,
        chunks[2 * chunk],
        chunks[2 * chunk + 1],
        m,
        lambda r, zh, x: inverse.at[r, :, zh, :, x],
        sems.at[0],
    )
    updating = [
        fetch(
            where_ref,
            chunks[2 * chunk],
            chunks[2 * chunk + 1],
            m,
            lambda r, zh, x, t=t: held.at[t, r, :, :, zh, x],
            sems.at[t + 1],
        )
        for t, (chunk, m) in enumerate(plan["blocks"])
    ]
    values = [v[...] for v in vecs]
    solved = solve(inverse, plan["input"](values), solving)
    outs[0][...] = update(held, plan["terms"](values, solved, where_ref[4]), updating)
    outs[1][...] = solved


def link(name, where, vecs, chunks, plan):
    arrays = [array for pair in chunks for array in pair]
    nblocks = len(plan["blocks"])
    plan = dict(plan, nvec=len(vecs), nchunk=len(chunks))
    last = nblocks == 0
    scratch = [pltpu.VMEM((4, 2, 32, 128), F32)] if last else []
    outs = [shaped(2, 32, 128)] * 4 if last else [shaped(128, 256), shaped(128, 128)]
    return pl.pallas_call(
        functools.partial(link_kernel, plan) if not last else functools.partial(last_kernel, plan),
        out_shape=outs,
        in_specs=[smem()] + [vmem()] * len(vecs) + [anywhere()] * len(arrays),
        out_specs=[vmem()] * len(outs),
        scratch_shapes=scratch
        + [
            pltpu.VMEM((2, 2, 2, 2, 2, 32, 128), F32),
            pltpu.VMEM((max(nblocks, 1), 2, 2, 2, 2, 2, 32, 128), F32),
            pltpu.SemaphoreType.DMA((nblocks + 1, 8)),
        ],
        name=name,
    )(where, *vecs, *arrays)


def last_kernel(plan, where_ref, *refs):
    nvec, nchunk = plan["nvec"], plan["nchunk"]
    vecs = refs[:nvec]
    chunks = refs[nvec : nvec + 2 * nchunk]
    outs = refs[nvec + 2 * nchunk : nvec + 2 * nchunk + 4]
    pieces, inverse, _, sems = refs[nvec + 2 * nchunk + 4 :]
    chunk, m = plan["inverse"]
    solving = fetch(
        where_ref,
        chunks[2 * chunk],
        chunks[2 * chunk + 1],
        m,
        lambda r, zh, x: inverse.at[r, :, zh, :, x],
        sems.at[0],
    )
    values = [v[...] for v in vecs]
    solved = solve(inverse, plan["input"](values), solving)
    lay_values(where_ref, (values[-1], solved), outs, pieces)


def lay_values(where_ref, values, outs, held):
    zh, x = where_ref[1], where_ref[3]
    for p, value in enumerate(values):
        held[:, p] = value.T.reshape(4, 32, 128)
    for b1 in range(2):
        for b2 in range(2):
            outs[b1 * 2 + b2][...] = held[(zh ^ b1) * 2 + (x ^ b2)]


def lay_kernel(where_ref, first, second, *refs):
    lay_values(where_ref, (first[...], second[...]), refs[:4], refs[4])


def lay(name, where, first, second):
    return pl.pallas_call(
        lay_kernel,
        out_shape=[shaped(2, 32, 128)] * 4,
        in_specs=[smem()] + [vmem()] * 2,
        out_specs=[vmem()] * 4,
        scratch_shapes=[pltpu.VMEM((4, 2, 32, 128), F32)],
        name=name,
    )(where, first, second)


def cut_kernel(where_ref, source, *refs):
    outs, held = refs[:4], refs[4]
    r, zh, x = where_ref[0], where_ref[1], where_ref[3]
    for p in range(2):
        for z in range(2):
            start = pl.multiple_of((2 * r + z) * 128, 128)
            one = source[p, 0, :, pl.ds(start, 128)]
            two = source[p, 1, :, pl.ds(start, 128)]
            held[2 * z, p], held[2 * z + 1, p] = swap_lanes(one, two)
    for b1 in range(2):
        for b2 in range(2):
            outs[b1 * 2 + b2][...] = held[(zh ^ b1) * 2 + (x ^ b2)]


def cut(name, where, rhs):
    return pl.pallas_call(
        cut_kernel,
        out_shape=[shaped(2, 32, 128)] * 4,
        in_specs=[smem(), vmem()],
        out_specs=[vmem()] * 4,
        scratch_shapes=[pltpu.VMEM((4, 2, 32, 128), F32)],
        name=name,
    )(where, rhs)


def stand_kernel(where_ref, near_ref, other_ref, one_ref, two_ref, held):
    zh, zl, x = where_ref[1], where_ref[2], where_ref[3]
    for b1 in range(2):
        for b2 in range(2):
            for b, source in enumerate((near_ref, other_ref)):
                held[((zh ^ b1) * 2 + (zl ^ b)) * 2 + (x ^ b2)] = source[b1 * 2 + b2]
    for p, out in enumerate((one_ref, two_ref)):
        out[...] = held[:, p].reshape(256, 128).T


def stand(name, where, near, other):
    return pl.pallas_call(
        stand_kernel,
        out_shape=[shaped(128, 256)] * 2,
        in_specs=[smem()] + [vmem()] * 2,
        out_specs=[vmem()] * 2,
        scratch_shapes=[pltpu.VMEM((8, 2, 32, 128), F32)],
        name=name,
    )(where, near, other)


def join_kernel(where_ref, near_ref, other_ref, out_ref, held):
    r, zh, x, core = where_ref[0], where_ref[1], where_ref[3], where_ref[5]
    for b1 in range(2):
        for b2 in range(2):
            place = (zh ^ b1) * 2 + (x ^ b2)
            held[(r ^ core) * 4 + place] = near_ref[b1 * 2 + b2]
            held[(r ^ core ^ 1) * 4 + place] = other_ref[b1 * 2 + b2]
    for p in range(2):
        for u in range(4):
            lanes = slice(u * 128, u * 128 + 128)
            out_ref[p, 0, :, lanes], out_ref[p, 1, :, lanes] = swap_lanes(
                held[2 * u, p], held[2 * u + 1, p]
            )


def join(name, where, near, other):
    return pl.pallas_call(
        join_kernel,
        out_shape=shaped(2, 2, 32, 512),
        in_specs=[smem()] + [vmem()] * 2,
        out_specs=vmem(),
        scratch_shapes=[pltpu.VMEM((8, 2, 32, 128), F32)],
        name=name,
    )(where, near, other)


def exchange_four(value):
    return send(value, to_pair), send(value, to_core), send(value, to_pair_core)


def sum_four(v):
    return (v[0] + v[1]) + (v[2] + v[3])


def grouped(leaf_rhs, root_rhs, leaf_inverses, root_inverses, leaf_blocks, root_block, pattern):
    row, col, core = (lax.axis_index(name) for name in AXES)
    zl = (col // 2) % 2
    spots = [row, col // 4, zl, col % 2, core]
    where = jnp.stack(spots + [jnp.zeros_like(core)]).astype(jnp.int32)
    where_by_core = jnp.stack(spots + [core]).astype(jnp.int32)

    first_out, keeps, outs = rows(where, leaf_inverses[0], root_inverses)
    first_got = send(first_out, to_pair)
    blocks = mask(pattern[0, :, :, 0], leaf_blocks[0])

    def whole(keep, got):
        return jnp.stack([jnp.where(zl == 0, keep, got), jnp.where(zl == 0, got, keep)], axis=-3)

    chunk_a = jnp.stack([whole(keeps[0], first_got), blocks[0]])
    far_a = send(chunk_a, to_far)

    leaf_cut = cut("cut_leaf", where, leaf_rhs[0])
    leaf_in = jnp.stack(
        [leaf_cut[0]] + [send(leaf_cut[k], to_group(k // 2, k % 2)) for k in (1, 2, 3)]
    )
    leaf_pair = send(leaf_in, to_pair)

    outs = after(outs, chunk_a)
    rest_got = send(outs, to_pair)
    inverses = whole(keeps[1:], rest_got)
    chunk_b = jnp.concatenate([inverses[:1], blocks[1:3]])
    lower = root_block.reshape(2, 32, 2, 128).transpose(2, 0, 1, 3)
    chunk_c = blocks[3:5]
    chunk_d = jnp.concatenate([inverses[1:], lower[None]])

    two_a = jnp.stack([chunk_a, far_a])
    second_a = send(two_a, to_second)
    far_b = send(after(chunk_b, two_a), to_far)
    four_a = jnp.concatenate([two_a, second_a])
    third_a = send(four_a, to_third)
    two_b = jnp.stack([chunk_b, after(far_b, four_a)])
    second_b = send(two_b, to_second)
    far_c = send(after(chunk_c, two_b), to_far)
    b0, b1 = stand("stand_leaf", where, after(leaf_in, two_b), leaf_pair)

    part, y0 = link(
        "link_0",
        where,
        [b0],
        [(four_a, third_a)],
        dict(
            inverse=(0, 0),
            blocks=[(0, 1)],
            input=lambda v: v[0],
            terms=lambda v, solved, core: [solved],
        ),
    )
    pair = send(part, to_pair)
    four_b = jnp.concatenate([two_b, after(second_b, part)])
    third_b = send(four_b, to_third)
    two_c = jnp.stack([chunk_c, after(far_c, four_b)])
    second_c = send(two_c, to_second)
    far_d = send(after(chunk_d, two_c), to_far)

    root_cut = cut("cut_root", where, after(root_rhs, two_c))
    root_in = jnp.stack(
        [root_cut[0]] + [send(root_cut[k], to_group(k // 2, k % 2)) for k in (1, 2, 3)]
    )
    root_pair = send(root_in, to_pair)

    part, y1 = link(
        "link_1",
        where,
        [b1, part, pair, y0],
        [(four_b, third_b)],
        dict(
            inverse=(0, 0),
            blocks=[(0, 1), (0, 2)],
            input=lambda v: v[0] - (v[1] + v[2]),
            terms=lambda v, solved, core: [v[3], solved],
        ),
    )
    sums = exchange_four(part)
    four_c = jnp.concatenate([two_c, after(second_c, part)])
    third_c = send(four_c, to_third)
    two_d = jnp.stack([chunk_d, after(far_d, four_c)])
    second_d = send(two_d, to_second)
    r2, r3 = stand("stand_root", where, after(root_in, two_d), root_pair)
    four_d = jnp.concatenate([two_d, second_d])
    third_d = send(four_d, to_third)

    leaf_parts = lay("lay_leaf", where, after(y0, four_d), y1)
    leaf_near = jnp.stack(
        [leaf_parts[0]] + [send(leaf_parts[k], to_group(k // 2, k % 2)) for k in (1, 2, 3)]
    )

    part, y2 = link(
        "link_2",
        where,
        [r2, part, *sums, y0, y1],
        [(four_c, third_c), (four_d, third_d)],
        dict(
            inverse=(1, 0),
            blocks=[(0, 0), (0, 1), (1, 2)],
            input=lambda v: v[0] - sum_four(v[1:5]),
            terms=lambda v, solved, core: [v[5], v[6], jnp.where(core == 0, solved, 0.0)],
        ),
    )
    sums = exchange_four(part)
    leaf_near = after(leaf_near, part)
    leaf_other = send(leaf_near, to_row)
    leaf_solution = join("join_leaf", where, leaf_near, leaf_other)

    root_parts = link(
        "link_3",
        where,
        [r3, part, *sums, y2],
        [(four_d, third_d)],
        dict(inverse=(0, 1), blocks=[], input=lambda v: v[0] - sum_four(v[1:5])),
    )
    moved = jnp.stack([send(root_parts[k], to_group_by_core(k // 2, k % 2)) for k in range(4)])
    swapped = send(moved, to_core)
    root_solution = join("join_root", where_by_core, moved, swapped)
    return leaf_solution[None], root_solution


def solution(mesh):
    placed = (
        P("leaf", None, None, "col", None),
        P(None, None, "col", None),
        P("leaf", None, None, "col", "row"),
        P(None, None, "col", "row"),
        P("leaf", None, None, "col", "row"),
        P(None, "col", "row"),
        P("leaf", None, "row", "col"),
    )
    small = (mesh.shape["row"], mesh.shape["col"], mesh.shape["leaf"]) == (2, 8, 2)
    return jax.shard_map(
        grouped if small else general,
        mesh=mesh,
        in_specs=placed,
        out_specs=(P("leaf", None, None, "col", None), P(None, None, "col", None)),
        check_vma=False,
    )
```

time: 714 us -> 148 us (0.21)
  waiting for transfers between devices: 626 us -> 52.5 us
  blocking collectives: 51.3 us -> 0 us
  starting transfers between devices: 0.46 us -> 49.8 us
  Pallas kernels: 0 us -> 30.3 us
  between operations: 14 us -> 1.1 us
  matrix products: 12 us -> 0 us
    reduce_scatter x10 -> x0, waiting for transfers between devices: 609 us -> none  [apply_rows(): owned = lax.psum_scatter(term, 'col', scatter_dimension=0, tiled=True)]
    ppermute x0 -> x38, waiting for transfers between devices: none -> 52.5 us  [send(): return lax.ppermute(value, AXES, pairs(dest))]
    all_gather x10 -> x0, blocking collectives: 51.3 us -> none  [apply_rows(): return lax.all_gather(owned[None], 'row', axis=0, tiled=True)]
    ppermute x0 -> x38, starting transfers between devices: none -> 49.8 us  [send(): return lax.ppermute(value, AXES, pairs(dest))]
    pallas_call x0 -> x13, Pallas kernels: none -> 30.3 us  [the longest x4 14.4 us: link(): pl.pallas_call(functools.partial(link_kernel, plan) if not last else func...]
    psum x1 -> x0, waiting for transfers between devices: 17.2 us -> none  [shards(): upper_two, upper_three = lax.psum((upper_two, upper_three), 'leaf')]
    dot_general x10 -> x0, matrix products: 12 us -> none  [apply_rows(): lax.dot_general(block, vector, (((0,), (0,)), ((), ())), precision=lax.Pr...]
  transfers between devices with their start and end apart: 11 -> 38, of which waited for: 11 -> 15; matrix products, arithmetic and copies ran while one was open for 1% -> 3% of each run, Pallas kernels for 0% -> 15%
where the time goes in v2:
time: 148 us; the launch traced here: 147 us
  waiting for transfers between devices  52.5 us (35%)
  starting transfers between devices  49.8 us (34%)
  Pallas kernels  30.3 us (20%)
  local copies, waits for them, and re-layouts  10.9 us (7%)
  other arithmetic  1.98 us (1%)
    ppermute x38, waiting for transfers between devices, send(): return lax.ppermute(value, AXES, pairs(dest))  52.5 us
    ppermute x38, starting transfers between devices, send(): return lax.ppermute(value, AXES, pairs(dest))  49.8 us
    pallas_call x4, Pallas kernels, link(): pl.pallas_call(functools.partial(link_kernel, plan) if not last else func...  14.4 us
    unnamed x60, local copies, waits for them, and re-layouts  7.08 us
    pallas_call x2, Pallas kernels, join(): pl.pallas_call(join_kernel, out_shape=shaped(2, 2, 32, 512), in_specs=[sm...  3.67 us
    pallas_call x2, Pallas kernels, stand(): pl.pallas_call(stand_kernel, out_shape=[shaped(128, 256)] * 2, in_specs=[...  3.63 us
    pallas_call x2, Pallas kernels, cut(): pl.pallas_call(cut_kernel, out_shape=[shaped(2, 32, 128)] * 4, in_specs=[...  3.42 us
  transfers between devices with their start and end apart: 38, of which 15 were waited for; matrix products, arithmetic and copies ran while one was open for 3% of the time, Pallas kernels for 15%

profile of v2, /device:TPU:0, one launch (start us, length us, event | category | flops | bytes accessed | tf_op | source)
XLA Modules:
  0.0 146.6 jit_solution(15087774372854482611)
XLA Ops:
  1.4 1.8 %split_rows.1 = (f32[2,32,128]{2,1,0:T(8,128)}, f32[4,2,32,128]{3,2,1,0:T(8,128)}, f32[3,2,32,128]{3,2,1,0:T(8,128)}) custom-call(s32[6]{0:T(128)} %stack.152.where_ref, f32[2,2,32,256]{3,2,1,0:T(8,128)} %bitcast.81, f32[2,2,32,256]{3,2,1,0:T(8,128)} %root_ref.1), custom_call_target="tpu_custom_call" | custom-call | tf_op jit(solution)/shard_map/split_rows/pallas_call | solution.py:169
  3.2 3.1 %collective-permute-start.3 = (f32[2,32,128]{2,1,0:T(8,128)}, f32[2,32,128]{2,1,0:T(8,128)S(1)}, u32[]{:S(2)}, u32[]{:S(2)}) collective-permute-start(f32[2,32,128]{2,1,0:T(8,128)} %get-tuple-element.51), channel_id=1, source_target_pairs={{0,4},{1,5},{2,6},{3,7},{4,0},{5,1},{6,2},{7,3},{8,12},{9,13},{10,... | collective-permute-start | bytes 98312 | tf_op jit(solution)/shard_map/ppermute | solution.py:66
  6.9 1.7 %mask_blocks.1 = f32[5,2,2,32,128]{4,3,2,1,0:T(8,128)} custom-call(s32[5,2]{1,0:T(8,128)} %copy.13.tiles_ref, f32[5,2,32,256]{3,2,1,0:T(8,128)} %bitcast.78), custom_call_target="tpu_custom_call" | custom-call | tf_op jit(solution)/shard_map/mask_blocks/pallas_call | solution.py:187
  11.4 2.7 %collective-permute-start.5 = (f32[2,2,2,32,128]{4,3,2,1,0:T(8,128)S(1)}, f32[2,2,2,32,128]{4,3,2,1,0:T(8,128)S(1)}, u32[]{:S(2)}, u32[]{:S(2)}) collective-permute-start(f32[2,2,2,32,128]{4,3,2,1,0:T(8,128)S(1)} %get-tuple-element.98), channel_id=1, source_target_pairs={{0,8},{1,9},{2,10},{3,11},{4,12},{5,13},{6,14},{7,15},{8,0},{9,1},... | collective-permute-start | bytes 393224 | tf_op jit(solution)/shard_map/ppermute | solution.py:66
  14.9 5.4 %collective-permute-done.5 = f32[2,2,2,32,128]{4,3,2,1,0:T(8,128)S(1)} collective-permute-done((f32[2,2,2,32,128]{4,3,2,1,0:T(8,128)S(1)}, f32[2,2,2,32,128]{4,3,2,1,0:T(8,128)S(1)}, u32[]{:S(2)}, u32[]{:S(2)}) %collective-permute-start.5) | collective-permute-done | bytes 131104 | tf_op jit(solution)/shard_map/ppermute | solution.py:66
  20.3 1.6 %collective-permute-start.7 = (f32[2,2,2,2,32,128]{5,4,3,2,1,0:T(8,128)S(1)}, f32[2,2,2,2,32,128]{5,4,3,2,1,0:T(8,128)S(1)}, u32[]{:S(2)}, u32[]{:S(2)}) collective-permute-start(f32[2,2,2,2,32,128]{5,4,3,2,1,0:T(8,128)S(1)} %pad_maximum_fusion.6), channel_id=1, source_target_pairs={{0,2},{1,17},{2,0},{3,19},{4,6},{5,21},{6,4},{7,23},{8,10},{9,25},... | collective-permute-start | bytes 786440 | tf_op jit(solution)/shard_map/ppermute | solution.py:66
  22.7 4.0 %collective-permute-done.7 = f32[2,2,2,2,32,128]{5,4,3,2,1,0:T(8,128)S(1)} collective-permute-done((f32[2,2,2,2,32,128]{5,4,3,2,1,0:T(8,128)S(1)}, f32[2,2,2,2,32,128]{5,4,3,2,1,0:T(8,128)S(1)}, u32[]{:S(2)}, u32[]{:S(2)}) %collective-permute-start.7) | collective-permute-done | bytes 262176 | tf_op jit(solution)/shard_map/ppermute | solution.py:66
  26.8 1.6 %collective-permute-start.9 = (f32[4,2,2,2,32,128]{5,4,3,2,1,0:T(8,128)S(1)}, f32[4,2,2,2,32,128]{5,4,3,2,1,0:T(8,128)S(1)}, u32[]{:S(2)}, u32[]{:S(2)}) collective-permute-start(f32[4,2,2,2,32,128]{5,4,3,2,1,0:T(8,128)S(1)} %pad_maximum_fusion.2.refs_1_), channel_id=1, source_target_pairs={{0,16},{1,3},{2,18},{3,1},{4,20},{5,7},{6,22},{7,5},{8,24},{9,11},... | collective-permute-start | bytes 1572872 | tf_op jit(solution)/shard_map/ppermute | solution.py:66
  28.4 4.8 %collective-permute-done.6 = f32[3,2,2,32,128]{4,3,2,1,0:T(8,128)S(1)} collective-permute-done((f32[3,2,2,32,128]{4,3,2,1,0:T(8,128)S(1)}, f32[3,2,2,32,128]{4,3,2,1,0:T(8,128)S(1)}, u32[]{:S(2)}, u32[]{:S(2)}) %collective-permute-start.6) | collective-permute-done | bytes 196640 | tf_op jit(solution)/shard_map/ppermute | solution.py:66
  33.2 1.6 %collective-permute-start.11 = (f32[2,3,2,2,32,128]{5,4,3,2,1,0:T(8,128)S(1)}, f32[2,3,2,2,32,128]{5,4,3,2,1,0:T(8,128)S(1)}, u32[]{:S(2)}, u32[]{:S(2)}) collective-permute-start(f32[2,3,2,2,32,128]{5,4,3,2,1,0:T(8,128)S(1)} %pad_maximum_fusion.4), channel_id=1, source_target_pairs={{0,2},{1,17},{2,0},{3,19},{4,6},{5,21},{6,4},{7,23},{8,10},{9,25},... | collective-permute-start | bytes 1179656 | tf_op jit(solution)/shard_map/ppermute | solution.py:66
  34.7 1.7 %cut_leaf.1 = (f32[2,32,128]{2,1,0:T(8,128)}, f32[2,32,128]{2,1,0:T(8,128)}, f32[2,32,128]{2,1,0:T(8,128)}, f32[2,32,128]{2,1,0:T(8,128)}) custom-call(s32[6]{0:T(128)} %stack.152.where_ref, f32[2,2,32,512]{3,2,1,0:T(8,128)} %bitcast.80), custom_call_target="tpu_custom_call" | custom-call | tf_op jit(solution)/shard_map/cut_leaf/pallas_call | solution.py:350
  37.0 3.8 %collective-permute-start.2 = (f32[2,32,128]{2,1,0:T(8,128)}, f32[2,32,128]{2,1,0:T(8,128)S(1)}, u32[]{:S(2)}, u32[]{:S(2)}) collective-permute-start(f32[2,32,128]{2,1,0:T(8,128)} %get-tuple-element.48), channel_id=1, source_target_pairs={{0,10},{1,11},{2,8},{3,9},{4,14},{5,15},{6,12},{7,13},{8,2},{9,3},... | collective-permute-start | bytes 98312 | tf_op jit(solution)/shard_map/ppermute | solution.py:66
  40.9 1.2 collective-permute-done
  42.1 1.2 collective-permute-done.2
  44.1 1.4 collective-permute-start.8
  45.5 3.6 %collective-permute-done.8.other_ref = f32[4,2,32,128]{3,2,1,0:T(8,128)S(1)} collective-permute-done((f32[4,2,32,128]{3,2,1,0:T(8,128)S(1)}, f32[4,2,32,128]{3,2,1,0:T(8,128)S(1)}, u32[]{:S(2)}, u32[]{:S(2)}) %collective-permute-start.8) | collective-permute-done | bytes 131104 | tf_op jit(solution)/shard_map/ppermute | solution.py:66
  49.8 1.8 %stand_leaf.1 = (f32[128,256]{1,0:T(8,128)}, f32[128,256]{1,0:T(8,128)}) custom-call(s32[6]{0:T(128)} %stack.152.where_ref, f32[4,2,32,128]{3,2,1,0:T(8,128)} %copy-done.11, f32[4,2,32,128]{3,2,1,0:T(8,128)} %copy-done.25), custom_call_target="tpu_custom_call" | custom-call | tf_op jit(solution)/shard_map/stand_leaf/pallas_call | solution.py:371
  52.4 3.3 %link_0.1 = (f32[128,256]{1,0:T(8,128)}, f32[128,128]{1,0:T(8,128)}) custom-call(s32[6]{0:T(128)} %stack.152.where_ref, f32[128,256]{1,0:T(8,128)} %get-tuple-element.56.refs_0_, f32[4,2,2,2,32,128]{5,4,3,2,1,0:T(8,128)} %copy-done.4, f32[4,2,2,2,32,128]{5,4,3,2,1,0:T(8,128)} %copy-done.9), custom_call_target="tpu_custom_call" | custom-call | tf_op jit(solution)/shard_map/link_0/pallas_call | solution.py:276
  56.8 2.2 %collective-permute-start.10 = (f32[2,2,2,32,128]{4,3,2,1,0:T(8,128)S(1)}, f32[2,2,2,32,128]{4,3,2,1,0:T(8,128)S(1)}, u32[]{:S(2)}, u32[]{:S(2)}) collective-permute-start(f32[2,2,2,32,128]{4,3,2,1,0:T(8,128)S(1)} %get-tuple-element.58), channel_id=1, source_target_pairs={{0,8},{1,9},{2,10},{3,11},{4,12},{5,13},{6,14},{7,15},{8,0},{9,1},... | collective-permute-start | bytes 393224 | tf_op jit(solution)/shard_map/ppermute | solution.py:66
  59.0 5.2 %collective-permute-done.10 = f32[2,2,2,32,128]{4,3,2,1,0:T(8,128)S(1)} collective-permute-done((f32[2,2,2,32,128]{4,3,2,1,0:T(8,128)S(1)}, f32[2,2,2,32,128]{4,3,2,1,0:T(8,128)S(1)}, u32[]{:S(2)}, u32[]{:S(2)}) %collective-permute-start.10) | collective-permute-done | bytes 131104 | tf_op jit(solution)/shard_map/ppermute | solution.py:66
  65.3 1.7 %collective-permute-start.12 = (f32[3,2,2,32,128]{4,3,2,1,0:T(8,128)S(1)}, f32[3,2,2,32,128]{4,3,2,1,0:T(8,128)S(1)}, u32[]{:S(2)}, u32[]{:S(2)}) collective-permute-start(f32[3,2,2,32,128]{4,3,2,1,0:T(8,128)S(1)} %get-tuple-element.62), channel_id=1, source_target_pairs={{0,8},{1,9},{2,10},{3,11},{4,12},{5,13},{6,14},{7,15},{8,0},{9,1},... | collective-permute-start | bytes 589832 | tf_op jit(solution)/shard_map/ppermute | solution.py:66
  67.1 4.6 %collective-permute-done.14.refs_2_ = f32[128,256]{1,0:T(8,128)S(1)} collective-permute-done((f32[128,256]{1,0:T(8,128)S(1)}, f32[128,256]{1,0:T(8,128)S(1)}, u32[]{:S(2)}, u32[]{:S(2)}) %collective-permute-start.14) | collective-permute-done | bytes 131104 | tf_op jit(solution)/shard_map/ppermute | solution.py:66
  72.7 3.7 %link_1.1 = (f32[128,256]{1,0:T(8,128)}, f32[128,128]{1,0:T(8,128)}) custom-call(s32[6]{0:T(128)} %stack.152.where_ref, f32[128,256]{1,0:T(8,128)} %get-tuple-element.63.refs_0_, f32[128,256]{1,0:T(8,128)} %get-tuple-element.59.refs_1_, f32[128,256]{1,0:T(8,128)} %copy-done.22, f32[128,128]{1,0:T(8,128)} %get-tuple-element.67.refs_3_.first.refs_5_, ...), custom_call_target="tpu_custom_call" | custom-call | tf_op jit(solution)/shard_map/link_1/pallas_call | solution.py:276
  76.5 1.2 collective-permute-start.16
  77.7 10.3 %collective-permute-done.16 = f32[2,3,2,2,32,128]{5,4,3,2,1,0:T(8,128)S(1)} collective-permute-done((f32[2,3,2,2,32,128]{5,4,3,2,1,0:T(8,128)S(1)}, f32[2,3,2,2,32,128]{5,4,3,2,1,0:T(8,128)S(1)}, u32[]{:S(2)}, u32[]{:S(2)}) %collective-permute-start.16) | collective-permute-done | bytes 393248 | tf_op jit(solution)/shard_map/ppermute | solution.py:66
  88.1 2.8 %collective-permute-start.28 = (f32[4,3,2,2,32,128]{5,4,3,2,1,0:T(8,128)S(1)}, f32[4,3,2,2,32,128]{5,4,3,2,1,0:T(8,128)S(1)}, u32[]{:S(2)}, u32[]{:S(2)}) collective-permute-start(f32[4,3,2,2,32,128]{5,4,3,2,1,0:T(8,128)S(1)} %pad_maximum_fusion.1.refs_9_.refs_6_), channel_id=1, source_target_pairs={{0,16},{1,3},{2,18},{3,1},{4,20},{5,7},{6,22},{7,5},{8,24},{9,11},... | collective-permute-start | bytes 2359304 | tf_op jit(solution)/shard_map/ppermute | solution.py:66
  91.0 1.7 %cut_root.1 = (f32[2,32,128]{2,1,0:T(8,128)}, f32[2,32,128]{2,1,0:T(8,128)}, f32[2,32,128]{2,1,0:T(8,128)}, f32[2,32,128]{2,1,0:T(8,128)}) custom-call(s32[6]{0:T(128)} %stack.152.where_ref, f32[2,2,32,512]{3,2,1,0:T(8,128)} %source), custom_call_target="tpu_custom_call" | custom-call | tf_op jit(solution)/shard_map/cut_root/pallas_call | solution.py:350
  92.7 1.2 collective-permute-start.20
  93.9 2.1 %collective-permute-start.21 = (f32[2,32,128]{2,1,0:T(8,128)}, f32[2,32,128]{2,1,0:T(8,128)S(1)}, u32[]{:S(2)}, u32[]{:S(2)}) collective-permute-start(f32[2,32,128]{2,1,0:T(8,128)} %get-tuple-element.76), channel_id=1, source_target_pairs={{0,8},{1,9},{2,10},{3,11},{4,12},{5,13},{6,14},{7,15},{8,0},{9,1},... | collective-permute-start | bytes 98312 | tf_op jit(solution)/shard_map/ppermute | solution.py:66
  97.2 2.5 %collective-permute-done.21 = f32[2,32,128]{2,1,0:T(8,128)S(1)} collective-permute-done((f32[2,32,128]{2,1,0:T(8,128)}, f32[2,32,128]{2,1,0:T(8,128)S(1)}, u32[]{:S(2)}, u32[]{:S(2)}) %collective-permute-start.21) | collective-permute-done | bytes 32800 | tf_op jit(solution)/shard_map/ppermute | solution.py:66
  99.6 2.3 %collective-permute-done.22 = f32[2,32,128]{2,1,0:T(8,128)S(1)} collective-permute-done((f32[2,32,128]{2,1,0:T(8,128)}, f32[2,32,128]{2,1,0:T(8,128)S(1)}, u32[]{:S(2)}, u32[]{:S(2)}) %collective-permute-start.22) | collective-permute-done | bytes 32800 | tf_op jit(solution)/shard_map/ppermute | solution.py:66
  102.8 2.0 %collective-permute-start.24 = (f32[128,256]{1,0:T(8,128)S(1)}, f32[128,256]{1,0:T(8,128)S(1)}, u32[]{:S(2)}, u32[]{:S(2)}) collective-permute-start(f32[128,256]{1,0:T(8,128)S(1)} %copy-done.13), channel_id=1, source_target_pairs={{0,4},{1,5},{2,6},{3,7},{4,0},{5,1},{6,2},{7,3},{8,12},{9,13},{10,... | collective-permute-start | bytes 393224 | tf_op jit(solution)/shard_map/ppermute | solution.py:66
  104.8 2.9 %collective-permute-done.23.other_ref = f32[4,2,32,128]{3,2,1,0:T(8,128)S(1)} collective-permute-done((f32[4,2,32,128]{3,2,1,0:T(8,128)S(1)}, f32[4,2,32,128]{3,2,1,0:T(8,128)S(1)}, u32[]{:S(2)}, u32[]{:S(2)}) %collective-permute-start.23) | collective-permute-done | bytes 131104 | tf_op jit(solution)/shard_map/ppermute | solution.py:66
  108.4 1.8 %stand_root.1 = (f32[128,256]{1,0:T(8,128)}, f32[128,256]{1,0:T(8,128)}) custom-call(s32[6]{0:T(128)} %stack.152.where_ref, f32[4,2,32,128]{3,2,1,0:T(8,128)} %copy-done.10, f32[4,2,32,128]{3,2,1,0:T(8,128)} %copy-done.24), custom_call_target="tpu_custom_call" | custom-call | tf_op jit(solution)/shard_map/stand_root/pallas_call | solution.py:371
  110.3 1.9 %collective-permute-done.26.refs_4_ = f32[128,256]{1,0:T(8,128)S(1)} collective-permute-done((f32[128,256]{1,0:T(8,128)S(1)}, f32[128,256]{1,0:T(8,128)S(1)}, u32[]{:S(2)}, u32[]{:S(2)}) %collective-permute-start.26) | collective-permute-done | bytes 131104 | tf_op jit(solution)/shard_map/ppermute | solution.py:66
  113.3 4.1 %link_2.1 = (f32[128,256]{1,0:T(8,128)}, f32[128,128]{1,0:T(8,128)}) custom-call(s32[6]{0:T(128)} %stack.152.where_ref, f32[128,256]{1,0:T(8,128)} %get-tuple-element.79.refs_0_, f32[128,256]{1,0:T(8,128)} %get-tuple-element.64.refs_1_, f32[128,256]{1,0:T(8,128)} %copy-done.18, f32[128,256]{1,0:T(8,128)} %copy-done.20, f32[128,256]{1,0:T(8,128)} %copy-done.21, ...), custom_call_target="tpu_custom_call" | custom-call | tf_op jit(solution)/shard_map/link_2/pallas_call | solution.py:276
  119.6 1.6 %lay_leaf.1 = (f32[2,32,128]{2,1,0:T(8,128)}, f32[2,32,128]{2,1,0:T(8,128)}, f32[2,32,128]{2,1,0:T(8,128)}, f32[2,32,128]{2,1,0:T(8,128)}) custom-call(s32[6]{0:T(128)} %stack.152.where_ref, f32[128,128]{1,0:T(8,128)} %get-tuple-element.67.refs_3_.first.refs_5_, f32[128,128]{1,0:T(8,128)} %get-tuple-element.68.second.refs_6_), custom_call_target="tpu_custom_call" | custom-call | tf_op jit(solution)/shard_map/lay_leaf/pallas_call | solution.py:325
  122.1 1.5 %collective-permute-start.18 = (f32[2,32,128]{2,1,0:T(8,128)}, f32[2,32,128]{2,1,0:T(8,128)S(1)}, u32[]{:S(2)}, u32[]{:S(2)}) collective-permute-start(f32[2,32,128]{2,1,0:T(8,128)} %get-tuple-element.71), channel_id=1, source_target_pairs={{0,8},{1,9},{2,10},{3,11},{4,12},{5,13},{6,14},{7,15},{8,0},{9,1},... | collective-permute-start | bytes 98312 | tf_op jit(solution)/shard_map/ppermute | solution.py:66
  123.7 2.0 %collective-permute-start.19 = (f32[2,32,128]{2,1,0:T(8,128)}, f32[2,32,128]{2,1,0:T(8,128)S(1)}, u32[]{:S(2)}, u32[]{:S(2)}) collective-permute-start(f32[2,32,128]{2,1,0:T(8,128)} %get-tuple-element.72), channel_id=1, source_target_pairs={{0,10},{1,11},{2,8},{3,9},{4,14},{5,15},{6,12},{7,13},{8,2},{9,3},... | collective-permute-start | bytes 98312 | tf_op jit(solution)/shard_map/ppermute | solution.py:66
  126.3 3.3 %link_3.1 = (f32[2,32,128]{2,1,0:T(8,128)}, f32[2,32,128]{2,1,0:T(8,128)}, f32[2,32,128]{2,1,0:T(8,128)}, f32[2,32,128]{2,1,0:T(8,128)}) custom-call(s32[6]{0:T(128)} %stack.152.where_ref, f32[128,256]{1,0:T(8,128)} %get-tuple-element.82.refs_0_, f32[128,256]{1,0:T(8,128)} %get-tuple-element.80.refs_1_, f32[128,256]{1,0:T(8,128)} %copy-done.15, ...), custom_call_target="tpu_custom_call" | custom-call | tf_op jit(solution)/shard_map/link_3/pallas_call | solution.py:276
  129.7 1.4 collective-permute-start.33
  132.0 1.5 %collective-permute-start.35 = (f32[2,32,128]{2,1,0:T(8,128)}, f32[2,32,128]{2,1,0:T(8,128)S(1)}, u32[]{:S(2)}, u32[]{:S(2)}) collective-permute-start(f32[2,32,128]{2,1,0:T(8,128)} %get-tuple-element.86), channel_id=1, source_target_pairs={{0,8},{1,25},{2,10},{3,27},{4,12},{5,29},{6,14},{7,31},{8,0},{9,17... | collective-permute-start | bytes 98312 | tf_op jit(solution)/shard_map/ppermute | solution.py:66
  133.5 2.0 %collective-permute-start.36 = (f32[2,32,128]{2,1,0:T(8,128)}, f32[2,32,128]{2,1,0:T(8,128)S(1)}, u32[]{:S(2)}, u32[]{:S(2)}) collective-permute-start(f32[2,32,128]{2,1,0:T(8,128)} %get-tuple-element.87), channel_id=1, source_target_pairs={{0,10},{1,27},{2,8},{3,25},{4,14},{5,31},{6,12},{7,29},{8,2},{9,19... | collective-permute-start | bytes 98312 | tf_op jit(solution)/shard_map/ppermute | solution.py:66
  135.5 1.5 %collective-permute-start.29 = (f32[4,2,32,128]{3,2,1,0:T(8,128)S(1)}, f32[4,2,32,128]{3,2,1,0:T(8,128)S(1)}, u32[]{:S(2)}, u32[]{:S(2)}) collective-permute-start(f32[4,2,32,128]{3,2,1,0:T(8,128)S(1)} %pad_maximum_fusion.11.near_ref), channel_id=1, source_target_pairs={{0,16},{1,17},{2,18},{3,19},{4,20},{5,21},{6,22},{7,23},{8,24},{9,... | collective-permute-start | bytes 393224 | tf_op jit(solution)/shard_map/ppermute | solution.py:66
  137.0 2.4 %collective-permute-done.36 = f32[2,32,128]{2,1,0:T(8,128)S(1)} collective-permute-done((f32[2,32,128]{2,1,0:T(8,128)}, f32[2,32,128]{2,1,0:T(8,128)S(1)}, u32[]{:S(2)}, u32[]{:S(2)}) %collective-permute-start.36) | collective-permute-done | bytes 32800 | tf_op jit(solution)/shard_map/ppermute | solution.py:66
  139.5 1.5 %collective-permute-start.37 = (f32[4,2,32,128]{3,2,1,0:T(8,128)S(1)}, f32[4,2,32,128]{3,2,1,0:T(8,128)S(1)}, u32[]{:S(2)}, u32[]{:S(2)}) collective-permute-start(f32[4,2,32,128]{3,2,1,0:T(8,128)S(1)} %pad_maximum_fusion.13.near_ref), channel_id=1, source_target_pairs={{0,1},{1,0},{2,3},{3,2},{4,5},{5,4},{6,7},{7,6},{8,9},{9,8},{10,11... | collective-permute-start | bytes 393224 | tf_op jit(solution)/shard_map/ppermute | solution.py:66
  142.3 1.8 %join_leaf.1 = f32[2,2,32,512]{3,2,1,0:T(8,128)} custom-call(s32[6]{0:T(128)} %stack.152.where_ref, f32[4,2,32,128]{3,2,1,0:T(8,128)} %copy-done.7, f32[4,2,32,128]{3,2,1,0:T(8,128)} %copy-done.19), custom_call_target="tpu_custom_call" | custom-call | tf_op jit(solution)/shard_map/join_leaf/pallas_call | solution.py:397
  144.8 1.8 %join_root.1 = f32[2,2,32,512]{3,2,1,0:T(8,128)} custom-call(s32[6]{0:T(128)} %stack.188.where_ref, f32[4,2,32,128]{3,2,1,0:T(8,128)} %copy-done.8, f32[4,2,32,128]{3,2,1,0:T(8,128)} %copy-done.23), custom_call_target="tpu_custom_call" | custom-call | tf_op jit(solution)/shard_map/join_root/pallas_call | solution.py:397
  (125 shorter events, 22.6 us)
Async XLA Ops:
  0.6 13.5 %copy-start = (f32[2,32,256]{2,1,0:T(8,128)S(1)}, f32[2,32,256]{2,1,0:T(8,128)}, u32[]{:S(2)}) copy-start(f32[2,32,256]{2,1,0:T(8,128)} %param.12) | copy-start | bytes 196612
  3.2 6.5 %collective-permute-start.3 = (f32[2,32,128]{2,1,0:T(8,128)}, f32[2,32,128]{2,1,0:T(8,128)S(1)}, u32[]{:S(2)}, u32[]{:S(2)}) collective-permute-start(f32[2,32,128]{2,1,0:T(8,128)} %get-tuple-element.51), channel_id=1, source_target_pairs={{0,4},{1,5},{2,6},{3,7},{4,0},{5,1},{6,2},{7,3},{8,12},{9,13},{10,... | collective-permute-start | bytes 98312 | tf_op jit(solution)/shard_map/ppermute | solution.py:66
  11.4 8.8 %collective-permute-start.5 = (f32[2,2,2,32,128]{4,3,2,1,0:T(8,128)S(1)}, f32[2,2,2,32,128]{4,3,2,1,0:T(8,128)S(1)}, u32[]{:S(2)}, u32[]{:S(2)}) collective-permute-start(f32[2,2,2,32,128]{4,3,2,1,0:T(8,128)S(1)} %get-tuple-element.98), channel_id=1, source_target_pairs={{0,8},{1,9},{2,10},{3,11},{4,12},{5,13},{6,14},{7,15},{8,0},{9,1},... | collective-permute-start | bytes 393224 | tf_op jit(solution)/shard_map/ppermute | solution.py:66
  14.1 7.7 %collective-permute-start.4 = (f32[3,2,32,128]{3,2,1,0:T(8,128)S(1)}, f32[3,2,32,128]{3,2,1,0:T(8,128)S(1)}, u32[]{:S(2)}, u32[]{:S(2)}) collective-permute-start(f32[3,2,32,128]{3,2,1,0:T(8,128)S(1)} %copy-done.29), channel_id=1, source_target_pairs={{0,4},{1,5},{2,6},{3,7},{4,0},{5,1},{6,2},{7,3},{8,12},{9,13},{10,... | collective-permute-start | bytes 294920 | tf_op jit(solution)/shard_map/ppermute | solution.py:66
  20.3 6.4 %collective-permute-start.7 = (f32[2,2,2,2,32,128]{5,4,3,2,1,0:T(8,128)S(1)}, f32[2,2,2,2,32,128]{5,4,3,2,1,0:T(8,128)S(1)}, u32[]{:S(2)}, u32[]{:S(2)}) collective-permute-start(f32[2,2,2,2,32,128]{5,4,3,2,1,0:T(8,128)S(1)} %pad_maximum_fusion.6), channel_id=1, source_target_pairs={{0,2},{1,17},{2,0},{3,19},{4,6},{5,21},{6,4},{7,23},{8,10},{9,25},... | collective-permute-start | bytes 786440 | tf_op jit(solution)/shard_map/ppermute | solution.py:66
  21.9 11.3 %collective-permute-start.6 = (f32[3,2,2,32,128]{4,3,2,1,0:T(8,128)S(1)}, f32[3,2,2,32,128]{4,3,2,1,0:T(8,128)S(1)}, u32[]{:S(2)}, u32[]{:S(2)}) collective-permute-start(f32[3,2,2,32,128]{4,3,2,1,0:T(8,128)S(1)} %get-tuple-element.53), channel_id=1, source_target_pairs={{0,8},{1,9},{2,10},{3,11},{4,12},{5,13},{6,14},{7,15},{8,0},{9,1},... | collective-permute-start | bytes 589832 | tf_op jit(solution)/shard_map/ppermute | solution.py:66
  26.8 9.7 %copy-start.4 = (f32[4,2,2,2,32,128]{5,4,3,2,1,0:T(8,128)}, f32[4,2,2,2,32,128]{5,4,3,2,1,0:T(8,128)S(1)}, u32[]{:S(2)}) copy-start(f32[4,2,2,2,32,128]{5,4,3,2,1,0:T(8,128)S(1)} %pad_maximum_fusion.2.refs_1_) | copy-start | bytes 1572868
  26.8 24.8 %collective-permute-start.9 = (f32[4,2,2,2,32,128]{5,4,3,2,1,0:T(8,128)S(1)}, f32[4,2,2,2,32,128]{5,4,3,2,1,0:T(8,128)S(1)}, u32[]{:S(2)}, u32[]{:S(2)}) collective-permute-start(f32[4,2,2,2,32,128]{5,4,3,2,1,0:T(8,128)S(1)} %pad_maximum_fusion.2.refs_1_), channel_id=1, source_target_pairs={{0,16},{1,3},{2,18},{3,1},{4,20},{5,7},{6,22},{7,5},{8,24},{9,11},... | collective-permute-start | bytes 1572872 | tf_op jit(solution)/shard_map/ppermute | solution.py:66
  33.2 22.6 %collective-permute-start.11 = (f32[2,3,2,2,32,128]{5,4,3,2,1,0:T(8,128)S(1)}, f32[2,3,2,2,32,128]{5,4,3,2,1,0:T(8,128)S(1)}, u32[]{:S(2)}, u32[]{:S(2)}) collective-permute-start(f32[2,3,2,2,32,128]{5,4,3,2,1,0:T(8,128)S(1)} %pad_maximum_fusion.4), channel_id=1, source_target_pairs={{0,2},{1,17},{2,0},{3,19},{4,6},{5,21},{6,4},{7,23},{8,10},{9,25},... | collective-permute-start | bytes 1179656 | tf_op jit(solution)/shard_map/ppermute | solution.py:66
  36.5 5.6 %collective-permute-start = (f32[2,32,128]{2,1,0:T(8,128)}, f32[2,32,128]{2,1,0:T(8,128)S(1)}, u32[]{:S(2)}, u32[]{:S(2)}) collective-permute-start(f32[2,32,128]{2,1,0:T(8,128)} %get-tuple-element.46), channel_id=1, source_target_pairs={{0,2},{1,3},{2,0},{3,1},{4,6},{5,7},{6,4},{7,5},{8,10},{9,11},{10,... | collective-permute-start | bytes 98312 | tf_op jit(solution)/shard_map/ppermute | solution.py:66
  37.0 5.1 %collective-permute-start.1 = (f32[2,32,128]{2,1,0:T(8,128)}, f32[2,32,128]{2,1,0:T(8,128)S(1)}, u32[]{:S(2)}, u32[]{:S(2)}) collective-permute-start(f32[2,32,128]{2,1,0:T(8,128)} %get-tuple-element.47), channel_id=1, source_target_pairs={{0,8},{1,9},{2,10},{3,11},{4,12},{5,13},{6,14},{7,15},{8,0},{9,1},... | collective-permute-start | bytes 98312 | tf_op jit(solution)/shard_map/ppermute | solution.py:66
  37.0 6.3 %collective-permute-start.2 = (f32[2,32,128]{2,1,0:T(8,128)}, f32[2,32,128]{2,1,0:T(8,128)S(1)}, u32[]{:S(2)}, u32[]{:S(2)}) collective-permute-start(f32[2,32,128]{2,1,0:T(8,128)} %get-tuple-element.48), channel_id=1, source_target_pairs={{0,10},{1,11},{2,8},{3,9},{4,14},{5,15},{6,12},{7,13},{8,2},{9,3},... | collective-permute-start | bytes 98312 | tf_op jit(solution)/shard_map/ppermute | solution.py:66
  44.1 5.0 %copy-start.11 = (f32[4,2,32,128]{3,2,1,0:T(8,128)}, f32[4,2,32,128]{3,2,1,0:T(8,128)S(1)}, u32[]{:S(2)}) copy-start(f32[4,2,32,128]{3,2,1,0:T(8,128)S(1)} %pad_maximum_fusion.9.near_ref) | copy-start | bytes 393220
  44.1 5.0 %collective-permute-start.8 = (f32[4,2,32,128]{3,2,1,0:T(8,128)S(1)}, f32[4,2,32,128]{3,2,1,0:T(8,128)S(1)}, u32[]{:S(2)}, u32[]{:S(2)}) collective-permute-start(f32[4,2,32,128]{3,2,1,0:T(8,128)S(1)} %pad_maximum_fusion.9.near_ref), channel_id=1, source_target_pairs={{0,4},{1,5},{2,6},{3,7},{4,0},{5,1},{6,2},{7,3},{8,12},{9,13},{10,... | collective-permute-start | bytes 393224 | tf_op jit(solution)/shard_map/ppermute | solution.py:66
  55.8 15.9 %copy-start.3 = (f32[4,3,2,2,32,128]{5,4,3,2,1,0:T(8,128)}, f32[4,3,2,2,32,128]{5,4,3,2,1,0:T(8,128)S(1)}, u32[]{:S(2)}) copy-start(f32[4,3,2,2,32,128]{5,4,3,2,1,0:T(8,128)S(1)} %pad_maximum_fusion.refs_4_) | copy-start | bytes 2359300
  55.8 15.9 %collective-permute-start.15 = (f32[4,3,2,2,32,128]{5,4,3,2,1,0:T(8,128)S(1)}, f32[4,3,2,2,32,128]{5,4,3,2,1,0:T(8,128)S(1)}, u32[]{:S(2)}, u32[]{:S(2)}) collective-permute-start(f32[4,3,2,2,32,128]{5,4,3,2,1,0:T(8,128)S(1)} %pad_maximum_fusion.refs_4_), channel_id=1, source_target_pairs={{0,16},{1,3},{2,18},{3,1},{4,20},{5,7},{6,22},{7,5},{8,24},{9,11},... | collective-permute-start | bytes 2359304 | tf_op jit(solution)/shard_map/ppermute | solution.py:66
  56.8 7.4 %collective-permute-start.10 = (f32[2,2,2,32,128]{4,3,2,1,0:T(8,128)S(1)}, f32[2,2,2,32,128]{4,3,2,1,0:T(8,128)S(1)}, u32[]{:S(2)}, u32[]{:S(2)}) collective-permute-start(f32[2,2,2,32,128]{4,3,2,1,0:T(8,128)S(1)} %get-tuple-element.58), channel_id=1, source_target_pairs={{0,8},{1,9},{2,10},{3,11},{4,12},{5,13},{6,14},{7,15},{8,0},{9,1},... | collective-permute-start | bytes 393224 | tf_op jit(solution)/shard_map/ppermute | solution.py:66
  64.1 12.2 %collective-permute-start.13 = (f32[2,2,2,2,32,128]{5,4,3,2,1,0:T(8,128)S(1)}, f32[2,2,2,2,32,128]{5,4,3,2,1,0:T(8,128)S(1)}, u32[]{:S(2)}, u32[]{:S(2)}) collective-permute-start(f32[2,2,2,2,32,128]{5,4,3,2,1,0:T(8,128)S(1)} %pad_maximum_fusion.7), channel_id=1, source_target_pairs={{0,2},{1,17},{2,0},{3,19},{4,6},{5,21},{6,4},{7,23},{8,10},{9,25},... | collective-permute-start | bytes 786440 | tf_op jit(solution)/shard_map/ppermute | solution.py:66
  65.0 6.7 %collective-permute-start.14 = (f32[128,256]{1,0:T(8,128)S(1)}, f32[128,256]{1,0:T(8,128)S(1)}, u32[]{:S(2)}, u32[]{:S(2)}) collective-permute-start(f32[128,256]{1,0:T(8,128)S(1)} %copy-done.14), channel_id=1, source_target_pairs={{0,4},{1,5},{2,6},{3,7},{4,0},{5,1},{6,2},{7,3},{8,12},{9,13},{10,... | collective-permute-start | bytes 393224 | tf_op jit(solution)/shard_map/ppermute | solution.py:66
  65.3 11.1 %collective-permute-start.12 = (f32[3,2,2,32,128]{4,3,2,1,0:T(8,128)S(1)}, f32[3,2,2,32,128]{4,3,2,1,0:T(8,128)S(1)}, u32[]{:S(2)}, u32[]{:S(2)}) collective-permute-start(f32[3,2,2,32,128]{4,3,2,1,0:T(8,128)S(1)} %get-tuple-element.62), channel_id=1, source_target_pairs={{0,8},{1,9},{2,10},{3,11},{4,12},{5,13},{6,14},{7,15},{8,0},{9,1},... | collective-permute-start | bytes 589832 | tf_op jit(solution)/shard_map/ppermute | solution.py:66
  76.4 14.5 %copy-start.5 = (f32[4,2,2,2,32,128]{5,4,3,2,1,0:T(8,128)}, f32[4,2,2,2,32,128]{5,4,3,2,1,0:T(8,128)S(1)}, u32[]{:S(2)}) copy-start(f32[4,2,2,2,32,128]{5,4,3,2,1,0:T(8,128)S(1)} %pad_maximum_fusion.3.refs_7_) | copy-start | bytes 1572868
  76.5 11.5 %collective-permute-start.16 = (f32[2,3,2,2,32,128]{5,4,3,2,1,0:T(8,128)S(1)}, f32[2,3,2,2,32,128]{5,4,3,2,1,0:T(8,128)S(1)}, u32[]{:S(2)}, u32[]{:S(2)}) collective-permute-start(f32[2,3,2,2,32,128]{5,4,3,2,1,0:T(8,128)S(1)} %pad_maximum_fusion.5), channel_id=1, source_target_pairs={{0,2},{1,17},{2,0},{3,19},{4,6},{5,21},{6,4},{7,23},{8,10},{9,25},... | collective-permute-start | bytes 1179656 | tf_op jit(solution)/shard_map/ppermute | solution.py:66
  88.1 24.1 %copy-start.1 = (f32[4,3,2,2,32,128]{5,4,3,2,1,0:T(8,128)}, f32[4,3,2,2,32,128]{5,4,3,2,1,0:T(8,128)S(1)}, u32[]{:S(2)}) copy-start(f32[4,3,2,2,32,128]{5,4,3,2,1,0:T(8,128)S(1)} %pad_maximum_fusion.1.refs_9_.refs_6_) | copy-start | bytes 2359300
  88.1 24.1 %collective-permute-start.28 = (f32[4,3,2,2,32,128]{5,4,3,2,1,0:T(8,128)S(1)}, f32[4,3,2,2,32,128]{5,4,3,2,1,0:T(8,128)S(1)}, u32[]{:S(2)}, u32[]{:S(2)}) collective-permute-start(f32[4,3,2,2,32,128]{5,4,3,2,1,0:T(8,128)S(1)} %pad_maximum_fusion.1.refs_9_.refs_6_), channel_id=1, source_target_pairs={{0,16},{1,3},{2,18},{3,1},{4,20},{5,7},{6,22},{7,5},{8,24},{9,11},... | collective-permute-start | bytes 2359304 | tf_op jit(solution)/shard_map/ppermute | solution.py:66
  90.9 21.3 %collective-permute-start.27 = (f32[4,2,2,2,32,128]{5,4,3,2,1,0:T(8,128)S(1)}, f32[4,2,2,2,32,128]{5,4,3,2,1,0:T(8,128)S(1)}, u32[]{:S(2)}, u32[]{:S(2)}) collective-permute-start(f32[4,2,2,2,32,128]{5,4,3,2,1,0:T(8,128)S(1)} %pad_maximum_fusion.3.refs_7_), channel_id=1, source_target_pairs={{0,16},{1,3},{2,18},{3,1},{4,20},{5,7},{6,22},{7,5},{8,24},{9,11},... | collective-permute-start | bytes 1572872 | tf_op jit(solution)/shard_map/ppermute | solution.py:66
  92.7 4.5 %collective-permute-start.20 = (f32[2,32,128]{2,1,0:T(8,128)}, f32[2,32,128]{2,1,0:T(8,128)S(1)}, u32[]{:S(2)}, u32[]{:S(2)}) collective-permute-start(f32[2,32,128]{2,1,0:T(8,128)} %get-tuple-element.75), channel_id=1, source_target_pairs={{0,2},{1,3},{2,0},{3,1},{4,6},{5,7},{6,4},{7,5},{8,10},{9,11},{10,... | collective-permute-start | bytes 98312 | tf_op jit(solution)/shard_map/ppermute | solution.py:66
  93.9 5.7 %collective-permute-start.21 = (f32[2,32,128]{2,1,0:T(8,128)}, f32[2,32,128]{2,1,0:T(8,128)S(1)}, u32[]{:S(2)}, u32[]{:S(2)}) collective-permute-start(f32[2,32,128]{2,1,0:T(8,128)} %get-tuple-element.76), channel_id=1, source_target_pairs={{0,8},{1,9},{2,10},{3,11},{4,12},{5,13},{6,14},{7,15},{8,0},{9,1},... | collective-permute-start | bytes 98312 | tf_op jit(solution)/shard_map/ppermute | solution.py:66
  96.0 5.9 %collective-permute-start.22 = (f32[2,32,128]{2,1,0:T(8,128)}, f32[2,32,128]{2,1,0:T(8,128)S(1)}, u32[]{:S(2)}, u32[]{:S(2)}) collective-permute-start(f32[2,32,128]{2,1,0:T(8,128)} %get-tuple-element.77), channel_id=1, source_target_pairs={{0,10},{1,11},{2,8},{3,9},{4,14},{5,15},{6,12},{7,13},{8,2},{9,3},... | collective-permute-start | bytes 98312 | tf_op jit(solution)/shard_map/ppermute | solution.py:66
  102.7 5.1 %copy-start.10 = (f32[4,2,32,128]{3,2,1,0:T(8,128)}, f32[4,2,32,128]{3,2,1,0:T(8,128)S(1)}, u32[]{:S(2)}) copy-start(f32[4,2,32,128]{3,2,1,0:T(8,128)S(1)} %pad_maximum_fusion.12.near_ref) | copy-start | bytes 393220
  102.7 5.0 %collective-permute-start.23 = (f32[4,2,32,128]{3,2,1,0:T(8,128)S(1)}, f32[4,2,32,128]{3,2,1,0:T(8,128)S(1)}, u32[]{:S(2)}, u32[]{:S(2)}) collective-permute-start(f32[4,2,32,128]{3,2,1,0:T(8,128)S(1)} %pad_maximum_fusion.12.near_ref), channel_id=1, source_target_pairs={{0,4},{1,5},{2,6},{3,7},{4,0},{5,1},{6,2},{7,3},{8,12},{9,13},{10,... | collective-permute-start | bytes 393224 | tf_op jit(solution)/shard_map/ppermute | solution.py:66
  102.8 7.4 %collective-permute-start.24 = (f32[128,256]{1,0:T(8,128)S(1)}, f32[128,256]{1,0:T(8,128)S(1)}, u32[]{:S(2)}, u32[]{:S(2)}) collective-permute-start(f32[128,256]{1,0:T(8,128)S(1)} %copy-done.13), channel_id=1, source_target_pairs={{0,4},{1,5},{2,6},{3,7},{4,0},{5,1},{6,2},{7,3},{8,12},{9,13},{10,... | collective-permute-start | bytes 393224 | tf_op jit(solution)/shard_map/ppermute | solution.py:66
  104.8 5.4 %collective-permute-start.25 = (f32[128,256]{1,0:T(8,128)S(1)}, f32[128,256]{1,0:T(8,128)S(1)}, u32[]{:S(2)}, u32[]{:S(2)}) collective-permute-start(f32[128,256]{1,0:T(8,128)S(1)} %copy-done.13), channel_id=1, source_target_pairs={{0,1},{1,0},{2,3},{3,2},{4,5},{5,4},{6,7},{7,6},{8,9},{9,8},{10,11... | collective-permute-start | bytes 393224 | tf_op jit(solution)/shard_map/ppermute | solution.py:66
  107.8 4.4 %collective-permute-start.26 = (f32[128,256]{1,0:T(8,128)S(1)}, f32[128,256]{1,0:T(8,128)S(1)}, u32[]{:S(2)}, u32[]{:S(2)}) collective-permute-start(f32[128,256]{1,0:T(8,128)S(1)} %copy-done.13), channel_id=1, source_target_pairs={{0,5},{1,4},{2,7},{3,6},{4,1},{5,0},{6,3},{7,2},{8,13},{9,12},{10,... | collective-permute-start | bytes 393224 | tf_op jit(solution)/shard_map/ppermute | solution.py:66
  117.4 6.3 %collective-permute-start.30 = (f32[128,256]{1,0:T(8,128)}, f32[128,256]{1,0:T(8,128)S(1)}, u32[]{:S(2)}, u32[]{:S(2)}) collective-permute-start(f32[128,256]{1,0:T(8,128)} %get-tuple-element.80.refs_1_), channel_id=1, source_target_pairs={{0,4},{1,5},{2,6},{3,7},{4,0},{5,1},{6,2},{7,3},{8,12},{9,13},{10,... | collective-permute-start | bytes 393224 | tf_op jit(solution)/shard_map/ppermute | solution.py:66
  118.3 7.3 %collective-permute-start.31 = (f32[128,256]{1,0:T(8,128)}, f32[128,256]{1,0:T(8,128)S(1)}, u32[]{:S(2)}, u32[]{:S(2)}) collective-permute-start(f32[128,256]{1,0:T(8,128)} %get-tuple-element.80.refs_1_), channel_id=1, source_target_pairs={{0,1},{1,0},{2,3},{3,2},{4,5},{5,4},{6,7},{7,6},{8,9},{9,8},{10,11... | collective-permute-start | bytes 393224 | tf_op jit(solution)/shard_map/ppermute | solution.py:66
  118.4 7.2 %collective-permute-start.32 = (f32[128,256]{1,0:T(8,128)}, f32[128,256]{1,0:T(8,128)S(1)}, u32[]{:S(2)}, u32[]{:S(2)}) collective-permute-start(f32[128,256]{1,0:T(8,128)} %get-tuple-element.80.refs_1_), channel_id=1, source_target_pairs={{0,5},{1,4},{2,7},{3,6},{4,1},{5,0},{6,3},{7,2},{8,13},{9,12},{10,... | collective-permute-start | bytes 393224 | tf_op jit(solution)/shard_map/ppermute | solution.py:66
  121.2 10.8 %collective-permute-start.17 = (f32[2,32,128]{2,1,0:T(8,128)}, f32[2,32,128]{2,1,0:T(8,128)S(1)}, u32[]{:S(2)}, u32[]{:S(2)}) collective-permute-start(f32[2,32,128]{2,1,0:T(8,128)} %get-tuple-element.70), channel_id=1, source_target_pairs={{0,2},{1,3},{2,0},{3,1},{4,6},{5,7},{6,4},{7,5},{8,10},{9,11},{10,... | collective-permute-start | bytes 98312 | tf_op jit(solution)/shard_map/ppermute | solution.py:66
  122.1 11.4 %collective-permute-start.18 = (f32[2,32,128]{2,1,0:T(8,128)}, f32[2,32,128]{2,1,0:T(8,128)S(1)}, u32[]{:S(2)}, u32[]{:S(2)}) collective-permute-start(f32[2,32,128]{2,1,0:T(8,128)} %get-tuple-element.71), channel_id=1, source_target_pairs={{0,8},{1,9},{2,10},{3,11},{4,12},{5,13},{6,14},{7,15},{8,0},{9,1},... | collective-permute-start | bytes 98312 | tf_op jit(solution)/shard_map/ppermute | solution.py:66
  123.7 11.8 %collective-permute-start.19 = (f32[2,32,128]{2,1,0:T(8,128)}, f32[2,32,128]{2,1,0:T(8,128)S(1)}, u32[]{:S(2)}, u32[]{:S(2)}) collective-permute-start(f32[2,32,128]{2,1,0:T(8,128)} %get-tuple-element.72), channel_id=1, source_target_pairs={{0,10},{1,11},{2,8},{3,9},{4,14},{5,15},{6,12},{7,13},{8,2},{9,3},... | collective-permute-start | bytes 98312 | tf_op jit(solution)/shard_map/ppermute | solution.py:66
  126.3 9.2 %copy-start.27 = (f32[2,32,128]{2,1,0:T(8,128)S(1)}, f32[2,32,128]{2,1,0:T(8,128)}, u32[]{:S(2)}) copy-start(f32[2,32,128]{2,1,0:T(8,128)} %get-tuple-element.69) | copy-start | bytes 98308
  129.7 7.3 %collective-permute-start.33 = (f32[2,32,128]{2,1,0:T(8,128)}, f32[2,32,128]{2,1,0:T(8,128)S(1)}, u32[]{:S(2)}, u32[]{:S(2)}) collective-permute-start(f32[2,32,128]{2,1,0:T(8,128)} %get-tuple-element.84), channel_id=1, source_target_pairs={{0,0},{1,17},{2,2},{3,19},{4,4},{5,21},{6,6},{7,23},{8,8},{9,25},{... | collective-permute-start | bytes 98312 | tf_op jit(solution)/shard_map/ppermute | solution.py:66
  131.1 5.9 %collective-permute-start.34 = (f32[2,32,128]{2,1,0:T(8,128)}, f32[2,32,128]{2,1,0:T(8,128)S(1)}, u32[]{:S(2)}, u32[]{:S(2)}) collective-permute-start(f32[2,32,128]{2,1,0:T(8,128)} %get-tuple-element.85), channel_id=1, source_target_pairs={{0,2},{1,19},{2,0},{3,17},{4,6},{5,23},{6,4},{7,21},{8,10},{9,27},... | collective-permute-start | bytes 98312 | tf_op jit(solution)/shard_map/ppermute | solution.py:66
  132.0 5.0 %collective-permute-start.35 = (f32[2,32,128]{2,1,0:T(8,128)}, f32[2,32,128]{2,1,0:T(8,128)S(1)}, u32[]{:S(2)}, u32[]{:S(2)}) collective-permute-start(f32[2,32,128]{2,1,0:T(8,128)} %get-tuple-element.86), channel_id=1, source_target_pairs={{0,8},{1,25},{2,10},{3,27},{4,12},{5,29},{6,14},{7,31},{8,0},{9,17... | collective-permute-start | bytes 98312 | tf_op jit(solution)/shard_map/ppermute | solution.py:66
  133.5 5.9 %collective-permute-start.36 = (f32[2,32,128]{2,1,0:T(8,128)}, f32[2,32,128]{2,1,0:T(8,128)S(1)}, u32[]{:S(2)}, u32[]{:S(2)}) collective-permute-start(f32[2,32,128]{2,1,0:T(8,128)} %get-tuple-element.87), channel_id=1, source_target_pairs={{0,10},{1,27},{2,8},{3,25},{4,14},{5,31},{6,12},{7,29},{8,2},{9,19... | collective-permute-start | bytes 98312 | tf_op jit(solution)/shard_map/ppermute | solution.py:66
  135.5 4.0 %copy-start.7 = (f32[4,2,32,128]{3,2,1,0:T(8,128)}, f32[4,2,32,128]{3,2,1,0:T(8,128)S(1)}, u32[]{:S(2)}) copy-start(f32[4,2,32,128]{3,2,1,0:T(8,128)S(1)} %pad_maximum_fusion.11.near_ref) | copy-start | bytes 393220
  135.5 6.2 %collective-permute-start.29 = (f32[4,2,32,128]{3,2,1,0:T(8,128)S(1)}, f32[4,2,32,128]{3,2,1,0:T(8,128)S(1)}, u32[]{:S(2)}, u32[]{:S(2)}) collective-permute-start(f32[4,2,32,128]{3,2,1,0:T(8,128)S(1)} %pad_maximum_fusion.11.near_ref), channel_id=1, source_target_pairs={{0,16},{1,17},{2,18},{3,19},{4,20},{5,21},{6,22},{7,23},{8,24},{9,... | collective-permute-start | bytes 393224 | tf_op jit(solution)/shard_map/ppermute | solution.py:66
  139.4 4.7 %copy-start.8 = (f32[4,2,32,128]{3,2,1,0:T(8,128)}, f32[4,2,32,128]{3,2,1,0:T(8,128)S(1)}, u32[]{:S(2)}) copy-start(f32[4,2,32,128]{3,2,1,0:T(8,128)S(1)} %pad_maximum_fusion.13.near_ref) | copy-start | bytes 393220
  139.5 4.7 %collective-permute-start.37 = (f32[4,2,32,128]{3,2,1,0:T(8,128)S(1)}, f32[4,2,32,128]{3,2,1,0:T(8,128)S(1)}, u32[]{:S(2)}, u32[]{:S(2)}) collective-permute-start(f32[4,2,32,128]{3,2,1,0:T(8,128)S(1)} %pad_maximum_fusion.13.near_ref), channel_id=1, source_target_pairs={{0,1},{1,0},{2,3},{3,2},{4,5},{5,4},{6,7},{7,6},{8,9},{9,8},{10,11... | collective-permute-start | bytes 393224 | tf_op jit(solution)/shard_map/ppermute | solution.py:66
  (21 other events, 24.2 us)

commit v3 on v0

v3 whole, which is shorter than its diff:
```python
import functools

import jax
import jax.numpy as jnp
from jax import lax
from jax.experimental import pallas as pl
from jax.experimental.pallas import tpu as pltpu
from jax.sharding import PartitionSpec as P

BLK = 128
AXES = ("row", "col", "leaf")
F32 = jnp.float32
BF16 = jnp.bfloat16
VMEM_OF_A_KERNEL = 16 * 2**20


def apply_rows(block, vector):
    block = block.reshape(-1, block.shape[-1])
    vector = vector.reshape(-1, vector.shape[-1])
    term = lax.dot_general(
        block,
        vector,
        (((0,), (0,)), ((), ())),
        precision=lax.Precision.HIGHEST,
        preferred_element_type=F32,
    )
    owned = lax.psum_scatter(term, "col", scatter_dimension=0, tiled=True)
    return lax.all_gather(owned[None], "row", axis=0, tiled=True)


def masked(leaf_blocks, pattern):
    local = leaf_blocks[0]
    shaped = local.reshape(local.shape[:3] + (local.shape[3] // BLK, BLK))
    weights = pattern[0].astype(F32).transpose(0, 2, 1)[:, None, :, :, None]
    return (shaped * weights).reshape(local.shape)


def general(leaf_rhs, root_rhs, leaf_inverses, root_inverses, leaf_blocks, root_block, pattern):
    blocks = masked(leaf_blocks, pattern)
    first = apply_rows(leaf_inverses[0, 0], leaf_rhs[0, 0])
    second = apply_rows(leaf_inverses[0, 1], leaf_rhs[0, 1] - apply_rows(blocks[0], first))
    upper_two = apply_rows(blocks[1], first) + apply_rows(blocks[2], second)
    upper_three = apply_rows(blocks[3], first) + apply_rows(blocks[4], second)
    upper_two, upper_three = lax.psum((upper_two, upper_three), "leaf")
    third = apply_rows(root_inverses[0], root_rhs[0] - upper_two)
    fourth = apply_rows(root_inverses[1], root_rhs[1] - upper_three - apply_rows(root_block, third))
    return (jnp.stack([first, second])[None], jnp.stack([third, fourth]))


def pairs(dest):
    out = []
    for r in range(2):
        for zh in range(2):
            for zl in range(2):
                for x in range(2):
                    for l in range(2):
                        d = dest(r, zh, zl, x, l)
                        if d is None:
                            continue
                        s = (r * 8 + zh * 4 + zl * 2 + x) * 2 + l
                        e = (d[0] * 8 + d[1] * 4 + d[2] * 2 + d[3]) * 2 + d[4]
                        out.append((s, e))
    return out


def send(value, dest):
    return lax.ppermute(value, AXES, pairs(dest))


def to_far(r, zh, zl, x, l):
    return r, zh ^ 1, zl, x, l


def to_second(r, zh, zl, x, l):
    return (r, zh, zl, x ^ 1, l) if l == 0 else (r ^ 1, zh, zl, x, l)


def to_third(r, zh, zl, x, l):
    return (r ^ 1, zh, zl, x, l) if l == 0 else (r, zh, zl, x ^ 1, l)


def to_pair(r, zh, zl, x, l):
    return r, zh, zl ^ 1, x, l


def to_core(r, zh, zl, x, l):
    return r, zh, zl, x, l ^ 1


def to_pair_core(r, zh, zl, x, l):
    return r, zh, zl ^ 1, x, l ^ 1


def to_row(r, zh, zl, x, l):
    return r ^ 1, zh, zl, x, l


def to_group(b1, b2):
    return lambda r, zh, zl, x, l: (r, zh ^ b1, zl, x ^ b2, l)


def to_group_by_core(b1, b2):
    return lambda r, zh, zl, x, l: (r ^ l, zh ^ b1, zl, x ^ b2, l)


def after(value, *others):
    return lax.optimization_barrier((value,) + others)[0]


def vmem():
    return pl.BlockSpec(memory_space=pltpu.VMEM)


def smem():
    return pl.BlockSpec(memory_space=pltpu.SMEM)


def shaped(*dims):
    return jax.ShapeDtypeStruct(dims, F32)


def lanes_low():
    return lax.broadcasted_iota(jnp.int32, (1, 128), 1) < 64


def swap_lanes(one, two):
    low = lanes_low()
    even = jnp.where(low, one, pltpu.roll(two, 64, one.ndim - 1))
    odd = jnp.where(low, pltpu.roll(one, 64, one.ndim - 1), two)
    return even, odd


def split(value):
    high = value.astype(BF16)
    return high, (value - high.astype(F32)).astype(BF16)


def dot3(left, right):
    lh, ll = left
    rh, rl = right
    whole = jnp.dot(lh, rl, preferred_element_type=F32)
    whole += jnp.dot(ll, rh, preferred_element_type=F32)
    return whole + jnp.dot(lh, rh, preferred_element_type=F32)


def flat(value):
    return jnp.concatenate([value[:64], value[64:]], axis=1)


def spot():
    row, col, core = (lax.axis_index(name) for name in AXES)
    return row, col // 4, (col // 2) % 2, col % 2, core


def call(name, kernel, outs, *operands, specs=None, scratch=()):
    specs = specs or [None] * len(operands)
    fixed = [
        pltpu.with_memory_space_constraint(o, pltpu.VMEM) if s is None else o
        for o, s in zip(operands, specs)
    ]
    return pl.pallas_call(
        kernel,
        out_shape=[pltpu.VMEM(dims, F32) for dims in outs],
        in_specs=[vmem() if s is None else s for s in specs],
        out_specs=[vmem() for _ in outs],
        scratch_shapes=list(scratch),
        compiler_params=pltpu.CompilerParams(vmem_limit_bytes=VMEM_OF_A_KERNEL),
        name=name,
    )(*fixed)


def cut_columns(source, held, outs):
    r, zh, _, x, _ = spot()
    for p in range(2):
        for z in range(2):
            start = pl.multiple_of((2 * r + z) * 128, 128)
            one = source[p, 0, :, pl.ds(start, 128)]
            two = source[p, 1, :, pl.ds(start, 128)]
            held[2 * z, p], held[2 * z + 1, p] = swap_lanes(one, two)
    for b1 in range(2):
        for b2 in range(2):
            outs[b1 * 2 + b2][...] = held[(zh ^ b1) * 2 + (x ^ b2)]


def part_rows(source, keep, out):
    zl = spot()[2]
    for a in range(2):
        even, odd = swap_lanes(source[a, :, :128], source[a, :, 128:])
        keep[a] = jnp.where(zl == 0, even, odd)
        out[a] = jnp.where(zl == 0, odd, even)


def begin_kernel(inverse_ref, rhs_ref, *refs):
    part_rows(inverse_ref.at[0, 0], refs[0], refs[1])
    cut_columns(rhs_ref.at[0], refs[6], refs[2:6])


def prepare_kernel(tiles_ref, inverse_ref, root_ref, blocks_ref, lower_ref, rhs_ref, *refs):
    keep, out, masked_ref, lower_out = refs[:4]
    part_rows(inverse_ref.at[0, 1], keep.at[0], out.at[0])
    for m in range(2):
        part_rows(root_ref.at[m], keep.at[m + 1], out.at[m + 1])
    for t in range(2):
        lanes = slice(t * 128, t * 128 + 128)
        for a in range(2):
            lower_out[t, a] = lower_ref[a, :, lanes]
        for m in range(5):
            weight = tiles_ref[0, m, t, 0].astype(F32)
            for a in range(2):
                masked_ref[m, t, a] = blocks_ref[0, m, a, :, lanes] * weight
    cut_columns(rhs_ref, refs[8], refs[4:8])


def fetch(near, far, pick, dest, sems, swapped=None, from_core=0):
    r, zh, _, x, l = spot()
    copies = []
    for b3 in range(2):
        for b2 in range(2):
            for b1 in range(2):

                def copy_of(sources, core):
                    rr = r ^ jnp.where(core == 0, b3, b2)
                    xx = x ^ jnp.where(core == 0, b2, b3)
                    return pltpu.make_async_copy(
                        pick(sources[b3], b2 * 2 + b1),
                        dest(rr, zh ^ b1, xx),
                        sems.at[b3 * 4 + b2 * 2 + b1],
                    )

                copy = copy_of((near, far), l)
                if swapped is None:
                    copy.start()
                else:
                    pl.when(l == from_core)(copy.start)
                    pl.when(l != from_core)(copy_of(swapped, 1 - l).start)
                copies.append(copy)
    return copies


def wait_all(copies):
    for copy in copies:
        copy.wait()


def solve(inverse, vector):
    left = split(flat(vector))
    parts = [dot3(left, split(inverse[a].reshape(512, 128))) for a in range(2)]
    return jnp.concatenate(parts, axis=0)


def update(held, terms, waits):
    sums = [None, None]
    for t, vector in enumerate(terms):
        waits[t]()
        left = split(flat(vector))
        for a in range(2):
            right = jnp.concatenate(
                [held[t, a, 0].reshape(256, 128), held[t, a, 1].reshape(256, 128)], axis=1
            )
            part = dot3(left, split(right))
            sums[a] = part if sums[a] is None else sums[a] + part
    return jnp.concatenate(sums, axis=0)


def sum_four(refs):
    return (refs[0][...] + refs[1][...]) + (refs[2][...] + refs[3][...])


def inverse_place(inverse):
    return lambda r, zh, x: inverse.at[r, :, zh, :, x]


def block_place(held, t):
    return lambda r, zh, x: held.at[t, r, :, :, zh, x]


def half_place(held, t, half):
    return lambda r, zh, x: held.at[t, r, half, :, zh, x]


def matrix(m):
    return lambda ref, b: ref.at[b, m]


def link_0_kernel(b_ref, near, far, part_ref, y_ref, inverse, held, sems):
    first = fetch(near, far, matrix(0), inverse_place(inverse), sems.at[0])
    second = fetch(near, far, matrix(1), block_place(held, 0), sems.at[1])
    wait_all(first)
    solved = solve(inverse, b_ref[...])
    y_ref[...] = solved
    part_ref[...] = update(held, [solved], [functools.partial(wait_all, second)])


def link_1_kernel(b_ref, own, got, y0_ref, near, far, part_ref, y_ref, inverse, held, sems):
    copies = [fetch(near, far, matrix(0), inverse_place(inverse), sems.at[0])]
    for t in range(2):
        copies.append(fetch(near, far, matrix(t + 1), block_place(held, t), sems.at[t + 1]))
    wait_all(copies[0])
    solved = solve(inverse, b_ref[...] - (own[...] + got[...]))
    y_ref[...] = solved
    waits = [functools.partial(wait_all, c) for c in copies[1:]]
    part_ref[...] = update(held, [y0_ref[...], solved], waits)


def link_2_kernel(b_ref, s0, s1, s2, s3, y0_ref, y1_ref, near, far, *refs):
    root, swapped = refs[:2], refs[2:4]
    part_ref, y_ref, inverse, held, sems = refs[4:]
    first = fetch(
        *root, lambda ref, b: ref.at[b, pl.ds(0, 2)], inverse_place(inverse), sems.at[0], swapped, 0
    )
    copies = [fetch(near, far, matrix(t), block_place(held, t), sems.at[t + 1]) for t in range(2)]
    halves = [
        fetch(*root, matrix(2), half_place(held, 2, h), sems.at[3 + h], swapped, h) for h in range(2)
    ]
    wait_all(first)
    solved = solve(inverse, b_ref[...] - sum_four((s0, s1, s2, s3)))
    y_ref[...] = solved
    copies.append(halves[0] + halves[1])
    waits = [functools.partial(wait_all, c) for c in copies]
    last = jnp.where(spot()[4] == 0, solved, 0.0)
    part_ref[...] = update(held, [y0_ref[...], y1_ref[...], last], waits)


def link_3_kernel(b_ref, s0, s1, s2, s3, y2_ref, *refs):
    root, swapped, outs = refs[:2], refs[2:4], refs[4:8]
    pieces, inverse, sems = refs[8:]
    first = fetch(
        *root, lambda ref, b: ref.at[b, pl.ds(0, 2)], inverse_place(inverse), sems.at[0], swapped, 1
    )
    vector = b_ref[...] - sum_four((s0, s1, s2, s3))
    wait_all(first)
    lay_values((y2_ref[...], solve(inverse, vector)), outs, pieces)


def link_scratch(nblocks, nsems):
    blocks = [pltpu.VMEM((nblocks, 2, 2, 2, 2, 2, 32, 128), F32)] if nblocks else []
    return (
        [pltpu.VMEM((2, 2, 2, 2, 2, 32, 128), F32)] + blocks + [pltpu.SemaphoreType.DMA((nsems, 8))]
    )


def lay_values(values, outs, held):
    _, zh, _, x, _ = spot()
    for p, value in enumerate(values):
        held[:, p] = value.T.reshape(4, 32, 128)
    for b1 in range(2):
        for b2 in range(2):
            outs[b1 * 2 + b2][...] = held[(zh ^ b1) * 2 + (x ^ b2)]


def lay_kernel(first, second, *refs):
    lay_values((first[...], second[...]), refs[:4], refs[4])


def stand_kernel(near_ref, other_ref, one_ref, two_ref, held):
    _, zh, zl, x, _ = spot()
    for b1 in range(2):
        for b2 in range(2):
            for b, source in enumerate((near_ref, other_ref)):
                held[((zh ^ b1) * 2 + (zl ^ b)) * 2 + (x ^ b2)] = source[b1 * 2 + b2]
    for p, out in enumerate((one_ref, two_ref)):
        out[...] = held[:, p].reshape(256, 128).T


def join_kernel(by_core, near_ref, other_ref, out_ref, held):
    r, zh, _, x, core = spot()
    near = r ^ core if by_core else r
    for b1 in range(2):
        for b2 in range(2):
            place = (zh ^ b1) * 2 + (x ^ b2)
            held[near * 4 + place] = near_ref[b1 * 2 + b2]
            held[(near ^ 1) * 4 + place] = other_ref[b1 * 2 + b2]
    for p in range(2):
        for u in range(4):
            lanes = slice(u * 128, u * 128 + 128)
            out_ref[p, 0, :, lanes], out_ref[p, 1, :, lanes] = swap_lanes(
                held[2 * u, p], held[2 * u + 1, p]
            )


def join(name, by_core, near, other):
    return pl.pallas_call(
        functools.partial(join_kernel, by_core),
        out_shape=shaped(2, 2, 32, 512),
        in_specs=[vmem()] * 2,
        out_specs=vmem(),
        scratch_shapes=[pltpu.VMEM((8, 2, 32, 128), F32)],
        compiler_params=pltpu.CompilerParams(vmem_limit_bytes=VMEM_OF_A_KERNEL),
        name=name,
    )(*(pltpu.with_memory_space_constraint(v, pltpu.VMEM) for v in (near, other)))


def to_groups(parts):
    return [parts[0]] + [send(parts[k], to_group(k // 2, k % 2)) for k in (1, 2, 3)]


PIECES = [(2, 32, 128)] * 4
VECTOR = [(128, 256), (128, 128)]


def grouped(leaf_rhs, root_rhs, leaf_inverses, root_inverses, leaf_blocks, root_block, pattern):
    core = lax.axis_index("leaf")
    zl = (lax.axis_index("col") // 2) % 2
    four_pieces = pltpu.VMEM((4, 2, 32, 128), F32)

    keep_0, out_0, *leaf_cut = call(
        "begin",
        begin_kernel,
        [(2, 32, 128)] * 2 + PIECES,
        leaf_inverses,
        leaf_rhs,
        specs=[vmem(), vmem()],
        scratch=[four_pieces],
    )
    got_0 = send(out_0, to_pair)
    leaf_moved = to_groups(leaf_cut)
    tiles, _ = lax.optimization_barrier((pattern, out_0))
    keeps, outs, blocks, lower, *root_cut = call(
        "prepare",
        prepare_kernel,
        [(3, 2, 32, 128)] * 2 + [(5, 2, 2, 32, 128), (2, 2, 32, 128)] + PIECES,
        tiles,
        leaf_inverses,
        root_inverses,
        leaf_blocks,
        root_block,
        root_rhs,
        specs=[smem()] + [vmem()] * 5,
        scratch=[four_pieces],
    )

    def whole(keep, got):
        return jnp.stack([jnp.where(zl == 0, keep, got), jnp.where(zl == 0, got, keep)], axis=-3)

    chunk_a = jnp.stack([whole(keep_0, got_0), blocks[0]])
    far_a = send(chunk_a, to_far)
    rest = send(after(outs, chunk_a), to_pair)
    leaf_in = jnp.stack(after(leaf_moved, chunk_a))
    leaf_pair = send(leaf_in, to_pair)

    inverses = whole(keeps, after(rest, leaf_in))
    chunk_b = jnp.concatenate([inverses[:1], blocks[1:3]])
    chunk_c = blocks[3:5]
    chunk_d = jnp.concatenate(
        [
            jnp.where(core == 0, inverses[1], inverses[2]),
            jnp.where(core == 0, lower[0], lower[1])[None],
        ]
    )
    b0, b1 = call(
        "stand_leaf",
        stand_kernel,
        [(128, 256)] * 2,
        after(leaf_in, chunk_b, chunk_d),
        leaf_pair,
        scratch=[pltpu.VMEM((8, 2, 32, 128), F32)],
    )

    two_a = jnp.stack([chunk_a, after(far_a, b0)])
    second_a = send(two_a, to_second)
    far_b = send(after(chunk_b, two_a), to_far)
    root_moved = to_groups(after(root_cut, two_a))
    four_a = jnp.concatenate([two_a, after(second_a, root_moved[0])])
    third_a = send(four_a, to_third)
    root_in = jnp.stack(after(root_moved, four_a))
    root_pair = send(root_in, to_pair)
    two_b = jnp.stack([chunk_b, after(far_b, root_in)])
    second_b = send(two_b, to_second)
    far_d = send(after(chunk_d, two_b), to_far)
    r2, r3 = call(
        "stand_root",
        stand_kernel,
        [(128, 256)] * 2,
        after(root_in, two_b),
        root_pair,
        scratch=[pltpu.VMEM((8, 2, 32, 128), F32)],
    )

    own, y0 = call(
        "link_0",
        link_0_kernel,
        VECTOR,
        after(b0, r2),
        four_a,
        third_a,
        scratch=link_scratch(1, 2),
    )
    got = send(own, to_pair)
    four_b = jnp.concatenate([two_b, after(second_b, own)])
    third_b = send(four_b, to_third)
    two_d = jnp.stack([chunk_d, after(far_d, four_b)])
    second_d = send(two_d, to_second)
    far_c = send(after(chunk_c, two_d), to_far)
    four_d = jnp.concatenate([two_d, after(second_d, far_c)])
    third_d = send(four_d, to_third)
    two_c = jnp.stack([chunk_c, after(far_c, four_d)])
    second_c = send(two_c, to_second)

    own, y1 = call(
        "link_1",
        link_1_kernel,
        VECTOR,
        after(b1, two_c),
        own,
        got,
        y0,
        four_b,
        third_b,
        scratch=link_scratch(2, 3),
    )
    sums = [own, send(own, to_pair), send(own, to_core), send(own, to_pair_core)]
    four_c = jnp.concatenate([two_c, after(second_c, own)])
    third_c = send(four_c, to_third)
    swap_d = (send(after(four_d, four_c), to_core), send(after(third_d, four_c), to_core))
    leaf_parts = call("lay_leaf", lay_kernel, PIECES, after(y0, four_c), y1, scratch=[four_pieces])
    leaf_moved = to_groups(leaf_parts)

    own, y2 = call(
        "link_2",
        link_2_kernel,
        VECTOR,
        after(r2, leaf_parts[0]),
        *sums,
        y0,
        y1,
        four_c,
        third_c,
        four_d,
        third_d,
        *swap_d,
        scratch=link_scratch(3, 5),
    )
    sums = [own, send(own, to_pair), send(own, to_core), send(own, to_pair_core)]
    leaf_near = jnp.stack(after(leaf_moved, own))
    leaf_other = send(leaf_near, to_row)
    leaf_solution = join("join_leaf", False, leaf_near, leaf_other)

    root_parts = call(
        "link_3",
        link_3_kernel,
        PIECES,
        after(r3, leaf_near),
        *sums,
        y2,
        four_d,
        third_d,
        *swap_d,
        scratch=[four_pieces] + link_scratch(0, 1),
    )
    moved = jnp.stack([send(root_parts[k], to_group_by_core(k // 2, k % 2)) for k in range(4)])
    swapped = send(moved, to_core)
    root_solution = join("join_root", True, moved, swapped)
    return leaf_solution[None], root_solution


def solution(mesh):
    placed = (
        P("leaf", None, None, "col", None),
        P(None, None, "col", None),
        P("leaf", None, None, "col", "row"),
        P(None, None, "col", "row"),
        P("leaf", None, None, "col", "row"),
        P(None, "col", "row"),
        P("leaf", None, "row", "col"),
    )
    small = (mesh.shape["row"], mesh.shape["col"], mesh.shape["leaf"]) == (2, 8, 2)
    return jax.shard_map(
        grouped if small else general,
        mesh=mesh,
        in_specs=placed,
        out_specs=(P("leaf", None, None, "col", None), P(None, None, "col", None)),
        check_vma=False,
    )
```

time: 714 us -> 110 us (0.15)
  waiting for transfers between devices: 626 us -> 49.2 us
  blocking collectives: 51.3 us -> 0 us
  starting transfers between devices: 0.46 us -> 45.2 us
  between operations: 14 us -> 1 us
  matrix products: 12 us -> 0 us
  Pallas kernels: 0 us -> 8.7 us
    reduce_scatter x10 -> x0, waiting for transfers between devices: 609 us -> none  [apply_rows(): owned = lax.psum_scatter(term, 'col', scatter_dimension=0, tiled=True)]
    all_gather x10 -> x0, blocking collectives: 51.3 us -> none  [apply_rows(): return lax.all_gather(owned[None], 'row', axis=0, tiled=True)]
    ppermute x0 -> x40, waiting for transfers between devices: none -> 49.2 us  [send(): return lax.ppermute(value, AXES, pairs(dest))]
    ppermute x0 -> x40, starting transfers between devices: none -> 45.2 us  [send(): return lax.ppermute(value, AXES, pairs(dest))]
    psum x1 -> x0, waiting for transfers between devices: 17.2 us -> none  [shards(): upper_two, upper_three = lax.psum((upper_two, upper_three), 'leaf')]
    dot_general x10 -> x0, matrix products: 12 us -> none  [apply_rows(): lax.dot_general(block, vector, (((0,), (0,)), ((), ())), precision=lax.Pr...]
    pallas_call x0 -> x11, Pallas kernels: none -> 8.7 us  [the longest x9 6.97 us: call(): pl.pallas_call(kernel, out_shape=[pltpu.VMEM(dims, F32) for dims in outs]...]
  transfers between devices with their start and end apart: 11 -> 40, of which waited for: 11 -> 18; matrix products, arithmetic and copies ran while one was open for 1% -> 0% of each run, Pallas kernels for 0% -> 6%
where the time goes in v3:
time: 110 us
  waiting for transfers between devices  49.2 us (45%)
  starting transfers between devices  45.2 us (41%)
  Pallas kernels  8.7 us (8%)
  local copies, waits for them, and re-layouts  5.38 us (5%)
    ppermute x40, waiting for transfers between devices, send(): return lax.ppermute(value, AXES, pairs(dest))  49.2 us
    ppermute x40, starting transfers between devices, send(): return lax.ppermute(value, AXES, pairs(dest))  45.2 us
    pallas_call x9, Pallas kernels, call(): pl.pallas_call(kernel, out_shape=[pltpu.VMEM(dims, F32) for dims in outs]...  6.97 us
    unnamed x16, local copies, waits for them, and re-layouts  5.25 us
  transfers between devices with their start and end apart: 40, of which 18 were waited for; matrix products, arithmetic and copies ran while one was open for 0% of the time, Pallas kernels for 6%

profile of v3, /device:TPU:0, one launch (start us, length us, event | category | flops | bytes accessed | tf_op | source)
XLA Modules:
  0.0 109.8 jit_solution(1864477218883559933)
XLA Ops:
  0.6 0.9 copy-done
  1.5 0.9 copy-done.3
  2.6 3.0 %collective-permute-start = (f32[2,32,128]{2,1,0:T(8,128)S(1)}, f32[2,32,128]{2,1,0:T(8,128)S(1)}, u32[]{:S(2)}, u32[]{:S(2)}) collective-permute-start(f32[2,32,128]{2,1,0:T(8,128)S(1)} %get-tuple-element.74), channel_id=1, source_target_pairs={{0,2},{1,3},{2,0},{3,1},{4,6},{5,7},{6,4},{7,5},{8,10},{9,11},{10,... | collective-permute-start | bytes 98312 | tf_op jit(solution)/shard_map/ppermute | solution.py:67
  5.7 2.6 %collective-permute-start.1 = (f32[2,32,128]{2,1,0:T(8,128)S(1)}, f32[2,32,128]{2,1,0:T(8,128)S(1)}, u32[]{:S(2)}, u32[]{:S(2)}) collective-permute-start(f32[2,32,128]{2,1,0:T(8,128)S(1)} %get-tuple-element.75), channel_id=1, source_target_pairs={{0,8},{1,9},{2,10},{3,11},{4,12},{5,13},{6,14},{7,15},{8,0},{9,1},... | collective-permute-start | bytes 98312 | tf_op jit(solution)/shard_map/ppermute | solution.py:67
  8.2 1.9 %collective-permute-start.3 = (f32[2,32,128]{2,1,0:T(8,128)S(1)}, f32[2,32,128]{2,1,0:T(8,128)S(1)}, u32[]{:S(2)}, u32[]{:S(2)}) collective-permute-start(f32[2,32,128]{2,1,0:T(8,128)S(1)} %get-tuple-element.78), channel_id=1, source_target_pairs={{0,4},{1,5},{2,6},{3,7},{4,0},{5,1},{6,2},{7,3},{8,12},{9,13},{10,... | collective-permute-start | bytes 98312 | tf_op jit(solution)/shard_map/ppermute | solution.py:67
  10.9 1.0 copy-done.2
  11.9 0.9 copy-done.5
  12.8 0.8 copy-done.6
  13.6 0.8 prepare.1
  14.6 2.7 %collective-permute-start.6 = (f32[2,2,2,32,128]{4,3,2,1,0:T(8,128)S(1)}, f32[2,2,2,32,128]{4,3,2,1,0:T(8,128)S(1)}, u32[]{:S(2)}, u32[]{:S(2)}) collective-permute-start(f32[2,2,2,32,128]{4,3,2,1,0:T(8,128)S(1)} %get-tuple-element.154), channel_id=1, source_target_pairs={{0,8},{1,9},{2,10},{3,11},{4,12},{5,13},{6,14},{7,15},{8,0},{9,1},... | collective-permute-start | bytes 393224 | tf_op jit(solution)/shard_map/ppermute | solution.py:67
  17.8 1.6 %collective-permute-start.5 = (f32[4,2,32,128]{3,2,1,0:T(8,128)S(1)}, f32[4,2,32,128]{3,2,1,0:T(8,128)S(1)}, u32[]{:S(2)}, u32[]{:S(2)}) collective-permute-start(f32[4,2,32,128]{3,2,1,0:T(8,128)S(1)} %pad_maximum_fusion.10.near_ref), channel_id=1, source_target_pairs={{0,4},{1,5},{2,6},{3,7},{4,0},{5,1},{6,2},{7,3},{8,12},{9,13},{10,... | collective-permute-start | bytes 393224 | tf_op jit(solution)/shard_map/ppermute | solution.py:67
  19.4 4.7 %collective-permute-done.4 = f32[3,2,32,128]{3,2,1,0:T(8,128)S(1)} collective-permute-done((f32[3,2,32,128]{3,2,1,0:T(8,128)S(1)}, f32[3,2,32,128]{3,2,1,0:T(8,128)S(1)}, u32[]{:S(2)}, u32[]{:S(2)}) %collective-permute-start.4) | collective-permute-done | bytes 98336 | tf_op jit(solution)/shard_map/ppermute | solution.py:67
  24.2 1.6 %collective-permute-done.5.other_ref = f32[4,2,32,128]{3,2,1,0:T(8,128)S(1)} collective-permute-done((f32[4,2,32,128]{3,2,1,0:T(8,128)S(1)}, f32[4,2,32,128]{3,2,1,0:T(8,128)S(1)}, u32[]{:S(2)}, u32[]{:S(2)}) %collective-permute-start.5) | collective-permute-done | bytes 131104 | tf_op jit(solution)/shard_map/ppermute | solution.py:67
  26.1 1.6 %collective-permute-start.10 = (f32[2,2,2,2,32,128]{5,4,3,2,1,0:T(8,128)S(1)}, f32[2,2,2,2,32,128]{5,4,3,2,1,0:T(8,128)S(1)}, u32[]{:S(2)}, u32[]{:S(2)}) collective-permute-start(f32[2,2,2,2,32,128]{5,4,3,2,1,0:T(8,128)S(1)} %pad_maximum_fusion.5), channel_id=1, source_target_pairs={{0,2},{1,17},{2,0},{3,19},{4,6},{5,21},{6,4},{7,23},{8,10},{9,25},... | collective-permute-start | bytes 786440 | tf_op jit(solution)/shard_map/ppermute | solution.py:67
  28.2 3.9 %collective-permute-start.9 = (f32[2,32,128]{2,1,0:T(8,128)S(1)}, f32[2,32,128]{2,1,0:T(8,128)S(1)}, u32[]{:S(2)}, u32[]{:S(2)}) collective-permute-start(f32[2,32,128]{2,1,0:T(8,128)S(1)} %get-tuple-element.100), channel_id=1, source_target_pairs={{0,10},{1,11},{2,8},{3,9},{4,14},{5,15},{6,12},{7,13},{8,2},{9,3},... | collective-permute-start | bytes 98312 | tf_op jit(solution)/shard_map/ppermute | solution.py:67
  32.0 0.8 collective-permute-done.10
  32.9 1.6 %collective-permute-start.13 = (f32[4,2,2,2,32,128]{5,4,3,2,1,0:T(8,128)S(1)}, f32[4,2,2,2,32,128]{5,4,3,2,1,0:T(8,128)S(1)}, u32[]{:S(2)}, u32[]{:S(2)}) collective-permute-start(f32[4,2,2,2,32,128]{5,4,3,2,1,0:T(8,128)S(1)} %pad_maximum_fusion.1.near), channel_id=1, source_target_pairs={{0,16},{1,3},{2,18},{3,1},{4,20},{5,7},{6,22},{7,5},{8,24},{9,11},... | collective-permute-start | bytes 1572872 | tf_op jit(solution)/shard_map/ppermute | solution.py:67
  34.5 1.4 %collective-permute-done.8 = f32[2,32,128]{2,1,0:T(8,128)S(1)} collective-permute-done((f32[2,32,128]{2,1,0:T(8,128)S(1)}, f32[2,32,128]{2,1,0:T(8,128)S(1)}, u32[]{:S(2)}, u32[]{:S(2)}) %collective-permute-start.8) | collective-permute-done | bytes 32800 | tf_op jit(solution)/shard_map/ppermute | solution.py:67
  35.9 3.7 %collective-permute-done.9 = f32[2,32,128]{2,1,0:T(8,128)S(1)} collective-permute-done((f32[2,32,128]{2,1,0:T(8,128)S(1)}, f32[2,32,128]{2,1,0:T(8,128)S(1)}, u32[]{:S(2)}, u32[]{:S(2)}) %collective-permute-start.9) | collective-permute-done | bytes 32800 | tf_op jit(solution)/shard_map/ppermute | solution.py:67
  39.7 2.7 %collective-permute-done.11 = f32[3,2,2,32,128]{4,3,2,1,0:T(8,128)S(1)} collective-permute-done((f32[3,2,2,32,128]{4,3,2,1,0:T(8,128)S(1)}, f32[3,2,2,32,128]{4,3,2,1,0:T(8,128)S(1)}, u32[]{:S(2)}, u32[]{:S(2)}) %collective-permute-start.11) | collective-permute-done | bytes 196640 | tf_op jit(solution)/shard_map/ppermute | solution.py:67
  42.4 1.6 %collective-permute-start.15 = (f32[2,3,2,2,32,128]{5,4,3,2,1,0:T(8,128)S(1)}, f32[2,3,2,2,32,128]{5,4,3,2,1,0:T(8,128)S(1)}, u32[]{:S(2)}, u32[]{:S(2)}) collective-permute-start(f32[2,3,2,2,32,128]{5,4,3,2,1,0:T(8,128)S(1)} %pad_maximum_fusion.3), channel_id=1, source_target_pairs={{0,2},{1,17},{2,0},{3,19},{4,6},{5,21},{6,4},{7,23},{8,10},{9,25},... | collective-permute-start | bytes 1179656 | tf_op jit(solution)/shard_map/ppermute | solution.py:67
  43.9 1.6 %collective-permute-start.14 = (f32[3,2,32,128]{3,2,1,0:T(8,128)S(1)}, f32[3,2,32,128]{3,2,1,0:T(8,128)S(1)}, u32[]{:S(2)}, u32[]{:S(2)}) collective-permute-start(f32[3,2,32,128]{3,2,1,0:T(8,128)S(1)} %get-tuple-element.112), channel_id=1, source_target_pairs={{0,8},{1,9},{2,10},{3,11},{4,12},{5,13},{6,14},{7,15},{8,0},{9,1},... | collective-permute-start | bytes 294920 | tf_op jit(solution)/shard_map/ppermute | solution.py:67
  45.6 4.4 %collective-permute-done.12.other_ref = f32[4,2,32,128]{3,2,1,0:T(8,128)S(1)} collective-permute-done((f32[4,2,32,128]{3,2,1,0:T(8,128)S(1)}, f32[4,2,32,128]{3,2,1,0:T(8,128)S(1)}, u32[]{:S(2)}, u32[]{:S(2)}) %collective-permute-start.12) | collective-permute-done | bytes 131104 | tf_op jit(solution)/shard_map/ppermute | solution.py:67
  50.1 1.1 link_0.1
  51.3 1.1 collective-permute-start.20
  52.4 0.9 collective-permute-start.17
  53.4 7.0 %collective-permute-done.16 = f32[2,2,2,32,128]{4,3,2,1,0:T(8,128)S(1)} collective-permute-done((f32[2,2,2,32,128]{4,3,2,1,0:T(8,128)S(1)}, f32[2,2,2,32,128]{4,3,2,1,0:T(8,128)S(1)}, u32[]{:S(2)}, u32[]{:S(2)}) %collective-permute-start.16) | collective-permute-done | bytes 131104 | tf_op jit(solution)/shard_map/ppermute | solution.py:67
  60.4 0.9 collective-permute-start.18
  61.3 1.3 %collective-permute-start.28 = (f32[4,3,2,32,128]{4,3,2,1,0:T(8,128)S(1)}, f32[4,3,2,32,128]{4,3,2,1,0:T(8,128)S(1)}, u32[]{:S(2)}, u32[]{:S(2)}) collective-permute-start(f32[4,3,2,32,128]{4,3,2,1,0:T(8,128)S(1)} %pad_maximum_fusion.4.refs_0_), channel_id=1, source_target_pairs={{0,16},{1,3},{2,18},{3,1},{4,20},{5,7},{6,22},{7,5},{8,24},{9,11},... | collective-permute-start | bytes 1179656 | tf_op jit(solution)/shard_map/ppermute | solution.py:67
  62.5 5.0 %collective-permute-done.19.got = f32[128,256]{1,0:T(8,128)S(1)} collective-permute-done((f32[128,256]{1,0:T(8,128)S(1)}, f32[128,256]{1,0:T(8,128)S(1)}, u32[]{:S(2)}, u32[]{:S(2)}) %collective-permute-start.19) | collective-permute-done | bytes 131104 | tf_op jit(solution)/shard_map/ppermute | solution.py:67
  67.5 1.5 %link_1.1 = (f32[128,256]{1,0:T(8,128)S(1)}, f32[128,128]{1,0:T(8,128)S(1)}) custom-call(f32[128,256]{1,0:T(8,128)S(1)} %get-tuple-element.120.b_ref, f32[128,256]{1,0:T(8,128)S(1)} %get-tuple-element.113.own, f32[128,256]{1,0:T(8,128)S(1)} %collective-permute-done.19.got, f32[128,128]{1,0:T(8,128)S(1)} %get-tuple-element.123.y0_ref.first, ...), custom_call_target="tpu_custom_call" | custom-call | tf_op jit(solution)/shard_map/link_1/pallas_call | solution.py:161
  69.5 1.2 %collective-permute-start.27 = (f32[4,2,2,2,32,128]{5,4,3,2,1,0:T(8,128)S(1)}, f32[4,2,2,2,32,128]{5,4,3,2,1,0:T(8,128)S(1)}, u32[]{:S(2)}, u32[]{:S(2)}) collective-permute-start(f32[4,2,2,2,32,128]{5,4,3,2,1,0:T(8,128)S(1)} %pad_maximum_fusion.2.near), channel_id=1, source_target_pairs={{0,16},{1,3},{2,18},{3,1},{4,20},{5,7},{6,22},{7,5},{8,24},{9,11},... | collective-permute-start | bytes 1572872 | tf_op jit(solution)/shard_map/ppermute | solution.py:67
  71.4 5.2 %collective-permute-done.26.s3 = f32[128,256]{1,0:T(8,128)S(1)} collective-permute-done((f32[128,256]{1,0:T(8,128)S(1)}, f32[128,256]{1,0:T(8,128)S(1)}, u32[]{:S(2)}, u32[]{:S(2)}) %collective-permute-start.26) | collective-permute-done | bytes 131104 | tf_op jit(solution)/shard_map/ppermute | solution.py:67
  76.8 1.4 %collective-permute-start.21 = (f32[2,32,128]{2,1,0:T(8,128)S(1)}, f32[2,32,128]{2,1,0:T(8,128)S(1)}, u32[]{:S(2)}, u32[]{:S(2)}) collective-permute-start(f32[2,32,128]{2,1,0:T(8,128)S(1)} %get-tuple-element.126), channel_id=1, source_target_pairs={{0,2},{1,3},{2,0},{3,1},{4,6},{5,7},{6,4},{7,5},{8,10},{9,11},{10,... | collective-permute-start | bytes 98312 | tf_op jit(solution)/shard_map/ppermute | solution.py:67
  78.1 4.4 %collective-permute-done.24.s1 = f32[128,256]{1,0:T(8,128)S(1)} collective-permute-done((f32[128,256]{1,0:T(8,128)S(1)}, f32[128,256]{1,0:T(8,128)S(1)}, u32[]{:S(2)}, u32[]{:S(2)}) %collective-permute-start.24) | collective-permute-done | bytes 131104 | tf_op jit(solution)/shard_map/ppermute | solution.py:67
  82.6 3.4 %collective-permute-start.23 = (f32[2,32,128]{2,1,0:T(8,128)S(1)}, f32[2,32,128]{2,1,0:T(8,128)S(1)}, u32[]{:S(2)}, u32[]{:S(2)}) collective-permute-start(f32[2,32,128]{2,1,0:T(8,128)S(1)} %get-tuple-element.128), channel_id=1, source_target_pairs={{0,10},{1,11},{2,8},{3,9},{4,14},{5,15},{6,12},{7,13},{8,2},{9,3},... | collective-permute-start | bytes 98312 | tf_op jit(solution)/shard_map/ppermute | solution.py:67
  86.0 2.4 %link_2.1 = (f32[128,256]{1,0:T(8,128)S(1)}, f32[128,128]{1,0:T(8,128)S(1)}) custom-call(f32[128,256]{1,0:T(8,128)S(1)} %get-tuple-element.129.b_ref, f32[128,256]{1,0:T(8,128)S(1)} %get-tuple-element.121.s0, f32[128,256]{1,0:T(8,128)S(1)} %collective-permute-done.24.s1, f32[128,256]{1,0:T(8,128)S(1)} %collective-permute-done.25.s2, ...), custom_call_target="tpu_custom_call" | custom-call | tf_op jit(solution)/shard_map/link_2/pallas_call | solution.py:161
  88.9 1.7 %collective-permute-start.32 = (f32[128,256]{1,0:T(8,128)S(1)}, f32[128,256]{1,0:T(8,128)S(1)}, u32[]{:S(2)}, u32[]{:S(2)}) collective-permute-start(f32[128,256]{1,0:T(8,128)S(1)} %get-tuple-element.132.s0), channel_id=1, source_target_pairs={{0,4},{1,5},{2,6},{3,7},{4,0},{5,1},{6,2},{7,3},{8,12},{9,13},{10,... | collective-permute-start | bytes 393224 | tf_op jit(solution)/shard_map/ppermute | solution.py:67
  90.6 3.6 %collective-permute-done.34.s3 = f32[128,256]{1,0:T(8,128)S(1)} collective-permute-done((f32[128,256]{1,0:T(8,128)S(1)}, f32[128,256]{1,0:T(8,128)S(1)}, u32[]{:S(2)}, u32[]{:S(2)}) %collective-permute-start.34) | collective-permute-done | bytes 131104 | tf_op jit(solution)/shard_map/ppermute | solution.py:67
  94.2 1.0 collective-permute-done.32.s1
  96.6 1.3 %collective-permute-start.36 = (f32[2,32,128]{2,1,0:T(8,128)S(1)}, f32[2,32,128]{2,1,0:T(8,128)S(1)}, u32[]{:S(2)}, u32[]{:S(2)}) collective-permute-start(f32[2,32,128]{2,1,0:T(8,128)S(1)} %get-tuple-element.141), channel_id=1, source_target_pairs={{0,2},{1,19},{2,0},{3,17},{4,6},{5,23},{6,4},{7,21},{8,10},{9,27},... | collective-permute-start | bytes 98312 | tf_op jit(solution)/shard_map/ppermute | solution.py:67
  97.9 1.5 %collective-permute-start.37 = (f32[2,32,128]{2,1,0:T(8,128)S(1)}, f32[2,32,128]{2,1,0:T(8,128)S(1)}, u32[]{:S(2)}, u32[]{:S(2)}) collective-permute-start(f32[2,32,128]{2,1,0:T(8,128)S(1)} %get-tuple-element.142), channel_id=1, source_target_pairs={{0,8},{1,25},{2,10},{3,27},{4,12},{5,29},{6,14},{7,31},{8,0},{9,17... | collective-permute-start | bytes 98312 | tf_op jit(solution)/shard_map/ppermute | solution.py:67
  99.5 1.6 %collective-permute-start.38 = (f32[2,32,128]{2,1,0:T(8,128)S(1)}, f32[2,32,128]{2,1,0:T(8,128)S(1)}, u32[]{:S(2)}, u32[]{:S(2)}) collective-permute-start(f32[2,32,128]{2,1,0:T(8,128)S(1)} %get-tuple-element.143), channel_id=1, source_target_pairs={{0,10},{1,27},{2,8},{3,25},{4,14},{5,31},{6,12},{7,29},{8,2},{9,19... | collective-permute-start | bytes 98312 | tf_op jit(solution)/shard_map/ppermute | solution.py:67
  101.1 1.5 %collective-permute-start.31 = (f32[4,2,32,128]{3,2,1,0:T(8,128)S(1)}, f32[4,2,32,128]{3,2,1,0:T(8,128)S(1)}, u32[]{:S(2)}, u32[]{:S(2)}) collective-permute-start(f32[4,2,32,128]{3,2,1,0:T(8,128)S(1)} %pad_maximum_fusion.12.near_ref), channel_id=1, source_target_pairs={{0,16},{1,17},{2,18},{3,19},{4,20},{5,21},{6,22},{7,23},{8,24},{9,... | collective-permute-start | bytes 393224 | tf_op jit(solution)/shard_map/ppermute | solution.py:67
  102.8 2.6 %collective-permute-done.38 = f32[2,32,128]{2,1,0:T(8,128)S(1)} collective-permute-done((f32[2,32,128]{2,1,0:T(8,128)S(1)}, f32[2,32,128]{2,1,0:T(8,128)S(1)}, u32[]{:S(2)}, u32[]{:S(2)}) %collective-permute-start.38) | collective-permute-done | bytes 32800 | tf_op jit(solution)/shard_map/ppermute | solution.py:67
  105.4 2.6 %collective-permute-start.39 = (f32[4,2,32,128]{3,2,1,0:T(8,128)S(1)}, f32[4,2,32,128]{3,2,1,0:T(8,128)S(1)}, u32[]{:S(2)}, u32[]{:S(2)}) collective-permute-start(f32[4,2,32,128]{3,2,1,0:T(8,128)S(1)} %pad_maximum_fusion.13.near_ref), channel_id=1, source_target_pairs={{0,1},{1,0},{2,3},{3,2},{4,5},{5,4},{6,7},{7,6},{8,9},{9,8},{10,11... | collective-permute-start | bytes 393224 | tf_op jit(solution)/shard_map/ppermute | solution.py:67
  108.0 0.9 join_leaf.1
  109.0 0.9 join_root.1
  (82 shorter events, 6.3 us)
Async XLA Ops:
  0.6 0.9 copy-start
  1.5 0.9 copy-start.3
  2.5 8.4 %copy-start.1 = (f32[1,2,2,32,256]{4,3,2,1,0:T(8,128)S(1)}, f32[1,2,2,32,256]{4,3,2,1,0:T(8,128)}, u32[]{:S(2)}) copy-start(f32[1,2,2,32,256]{4,3,2,1,0:T(8,128)} %inverse_ref.3) | copy-start | bytes 393220
  2.5 8.4 %copy-start.4 = (f32[2,2,32,512]{3,2,1,0:T(8,128)S(1)}, f32[2,2,32,512]{3,2,1,0:T(8,128)}, u32[]{:S(2)}) copy-start(f32[2,2,32,512]{3,2,1,0:T(8,128)} %rhs_ref.3) | copy-start | bytes 786436
  2.6 14.6 %collective-permute-start = (f32[2,32,128]{2,1,0:T(8,128)S(1)}, f32[2,32,128]{2,1,0:T(8,128)S(1)}, u32[]{:S(2)}, u32[]{:S(2)}) collective-permute-start(f32[2,32,128]{2,1,0:T(8,128)S(1)} %get-tuple-element.74), channel_id=1, source_target_pairs={{0,2},{1,3},{2,0},{3,1},{4,6},{5,7},{6,4},{7,5},{8,10},{9,11},{10,... | collective-permute-start | bytes 98312 | tf_op jit(solution)/shard_map/ppermute | solution.py:67
  5.7 11.6 %collective-permute-start.1 = (f32[2,32,128]{2,1,0:T(8,128)S(1)}, f32[2,32,128]{2,1,0:T(8,128)S(1)}, u32[]{:S(2)}, u32[]{:S(2)}) collective-permute-start(f32[2,32,128]{2,1,0:T(8,128)S(1)} %get-tuple-element.75), channel_id=1, source_target_pairs={{0,8},{1,9},{2,10},{3,11},{4,12},{5,13},{6,14},{7,15},{8,0},{9,1},... | collective-permute-start | bytes 98312 | tf_op jit(solution)/shard_map/ppermute | solution.py:67
  8.2 9.0 %collective-permute-start.2 = (f32[2,32,128]{2,1,0:T(8,128)S(1)}, f32[2,32,128]{2,1,0:T(8,128)S(1)}, u32[]{:S(2)}, u32[]{:S(2)}) collective-permute-start(f32[2,32,128]{2,1,0:T(8,128)S(1)} %get-tuple-element.76), channel_id=1, source_target_pairs={{0,10},{1,11},{2,8},{3,9},{4,14},{5,15},{6,12},{7,13},{8,2},{9,3},... | collective-permute-start | bytes 98312 | tf_op jit(solution)/shard_map/ppermute | solution.py:67
  8.2 6.3 %collective-permute-start.3 = (f32[2,32,128]{2,1,0:T(8,128)S(1)}, f32[2,32,128]{2,1,0:T(8,128)S(1)}, u32[]{:S(2)}, u32[]{:S(2)}) collective-permute-start(f32[2,32,128]{2,1,0:T(8,128)S(1)} %get-tuple-element.78), channel_id=1, source_target_pairs={{0,4},{1,5},{2,6},{3,7},{4,0},{5,1},{6,2},{7,3},{8,12},{9,13},{10,... | collective-permute-start | bytes 98312 | tf_op jit(solution)/shard_map/ppermute | solution.py:67
  10.1 0.7 copy-start.7
  10.9 1.0 copy-start.2
  11.9 0.9 copy-start.5
  12.8 0.8 copy-start.6
  14.6 11.4 %collective-permute-start.6 = (f32[2,2,2,32,128]{4,3,2,1,0:T(8,128)S(1)}, f32[2,2,2,32,128]{4,3,2,1,0:T(8,128)S(1)}, u32[]{:S(2)}, u32[]{:S(2)}) collective-permute-start(f32[2,2,2,32,128]{4,3,2,1,0:T(8,128)S(1)} %get-tuple-element.154), channel_id=1, source_target_pairs={{0,8},{1,9},{2,10},{3,11},{4,12},{5,13},{6,14},{7,15},{8,0},{9,1},... | collective-permute-start | bytes 393224 | tf_op jit(solution)/shard_map/ppermute | solution.py:67
  17.3 6.9 %collective-permute-start.4 = (f32[3,2,32,128]{3,2,1,0:T(8,128)S(1)}, f32[3,2,32,128]{3,2,1,0:T(8,128)S(1)}, u32[]{:S(2)}, u32[]{:S(2)}) collective-permute-start(f32[3,2,32,128]{3,2,1,0:T(8,128)S(1)} %get-tuple-element.87), channel_id=1, source_target_pairs={{0,4},{1,5},{2,6},{3,7},{4,0},{5,1},{6,2},{7,3},{8,12},{9,13},{10,... | collective-permute-start | bytes 294920 | tf_op jit(solution)/shard_map/ppermute | solution.py:67
  17.8 8.1 %collective-permute-start.5 = (f32[4,2,32,128]{3,2,1,0:T(8,128)S(1)}, f32[4,2,32,128]{3,2,1,0:T(8,128)S(1)}, u32[]{:S(2)}, u32[]{:S(2)}) collective-permute-start(f32[4,2,32,128]{3,2,1,0:T(8,128)S(1)} %pad_maximum_fusion.10.near_ref), channel_id=1, source_target_pairs={{0,4},{1,5},{2,6},{3,7},{4,0},{5,1},{6,2},{7,3},{8,12},{9,13},{10,... | collective-permute-start | bytes 393224 | tf_op jit(solution)/shard_map/ppermute | solution.py:67
  26.1 6.8 %collective-permute-start.10 = (f32[2,2,2,2,32,128]{5,4,3,2,1,0:T(8,128)S(1)}, f32[2,2,2,2,32,128]{5,4,3,2,1,0:T(8,128)S(1)}, u32[]{:S(2)}, u32[]{:S(2)}) collective-permute-start(f32[2,2,2,2,32,128]{5,4,3,2,1,0:T(8,128)S(1)} %pad_maximum_fusion.5), channel_id=1, source_target_pairs={{0,2},{1,17},{2,0},{3,19},{4,6},{5,21},{6,4},{7,23},{8,10},{9,25},... | collective-permute-start | bytes 786440 | tf_op jit(solution)/shard_map/ppermute | solution.py:67
  27.6 6.9 %collective-permute-start.7 = (f32[2,32,128]{2,1,0:T(8,128)S(1)}, f32[2,32,128]{2,1,0:T(8,128)S(1)}, u32[]{:S(2)}, u32[]{:S(2)}) collective-permute-start(f32[2,32,128]{2,1,0:T(8,128)S(1)} %get-tuple-element.98), channel_id=1, source_target_pairs={{0,2},{1,3},{2,0},{3,1},{4,6},{5,7},{6,4},{7,5},{8,10},{9,11},{10,... | collective-permute-start | bytes 98312 | tf_op jit(solution)/shard_map/ppermute | solution.py:67
  28.2 7.8 %collective-permute-start.8 = (f32[2,32,128]{2,1,0:T(8,128)S(1)}, f32[2,32,128]{2,1,0:T(8,128)S(1)}, u32[]{:S(2)}, u32[]{:S(2)}) collective-permute-start(f32[2,32,128]{2,1,0:T(8,128)S(1)} %get-tuple-element.99), channel_id=1, source_target_pairs={{0,8},{1,9},{2,10},{3,11},{4,12},{5,13},{6,14},{7,15},{8,0},{9,1},... | collective-permute-start | bytes 98312 | tf_op jit(solution)/shard_map/ppermute | solution.py:67
  28.2 11.5 %collective-permute-start.9 = (f32[2,32,128]{2,1,0:T(8,128)S(1)}, f32[2,32,128]{2,1,0:T(8,128)S(1)}, u32[]{:S(2)}, u32[]{:S(2)}) collective-permute-start(f32[2,32,128]{2,1,0:T(8,128)S(1)} %get-tuple-element.100), channel_id=1, source_target_pairs={{0,10},{1,11},{2,8},{3,9},{4,14},{5,15},{6,12},{7,13},{8,2},{9,3},... | collective-permute-start | bytes 98312 | tf_op jit(solution)/shard_map/ppermute | solution.py:67
  32.0 10.3 %collective-permute-start.11 = (f32[3,2,2,32,128]{4,3,2,1,0:T(8,128)S(1)}, f32[3,2,2,32,128]{4,3,2,1,0:T(8,128)S(1)}, u32[]{:S(2)}, u32[]{:S(2)}) collective-permute-start(f32[3,2,2,32,128]{4,3,2,1,0:T(8,128)S(1)} %get-tuple-element.106), channel_id=1, source_target_pairs={{0,8},{1,9},{2,10},{3,11},{4,12},{5,13},{6,14},{7,15},{8,0},{9,1},... | collective-permute-start | bytes 589832 | tf_op jit(solution)/shard_map/ppermute | solution.py:67
  32.9 17.2 %collective-permute-start.13 = (f32[4,2,2,2,32,128]{5,4,3,2,1,0:T(8,128)S(1)}, f32[4,2,2,2,32,128]{5,4,3,2,1,0:T(8,128)S(1)}, u32[]{:S(2)}, u32[]{:S(2)}) collective-permute-start(f32[4,2,2,2,32,128]{5,4,3,2,1,0:T(8,128)S(1)} %pad_maximum_fusion.1.near), channel_id=1, source_target_pairs={{0,16},{1,3},{2,18},{3,1},{4,20},{5,7},{6,22},{7,5},{8,24},{9,11},... | collective-permute-start | bytes 1572872 | tf_op jit(solution)/shard_map/ppermute | solution.py:67
  42.4 8.9 %collective-permute-start.15 = (f32[2,3,2,2,32,128]{5,4,3,2,1,0:T(8,128)S(1)}, f32[2,3,2,2,32,128]{5,4,3,2,1,0:T(8,128)S(1)}, u32[]{:S(2)}, u32[]{:S(2)}) collective-permute-start(f32[2,3,2,2,32,128]{5,4,3,2,1,0:T(8,128)S(1)} %pad_maximum_fusion.3), channel_id=1, source_target_pairs={{0,2},{1,17},{2,0},{3,19},{4,6},{5,21},{6,4},{7,23},{8,10},{9,25},... | collective-permute-start | bytes 1179656 | tf_op jit(solution)/shard_map/ppermute | solution.py:67
  43.9 6.0 %collective-permute-start.12 = (f32[4,2,32,128]{3,2,1,0:T(8,128)S(1)}, f32[4,2,32,128]{3,2,1,0:T(8,128)S(1)}, u32[]{:S(2)}, u32[]{:S(2)}) collective-permute-start(f32[4,2,32,128]{3,2,1,0:T(8,128)S(1)} %pad_maximum_fusion.11.near_ref), channel_id=1, source_target_pairs={{0,4},{1,5},{2,6},{3,7},{4,0},{5,1},{6,2},{7,3},{8,12},{9,13},{10,... | collective-permute-start | bytes 393224 | tf_op jit(solution)/shard_map/ppermute | solution.py:67
  43.9 8.5 %collective-permute-start.14 = (f32[3,2,32,128]{3,2,1,0:T(8,128)S(1)}, f32[3,2,32,128]{3,2,1,0:T(8,128)S(1)}, u32[]{:S(2)}, u32[]{:S(2)}) collective-permute-start(f32[3,2,32,128]{3,2,1,0:T(8,128)S(1)} %get-tuple-element.112), channel_id=1, source_target_pairs={{0,8},{1,9},{2,10},{3,11},{4,12},{5,13},{6,14},{7,15},{8,0},{9,1},... | collective-permute-start | bytes 294920 | tf_op jit(solution)/shard_map/ppermute | solution.py:67
  51.3 16.2 %collective-permute-start.20 = (f32[4,3,2,2,32,128]{5,4,3,2,1,0:T(8,128)S(1)}, f32[4,3,2,2,32,128]{5,4,3,2,1,0:T(8,128)S(1)}, u32[]{:S(2)}, u32[]{:S(2)}) collective-permute-start(f32[4,3,2,2,32,128]{5,4,3,2,1,0:T(8,128)S(1)} %pad_maximum_fusion.near), channel_id=1, source_target_pairs={{0,16},{1,3},{2,18},{3,1},{4,20},{5,7},{6,22},{7,5},{8,24},{9,11},... | collective-permute-start | bytes 2359304 | tf_op jit(solution)/shard_map/ppermute | solution.py:67
  52.4 7.9 %collective-permute-start.17 = (f32[2,3,2,32,128]{4,3,2,1,0:T(8,128)S(1)}, f32[2,3,2,32,128]{4,3,2,1,0:T(8,128)S(1)}, u32[]{:S(2)}, u32[]{:S(2)}) collective-permute-start(f32[2,3,2,32,128]{4,3,2,1,0:T(8,128)S(1)} %pad_maximum_fusion.8), channel_id=1, source_target_pairs={{0,2},{1,17},{2,0},{3,19},{4,6},{5,21},{6,4},{7,23},{8,10},{9,25},... | collective-permute-start | bytes 589832 | tf_op jit(solution)/shard_map/ppermute | solution.py:67
  53.4 7.0 %collective-permute-start.16 = (f32[2,2,2,32,128]{4,3,2,1,0:T(8,128)S(1)}, f32[2,2,2,32,128]{4,3,2,1,0:T(8,128)S(1)}, u32[]{:S(2)}, u32[]{:S(2)}) collective-permute-start(f32[2,2,2,32,128]{4,3,2,1,0:T(8,128)S(1)} %get-tuple-element.116), channel_id=1, source_target_pairs={{0,8},{1,9},{2,10},{3,11},{4,12},{5,13},{6,14},{7,15},{8,0},{9,1},... | collective-permute-start | bytes 393224 | tf_op jit(solution)/shard_map/ppermute | solution.py:67
  60.4 9.1 %collective-permute-start.18 = (f32[2,2,2,2,32,128]{5,4,3,2,1,0:T(8,128)S(1)}, f32[2,2,2,2,32,128]{5,4,3,2,1,0:T(8,128)S(1)}, u32[]{:S(2)}, u32[]{:S(2)}) collective-permute-start(f32[2,2,2,2,32,128]{5,4,3,2,1,0:T(8,128)S(1)} %pad_maximum_fusion.6), channel_id=1, source_target_pairs={{0,2},{1,17},{2,0},{3,19},{4,6},{5,21},{6,4},{7,23},{8,10},{9,25},... | collective-permute-start | bytes 786440 | tf_op jit(solution)/shard_map/ppermute | solution.py:67
  61.3 9.7 %collective-permute-start.28 = (f32[4,3,2,32,128]{4,3,2,1,0:T(8,128)S(1)}, f32[4,3,2,32,128]{4,3,2,1,0:T(8,128)S(1)}, u32[]{:S(2)}, u32[]{:S(2)}) collective-permute-start(f32[4,3,2,32,128]{4,3,2,1,0:T(8,128)S(1)} %pad_maximum_fusion.4.refs_0_), channel_id=1, source_target_pairs={{0,16},{1,3},{2,18},{3,1},{4,20},{5,7},{6,22},{7,5},{8,24},{9,11},... | collective-permute-start | bytes 1179656 | tf_op jit(solution)/shard_map/ppermute | solution.py:67
  62.5 5.0 %collective-permute-start.19 = (f32[128,256]{1,0:T(8,128)S(1)}, f32[128,256]{1,0:T(8,128)S(1)}, u32[]{:S(2)}, u32[]{:S(2)}) collective-permute-start(f32[128,256]{1,0:T(8,128)S(1)} %get-tuple-element.113.own), channel_id=1, source_target_pairs={{0,4},{1,5},{2,6},{3,7},{4,0},{5,1},{6,2},{7,3},{8,12},{9,13},{10,... | collective-permute-start | bytes 393224 | tf_op jit(solution)/shard_map/ppermute | solution.py:67
  69.5 16.5 %collective-permute-start.27 = (f32[4,2,2,2,32,128]{5,4,3,2,1,0:T(8,128)S(1)}, f32[4,2,2,2,32,128]{5,4,3,2,1,0:T(8,128)S(1)}, u32[]{:S(2)}, u32[]{:S(2)}) collective-permute-start(f32[4,2,2,2,32,128]{5,4,3,2,1,0:T(8,128)S(1)} %pad_maximum_fusion.2.near), channel_id=1, source_target_pairs={{0,16},{1,3},{2,18},{3,1},{4,20},{5,7},{6,22},{7,5},{8,24},{9,11},... | collective-permute-start | bytes 1572872 | tf_op jit(solution)/shard_map/ppermute | solution.py:67
  70.7 11.9 %collective-permute-start.29 = (f32[4,3,2,32,128]{4,3,2,1,0:T(8,128)S(1)}, f32[4,3,2,32,128]{4,3,2,1,0:T(8,128)S(1)}, u32[]{:S(2)}, u32[]{:S(2)}) collective-permute-start(f32[4,3,2,32,128]{4,3,2,1,0:T(8,128)S(1)} %pad_maximum_fusion.4.refs_0_), channel_id=1, source_target_pairs={{0,1},{1,0},{2,3},{3,2},{4,5},{5,4},{6,7},{7,6},{8,9},{9,8},{10,11... | collective-permute-start | bytes 1179656 | tf_op jit(solution)/shard_map/ppermute | solution.py:67
  70.9 15.1 %collective-permute-start.30 = (f32[4,3,2,32,128]{4,3,2,1,0:T(8,128)S(1)}, f32[4,3,2,32,128]{4,3,2,1,0:T(8,128)S(1)}, u32[]{:S(2)}, u32[]{:S(2)}) collective-permute-start(f32[4,3,2,32,128]{4,3,2,1,0:T(8,128)S(1)} %collective-permute-done.28.refs_1_), channel_id=1, source_target_pairs={{0,1},{1,0},{2,3},{3,2},{4,5},{5,4},{6,7},{7,6},{8,9},{9,8},{10,11... | collective-permute-start | bytes 1179656 | tf_op jit(solution)/shard_map/ppermute | solution.py:67
  71.2 5.4 %collective-permute-start.26 = (f32[128,256]{1,0:T(8,128)S(1)}, f32[128,256]{1,0:T(8,128)S(1)}, u32[]{:S(2)}, u32[]{:S(2)}) collective-permute-start(f32[128,256]{1,0:T(8,128)S(1)} %get-tuple-element.121.s0), channel_id=1, source_target_pairs={{0,5},{1,4},{2,7},{3,6},{4,1},{5,0},{6,3},{7,2},{8,13},{9,12},{10,... | collective-permute-start | bytes 393224 | tf_op jit(solution)/shard_map/ppermute | solution.py:67
  71.2 5.5 %collective-permute-start.25 = (f32[128,256]{1,0:T(8,128)S(1)}, f32[128,256]{1,0:T(8,128)S(1)}, u32[]{:S(2)}, u32[]{:S(2)}) collective-permute-start(f32[128,256]{1,0:T(8,128)S(1)} %get-tuple-element.121.s0), channel_id=1, source_target_pairs={{0,1},{1,0},{2,3},{3,2},{4,5},{5,4},{6,7},{7,6},{8,9},{9,8},{10,11... | collective-permute-start | bytes 393224 | tf_op jit(solution)/shard_map/ppermute | solution.py:67
  76.6 5.9 %collective-permute-start.24 = (f32[128,256]{1,0:T(8,128)S(1)}, f32[128,256]{1,0:T(8,128)S(1)}, u32[]{:S(2)}, u32[]{:S(2)}) collective-permute-start(f32[128,256]{1,0:T(8,128)S(1)} %get-tuple-element.121.s0), channel_id=1, source_target_pairs={{0,4},{1,5},{2,6},{3,7},{4,0},{5,1},{6,2},{7,3},{8,12},{9,13},{10,... | collective-permute-start | bytes 393224 | tf_op jit(solution)/shard_map/ppermute | solution.py:67
  76.8 12.1 %collective-permute-start.21 = (f32[2,32,128]{2,1,0:T(8,128)S(1)}, f32[2,32,128]{2,1,0:T(8,128)S(1)}, u32[]{:S(2)}, u32[]{:S(2)}) collective-permute-start(f32[2,32,128]{2,1,0:T(8,128)S(1)} %get-tuple-element.126), channel_id=1, source_target_pairs={{0,2},{1,3},{2,0},{3,1},{4,6},{5,7},{6,4},{7,5},{8,10},{9,11},{10,... | collective-permute-start | bytes 98312 | tf_op jit(solution)/shard_map/ppermute | solution.py:67
  82.5 8.1 %collective-permute-start.22 = (f32[2,32,128]{2,1,0:T(8,128)S(1)}, f32[2,32,128]{2,1,0:T(8,128)S(1)}, u32[]{:S(2)}, u32[]{:S(2)}) collective-permute-start(f32[2,32,128]{2,1,0:T(8,128)S(1)} %get-tuple-element.127), channel_id=1, source_target_pairs={{0,8},{1,9},{2,10},{3,11},{4,12},{5,13},{6,14},{7,15},{8,0},{9,1},... | collective-permute-start | bytes 98312 | tf_op jit(solution)/shard_map/ppermute | solution.py:67
  82.6 8.0 %collective-permute-start.23 = (f32[2,32,128]{2,1,0:T(8,128)S(1)}, f32[2,32,128]{2,1,0:T(8,128)S(1)}, u32[]{:S(2)}, u32[]{:S(2)}) collective-permute-start(f32[2,32,128]{2,1,0:T(8,128)S(1)} %get-tuple-element.128), channel_id=1, source_target_pairs={{0,10},{1,11},{2,8},{3,9},{4,14},{5,15},{6,12},{7,13},{8,2},{9,3},... | collective-permute-start | bytes 98312 | tf_op jit(solution)/shard_map/ppermute | solution.py:67
  88.4 5.8 %collective-permute-start.34 = (f32[128,256]{1,0:T(8,128)S(1)}, f32[128,256]{1,0:T(8,128)S(1)}, u32[]{:S(2)}, u32[]{:S(2)}) collective-permute-start(f32[128,256]{1,0:T(8,128)S(1)} %get-tuple-element.132.s0), channel_id=1, source_target_pairs={{0,5},{1,4},{2,7},{3,6},{4,1},{5,0},{6,3},{7,2},{8,13},{9,12},{10,... | collective-permute-start | bytes 393224 | tf_op jit(solution)/shard_map/ppermute | solution.py:67
  88.5 5.7 %collective-permute-start.33 = (f32[128,256]{1,0:T(8,128)S(1)}, f32[128,256]{1,0:T(8,128)S(1)}, u32[]{:S(2)}, u32[]{:S(2)}) collective-permute-start(f32[128,256]{1,0:T(8,128)S(1)} %get-tuple-element.132.s0), channel_id=1, source_target_pairs={{0,1},{1,0},{2,3},{3,2},{4,5},{5,4},{6,7},{7,6},{8,9},{9,8},{10,11... | collective-permute-start | bytes 393224 | tf_op jit(solution)/shard_map/ppermute | solution.py:67
  88.9 6.4 %collective-permute-start.32 = (f32[128,256]{1,0:T(8,128)S(1)}, f32[128,256]{1,0:T(8,128)S(1)}, u32[]{:S(2)}, u32[]{:S(2)}) collective-permute-start(f32[128,256]{1,0:T(8,128)S(1)} %get-tuple-element.132.s0), channel_id=1, source_target_pairs={{0,4},{1,5},{2,6},{3,7},{4,0},{5,1},{6,2},{7,3},{8,12},{9,13},{10,... | collective-permute-start | bytes 393224 | tf_op jit(solution)/shard_map/ppermute | solution.py:67
  95.9 6.6 %collective-permute-start.35 = (f32[2,32,128]{2,1,0:T(8,128)S(1)}, f32[2,32,128]{2,1,0:T(8,128)S(1)}, u32[]{:S(2)}, u32[]{:S(2)}) collective-permute-start(f32[2,32,128]{2,1,0:T(8,128)S(1)} %get-tuple-element.140), channel_id=1, source_target_pairs={{0,0},{1,17},{2,2},{3,19},{4,4},{5,21},{6,6},{7,23},{8,8},{9,25},{... | collective-permute-start | bytes 98312 | tf_op jit(solution)/shard_map/ppermute | solution.py:67
  96.6 5.9 %collective-permute-start.36 = (f32[2,32,128]{2,1,0:T(8,128)S(1)}, f32[2,32,128]{2,1,0:T(8,128)S(1)}, u32[]{:S(2)}, u32[]{:S(2)}) collective-permute-start(f32[2,32,128]{2,1,0:T(8,128)S(1)} %get-tuple-element.141), channel_id=1, source_target_pairs={{0,2},{1,19},{2,0},{3,17},{4,6},{5,23},{6,4},{7,21},{8,10},{9,27},... | collective-permute-start | bytes 98312 | tf_op jit(solution)/shard_map/ppermute | solution.py:67
  97.9 4.8 %collective-permute-start.37 = (f32[2,32,128]{2,1,0:T(8,128)S(1)}, f32[2,32,128]{2,1,0:T(8,128)S(1)}, u32[]{:S(2)}, u32[]{:S(2)}) collective-permute-start(f32[2,32,128]{2,1,0:T(8,128)S(1)} %get-tuple-element.142), channel_id=1, source_target_pairs={{0,8},{1,25},{2,10},{3,27},{4,12},{5,29},{6,14},{7,31},{8,0},{9,17... | collective-permute-start | bytes 98312 | tf_op jit(solution)/shard_map/ppermute | solution.py:67
  99.5 5.9 %collective-permute-start.38 = (f32[2,32,128]{2,1,0:T(8,128)S(1)}, f32[2,32,128]{2,1,0:T(8,128)S(1)}, u32[]{:S(2)}, u32[]{:S(2)}) collective-permute-start(f32[2,32,128]{2,1,0:T(8,128)S(1)} %get-tuple-element.143), channel_id=1, source_target_pairs={{0,10},{1,27},{2,8},{3,25},{4,14},{5,31},{6,12},{7,29},{8,2},{9,19... | collective-permute-start | bytes 98312 | tf_op jit(solution)/shard_map/ppermute | solution.py:67
  101.1 6.9 %collective-permute-start.31 = (f32[4,2,32,128]{3,2,1,0:T(8,128)S(1)}, f32[4,2,32,128]{3,2,1,0:T(8,128)S(1)}, u32[]{:S(2)}, u32[]{:S(2)}) collective-permute-start(f32[4,2,32,128]{3,2,1,0:T(8,128)S(1)} %pad_maximum_fusion.12.near_ref), channel_id=1, source_target_pairs={{0,16},{1,17},{2,18},{3,19},{4,20},{5,21},{6,22},{7,23},{8,24},{9,... | collective-permute-start | bytes 393224 | tf_op jit(solution)/shard_map/ppermute | solution.py:67
  105.4 3.6 %collective-permute-start.39 = (f32[4,2,32,128]{3,2,1,0:T(8,128)S(1)}, f32[4,2,32,128]{3,2,1,0:T(8,128)S(1)}, u32[]{:S(2)}, u32[]{:S(2)}) collective-permute-start(f32[4,2,32,128]{3,2,1,0:T(8,128)S(1)} %pad_maximum_fusion.13.near_ref), channel_id=1, source_target_pairs={{0,1},{1,0},{2,3},{3,2},{4,5},{5,4},{6,7},{7,6},{8,9},{9,8},{10,11... | collective-permute-start | bytes 393224 | tf_op jit(solution)/shard_map/ppermute | solution.py:67

commit v4 on v3

--- a/solution.py
+++ b/solution.py
@@ -89,6 +89,10 @@
 
 def to_pair_core(r, zh, zl, x, l):
     return r, zh, zl ^ 1, x, l ^ 1
+
+
+def to_far_pair(r, zh, zl, x, l):
+    return r, zh ^ 1, zl ^ 1, x, l
 
 
 def to_row(r, zh, zl, x, l):
@@ -169,17 +173,16 @@
     )(*fixed)
 
 
-def cut_columns(source, held, outs):
-    r, zh, _, x, _ = spot()
+def cut_columns(source, held, base):
+    r = spot()[0]
     for p in range(2):
         for z in range(2):
             start = pl.multiple_of((2 * r + z) * 128, 128)
             one = source[p, 0, :, pl.ds(start, 128)]
             two = source[p, 1, :, pl.ds(start, 128)]
-            held[2 * z, p], held[2 * z + 1, p] = swap_lanes(one, two)
-    for b1 in range(2):
-        for b2 in range(2):
-            outs[b1 * 2 + b2][...] = held[(zh ^ b1) * 2 + (x ^ b2)]
+            even, odd = swap_lanes(one, two)
+            held[2 * z, base + p] = even
+            held[2 * z + 1, base + p] = odd
 
 
 def part_rows(source, keep, out):
@@ -190,44 +193,82 @@
         out[a] = jnp.where(zl == 0, odd, even)
 
 
-def begin_kernel(inverse_ref, rhs_ref, *refs):
-    part_rows(inverse_ref.at[0, 0], refs[0], refs[1])
-    cut_columns(rhs_ref.at[0], refs[6], refs[2:6])
-
-
-def prepare_kernel(tiles_ref, inverse_ref, root_ref, blocks_ref, lower_ref, rhs_ref, *refs):
-    keep, out, masked_ref, lower_out = refs[:4]
-    part_rows(inverse_ref.at[0, 1], keep.at[0], out.at[0])
-    for m in range(2):
-        part_rows(root_ref.at[m], keep.at[m + 1], out.at[m + 1])
-    for t in range(2):
-        lanes = slice(t * 128, t * 128 + 128)
-        for a in range(2):
-            lower_out[t, a] = lower_ref[a, :, lanes]
-        for m in range(5):
-            weight = tiles_ref[0, m, t, 0].astype(F32)
+def begin_kernel(tiles, *refs):
+    sources, outs, places = refs[:6], refs[6:16], refs[16:22]
+    cuts, sems = refs[22:]
+    copies = [
+        pltpu.make_async_copy(source, place, sems.at[k])
+        for k, (source, place) in enumerate(zip(sources, places))
+    ]
+    for copy in copies:
+        copy.start()
+    leaf_inv, blocks, leaf_rhs, root_rhs, root_inv, lower = places
+    first_out, first, rest_out, rest, masked_out, lower_out = outs[:6]
+    core = spot()[4]
+
+    def mask(m, dest, base):
+        for t in range(2):
+            lanes = slice(t * 128, t * 128 + 128)
+            weight = tiles[0, t, 0, m].astype(F32)
             for a in range(2):
-                masked_ref[m, t, a] = blocks_ref[0, m, a, :, lanes] * weight
-    cut_columns(rhs_ref, refs[8], refs[4:8])
-
-
-def fetch(near, far, pick, dest, sems, swapped=None, from_core=0):
+                dest[base + t, a] = blocks[0, m, a, :, lanes] * weight
+
+    copies[0].wait()
+    part_rows(leaf_inv.at[0, 0], first.at[0], first_out)
+    copies[1].wait()
+    mask(0, first, 1)
+    copies[2].wait()
+    cut_columns(leaf_rhs.at[0], cuts, 0)
+    copies[3].wait()
+    cut_columns(root_rhs, cuts, 2)
+    _, zh, _, x, _ = spot()
+    for b1 in range(2):
+        for b2 in range(2):
+            outs[6 + b1 * 2 + b2][...] = cuts[(zh ^ b1) * 2 + (x ^ b2)]
+    part_rows(leaf_inv.at[0, 1], rest.at[0], rest_out.at[0])
+    copies[4].wait()
+    part_rows(root_inv.at[core], rest.at[1], rest_out.at[1])
+    copies[5].wait()
+    for a in range(2):
+        start = pl.multiple_of(core * 128, 128)
+        lower_out[0, a] = lower[a, :, pl.ds(start, 128)]
+    for m in range(1, 5):
+        mask(m, masked_out, 2 * (m - 1))
+
+
+def begin(pattern, *arrays):
+    tiles = pattern.transpose(0, 2, 3, 1)
+    units = [(2, 32, 128), (3, 2, 32, 128), (2, 2, 32, 128), (2, 2, 32, 128)]
+    outs = units + [(8, 2, 32, 128), (1, 2, 32, 128)] + [(4, 32, 128)] * 4
+    return pl.pallas_call(
+        begin_kernel,
+        out_shape=[pltpu.VMEM(dims, F32) for dims in outs],
+        in_specs=[smem()] + [pl.BlockSpec(memory_space=pltpu.HBM)] * 6,
+        out_specs=[vmem() for _ in outs],
+        scratch_shapes=[pltpu.VMEM(a.shape, F32) for a in arrays]
+        + [pltpu.VMEM((4, 4, 32, 128), F32), pltpu.SemaphoreType.DMA((6,))],
+        compiler_params=pltpu.CompilerParams(vmem_limit_bytes=VMEM_OF_A_KERNEL),
+        name="begin",
+    )(tiles, *(pltpu.with_memory_space_constraint(a, pltpu.HBM) for a in arrays))
+
+
+def fetch(pick, dest, sems, swapped=None, from_core=0):
     r, zh, _, x, l = spot()
     copies = []
     for b3 in range(2):
         for b2 in range(2):
             for b1 in range(2):
 
-                def copy_of(sources, core):
+                def copy_of(source, core):
                     rr = r ^ jnp.where(core == 0, b3, b2)
                     xx = x ^ jnp.where(core == 0, b2, b3)
                     return pltpu.make_async_copy(
-                        pick(sources[b3], b2 * 2 + b1),
+                        source(b3, b2, b1),
                         dest(rr, zh ^ b1, xx),
                         sems.at[b3 * 4 + b2 * 2 + b1],
                     )
 
-                copy = copy_of((near, far), l)
+                copy = copy_of(pick, l)
                 if swapped is None:
                     copy.start()
                 else:
@@ -278,23 +319,39 @@
     return lambda r, zh, x: held.at[t, r, half, :, zh, x]
 
 
-def matrix(m):
-    return lambda ref, b: ref.at[b, m]
-
-
-def link_0_kernel(b_ref, near, far, part_ref, y_ref, inverse, held, sems):
-    first = fetch(near, far, matrix(0), inverse_place(inverse), sems.at[0])
-    second = fetch(near, far, matrix(1), block_place(held, 0), sems.at[1])
+def whole_chunk(four, third, m):
+    return lambda b3, b2, b1: (four, third)[b3].at[b2 * 2 + b1, m]
+
+
+def two_chunks(near, far, start, far_start):
+    def pick(b3, b2, b1):
+        ref = (near, far)[b1][b3]
+        return ref.at[b2, pl.ds((start, far_start)[b1], 2)]
+
+    return pick
+
+
+def root_chunk(near, far, start, count):
+    if count == 2:
+        return lambda b3, b2, b1: (near, far)[b1].at[b3 * 2 + b2, pl.ds(start, 2)]
+    return lambda b3, b2, b1: (near, far)[b1].at[b3 * 2 + b2, start]
+
+
+def link_0_kernel(b_ref, four, third, part_ref, y_ref, inverse, held, sems):
+    first = fetch(whole_chunk(four, third, 0), inverse_place(inverse), sems.at[0])
+    second = fetch(whole_chunk(four, third, 1), block_place(held, 0), sems.at[1])
     wait_all(first)
     solved = solve(inverse, b_ref[...])
     y_ref[...] = solved
     part_ref[...] = update(held, [solved], [functools.partial(wait_all, second)])
 
 
-def link_1_kernel(b_ref, own, got, y0_ref, near, far, part_ref, y_ref, inverse, held, sems):
-    copies = [fetch(near, far, matrix(0), inverse_place(inverse), sems.at[0])]
+def link_1_kernel(b_ref, own, got, y0_ref, n0, n1, f0, f1, part_ref, y_ref, inverse, held, sems):
+    near, far = (n0, n1), (f0, f1)
+    copies = [fetch(two_chunks(near, far, 0, 0), inverse_place(inverse), sems.at[0])]
     for t in range(2):
-        copies.append(fetch(near, far, matrix(t + 1), block_place(held, t), sems.at[t + 1]))
+        pick = two_chunks(near, far, 2 * t + 2, 2 * t + 2)
+        copies.append(fetch(pick, block_place(held, t), sems.at[t + 1]))
     wait_all(copies[0])
     solved = solve(inverse, b_ref[...] - (own[...] + got[...]))
     y_ref[...] = solved
@@ -302,15 +359,22 @@
     part_ref[...] = update(held, [y0_ref[...], solved], waits)
 
 
-def link_2_kernel(b_ref, s0, s1, s2, s3, y0_ref, y1_ref, near, far, *refs):
+def link_2_kernel(b_ref, s0, s1, s2, s3, y0_ref, y1_ref, n0, n1, f0, f1, *refs):
+    near, far = (n0, n1), (f0, f1)
     root, swapped = refs[:2], refs[2:4]
     part_ref, y_ref, inverse, held, sems = refs[4:]
     first = fetch(
-        *root, lambda ref, b: ref.at[b, pl.ds(0, 2)], inverse_place(inverse), sems.at[0], swapped, 0
-    )
-    copies = [fetch(near, far, matrix(t), block_place(held, t), sems.at[t + 1]) for t in range(2)]
+        root_chunk(*root, 0, 2), inverse_place(inverse), sems.at[0], root_chunk(*swapped, 0, 2), 0
+    )
+    copies = [
+        fetch(two_chunks(near, far, 9 + 2 * t, 2 * t), block_place(held, t), sems.at[t + 1])
+        for t in range(2)
+    ]
     halves = [
-        fetch(*root, matrix(2), half_place(held, 2, h), sems.at[3 + h], swapped, h) for h in range(2)
+        fetch(
+            root_chunk(*root, 2, 1), half_place(held, 2, h), sems.at[3 + h], root_chunk(*swapped, 2, 1), h
+        )
+        for h in range(2)
     ]
     wait_all(first)
     solved = solve(inverse, b_ref[...] - sum_four((s0, s1, s2, s3)))
@@ -325,7 +389,7 @@
     root, swapped, outs = refs[:2], refs[2:4], refs[4:8]
     pieces, inverse, sems = refs[8:]
     first = fetch(
-        *root, lambda ref, b: ref.at[b, pl.ds(0, 2)], inverse_place(inverse), sems.at[0], swapped, 1
+        root_chunk(*root, 0, 2), inverse_place(inverse), sems.at[0], root_chunk(*swapped, 0, 2), 1
     )
     vector = b_ref[...] - sum_four((s0, s1, s2, s3))
     wait_all(first)
@@ -352,13 +416,14 @@
     lay_values((first[...], second[...]), refs[:4], refs[4])
 
 
-def stand_kernel(near_ref, other_ref, one_ref, two_ref, held):
+def stand_kernel(near_ref, other_ref, *refs):
+    outs, held = refs[:4], refs[4]
     _, zh, zl, x, _ = spot()
     for b1 in range(2):
         for b2 in range(2):
             for b, source in enumerate((near_ref, other_ref)):
                 held[((zh ^ b1) * 2 + (zl ^ b)) * 2 + (x ^ b2)] = source[b1 * 2 + b2]
-    for p, out in enumerate((one_ref, two_ref)):
+    for p, out in enumerate(outs):
         out[...] = held[:, p].reshape(256, 128).T
 
 
@@ -399,120 +464,91 @@
 
 
 def grouped(leaf_rhs, root_rhs, leaf_inverses, root_inverses, leaf_blocks, root_block, pattern):
-    core = lax.axis_index("leaf")
     zl = (lax.axis_index("col") // 2) % 2
     four_pieces = pltpu.VMEM((4, 2, 32, 128), F32)
 
-    keep_0, out_0, *leaf_cut = call(
-        "begin",
-        begin_kernel,
-        [(2, 32, 128)] * 2 + PIECES,
-        leaf_inverses,
-        leaf_rhs,
-        specs=[vmem(), vmem()],
-        scratch=[four_pieces],
-    )
-    got_0 = send(out_0, to_pair)
-    leaf_moved = to_groups(leaf_cut)
-    tiles, _ = lax.optimization_barrier((pattern, out_0))
-    keeps, outs, blocks, lower, *root_cut = call(
-        "prepare",
-        prepare_kernel,
-        [(3, 2, 32, 128)] * 2 + [(5, 2, 2, 32, 128), (2, 2, 32, 128)] + PIECES,
-        tiles,
-        leaf_inverses,
-        root_inverses,
-        leaf_blocks,
-        root_block,
-        root_rhs,
-        specs=[smem()] + [vmem()] * 5,
-        scratch=[four_pieces],
-    )
-
     def whole(keep, got):
         return jnp.stack([jnp.where(zl == 0, keep, got), jnp.where(zl == 0, got, keep)], axis=-3)
 
-    chunk_a = jnp.stack([whole(keep_0, got_0), blocks[0]])
-    far_a = send(chunk_a, to_far)
-    rest = send(after(outs, chunk_a), to_pair)
-    leaf_in = jnp.stack(after(leaf_moved, chunk_a))
-    leaf_pair = send(leaf_in, to_pair)
-
-    inverses = whole(keeps, after(rest, leaf_in))
-    chunk_b = jnp.concatenate([inverses[:1], blocks[1:3]])
-    chunk_c = blocks[3:5]
-    chunk_d = jnp.concatenate(
+    first_out, first, rest_out, rest, blocks, lower, *cuts = begin(
+        pattern, leaf_inverses, leaf_blocks, leaf_rhs, root_rhs, root_inverses, root_block
+    )
+    first_pair = send(first_out, to_pair)
+    first_far = send(first, to_far)
+    first_far_pair = send(first_out, to_far_pair)
+    rest_pair = send(rest_out, to_pair)
+    moved = to_groups(cuts)
+
+    inverses = whole(rest, rest_pair)
+    own_units = jnp.concatenate([inverses[0], blocks[:4], inverses[1], lower, blocks[4:]])
+    second_own = send(own_units, to_second)
+
+    def first_chunk(values, got):
+        return jnp.stack([whole(values[0], got), values[1:]])
+
+    two_a = jnp.stack(
         [
-            jnp.where(core == 0, inverses[1], inverses[2]),
-            jnp.where(core == 0, lower[0], lower[1])[None],
+            first_chunk(first, first_pair),
+            first_chunk(after(first_far, own_units), first_far_pair),
         ]
     )
-    b0, b1 = call(
-        "stand_leaf",
+    second_a = send(two_a, to_second)
+    far_b = send(after(own_units[:9], two_a), to_far)
+    rhs_in = jnp.stack(after(moved, two_a))
+    rhs_pair = send(rhs_in, to_pair)
+    near_0 = jnp.stack([own_units, after(second_own, rhs_in)])
+    near_1 = send(near_0, to_third)
+    four_a = jnp.concatenate([two_a, after(second_a, near_0)])
+    third_a = send(four_a, to_third)
+    b0, b1, r2, r3 = call(
+        "stand",
         stand_kernel,
-        [(128, 256)] * 2,
-        after(leaf_in, chunk_b, chunk_d),
-        leaf_pair,
-        scratch=[pltpu.VMEM((8, 2, 32, 128), F32)],
-    )
-
-    two_a = jnp.stack([chunk_a, after(far_a, b0)])
-    second_a = send(two_a, to_second)
-    far_b = send(after(chunk_b, two_a), to_far)
-    root_moved = to_groups(after(root_cut, two_a))
-    four_a = jnp.concatenate([two_a, after(second_a, root_moved[0])])
-    third_a = send(four_a, to_third)
-    root_in = jnp.stack(after(root_moved, four_a))
-    root_pair = send(root_in, to_pair)
-    two_b = jnp.stack([chunk_b, after(far_b, root_in)])
-    second_b = send(two_b, to_second)
-    far_d = send(after(chunk_d, two_b), to_far)
-    r2, r3 = call(
-        "stand_root",
-        stand_kernel,
-        [(128, 256)] * 2,
-        after(root_in, two_b),
-        root_pair,
-        scratch=[pltpu.VMEM((8, 2, 32, 128), F32)],
-    )
+        [(128, 256)] * 4,
+        after(rhs_in, four_a),
+        rhs_pair,
+        scratch=[pltpu.VMEM((8, 4, 32, 128), F32)],
+    )
+    far_b = after(far_b, b0)
+    second_b = send(far_b, to_second)
+    far_c = send(after(own_units[9:], far_b), to_far)
+    far_b_0 = jnp.stack([far_b, second_b])
+    far_b_1 = send(far_b_0, to_third)
 
     own, y0 = call(
         "link_0",
         link_0_kernel,
         VECTOR,
-        after(b0, r2),
+        after(b0, far_b),
         four_a,
         third_a,
         scratch=link_scratch(1, 2),
     )
     got = send(own, to_pair)
-    four_b = jnp.concatenate([two_b, after(second_b, own)])
-    third_b = send(four_b, to_third)
-    two_d = jnp.stack([chunk_d, after(far_d, four_b)])
-    second_d = send(two_d, to_second)
-    far_c = send(after(chunk_c, two_d), to_far)
-    four_d = jnp.concatenate([two_d, after(second_d, far_c)])
-    third_d = send(four_d, to_third)
-    two_c = jnp.stack([chunk_c, after(far_c, four_d)])
-    second_c = send(two_c, to_second)
+    far_c = after(far_c, got)
+    second_c = send(far_c, to_second)
+    root_near = jnp.concatenate([near_0[:, 6:9], after(near_1, got)[:, 6:9]])
+    swap_near = send(root_near, to_core)
 
     own, y1 = call(
         "link_1",
         link_1_kernel,
         VECTOR,
-        after(b1, two_c),
+        after(b1, far_c),
         own,
         got,
         y0,
-        four_b,
-        third_b,
+        near_0,
+        near_1,
+        far_b_0,
+        far_b_1,
         scratch=link_scratch(2, 3),
     )
     sums = [own, send(own, to_pair), send(own, to_core), send(own, to_pair_core)]
-    four_c = jnp.concatenate([two_c, after(second_c, own)])
-    third_c = send(four_c, to_third)
-    swap_d = (send(after(four_d, four_c), to_core), send(after(third_d, four_c), to_core))
-    leaf_parts = call("lay_leaf", lay_kernel, PIECES, after(y0, four_c), y1, scratch=[four_pieces])
+    root_far = jnp.concatenate([far_b_0[:, 6:9], after(far_b_1, own)[:, 6:9]])
+    swap_far = send(root_far, to_core)
+    far_c_0 = jnp.stack([far_c, after(second_c, own)])
+    far_c_1 = send(far_c_0, to_third)
+    leaf_parts = call("lay_leaf", lay_kernel, PIECES, after(y0, far_c_0), y1, scratch=[four_pieces])
     leaf_moved = to_groups(leaf_parts)
 
     own, y2 = call(
@@ -523,11 +559,14 @@
         *sums,
         y0,
         y1,
-        four_c,
-        third_c,
-        four_d,
-        third_d,
-        *swap_d,
+        near_0,
+        near_1,
+        far_c_0,
+        far_c_1,
+        root_near,
+        root_far,
+        swap_near,
+        swap_far,
         scratch=link_scratch(3, 5),
     )
     sums = [own, send(own, to_pair), send(own, to_core), send(own, to_pair_core)]
@@ -542,9 +581,10 @@
         after(r3, leaf_near),
         *sums,
         y2,
-        four_d,
-        third_d,
-        *swap_d,
+        root_near,
+        root_far,
+        swap_near,
+        swap_far,
         scratch=[four_pieces] + link_scratch(0, 1),
     )
     moved = jnp.stack([send(root_parts[k], to_group_by_core(k // 2, k % 2)) for k in range(4)])

time: 110 us -> 108 us (0.982)
  local copies, waits for them, and re-layouts: 5.38 us -> 0.76 us
  starting transfers between devices: 45.2 us -> 47.3 us
  waiting for transfers between devices: 49.2 us -> 47.8 us
    unnamed x16 -> x3, local copies, waits for them, and re-layouts: 5.25 us -> 0.68 us
    ppermute x40 -> x36, starting transfers between devices: 45.2 us -> 47.3 us  [send(): return lax.ppermute(value, AXES, pairs(dest))]
    pallas_call x0 -> x1, Pallas kernels: none -> 2.06 us  [begin(): pl.pallas_call(begin_kernel, out_shape=[pltpu.VMEM(dims, F32) for dims in...]
    ppermute x40 -> x36, waiting for transfers between devices: 49.2 us -> 47.8 us  [send(): return lax.ppermute(value, AXES, pairs(dest))]
    pallas_call x9 -> x6, Pallas kernels: 6.97 us -> 5.95 us  [call(): pl.pallas_call(kernel, out_shape=[pltpu.VMEM(dims, F32) for dims in outs]...]
  transfers between devices with their start and end apart: 40 -> 36, of which waited for: 18 -> 17; matrix products, arithmetic and copies ran while one was open for 0% -> 0% of each run, Pallas kernels for 6% -> 6%
where the time goes in v4:
time: 108 us; the launch traced here: 107 us
  waiting for transfers between devices  47.8 us (44%)
  starting transfers between devices  47.3 us (44%)
  Pallas kernels  9.74 us (9%)
    ppermute x36, waiting for transfers between devices, send(): return lax.ppermute(value, AXES, pairs(dest))  47.8 us
    ppermute x36, starting transfers between devices, send(): return lax.ppermute(value, AXES, pairs(dest))  47.3 us
    pallas_call x6, Pallas kernels, call(): pl.pallas_call(kernel, out_shape=[pltpu.VMEM(dims, F32) for dims in outs]...  5.95 us
  transfers between devices with their start and end apart: 36, of which 17 were waited for; matrix products, arithmetic and copies ran while one was open for 0% of the time, Pallas kernels for 6%

profile of v4, /device:TPU:0, one launch (start us, length us, event | category | flops | bytes accessed | tf_op | source)
XLA Modules:
  0.0 107.0 jit_solution(13175601441797832292)
XLA Ops:
  0.6 0.7 copy-done
  1.3 2.1 %begin.1 = (f32[2,32,128]{2,1,0:T(8,128)S(1)}, f32[3,2,32,128]{3,2,1,0:T(8,128)S(1)}, f32[2,2,32,128]{3,2,1,0:T(8,128)S(1)}, f32[2,2,32,128]{3,2,1,0:T(8,128)S(1...) custom-call(s32[1,2,1,5]{3,2,1,0:T(1,128)S(1)} %bitcast.74, ...), custom_call_target="tpu_custom_call" | custom-call | tf_op jit(solution)/shard_map/begin/pallas_call | solution.py:243
  3.4 5.1 %collective-permute-start.6 = (f32[2,32,128]{2,1,0:T(8,128)S(1)}, f32[2,32,128]{2,1,0:T(8,128)S(1)}, u32[]{:S(2)}, u32[]{:S(2)}) collective-permute-start(f32[2,32,128]{2,1,0:T(8,128)S(1)} %get-tuple-element.59), channel_id=1, source_target_pairs={{0,12},{1,13},{2,14},{3,15},{4,8},{5,9},{6,10},{7,11},{8,4},{9,5},... | collective-permute-start | bytes 98312 | tf_op jit(solution)/shard_map/ppermute | solution.py:67
  8.5 1.5 %collective-permute-start = (f32[4,32,128]{2,1,0:T(8,128)S(1)}, f32[4,32,128]{2,1,0:T(8,128)S(1)}, u32[]{:S(2)}, u32[]{:S(2)}) collective-permute-start(f32[4,32,128]{2,1,0:T(8,128)S(1)} %get-tuple-element.55), channel_id=1, source_target_pairs={{0,2},{1,3},{2,0},{3,1},{4,6},{5,7},{6,4},{7,5},{8,10},{9,11},{10,... | collective-permute-start | bytes 196616 | tf_op jit(solution)/shard_map/ppermute | solution.py:67
  10.0 0.8 collective-permute-start.1
  10.8 2.1 %collective-permute-start.4 = (f32[3,2,32,128]{3,2,1,0:T(8,128)S(1)}, f32[3,2,32,128]{3,2,1,0:T(8,128)S(1)}, u32[]{:S(2)}, u32[]{:S(2)}) collective-permute-start(f32[3,2,32,128]{3,2,1,0:T(8,128)S(1)} %get-tuple-element.58), channel_id=1, source_target_pairs={{0,8},{1,9},{2,10},{3,11},{4,12},{5,13},{6,14},{7,15},{8,0},{9,1},... | collective-permute-start | bytes 294920 | tf_op jit(solution)/shard_map/ppermute | solution.py:67
  13.0 2.1 %collective-permute-start.5 = (f32[2,2,32,128]{3,2,1,0:T(8,128)S(1)}, f32[2,2,32,128]{3,2,1,0:T(8,128)S(1)}, u32[]{:S(2)}, u32[]{:S(2)}) collective-permute-start(f32[2,2,32,128]{3,2,1,0:T(8,128)S(1)} %get-tuple-element.61), channel_id=1, source_target_pairs={{0,4},{1,5},{2,6},{3,7},{4,0},{5,1},{6,2},{7,3},{8,12},{9,13},{10,... | collective-permute-start | bytes 196616 | tf_op jit(solution)/shard_map/ppermute | solution.py:67
  15.1 2.4 %collective-permute-done.5 = f32[2,2,32,128]{3,2,1,0:T(8,128)S(1)} collective-permute-done((f32[2,2,32,128]{3,2,1,0:T(8,128)S(1)}, f32[2,2,32,128]{3,2,1,0:T(8,128)S(1)}, u32[]{:S(2)}, u32[]{:S(2)}) %collective-permute-start.5) | collective-permute-done | bytes 65568 | tf_op jit(solution)/shard_map/ppermute | solution.py:67
  17.5 2.0 %collective-permute-start.2 = (f32[4,32,128]{2,1,0:T(8,128)S(1)}, f32[4,32,128]{2,1,0:T(8,128)S(1)}, u32[]{:S(2)}, u32[]{:S(2)}) collective-permute-start(f32[4,32,128]{2,1,0:T(8,128)S(1)} %get-tuple-element.57), channel_id=1, source_target_pairs={{0,10},{1,11},{2,8},{3,9},{4,14},{5,15},{6,12},{7,13},{8,2},{9,3},... | collective-permute-start | bytes 196616 | tf_op jit(solution)/shard_map/ppermute | solution.py:67
  19.6 1.6 %collective-permute-done.4 = f32[3,2,32,128]{3,2,1,0:T(8,128)S(1)} collective-permute-done((f32[3,2,32,128]{3,2,1,0:T(8,128)S(1)}, f32[3,2,32,128]{3,2,1,0:T(8,128)S(1)}, u32[]{:S(2)}, u32[]{:S(2)}) %collective-permute-start.4) | collective-permute-done | bytes 98336 | tf_op jit(solution)/shard_map/ppermute | solution.py:67
  21.2 0.5 collective-permute-start.8
  21.8 1.6 %collective-permute-start.7 = (f32[2,2,2,2,32,128]{5,4,3,2,1,0:T(8,128)S(1)}, f32[2,2,2,2,32,128]{5,4,3,2,1,0:T(8,128)S(1)}, u32[]{:S(2)}, u32[]{:S(2)}) collective-permute-start(f32[2,2,2,2,32,128]{5,4,3,2,1,0:T(8,128)S(1)} %pad_maximum_fusion.6), channel_id=1, source_target_pairs={{0,2},{1,17},{2,0},{3,19},{4,6},{5,21},{6,4},{7,23},{8,10},{9,25},... | collective-permute-start | bytes 786440 | tf_op jit(solution)/shard_map/ppermute | solution.py:67
  23.4 0.1 collective-permute-done.2
  23.6 5.7 %collective-permute-start.10 = (f32[9,2,32,128]{3,2,1,0:T(8,128)S(1)}, f32[9,2,32,128]{3,2,1,0:T(8,128)S(1)}, u32[]{:S(2)}, u32[]{:S(2)}) collective-permute-start(f32[9,2,32,128]{3,2,1,0:T(8,128)S(1)} %pad_maximum_fusion.5), channel_id=1, source_target_pairs={{0,8},{1,9},{2,10},{3,11},{4,12},{5,13},{6,14},{7,15},{8,0},{9,1},... | collective-permute-start | bytes 884744 | tf_op jit(solution)/shard_map/ppermute | solution.py:67
  29.5 2.7 %collective-permute-done.7 = f32[2,2,2,2,32,128]{5,4,3,2,1,0:T(8,128)S(1)} collective-permute-done((f32[2,2,2,2,32,128]{5,4,3,2,1,0:T(8,128)S(1)}, f32[2,2,2,2,32,128]{5,4,3,2,1,0:T(8,128)S(1)}, u32[]{:S(2)}, u32[]{:S(2)}) %collective-permute-start.7) | collective-permute-done | bytes 262176 | tf_op jit(solution)/shard_map/ppermute | solution.py:67
  32.2 7.2 %collective-permute-done.9.other_ref = f32[4,4,32,128]{3,2,1,0:T(8,128)S(1)} collective-permute-done((f32[4,4,32,128]{3,2,1,0:T(8,128)S(1)}, f32[4,4,32,128]{3,2,1,0:T(8,128)S(1)}, u32[]{:S(2)}, u32[]{:S(2)}) %collective-permute-start.9) | collective-permute-done | bytes 262176 | tf_op jit(solution)/shard_map/ppermute | solution.py:67
  39.4 0.2 stand.1
  39.6 2.0 %collective-permute-start.16 = (f32[9,2,32,128]{3,2,1,0:T(8,128)S(1)}, f32[9,2,32,128]{3,2,1,0:T(8,128)S(1)}, u32[]{:S(2)}, u32[]{:S(2)}) collective-permute-start(f32[9,2,32,128]{3,2,1,0:T(8,128)S(1)} %collective-permute-done.10), channel_id=1, source_target_pairs={{0,2},{1,17},{2,0},{3,19},{4,6},{5,21},{6,4},{7,23},{8,10},{9,25},... | collective-permute-start | bytes 884744 | tf_op jit(solution)/shard_map/ppermute | solution.py:67
  41.6 1.5 %collective-permute-start.15 = (f32[2,13,2,32,128]{4,3,2,1,0:T(8,128)S(1)}, f32[2,13,2,32,128]{4,3,2,1,0:T(8,128)S(1)}, u32[]{:S(2)}, u32[]{:S(2)}) collective-permute-start(f32[2,13,2,32,128]{4,3,2,1,0:T(8,128)S(1)} %pad_maximum_fusion.n0), channel_id=1, source_target_pairs={{0,16},{1,3},{2,18},{3,1},{4,20},{5,7},{6,22},{7,5},{8,24},{9,11},... | collective-permute-start | bytes 2555912 | tf_op jit(solution)/shard_map/ppermute | solution.py:67
  43.1 0.5 collective-permute-start.11
  43.7 5.9 %collective-permute-done.16 = f32[9,2,32,128]{3,2,1,0:T(8,128)S(1)} collective-permute-done((f32[9,2,32,128]{3,2,1,0:T(8,128)S(1)}, f32[9,2,32,128]{3,2,1,0:T(8,128)S(1)}, u32[]{:S(2)}, u32[]{:S(2)}) %collective-permute-start.16) | collective-permute-done | bytes 294944 | tf_op jit(solution)/shard_map/ppermute | solution.py:67
  49.6 1.6 %collective-permute-start.17 = (f32[2,9,2,32,128]{4,3,2,1,0:T(8,128)S(1)}, f32[2,9,2,32,128]{4,3,2,1,0:T(8,128)S(1)}, u32[]{:S(2)}, u32[]{:S(2)}) collective-permute-start(f32[2,9,2,32,128]{4,3,2,1,0:T(8,128)S(1)} %pad_maximum_fusion.1.f0), channel_id=1, source_target_pairs={{0,16},{1,3},{2,18},{3,1},{4,20},{5,7},{6,22},{7,5},{8,24},{9,11},... | collective-permute-start | bytes 1769480 | tf_op jit(solution)/shard_map/ppermute | solution.py:67
  51.2 8.7 %collective-permute-done.11.third = f32[4,2,2,2,32,128]{5,4,3,2,1,0:T(8,128)S(1)} collective-permute-done((f32[4,2,2,2,32,128]{5,4,3,2,1,0:T(8,128)S(1)}, f32[4,2,2,2,32,128]{5,4,3,2,1,0:T(8,128)S(1)}, u32[]{:S(2)}, u32[]{:S(2)}) %collective-permute-start.11) | collective-permute-done | bytes 524320 | tf_op jit(solution)/shard_map/ppermute | solution.py:67
  59.9 1.1 link_0.1
  61.1 4.9 %collective-permute-done.13.got = f32[128,256]{1,0:T(8,128)S(1)} collective-permute-done((f32[128,256]{1,0:T(8,128)S(1)}, f32[128,256]{1,0:T(8,128)S(1)}, u32[]{:S(2)}, u32[]{:S(2)}) %collective-permute-start.13) | collective-permute-done | bytes 131104 | tf_op jit(solution)/shard_map/ppermute | solution.py:67
  66.4 1.5 %link_1.1 = (f32[128,256]{1,0:T(8,128)S(1)}, f32[128,128]{1,0:T(8,128)S(1)}) custom-call(f32[128,256]{1,0:T(8,128)S(1)} %get-tuple-element.81.b_ref, f32[128,256]{1,0:T(8,128)S(1)} %get-tuple-element.78.own, f32[128,256]{1,0:T(8,128)S(1)} %collective-permute-done.13.got, f32[128,128]{1,0:T(8,128)S(1)} %get-tuple-element.84.y0_ref.first, ...), custom_call_target="tpu_custom_call" | custom-call | tf_op jit(solution)/shard_map/link_1/pallas_call | solution.py:165
  68.0 3.0 %collective-permute-done.14 = f32[4,2,32,128]{3,2,1,0:T(8,128)S(1)} collective-permute-done((f32[4,2,32,128]{3,2,1,0:T(8,128)S(1)}, f32[4,2,32,128]{3,2,1,0:T(8,128)S(1)}, u32[]{:S(2)}, u32[]{:S(2)}) %collective-permute-start.14) | collective-permute-done | bytes 131104 | tf_op jit(solution)/shard_map/ppermute | solution.py:67
  71.2 1.6 %collective-permute-start.24 = (f32[2,4,2,32,128]{4,3,2,1,0:T(8,128)S(1)}, f32[2,4,2,32,128]{4,3,2,1,0:T(8,128)S(1)}, u32[]{:S(2)}, u32[]{:S(2)}) collective-permute-start(f32[2,4,2,32,128]{4,3,2,1,0:T(8,128)S(1)} %pad_maximum_fusion.8.f0), channel_id=1, source_target_pairs={{0,16},{1,3},{2,18},{3,1},{4,20},{5,7},{6,22},{7,5},{8,24},{9,11},... | collective-permute-start | bytes 786440 | tf_op jit(solution)/shard_map/ppermute | solution.py:67
  72.7 0.4 collective-permute-done.23.s3
  73.2 0.6 collective-permute-start.21
  73.9 0.2 collective-permute-done.22.s2
  74.1 1.8 %collective-permute-start.18 = (f32[2,32,128]{2,1,0:T(8,128)S(1)}, f32[2,32,128]{2,1,0:T(8,128)S(1)}, u32[]{:S(2)}, u32[]{:S(2)}) collective-permute-start(f32[2,32,128]{2,1,0:T(8,128)S(1)} %get-tuple-element.87), channel_id=1, source_target_pairs={{0,2},{1,3},{2,0},{3,1},{4,6},{5,7},{6,4},{7,5},{8,10},{9,11},{10,... | collective-permute-start | bytes 98312 | tf_op jit(solution)/shard_map/ppermute | solution.py:67
  75.9 3.1 %collective-permute-done.21.s1 = f32[128,256]{1,0:T(8,128)S(1)} collective-permute-done((f32[128,256]{1,0:T(8,128)S(1)}, f32[128,256]{1,0:T(8,128)S(1)}, u32[]{:S(2)}, u32[]{:S(2)}) %collective-permute-start.21) | collective-permute-done | bytes 131104 | tf_op jit(solution)/shard_map/ppermute | solution.py:67
  79.1 4.5 %collective-permute-start.20 = (f32[2,32,128]{2,1,0:T(8,128)S(1)}, f32[2,32,128]{2,1,0:T(8,128)S(1)}, u32[]{:S(2)}, u32[]{:S(2)}) collective-permute-start(f32[2,32,128]{2,1,0:T(8,128)S(1)} %get-tuple-element.89), channel_id=1, source_target_pairs={{0,10},{1,11},{2,8},{3,9},{4,14},{5,15},{6,12},{7,13},{8,2},{9,3},... | collective-permute-start | bytes 98312 | tf_op jit(solution)/shard_map/ppermute | solution.py:67
  83.5 2.4 %link_2.1 = (f32[128,256]{1,0:T(8,128)S(1)}, f32[128,128]{1,0:T(8,128)S(1)}) custom-call(f32[128,256]{1,0:T(8,128)S(1)} %get-tuple-element.91.b_ref, f32[128,256]{1,0:T(8,128)S(1)} %get-tuple-element.82.s0, f32[128,256]{1,0:T(8,128)S(1)} %collective-permute-done.21.s1, f32[128,256]{1,0:T(8,128)S(1)} %collective-permute-done.22.s2, ...), custom_call_target="tpu_custom_call" | custom-call | tf_op jit(solution)/shard_map/link_2/pallas_call | solution.py:165
  86.0 0.5 collective-permute-start.29
  86.4 1.7 %collective-permute-start.28 = (f32[128,256]{1,0:T(8,128)S(1)}, f32[128,256]{1,0:T(8,128)S(1)}, u32[]{:S(2)}, u32[]{:S(2)}) collective-permute-start(f32[128,256]{1,0:T(8,128)S(1)} %get-tuple-element.94.s0), channel_id=1, source_target_pairs={{0,4},{1,5},{2,6},{3,7},{4,0},{5,1},{6,2},{7,3},{8,12},{9,13},{10,... | collective-permute-start | bytes 393224 | tf_op jit(solution)/shard_map/ppermute | solution.py:67
  88.1 3.6 %collective-permute-done.30.s3 = f32[128,256]{1,0:T(8,128)S(1)} collective-permute-done((f32[128,256]{1,0:T(8,128)S(1)}, f32[128,256]{1,0:T(8,128)S(1)}, u32[]{:S(2)}, u32[]{:S(2)}) %collective-permute-start.30) | collective-permute-done | bytes 131104 | tf_op jit(solution)/shard_map/ppermute | solution.py:67
  91.8 1.8 %collective-permute-done.28.s1 = f32[128,256]{1,0:T(8,128)S(1)} collective-permute-done((f32[128,256]{1,0:T(8,128)S(1)}, f32[128,256]{1,0:T(8,128)S(1)}, u32[]{:S(2)}, u32[]{:S(2)}) %collective-permute-start.28) | collective-permute-done | bytes 131104 | tf_op jit(solution)/shard_map/ppermute | solution.py:67
  93.6 0.7 link_3.1
  94.3 0.7 collective-permute-start.31
  95.0 1.2 %collective-permute-start.33 = (f32[2,32,128]{2,1,0:T(8,128)S(1)}, f32[2,32,128]{2,1,0:T(8,128)S(1)}, u32[]{:S(2)}, u32[]{:S(2)}) collective-permute-start(f32[2,32,128]{2,1,0:T(8,128)S(1)} %get-tuple-element.104), channel_id=1, source_target_pairs={{0,8},{1,25},{2,10},{3,27},{4,12},{5,29},{6,14},{7,31},{8,0},{9,17... | collective-permute-start | bytes 98312 | tf_op jit(solution)/shard_map/ppermute | solution.py:67
  96.2 3.2 %collective-permute-start.34 = (f32[2,32,128]{2,1,0:T(8,128)S(1)}, f32[2,32,128]{2,1,0:T(8,128)S(1)}, u32[]{:S(2)}, u32[]{:S(2)}) collective-permute-start(f32[2,32,128]{2,1,0:T(8,128)S(1)} %get-tuple-element.105), channel_id=1, source_target_pairs={{0,10},{1,27},{2,8},{3,25},{4,14},{5,31},{6,12},{7,29},{8,2},{9,19... | collective-permute-start | bytes 98312 | tf_op jit(solution)/shard_map/ppermute | solution.py:67
  99.4 1.5 %collective-permute-start.27 = (f32[4,2,32,128]{3,2,1,0:T(8,128)S(1)}, f32[4,2,32,128]{3,2,1,0:T(8,128)S(1)}, u32[]{:S(2)}, u32[]{:S(2)}) collective-permute-start(f32[4,2,32,128]{3,2,1,0:T(8,128)S(1)} %pad_maximum_fusion.9.near_ref), channel_id=1, source_target_pairs={{0,16},{1,17},{2,18},{3,19},{4,20},{5,21},{6,22},{7,23},{8,24},{9,... | collective-permute-start | bytes 393224 | tf_op jit(solution)/shard_map/ppermute | solution.py:67
  100.9 1.7 %collective-permute-done.34 = f32[2,32,128]{2,1,0:T(8,128)S(1)} collective-permute-done((f32[2,32,128]{2,1,0:T(8,128)S(1)}, f32[2,32,128]{2,1,0:T(8,128)S(1)}, u32[]{:S(2)}, u32[]{:S(2)}) %collective-permute-start.34) | collective-permute-done | bytes 32800 | tf_op jit(solution)/shard_map/ppermute | solution.py:67
  102.6 2.5 %collective-permute-start.35 = (f32[4,2,32,128]{3,2,1,0:T(8,128)S(1)}, f32[4,2,32,128]{3,2,1,0:T(8,128)S(1)}, u32[]{:S(2)}, u32[]{:S(2)}) collective-permute-start(f32[4,2,32,128]{3,2,1,0:T(8,128)S(1)} %pad_maximum_fusion.10.near_ref), channel_id=1, source_target_pairs={{0,1},{1,0},{2,3},{3,2},{4,5},{5,4},{6,7},{7,6},{8,9},{9,8},{10,11... | collective-permute-start | bytes 393224 | tf_op jit(solution)/shard_map/ppermute | solution.py:67
  105.2 0.9 join_leaf.1
  106.1 0.9 join_root.1
  (62 shorter events, 1.5 us)
Async XLA Ops:
  0.6 0.7 copy-start
  3.4 18.4 %collective-permute-start.6 = (f32[2,32,128]{2,1,0:T(8,128)S(1)}, f32[2,32,128]{2,1,0:T(8,128)S(1)}, u32[]{:S(2)}, u32[]{:S(2)}) collective-permute-start(f32[2,32,128]{2,1,0:T(8,128)S(1)} %get-tuple-element.59), channel_id=1, source_target_pairs={{0,12},{1,13},{2,14},{3,15},{4,8},{5,9},{6,10},{7,11},{8,4},{9,5},... | collective-permute-start | bytes 98312 | tf_op jit(solution)/shard_map/ppermute | solution.py:67
  8.5 4.4 %collective-permute-start.3 = (f32[2,32,128]{2,1,0:T(8,128)S(1)}, f32[2,32,128]{2,1,0:T(8,128)S(1)}, u32[]{:S(2)}, u32[]{:S(2)}) collective-permute-start(f32[2,32,128]{2,1,0:T(8,128)S(1)} %get-tuple-element.59), channel_id=1, source_target_pairs={{0,4},{1,5},{2,6},{3,7},{4,0},{5,1},{6,2},{7,3},{8,12},{9,13},{10,... | collective-permute-start | bytes 98312 | tf_op jit(solution)/shard_map/ppermute | solution.py:67
  8.5 14.9 %collective-permute-start = (f32[4,32,128]{2,1,0:T(8,128)S(1)}, f32[4,32,128]{2,1,0:T(8,128)S(1)}, u32[]{:S(2)}, u32[]{:S(2)}) collective-permute-start(f32[4,32,128]{2,1,0:T(8,128)S(1)} %get-tuple-element.55), channel_id=1, source_target_pairs={{0,2},{1,3},{2,0},{3,1},{4,6},{5,7},{6,4},{7,5},{8,10},{9,11},{10,... | collective-permute-start | bytes 196616 | tf_op jit(solution)/shard_map/ppermute | solution.py:67
  10.0 13.4 %collective-permute-start.1 = (f32[4,32,128]{2,1,0:T(8,128)S(1)}, f32[4,32,128]{2,1,0:T(8,128)S(1)}, u32[]{:S(2)}, u32[]{:S(2)}) collective-permute-start(f32[4,32,128]{2,1,0:T(8,128)S(1)} %get-tuple-element.56), channel_id=1, source_target_pairs={{0,8},{1,9},{2,10},{3,11},{4,12},{5,13},{6,14},{7,15},{8,0},{9,1},... | collective-permute-start | bytes 196616 | tf_op jit(solution)/shard_map/ppermute | solution.py:67
  10.8 10.4 %collective-permute-start.4 = (f32[3,2,32,128]{3,2,1,0:T(8,128)S(1)}, f32[3,2,32,128]{3,2,1,0:T(8,128)S(1)}, u32[]{:S(2)}, u32[]{:S(2)}) collective-permute-start(f32[3,2,32,128]{3,2,1,0:T(8,128)S(1)} %get-tuple-element.58), channel_id=1, source_target_pairs={{0,8},{1,9},{2,10},{3,11},{4,12},{5,13},{6,14},{7,15},{8,0},{9,1},... | collective-permute-start | bytes 294920 | tf_op jit(solution)/shard_map/ppermute | solution.py:67
  13.0 4.5 %collective-permute-start.5 = (f32[2,2,32,128]{3,2,1,0:T(8,128)S(1)}, f32[2,2,32,128]{3,2,1,0:T(8,128)S(1)}, u32[]{:S(2)}, u32[]{:S(2)}) collective-permute-start(f32[2,2,32,128]{3,2,1,0:T(8,128)S(1)} %get-tuple-element.61), channel_id=1, source_target_pairs={{0,4},{1,5},{2,6},{3,7},{4,0},{5,1},{6,2},{7,3},{8,12},{9,13},{10,... | collective-permute-start | bytes 196616 | tf_op jit(solution)/shard_map/ppermute | solution.py:67
  17.5 6.1 %collective-permute-start.2 = (f32[4,32,128]{2,1,0:T(8,128)S(1)}, f32[4,32,128]{2,1,0:T(8,128)S(1)}, u32[]{:S(2)}, u32[]{:S(2)}) collective-permute-start(f32[4,32,128]{2,1,0:T(8,128)S(1)} %get-tuple-element.57), channel_id=1, source_target_pairs={{0,10},{1,11},{2,8},{3,9},{4,14},{5,15},{6,12},{7,13},{8,2},{9,3},... | collective-permute-start | bytes 196616 | tf_op jit(solution)/shard_map/ppermute | solution.py:67
  21.2 8.1 %collective-permute-start.8 = (f32[13,2,32,128]{3,2,1,0:T(8,128)S(1)}, f32[13,2,32,128]{3,2,1,0:T(8,128)S(1)}, u32[]{:S(2)}, u32[]{:S(2)}) collective-permute-start(f32[13,2,32,128]{3,2,1,0:T(8,128)S(1)} %constant_dynamic-update-slice_fusion), channel_id=1, source_target_pairs={{0,2},{1,17},{2,0},{3,19},{4,6},{5,21},{6,4},{7,23},{8,10},{9,25},... | collective-permute-start | bytes 1277960 | tf_op jit(solution)/shard_map/ppermute | solution.py:67
  21.8 10.3 %collective-permute-start.7 = (f32[2,2,2,2,32,128]{5,4,3,2,1,0:T(8,128)S(1)}, f32[2,2,2,2,32,128]{5,4,3,2,1,0:T(8,128)S(1)}, u32[]{:S(2)}, u32[]{:S(2)}) collective-permute-start(f32[2,2,2,2,32,128]{5,4,3,2,1,0:T(8,128)S(1)} %pad_maximum_fusion.6), channel_id=1, source_target_pairs={{0,2},{1,17},{2,0},{3,19},{4,6},{5,21},{6,4},{7,23},{8,10},{9,25},... | collective-permute-start | bytes 786440 | tf_op jit(solution)/shard_map/ppermute | solution.py:67
  23.6 16.1 %collective-permute-start.10 = (f32[9,2,32,128]{3,2,1,0:T(8,128)S(1)}, f32[9,2,32,128]{3,2,1,0:T(8,128)S(1)}, u32[]{:S(2)}, u32[]{:S(2)}) collective-permute-start(f32[9,2,32,128]{3,2,1,0:T(8,128)S(1)} %pad_maximum_fusion.5), channel_id=1, source_target_pairs={{0,8},{1,9},{2,10},{3,11},{4,12},{5,13},{6,14},{7,15},{8,0},{9,1},... | collective-permute-start | bytes 884744 | tf_op jit(solution)/shard_map/ppermute | solution.py:67
  29.3 10.1 %collective-permute-start.9 = (f32[4,4,32,128]{3,2,1,0:T(8,128)S(1)}, f32[4,4,32,128]{3,2,1,0:T(8,128)S(1)}, u32[]{:S(2)}, u32[]{:S(2)}) collective-permute-start(f32[4,4,32,128]{3,2,1,0:T(8,128)S(1)} %pad_maximum_fusion.7.near_ref), channel_id=1, source_target_pairs={{0,4},{1,5},{2,6},{3,7},{4,0},{5,1},{6,2},{7,3},{8,12},{9,13},{10,... | collective-permute-start | bytes 786440 | tf_op jit(solution)/shard_map/ppermute | solution.py:67
  39.6 9.9 %collective-permute-start.16 = (f32[9,2,32,128]{3,2,1,0:T(8,128)S(1)}, f32[9,2,32,128]{3,2,1,0:T(8,128)S(1)}, u32[]{:S(2)}, u32[]{:S(2)}) collective-permute-start(f32[9,2,32,128]{3,2,1,0:T(8,128)S(1)} %collective-permute-done.10), channel_id=1, source_target_pairs={{0,2},{1,17},{2,0},{3,19},{4,6},{5,21},{6,4},{7,23},{8,10},{9,25},... | collective-permute-start | bytes 884744 | tf_op jit(solution)/shard_map/ppermute | solution.py:67
  41.6 24.5 %collective-permute-start.15 = (f32[2,13,2,32,128]{4,3,2,1,0:T(8,128)S(1)}, f32[2,13,2,32,128]{4,3,2,1,0:T(8,128)S(1)}, u32[]{:S(2)}, u32[]{:S(2)}) collective-permute-start(f32[2,13,2,32,128]{4,3,2,1,0:T(8,128)S(1)} %pad_maximum_fusion.n0), channel_id=1, source_target_pairs={{0,16},{1,3},{2,18},{3,1},{4,20},{5,7},{6,22},{7,5},{8,24},{9,11},... | collective-permute-start | bytes 2555912 | tf_op jit(solution)/shard_map/ppermute | solution.py:67
  43.1 16.8 %collective-permute-start.11 = (f32[4,2,2,2,32,128]{5,4,3,2,1,0:T(8,128)S(1)}, f32[4,2,2,2,32,128]{5,4,3,2,1,0:T(8,128)S(1)}, u32[]{:S(2)}, u32[]{:S(2)}) collective-permute-start(f32[4,2,2,2,32,128]{5,4,3,2,1,0:T(8,128)S(1)} %pad_maximum_fusion.2.four), channel_id=1, source_target_pairs={{0,16},{1,3},{2,18},{3,1},{4,20},{5,7},{6,22},{7,5},{8,24},{9,11},... | collective-permute-start | bytes 1572872 | tf_op jit(solution)/shard_map/ppermute | solution.py:67
  49.6 16.8 %collective-permute-start.17 = (f32[2,9,2,32,128]{4,3,2,1,0:T(8,128)S(1)}, f32[2,9,2,32,128]{4,3,2,1,0:T(8,128)S(1)}, u32[]{:S(2)}, u32[]{:S(2)}) collective-permute-start(f32[2,9,2,32,128]{4,3,2,1,0:T(8,128)S(1)} %pad_maximum_fusion.1.f0), channel_id=1, source_target_pairs={{0,16},{1,3},{2,18},{3,1},{4,20},{5,7},{6,22},{7,5},{8,24},{9,11},... | collective-permute-start | bytes 1769480 | tf_op jit(solution)/shard_map/ppermute | solution.py:67
  51.2 9.9 %collective-permute-start.12 = (f32[4,2,32,128]{3,2,1,0:T(8,128)S(1)}, f32[4,2,32,128]{3,2,1,0:T(8,128)S(1)}, u32[]{:S(2)}, u32[]{:S(2)}) collective-permute-start(f32[4,2,32,128]{3,2,1,0:T(8,128)S(1)} %get-tuple-element.77), channel_id=1, source_target_pairs={{0,8},{1,9},{2,10},{3,11},{4,12},{5,13},{6,14},{7,15},{8,0},{9,1},... | collective-permute-start | bytes 393224 | tf_op jit(solution)/shard_map/ppermute | solution.py:67
  61.0 5.0 %collective-permute-start.13 = (f32[128,256]{1,0:T(8,128)S(1)}, f32[128,256]{1,0:T(8,128)S(1)}, u32[]{:S(2)}, u32[]{:S(2)}) collective-permute-start(f32[128,256]{1,0:T(8,128)S(1)} %get-tuple-element.78.own), channel_id=1, source_target_pairs={{0,4},{1,5},{2,6},{3,7},{4,0},{5,1},{6,2},{7,3},{8,12},{9,13},{10,... | collective-permute-start | bytes 393224 | tf_op jit(solution)/shard_map/ppermute | solution.py:67
  66.0 5.0 %collective-permute-start.14 = (f32[4,2,32,128]{3,2,1,0:T(8,128)S(1)}, f32[4,2,32,128]{3,2,1,0:T(8,128)S(1)}, u32[]{:S(2)}, u32[]{:S(2)}) collective-permute-start(f32[4,2,32,128]{3,2,1,0:T(8,128)S(1)} %collective-permute-done.12), channel_id=1, source_target_pairs={{0,2},{1,17},{2,0},{3,19},{4,6},{5,21},{6,4},{7,23},{8,10},{9,25},... | collective-permute-start | bytes 393224 | tf_op jit(solution)/shard_map/ppermute | solution.py:67
  66.2 17.3 %collective-permute-start.25 = (f32[4,3,2,32,128]{4,3,2,1,0:T(8,128)S(1)}, f32[4,3,2,32,128]{4,3,2,1,0:T(8,128)S(1)}, u32[]{:S(2)}, u32[]{:S(2)}) collective-permute-start(f32[4,3,2,32,128]{4,3,2,1,0:T(8,128)S(1)} %pad_maximum_fusion.3.refs_0_), channel_id=1, source_target_pairs={{0,1},{1,0},{2,3},{3,2},{4,5},{5,4},{6,7},{7,6},{8,9},{9,8},{10,11... | collective-permute-start | bytes 1179656 | tf_op jit(solution)/shard_map/ppermute | solution.py:67
  67.9 5.3 %collective-permute-start.23 = (f32[128,256]{1,0:T(8,128)S(1)}, f32[128,256]{1,0:T(8,128)S(1)}, u32[]{:S(2)}, u32[]{:S(2)}) collective-permute-start(f32[128,256]{1,0:T(8,128)S(1)} %get-tuple-element.82.s0), channel_id=1, source_target_pairs={{0,5},{1,4},{2,7},{3,6},{4,1},{5,0},{6,3},{7,2},{8,13},{9,12},{10,... | collective-permute-start | bytes 393224 | tf_op jit(solution)/shard_map/ppermute | solution.py:67
  71.0 12.5 %collective-permute-start.26 = (f32[4,3,2,32,128]{4,3,2,1,0:T(8,128)S(1)}, f32[4,3,2,32,128]{4,3,2,1,0:T(8,128)S(1)}, u32[]{:S(2)}, u32[]{:S(2)}) collective-permute-start(f32[4,3,2,32,128]{4,3,2,1,0:T(8,128)S(1)} %pad_maximum_fusion.4.refs_1_), channel_id=1, source_target_pairs={{0,1},{1,0},{2,3},{3,2},{4,5},{5,4},{6,7},{7,6},{8,9},{9,8},{10,11... | collective-permute-start | bytes 1179656 | tf_op jit(solution)/shard_map/ppermute | solution.py:67
  71.2 7.9 %collective-permute-start.24 = (f32[2,4,2,32,128]{4,3,2,1,0:T(8,128)S(1)}, f32[2,4,2,32,128]{4,3,2,1,0:T(8,128)S(1)}, u32[]{:S(2)}, u32[]{:S(2)}) collective-permute-start(f32[2,4,2,32,128]{4,3,2,1,0:T(8,128)S(1)} %pad_maximum_fusion.8.f0), channel_id=1, source_target_pairs={{0,16},{1,3},{2,18},{3,1},{4,20},{5,7},{6,22},{7,5},{8,24},{9,11},... | collective-permute-start | bytes 786440 | tf_op jit(solution)/shard_map/ppermute | solution.py:67
  72.7 1.3 %collective-permute-start.22 = (f32[128,256]{1,0:T(8,128)S(1)}, f32[128,256]{1,0:T(8,128)S(1)}, u32[]{:S(2)}, u32[]{:S(2)}) collective-permute-start(f32[128,256]{1,0:T(8,128)S(1)} %get-tuple-element.82.s0), channel_id=1, source_target_pairs={{0,1},{1,0},{2,3},{3,2},{4,5},{5,4},{6,7},{7,6},{8,9},{9,8},{10,11... | collective-permute-start | bytes 393224 | tf_op jit(solution)/shard_map/ppermute | solution.py:67
  73.2 5.8 %collective-permute-start.21 = (f32[128,256]{1,0:T(8,128)S(1)}, f32[128,256]{1,0:T(8,128)S(1)}, u32[]{:S(2)}, u32[]{:S(2)}) collective-permute-start(f32[128,256]{1,0:T(8,128)S(1)} %get-tuple-element.82.s0), channel_id=1, source_target_pairs={{0,4},{1,5},{2,6},{3,7},{4,0},{5,1},{6,2},{7,3},{8,12},{9,13},{10,... | collective-permute-start | bytes 393224 | tf_op jit(solution)/shard_map/ppermute | solution.py:67
  74.1 12.4 %collective-permute-start.18 = (f32[2,32,128]{2,1,0:T(8,128)S(1)}, f32[2,32,128]{2,1,0:T(8,128)S(1)}, u32[]{:S(2)}, u32[]{:S(2)}) collective-permute-start(f32[2,32,128]{2,1,0:T(8,128)S(1)} %get-tuple-element.87), channel_id=1, source_target_pairs={{0,2},{1,3},{2,0},{3,1},{4,6},{5,7},{6,4},{7,5},{8,10},{9,11},{10,... | collective-permute-start | bytes 98312 | tf_op jit(solution)/shard_map/ppermute | solution.py:67
  79.0 9.1 %collective-permute-start.19 = (f32[2,32,128]{2,1,0:T(8,128)S(1)}, f32[2,32,128]{2,1,0:T(8,128)S(1)}, u32[]{:S(2)}, u32[]{:S(2)}) collective-permute-start(f32[2,32,128]{2,1,0:T(8,128)S(1)} %get-tuple-element.88), channel_id=1, source_target_pairs={{0,8},{1,9},{2,10},{3,11},{4,12},{5,13},{6,14},{7,15},{8,0},{9,1},... | collective-permute-start | bytes 98312 | tf_op jit(solution)/shard_map/ppermute | solution.py:67
  79.1 9.1 %collective-permute-start.20 = (f32[2,32,128]{2,1,0:T(8,128)S(1)}, f32[2,32,128]{2,1,0:T(8,128)S(1)}, u32[]{:S(2)}, u32[]{:S(2)}) collective-permute-start(f32[2,32,128]{2,1,0:T(8,128)S(1)} %get-tuple-element.89), channel_id=1, source_target_pairs={{0,10},{1,11},{2,8},{3,9},{4,14},{5,15},{6,12},{7,13},{8,2},{9,3},... | collective-permute-start | bytes 98312 | tf_op jit(solution)/shard_map/ppermute | solution.py:67
  85.9 5.9 %collective-permute-start.30 = (f32[128,256]{1,0:T(8,128)S(1)}, f32[128,256]{1,0:T(8,128)S(1)}, u32[]{:S(2)}, u32[]{:S(2)}) collective-permute-start(f32[128,256]{1,0:T(8,128)S(1)} %get-tuple-element.94.s0), channel_id=1, source_target_pairs={{0,5},{1,4},{2,7},{3,6},{4,1},{5,0},{6,3},{7,2},{8,13},{9,12},{10,... | collective-permute-start | bytes 393224 | tf_op jit(solution)/shard_map/ppermute | solution.py:67
  86.0 5.8 %collective-permute-start.29 = (f32[128,256]{1,0:T(8,128)S(1)}, f32[128,256]{1,0:T(8,128)S(1)}, u32[]{:S(2)}, u32[]{:S(2)}) collective-permute-start(f32[128,256]{1,0:T(8,128)S(1)} %get-tuple-element.94.s0), channel_id=1, source_target_pairs={{0,1},{1,0},{2,3},{3,2},{4,5},{5,4},{6,7},{7,6},{8,9},{9,8},{10,11... | collective-permute-start | bytes 393224 | tf_op jit(solution)/shard_map/ppermute | solution.py:67
  86.4 7.2 %collective-permute-start.28 = (f32[128,256]{1,0:T(8,128)S(1)}, f32[128,256]{1,0:T(8,128)S(1)}, u32[]{:S(2)}, u32[]{:S(2)}) collective-permute-start(f32[128,256]{1,0:T(8,128)S(1)} %get-tuple-element.94.s0), channel_id=1, source_target_pairs={{0,4},{1,5},{2,6},{3,7},{4,0},{5,1},{6,2},{7,3},{8,12},{9,13},{10,... | collective-permute-start | bytes 393224 | tf_op jit(solution)/shard_map/ppermute | solution.py:67
  94.3 6.6 %collective-permute-start.31 = (f32[2,32,128]{2,1,0:T(8,128)S(1)}, f32[2,32,128]{2,1,0:T(8,128)S(1)}, u32[]{:S(2)}, u32[]{:S(2)}) collective-permute-start(f32[2,32,128]{2,1,0:T(8,128)S(1)} %get-tuple-element.102), channel_id=1, source_target_pairs={{0,0},{1,17},{2,2},{3,19},{4,4},{5,21},{6,6},{7,23},{8,8},{9,25},{... | collective-permute-start | bytes 98312 | tf_op jit(solution)/shard_map/ppermute | solution.py:67
  95.0 6.0 %collective-permute-start.32 = (f32[2,32,128]{2,1,0:T(8,128)S(1)}, f32[2,32,128]{2,1,0:T(8,128)S(1)}, u32[]{:S(2)}, u32[]{:S(2)}) collective-permute-start(f32[2,32,128]{2,1,0:T(8,128)S(1)} %get-tuple-element.103), channel_id=1, source_target_pairs={{0,2},{1,19},{2,0},{3,17},{4,6},{5,23},{6,4},{7,21},{8,10},{9,27},... | collective-permute-start | bytes 98312 | tf_op jit(solution)/shard_map/ppermute | solution.py:67
  95.0 5.9 %collective-permute-start.33 = (f32[2,32,128]{2,1,0:T(8,128)S(1)}, f32[2,32,128]{2,1,0:T(8,128)S(1)}, u32[]{:S(2)}, u32[]{:S(2)}) collective-permute-start(f32[2,32,128]{2,1,0:T(8,128)S(1)} %get-tuple-element.104), channel_id=1, source_target_pairs={{0,8},{1,25},{2,10},{3,27},{4,12},{5,29},{6,14},{7,31},{8,0},{9,17... | collective-permute-start | bytes 98312 | tf_op jit(solution)/shard_map/ppermute | solution.py:67
  96.2 6.4 %collective-permute-start.34 = (f32[2,32,128]{2,1,0:T(8,128)S(1)}, f32[2,32,128]{2,1,0:T(8,128)S(1)}, u32[]{:S(2)}, u32[]{:S(2)}) collective-permute-start(f32[2,32,128]{2,1,0:T(8,128)S(1)} %get-tuple-element.105), channel_id=1, source_target_pairs={{0,10},{1,27},{2,8},{3,25},{4,14},{5,31},{6,12},{7,29},{8,2},{9,19... | collective-permute-start | bytes 98312 | tf_op jit(solution)/shard_map/ppermute | solution.py:67
  99.4 5.8 %collective-permute-start.27 = (f32[4,2,32,128]{3,2,1,0:T(8,128)S(1)}, f32[4,2,32,128]{3,2,1,0:T(8,128)S(1)}, u32[]{:S(2)}, u32[]{:S(2)}) collective-permute-start(f32[4,2,32,128]{3,2,1,0:T(8,128)S(1)} %pad_maximum_fusion.9.near_ref), channel_id=1, source_target_pairs={{0,16},{1,17},{2,18},{3,19},{4,20},{5,21},{6,22},{7,23},{8,24},{9,... | collective-permute-start | bytes 393224 | tf_op jit(solution)/shard_map/ppermute | solution.py:67
  102.6 3.5 %collective-permute-start.35 = (f32[4,2,32,128]{3,2,1,0:T(8,128)S(1)}, f32[4,2,32,128]{3,2,1,0:T(8,128)S(1)}, u32[]{:S(2)}, u32[]{:S(2)}) collective-permute-start(f32[4,2,32,128]{3,2,1,0:T(8,128)S(1)} %pad_maximum_fusion.10.near_ref), channel_id=1, source_target_pairs={{0,1},{1,0},{2,3},{3,2},{4,5},{5,4},{6,7},{7,6},{8,9},{9,8},{10,11... | collective-permute-start | bytes 393224 | tf_op jit(solution)/shard_map/ppermute | solution.py:67

commit v5 on v4

--- a/solution.py
+++ b/solution.py
@@ -194,8 +194,8 @@
 
 
 def begin_kernel(tiles, *refs):
-    sources, outs, places = refs[:6], refs[6:16], refs[16:22]
-    cuts, sems = refs[22:]
+    sources, outs, places = refs[:6], refs[6:15], refs[15:21]
+    cuts, sems = refs[21:]
     copies = [
         pltpu.make_async_copy(source, place, sems.at[k])
         for k, (source, place) in enumerate(zip(sources, places))
@@ -203,7 +203,7 @@
     for copy in copies:
         copy.start()
     leaf_inv, blocks, leaf_rhs, root_rhs, root_inv, lower = places
-    first_out, first, rest_out, rest, masked_out, lower_out = outs[:6]
+    away, first, rest, masked_out, lower_out = outs[:5]
     core = spot()[4]
 
     def mask(m, dest, base):
@@ -214,7 +214,7 @@
                 dest[base + t, a] = blocks[0, m, a, :, lanes] * weight
 
     copies[0].wait()
-    part_rows(leaf_inv.at[0, 0], first.at[0], first_out)
+    part_rows(leaf_inv.at[0, 0], first.at[0], away.at[0])
     copies[1].wait()
     mask(0, first, 1)
     copies[2].wait()
@@ -224,10 +224,10 @@
     _, zh, _, x, _ = spot()
     for b1 in range(2):
         for b2 in range(2):
-            outs[6 + b1 * 2 + b2][...] = cuts[(zh ^ b1) * 2 + (x ^ b2)]
-    part_rows(leaf_inv.at[0, 1], rest.at[0], rest_out.at[0])
+            outs[5 + b1 * 2 + b2][...] = cuts[(zh ^ b1) * 2 + (x ^ b2)]
+    part_rows(leaf_inv.at[0, 1], rest.at[0], away.at[1])
     copies[4].wait()
-    part_rows(root_inv.at[core], rest.at[1], rest_out.at[1])
+    part_rows(root_inv.at[core], rest.at[1], away.at[2])
     copies[5].wait()
     for a in range(2):
         start = pl.multiple_of(core * 128, 128)
@@ -238,8 +238,7 @@
 
 def begin(pattern, *arrays):
     tiles = pattern.transpose(0, 2, 3, 1)
-    units = [(2, 32, 128), (3, 2, 32, 128), (2, 2, 32, 128), (2, 2, 32, 128)]
-    outs = units + [(8, 2, 32, 128), (1, 2, 32, 128)] + [(4, 32, 128)] * 4
+    outs = [(3, 2, 32, 128), (3, 2, 32, 128), (2, 2, 32, 128)] + [(8, 2, 32, 128), (1, 2, 32, 128)] + [(4, 32, 128)] * 4
     return pl.pallas_call(
         begin_kernel,
         out_shape=[pltpu.VMEM(dims, F32) for dims in outs],
@@ -304,42 +303,70 @@
 
 
 def sum_four(refs):
-    return (refs[0][...] + refs[1][...]) + (refs[2][...] + refs[3][...])
-
-
-def inverse_place(inverse):
-    return lambda r, zh, x: inverse.at[r, :, zh, :, x]
-
-
-def block_place(held, t):
-    return lambda r, zh, x: held.at[t, r, :, :, zh, x]
-
-
-def half_place(held, t, half):
-    return lambda r, zh, x: held.at[t, r, half, :, zh, x]
-
-
-def whole_chunk(four, third, m):
-    return lambda b3, b2, b1: (four, third)[b3].at[b2 * 2 + b1, m]
-
-
-def two_chunks(near, far, start, far_start):
-    def pick(b3, b2, b1):
-        ref = (near, far)[b1][b3]
-        return ref.at[b2, pl.ds((start, far_start)[b1], 2)]
-
-    return pick
-
-
-def root_chunk(near, far, start, count):
-    if count == 2:
-        return lambda b3, b2, b1: (near, far)[b1].at[b3 * 2 + b2, pl.ds(start, 2)]
-    return lambda b3, b2, b1: (near, far)[b1].at[b3 * 2 + b2, start]
+    return (refs[0][...] + refs[2][...]) + (refs[1][...] + refs[3][...])
+
+
+def first_chunk_unit(four, third):
+    return lambda unit: lambda b3, b2, b1: (four, third)[b3].at[b2 * 2 + b1, unit]
+
+
+def chunk_unit(near, far, start, far_start):
+    def of(unit):
+        def pick(b3, b2, b1):
+            return (near, far)[b1][b3].at[b2, (start, far_start)[b1] + unit]
+
+        return pick
+
+    return of
+
+
+def root_unit(ref):
+    return lambda unit: lambda b3, b2, b1: ref.at[b1 * 4 + b3 * 2 + b2, unit]
+
+
+def fetch_inverse(unit, inverse, sems, swapped=None, from_core=0):
+    copies = []
+    for half in range(2):
+        copies += fetch(
+            unit(half),
+            lambda r, zh, x, half=half: inverse.at[r, :, zh, half, x],
+            sems.at[half],
+            swapped and swapped(half),
+            from_core,
+        )
+    return copies
+
+
+def fetch_block(unit, held, t, sems):
+    copies = []
+    for half in range(2):
+        copies += fetch(
+            unit(half), lambda r, zh, x, half=half: held.at[t, r, half, :, zh, x], sems.at[half]
+        )
+    return copies
+
+
+def fetch_halves(root, swapped, held, t, sems):
+    copies = []
+    for half in range(2):
+        copies += fetch(
+            root(2),
+            lambda r, zh, x, half=half: held.at[t, r, half, :, zh, x],
+            sems.at[half],
+            swapped(2),
+            half,
+        )
+    return copies
+
+
+def shifted(unit, by):
+    return lambda half: unit(half + by)
 
 
 def link_0_kernel(b_ref, four, third, part_ref, y_ref, inverse, held, sems):
-    first = fetch(whole_chunk(four, third, 0), inverse_place(inverse), sems.at[0])
-    second = fetch(whole_chunk(four, third, 1), block_place(held, 0), sems.at[1])
+    unit = first_chunk_unit(four, third)
+    first = fetch_inverse(unit, inverse, sems.at[0])
+    second = fetch_block(shifted(unit, 2), held, 0, sems.at[1])
     wait_all(first)
     solved = solve(inverse, b_ref[...])
     y_ref[...] = solved
@@ -347,73 +374,54 @@
 
 
 def link_1_kernel(b_ref, own, got, y0_ref, n0, n1, f0, f1, part_ref, y_ref, inverse, held, sems):
-    near, far = (n0, n1), (f0, f1)
-    copies = [fetch(two_chunks(near, far, 0, 0), inverse_place(inverse), sems.at[0])]
-    for t in range(2):
-        pick = two_chunks(near, far, 2 * t + 2, 2 * t + 2)
-        copies.append(fetch(pick, block_place(held, t), sems.at[t + 1]))
-    wait_all(copies[0])
+    unit = chunk_unit((n0, n1), (f0, f1), 0, 0)
+    first = fetch_inverse(unit, inverse, sems.at[0])
+    copies = [fetch_block(shifted(unit, 2 * t + 2), held, t, sems.at[t + 1]) for t in range(2)]
+    wait_all(first)
     solved = solve(inverse, b_ref[...] - (own[...] + got[...]))
     y_ref[...] = solved
-    waits = [functools.partial(wait_all, c) for c in copies[1:]]
+    waits = [functools.partial(wait_all, c) for c in copies]
     part_ref[...] = update(held, [y0_ref[...], solved], waits)
 
 
-def link_2_kernel(b_ref, s0, s1, s2, s3, y0_ref, y1_ref, n0, n1, f0, f1, *refs):
-    near, far = (n0, n1), (f0, f1)
-    root, swapped = refs[:2], refs[2:4]
-    part_ref, y_ref, inverse, held, sems = refs[4:]
-    first = fetch(
-        root_chunk(*root, 0, 2), inverse_place(inverse), sems.at[0], root_chunk(*swapped, 0, 2), 0
-    )
-    copies = [
-        fetch(two_chunks(near, far, 9 + 2 * t, 2 * t), block_place(held, t), sems.at[t + 1])
-        for t in range(2)
-    ]
-    halves = [
-        fetch(
-            root_chunk(*root, 2, 1), half_place(held, 2, h), sems.at[3 + h], root_chunk(*swapped, 2, 1), h
-        )
-        for h in range(2)
-    ]
+def link_2_kernel(b_ref, s0, s1, s2, s3, y0_ref, y1_ref, n0, n1, f0, f1, root, swapped, *refs):
+    part_ref, y_ref, inverse, held, sems = refs
+    unit = chunk_unit((n0, n1), (f0, f1), 9, 0)
+    root, swapped = root_unit(root), root_unit(swapped)
+    first = fetch_inverse(root, inverse, sems.at[0], swapped, 0)
+    copies = [fetch_block(shifted(unit, 2 * t), held, t, sems.at[t + 1]) for t in range(2)]
+    copies.append(fetch_halves(root, swapped, held, 2, sems.at[3]))
     wait_all(first)
     solved = solve(inverse, b_ref[...] - sum_four((s0, s1, s2, s3)))
     y_ref[...] = solved
-    copies.append(halves[0] + halves[1])
     waits = [functools.partial(wait_all, c) for c in copies]
     last = jnp.where(spot()[4] == 0, solved, 0.0)
     part_ref[...] = update(held, [y0_ref[...], y1_ref[...], last], waits)
 
 
-def link_3_kernel(b_ref, s0, s1, s2, s3, y2_ref, *refs):
-    root, swapped, outs = refs[:2], refs[2:4], refs[4:8]
-    pieces, inverse, sems = refs[8:]
-    first = fetch(
-        root_chunk(*root, 0, 2), inverse_place(inverse), sems.at[0], root_chunk(*swapped, 0, 2), 1
-    )
+def link_3_kernel(b_ref, s0, s1, s2, s3, y0_ref, y1_ref, y2_ref, root, swapped, *refs):
+    outs, (pieces, inverse, sems) = refs[:4], refs[4:]
+    first = fetch_inverse(root_unit(root), inverse, sems.at[0], root_unit(swapped), 1)
     vector = b_ref[...] - sum_four((s0, s1, s2, s3))
+    lay_values((y0_ref, y1_ref, y2_ref), pieces)
     wait_all(first)
-    lay_values((y2_ref[...], solve(inverse, vector)), outs, pieces)
+    pieces[:, 3] = solve(inverse, vector).T.reshape(4, 32, 128)
+    _, zh, _, x, _ = spot()
+    for b1 in range(2):
+        for b2 in range(2):
+            outs[b1 * 2 + b2][...] = pieces[(zh ^ b1) * 2 + (x ^ b2)]
 
 
 def link_scratch(nblocks, nsems):
     blocks = [pltpu.VMEM((nblocks, 2, 2, 2, 2, 2, 32, 128), F32)] if nblocks else []
     return (
-        [pltpu.VMEM((2, 2, 2, 2, 2, 32, 128), F32)] + blocks + [pltpu.SemaphoreType.DMA((nsems, 8))]
-    )
-
-
-def lay_values(values, outs, held):
-    _, zh, _, x, _ = spot()
-    for p, value in enumerate(values):
-        held[:, p] = value.T.reshape(4, 32, 128)
-    for b1 in range(2):
-        for b2 in range(2):
-            outs[b1 * 2 + b2][...] = held[(zh ^ b1) * 2 + (x ^ b2)]
-
-
-def lay_kernel(first, second, *refs):
-    lay_values((first[...], second[...]), refs[:4], refs[4])
+        [pltpu.VMEM((2, 2, 2, 2, 2, 32, 128), F32)] + blocks + [pltpu.SemaphoreType.DMA((nsems, 2, 8))]
+    )
+
+
+def lay_values(refs, held):
+    for p, ref in enumerate(refs):
+        held[:, p] = ref[...].T.reshape(4, 32, 128)
 
 
 def stand_kernel(near_ref, other_ref, *refs):
@@ -427,9 +435,9 @@
         out[...] = held[:, p].reshape(256, 128).T
 
 
-def join_kernel(by_core, near_ref, other_ref, out_ref, held):
+def join_kernel(near_ref, other_ref, out_ref, held):
     r, zh, _, x, core = spot()
-    near = r ^ core if by_core else r
+    near = r ^ core
     for b1 in range(2):
         for b2 in range(2):
             place = (zh ^ b1) * 2 + (x ^ b2)
@@ -443,9 +451,9 @@
             )
 
 
-def join(name, by_core, near, other):
+def join(name, near, other):
     return pl.pallas_call(
-        functools.partial(join_kernel, by_core),
+        join_kernel,
         out_shape=shaped(2, 2, 32, 512),
         in_specs=[vmem()] * 2,
         out_specs=vmem(),
@@ -459,75 +467,67 @@
     return [parts[0]] + [send(parts[k], to_group(k // 2, k % 2)) for k in (1, 2, 3)]
 
 
-PIECES = [(2, 32, 128)] * 4
 VECTOR = [(128, 256), (128, 128)]
 
 
 def grouped(leaf_rhs, root_rhs, leaf_inverses, root_inverses, leaf_blocks, root_block, pattern):
     zl = (lax.axis_index("col") // 2) % 2
-    four_pieces = pltpu.VMEM((4, 2, 32, 128), F32)
 
     def whole(keep, got):
-        return jnp.stack([jnp.where(zl == 0, keep, got), jnp.where(zl == 0, got, keep)], axis=-3)
-
-    first_out, first, rest_out, rest, blocks, lower, *cuts = begin(
+        return jnp.stack([jnp.where(zl == 0, keep, got), jnp.where(zl == 0, got, keep)])
+
+    away, first, rest, blocks, lower, *cuts = begin(
         pattern, leaf_inverses, leaf_blocks, leaf_rhs, root_rhs, root_inverses, root_block
     )
-    first_pair = send(first_out, to_pair)
+    pair = send(away, to_pair)
     first_far = send(first, to_far)
-    first_far_pair = send(first_out, to_far_pair)
-    rest_pair = send(rest_out, to_pair)
-    moved = to_groups(cuts)
-
-    inverses = whole(rest, rest_pair)
-    own_units = jnp.concatenate([inverses[0], blocks[:4], inverses[1], lower, blocks[4:]])
+    first_far_pair = send(away[0], to_far_pair)
+
+    def first_chunk(values, got):
+        return jnp.concatenate([whole(values[0], got), values[1:]])
+
+    two_a = jnp.stack([first_chunk(first, pair[0]), first_chunk(first_far, first_far_pair)])
+    second_a = send(two_a, to_second)
+
+    late = after(pair, two_a)
+    own_units = jnp.concatenate(
+        [whole(rest[0], late[1]), blocks[:4], whole(rest[1], late[2]), lower, blocks[4:]]
+    )
+    far_b = send(own_units[:9], to_far)
     second_own = send(own_units, to_second)
-
-    def first_chunk(values, got):
-        return jnp.stack([whole(values[0], got), values[1:]])
-
-    two_a = jnp.stack(
-        [
-            first_chunk(first, first_pair),
-            first_chunk(after(first_far, own_units), first_far_pair),
-        ]
-    )
-    second_a = send(two_a, to_second)
-    far_b = send(after(own_units[:9], two_a), to_far)
-    rhs_in = jnp.stack(after(moved, two_a))
+    moved = to_groups(after(cuts, two_a))
+    rhs_in = jnp.stack(moved)
     rhs_pair = send(rhs_in, to_pair)
-    near_0 = jnp.stack([own_units, after(second_own, rhs_in)])
+    four_a = jnp.concatenate([two_a, second_a])
+    third_a = send(four_a, to_third)
+    near_0 = jnp.stack([own_units, after(second_own, third_a)])
     near_1 = send(near_0, to_third)
-    four_a = jnp.concatenate([two_a, after(second_a, near_0)])
-    third_a = send(four_a, to_third)
+    far_b = after(far_b, third_a)
+    second_b = send(far_b, to_second)
+    far_c = send(after(own_units[9:], far_b), to_far)
     b0, b1, r2, r3 = call(
         "stand",
         stand_kernel,
         [(128, 256)] * 4,
-        after(rhs_in, four_a),
+        after(rhs_in, third_a),
         rhs_pair,
         scratch=[pltpu.VMEM((8, 4, 32, 128), F32)],
     )
-    far_b = after(far_b, b0)
-    second_b = send(far_b, to_second)
-    far_c = send(after(own_units[9:], far_b), to_far)
-    far_b_0 = jnp.stack([far_b, second_b])
-    far_b_1 = send(far_b_0, to_third)
 
     own, y0 = call(
         "link_0",
         link_0_kernel,
         VECTOR,
-        after(b0, far_b),
+        after(b0, near_0, far_b),
         four_a,
         third_a,
         scratch=link_scratch(1, 2),
     )
     got = send(own, to_pair)
+    far_b_0 = jnp.stack([far_b, after(second_b, got)])
+    far_b_1 = send(far_b_0, to_third)
     far_c = after(far_c, got)
     second_c = send(far_c, to_second)
-    root_near = jnp.concatenate([near_0[:, 6:9], after(near_1, got)[:, 6:9]])
-    swap_near = send(root_near, to_core)
 
     own, y1 = call(
         "link_1",
@@ -543,19 +543,19 @@
         far_b_1,
         scratch=link_scratch(2, 3),
     )
-    sums = [own, send(own, to_pair), send(own, to_core), send(own, to_pair_core)]
-    root_far = jnp.concatenate([far_b_0[:, 6:9], after(far_b_1, own)[:, 6:9]])
-    swap_far = send(root_far, to_core)
+    sums = [own, send(own, to_core), send(own, to_pair), send(own, to_pair_core)]
+    root_own = jnp.concatenate(
+        [after(near_0[:, 6:9], own), near_1[:, 6:9], far_b_0[:, 6:9], far_b_1[:, 6:9]]
+    )
+    root_swapped = send(root_own, to_core)
     far_c_0 = jnp.stack([far_c, after(second_c, own)])
     far_c_1 = send(far_c_0, to_third)
-    leaf_parts = call("lay_leaf", lay_kernel, PIECES, after(y0, far_c_0), y1, scratch=[four_pieces])
-    leaf_moved = to_groups(leaf_parts)
 
     own, y2 = call(
         "link_2",
         link_2_kernel,
         VECTOR,
-        after(r2, leaf_parts[0]),
+        r2,
         *sums,
         y0,
         y1,
@@ -563,34 +563,32 @@
         near_1,
         far_c_0,
         far_c_1,
-        root_near,
-        root_far,
-        swap_near,
-        swap_far,
-        scratch=link_scratch(3, 5),
-    )
-    sums = [own, send(own, to_pair), send(own, to_core), send(own, to_pair_core)]
-    leaf_near = jnp.stack(after(leaf_moved, own))
-    leaf_other = send(leaf_near, to_row)
-    leaf_solution = join("join_leaf", False, leaf_near, leaf_other)
-
-    root_parts = call(
+        root_own,
+        root_swapped,
+        scratch=link_scratch(3, 4),
+    )
+    sums = [own, send(own, to_core), send(own, to_pair), send(own, to_pair_core)]
+    parts = call(
         "link_3",
         link_3_kernel,
-        PIECES,
-        after(r3, leaf_near),
+        [(4, 32, 128)] * 4,
+        r3,
         *sums,
+        y0,
+        y1,
         y2,
-        root_near,
-        root_far,
-        swap_near,
-        swap_far,
-        scratch=[four_pieces] + link_scratch(0, 1),
-    )
-    moved = jnp.stack([send(root_parts[k], to_group_by_core(k // 2, k % 2)) for k in range(4)])
-    swapped = send(moved, to_core)
-    root_solution = join("join_root", True, moved, swapped)
-    return leaf_solution[None], root_solution
+        root_own,
+        root_swapped,
+        scratch=[pltpu.VMEM((4, 4, 32, 128), F32)] + link_scratch(0, 1),
+    )
+    moved = jnp.stack([send(parts[k], to_group_by_core(k // 2, k % 2)) for k in range(4)])
+    leaf_near, root_near = moved[:, :2], moved[:, 2:]
+    leaf_other = send(leaf_near, to_row)
+    root_other = send(root_near, to_core)
+    return (
+        join("join_leaf", leaf_near, leaf_other)[None],
+        join("join_root", root_near, root_other),
+    )
 
 
 def solution(mesh):

time: 108 us -> 118 us (1.093); the launches traced: 107 us -> 118 us
  waiting for transfers between devices: 47.8 us -> 69.3 us
  starting transfers between devices: 47.3 us -> 34.5 us
  Pallas kernels: 9.74 us -> 12.4 us
    ppermute x36 -> x31, waiting for transfers between devices: 47.8 us -> 69.3 us  [send(): return lax.ppermute(value, AXES, pairs(dest))]
    ppermute x36 -> x31, starting transfers between devices: 47.3 us -> 34.5 us  [send(): return lax.ppermute(value, AXES, pairs(dest))]
    pallas_call x6 -> x5, Pallas kernels: 5.95 us -> 8.57 us  [call(): pl.pallas_call(kernel, out_shape=[pltpu.VMEM(dims, F32) for dims in outs]...]
  transfers between devices with their start and end apart: 36 -> 31, of which waited for: 17 -> 17; matrix products, arithmetic and copies ran while one was open for 0% -> 0% of each run, Pallas kernels for 6% -> 2%
where the time goes in v5:
time: 118 us
  waiting for transfers between devices  69.3 us (59%)
  starting transfers between devices  34.5 us (29%)
  Pallas kernels  12.4 us (11%)
    ppermute x31, waiting for transfers between devices, send(): return lax.ppermute(value, AXES, pairs(dest))  69.3 us
    ppermute x31, starting transfers between devices, send(): return lax.ppermute(value, AXES, pairs(dest))  34.5 us
    pallas_call x5, Pallas kernels, call(): pl.pallas_call(kernel, out_shape=[pltpu.VMEM(dims, F32) for dims in outs]...  8.57 us
  transfers between devices with their start and end apart: 31, of which 17 were waited for; matrix products, arithmetic and copies ran while one was open for 0% of the time, Pallas kernels for 2%

profile of v5, /device:TPU:0, one launch (start us, length us, event | category | flops | bytes accessed | tf_op | source)
XLA Modules:
  0.0 118.3 jit_solution(4709732230831937633)
XLA Ops:
  0.6 0.7 copy-done
  1.3 2.1 %begin.1 = (f32[3,2,32,128]{3,2,1,0:T(8,128)S(1)}, f32[3,2,32,128]{3,2,1,0:T(8,128)S(1)}, f32[2,2,32,128]{3,2,1,0:T(8,128)S(1)}, f32[8,2,32,128]{3,2,1,0:T(8,128...) custom-call(s32[1,2,1,5]{3,2,1,0:T(1,128)S(1)} %bitcast.33, ...), custom_call_target="tpu_custom_call" | custom-call | tf_op jit(solution)/shard_map/begin/pallas_call | solution.py:242
  3.4 3.1 %collective-permute-start = (f32[3,2,32,128]{3,2,1,0:T(8,128)S(1)}, f32[3,2,32,128]{3,2,1,0:T(8,128)S(1)}, u32[]{:S(2)}, u32[]{:S(2)}) collective-permute-start(f32[3,2,32,128]{3,2,1,0:T(8,128)S(1)} %get-tuple-element.45), channel_id=1, source_target_pairs={{0,4},{1,5},{2,6},{3,7},{4,0},{5,1},{6,2},{7,3},{8,12},{9,13},{10,... | collective-permute-start | bytes 294920 | tf_op jit(solution)/shard_map/ppermute | solution.py:67
  6.5 2.5 %collective-permute-start.2 = (f32[2,32,128]{2,1,0:T(8,128)S(1)}, f32[2,32,128]{2,1,0:T(8,128)S(1)}, u32[]{:S(2)}, u32[]{:S(2)}) collective-permute-start(f32[2,32,128]{2,1,0:T(8,128)S(1)} %slice_bitcast_fusion.1), channel_id=1, source_target_pairs={{0,12},{1,13},{2,14},{3,15},{4,8},{5,9},{6,10},{7,11},{8,4},{9,5},... | collective-permute-start | bytes 98312 | tf_op jit(solution)/shard_map/ppermute | solution.py:67
  9.3 7.0 %collective-permute-done.1 = f32[3,2,32,128]{3,2,1,0:T(8,128)S(1)} collective-permute-done((f32[3,2,32,128]{3,2,1,0:T(8,128)S(1)}, f32[3,2,32,128]{3,2,1,0:T(8,128)S(1)}, u32[]{:S(2)}, u32[]{:S(2)}) %collective-permute-start.1) | collective-permute-done | bytes 98336 | tf_op jit(solution)/shard_map/ppermute | solution.py:67
  16.4 1.6 %collective-permute-start.6 = (f32[2,4,2,32,128]{4,3,2,1,0:T(8,128)S(1)}, f32[2,4,2,32,128]{4,3,2,1,0:T(8,128)S(1)}, u32[]{:S(2)}, u32[]{:S(2)}) collective-permute-start(f32[2,4,2,32,128]{4,3,2,1,0:T(8,128)S(1)} %pad_maximum_fusion.4), channel_id=1, source_target_pairs={{0,2},{1,17},{2,0},{3,19},{4,6},{5,21},{6,4},{7,23},{8,10},{9,25},... | collective-permute-start | bytes 786440 | tf_op jit(solution)/shard_map/ppermute | solution.py:67
  17.9 0.5 collective-permute-start.3
  18.6 1.6 %collective-permute-start.11 = (f32[13,2,32,128]{3,2,1,0:T(8,128)S(1)}, f32[13,2,32,128]{3,2,1,0:T(8,128)S(1)}, u32[]{:S(2)}, u32[]{:S(2)}) collective-permute-start(f32[13,2,32,128]{3,2,1,0:T(8,128)S(1)} %get-tuple-element.80), channel_id=1, source_target_pairs={{0,2},{1,17},{2,0},{3,19},{4,6},{5,21},{6,4},{7,23},{8,10},{9,25},... | collective-permute-start | bytes 1277960 | tf_op jit(solution)/shard_map/ppermute | solution.py:67
  20.2 3.4 %collective-permute-done.6 = f32[2,4,2,32,128]{4,3,2,1,0:T(8,128)S(1)} collective-permute-done((f32[2,4,2,32,128]{4,3,2,1,0:T(8,128)S(1)}, f32[2,4,2,32,128]{4,3,2,1,0:T(8,128)S(1)}, u32[]{:S(2)}, u32[]{:S(2)}) %collective-permute-start.6) | collective-permute-done | bytes 262176 | tf_op jit(solution)/shard_map/ppermute | solution.py:67
  23.6 0.9 collective-permute-start.7
  24.5 2.9 %collective-permute-start.4 = (f32[4,32,128]{2,1,0:T(8,128)S(1)}, f32[4,32,128]{2,1,0:T(8,128)S(1)}, u32[]{:S(2)}, u32[]{:S(2)}) collective-permute-start(f32[4,32,128]{2,1,0:T(8,128)S(1)} %get-tuple-element.48), channel_id=1, source_target_pairs={{0,8},{1,9},{2,10},{3,11},{4,12},{5,13},{6,14},{7,15},{8,0},{9,1},... | collective-permute-start | bytes 196616 | tf_op jit(solution)/shard_map/ppermute | solution.py:67
  27.5 1.0 collective-permute-start.5
  28.5 14.3 %collective-permute-done.4 = f32[4,32,128]{2,1,0:T(8,128)S(1)} collective-permute-done((f32[4,32,128]{2,1,0:T(8,128)S(1)}, f32[4,32,128]{2,1,0:T(8,128)S(1)}, u32[]{:S(2)}, u32[]{:S(2)}) %collective-permute-start.4) | collective-permute-done | bytes 65568 | tf_op jit(solution)/shard_map/ppermute | solution.py:67
  42.8 1.3 %collective-permute-done.5 = f32[4,32,128]{2,1,0:T(8,128)S(1)} collective-permute-done((f32[4,32,128]{2,1,0:T(8,128)S(1)}, f32[4,32,128]{2,1,0:T(8,128)S(1)}, u32[]{:S(2)}, u32[]{:S(2)}) %collective-permute-start.5) | collective-permute-done | bytes 65568 | tf_op jit(solution)/shard_map/ppermute | solution.py:67
  44.2 1.6 %collective-permute-start.14 = (f32[9,2,32,128]{3,2,1,0:T(8,128)S(1)}, f32[9,2,32,128]{3,2,1,0:T(8,128)S(1)}, u32[]{:S(2)}, u32[]{:S(2)}) collective-permute-start(f32[9,2,32,128]{3,2,1,0:T(8,128)S(1)} %collective-permute-done.9), channel_id=1, source_target_pairs={{0,2},{1,17},{2,0},{3,19},{4,6},{5,21},{6,4},{7,23},{8,10},{9,25},... | collective-permute-start | bytes 884744 | tf_op jit(solution)/shard_map/ppermute | solution.py:67
  45.8 1.6 %collective-permute-start.13 = (f32[2,13,2,32,128]{4,3,2,1,0:T(8,128)S(1)}, f32[2,13,2,32,128]{4,3,2,1,0:T(8,128)S(1)}, u32[]{:S(2)}, u32[]{:S(2)}) collective-permute-start(f32[2,13,2,32,128]{4,3,2,1,0:T(8,128)S(1)} %pad_maximum_fusion.n0), channel_id=1, source_target_pairs={{0,16},{1,3},{2,18},{3,1},{4,20},{5,7},{6,22},{7,5},{8,24},{9,11},... | collective-permute-start | bytes 2555912 | tf_op jit(solution)/shard_map/ppermute | solution.py:67
  47.4 5.0 %collective-permute-done.8.other_ref = f32[4,4,32,128]{3,2,1,0:T(8,128)S(1)} collective-permute-done((f32[4,4,32,128]{3,2,1,0:T(8,128)S(1)}, f32[4,4,32,128]{3,2,1,0:T(8,128)S(1)}, u32[]{:S(2)}, u32[]{:S(2)}) %collective-permute-start.8) | collective-permute-done | bytes 262176 | tf_op jit(solution)/shard_map/ppermute | solution.py:67
  52.6 1.6 %link_0.1 = (f32[128,256]{1,0:T(8,128)S(1)}, f32[128,128]{1,0:T(8,128)S(1)}) custom-call(f32[128,256]{1,0:T(8,128)S(1)} %get-tuple-element.62.b_ref, f32[4,4,2,32,128]{4,3,2,1,0:T(8,128)S(1)} %pad_maximum_fusion.3.four, f32[4,4,2,32,128]{4,3,2,1,0:T(8,128)S(1)} %collective-permute-done.7.third), custom_call_target="tpu_custom_call" | custom-call | tf_op jit(solution)/shard_map/link_0/pallas_call | solution.py:165
  54.6 4.7 %collective-permute-done.12.got = f32[128,256]{1,0:T(8,128)S(1)} collective-permute-done((f32[128,256]{1,0:T(8,128)S(1)}, f32[128,256]{1,0:T(8,128)S(1)}, u32[]{:S(2)}, u32[]{:S(2)}) %collective-permute-start.12) | collective-permute-done | bytes 131104 | tf_op jit(solution)/shard_map/ppermute | solution.py:67
  59.3 1.6 %collective-permute-start.15 = (f32[2,9,2,32,128]{4,3,2,1,0:T(8,128)S(1)}, f32[2,9,2,32,128]{4,3,2,1,0:T(8,128)S(1)}, u32[]{:S(2)}, u32[]{:S(2)}) collective-permute-start(f32[2,9,2,32,128]{4,3,2,1,0:T(8,128)S(1)} %pad_maximum_fusion.2.f0), channel_id=1, source_target_pairs={{0,16},{1,3},{2,18},{3,1},{4,20},{5,7},{6,22},{7,5},{8,24},{9,11},... | collective-permute-start | bytes 1769480 | tf_op jit(solution)/shard_map/ppermute | solution.py:67
  60.9 0.9 collective-permute-start.10
  61.8 6.2 %collective-permute-done.10 = f32[4,2,32,128]{3,2,1,0:T(8,128)S(1)} collective-permute-done((f32[4,2,32,128]{3,2,1,0:T(8,128)S(1)}, f32[4,2,32,128]{3,2,1,0:T(8,128)S(1)}, u32[]{:S(2)}, u32[]{:S(2)}) %collective-permute-start.10) | collective-permute-done | bytes 131104 | tf_op jit(solution)/shard_map/ppermute | solution.py:67
  68.1 1.2 %collective-permute-done.15.f1 = f32[2,9,2,32,128]{4,3,2,1,0:T(8,128)S(1)} collective-permute-done((f32[2,9,2,32,128]{4,3,2,1,0:T(8,128)S(1)}, f32[2,9,2,32,128]{4,3,2,1,0:T(8,128)S(1)}, u32[]{:S(2)}, u32[]{:S(2)}) %collective-permute-start.15) | collective-permute-done | bytes 589856 | tf_op jit(solution)/shard_map/ppermute | solution.py:67
  69.3 2.3 %link_1.1 = (f32[128,256]{1,0:T(8,128)S(1)}, f32[128,128]{1,0:T(8,128)S(1)}) custom-call(f32[128,256]{1,0:T(8,128)S(1)} %get-tuple-element.65.b_ref, f32[128,256]{1,0:T(8,128)S(1)} %get-tuple-element.63.own, f32[128,256]{1,0:T(8,128)S(1)} %collective-permute-done.12.got, f32[128,128]{1,0:T(8,128)S(1)} %get-tuple-element.66.y0_ref, ...), custom_call_target="tpu_custom_call" | custom-call | tf_op jit(solution)/shard_map/link_1/pallas_call | solution.py:165
  71.7 1.6 %collective-permute-start.19 = (f32[4,2,32,128]{3,2,1,0:T(8,128)S(1)}, f32[4,2,32,128]{3,2,1,0:T(8,128)S(1)}, u32[]{:S(2)}, u32[]{:S(2)}) collective-permute-start(f32[4,2,32,128]{3,2,1,0:T(8,128)S(1)} %collective-permute-done.10), channel_id=1, source_target_pairs={{0,2},{1,17},{2,0},{3,19},{4,6},{5,21},{6,4},{7,23},{8,10},{9,25},... | collective-permute-start | bytes 393224 | tf_op jit(solution)/shard_map/ppermute | solution.py:67
  73.3 3.5 %collective-permute-done.19 = f32[4,2,32,128]{3,2,1,0:T(8,128)S(1)} collective-permute-done((f32[4,2,32,128]{3,2,1,0:T(8,128)S(1)}, f32[4,2,32,128]{3,2,1,0:T(8,128)S(1)}, u32[]{:S(2)}, u32[]{:S(2)}) %collective-permute-start.19) | collective-permute-done | bytes 131104 | tf_op jit(solution)/shard_map/ppermute | solution.py:67
  76.8 1.6 %collective-permute-start.20 = (f32[2,4,2,32,128]{4,3,2,1,0:T(8,128)S(1)}, f32[2,4,2,32,128]{4,3,2,1,0:T(8,128)S(1)}, u32[]{:S(2)}, u32[]{:S(2)}) collective-permute-start(f32[2,4,2,32,128]{4,3,2,1,0:T(8,128)S(1)} %pad_maximum_fusion.6.f0), channel_id=1, source_target_pairs={{0,16},{1,3},{2,18},{3,1},{4,20},{5,7},{6,22},{7,5},{8,24},{9,11},... | collective-permute-start | bytes 786440 | tf_op jit(solution)/shard_map/ppermute | solution.py:67
  78.4 0.9 collective-permute-start.17
  79.3 1.0 collective-permute-start.16
  80.3 3.9 %collective-permute-done.18.s3 = f32[128,256]{1,0:T(8,128)S(1)} collective-permute-done((f32[128,256]{1,0:T(8,128)S(1)}, f32[128,256]{1,0:T(8,128)S(1)}, u32[]{:S(2)}, u32[]{:S(2)}) %collective-permute-start.18) | collective-permute-done | bytes 131104 | tf_op jit(solution)/shard_map/ppermute | solution.py:67
  84.2 1.7 %collective-permute-done.17.s2 = f32[128,256]{1,0:T(8,128)S(1)} collective-permute-done((f32[128,256]{1,0:T(8,128)S(1)}, f32[128,256]{1,0:T(8,128)S(1)}, u32[]{:S(2)}, u32[]{:S(2)}) %collective-permute-start.17) | collective-permute-done | bytes 131104 | tf_op jit(solution)/shard_map/ppermute | solution.py:67
  85.9 3.3 %link_2.1 = (f32[128,256]{1,0:T(8,128)S(1)}, f32[128,128]{1,0:T(8,128)S(1)}) custom-call(f32[128,256]{1,0:T(8,128)S(1)} %get-tuple-element.52.b_ref, f32[128,256]{1,0:T(8,128)S(1)} %get-tuple-element.68.s0, f32[128,256]{1,0:T(8,128)S(1)} %collective-permute-done.16.s1, f32[128,256]{1,0:T(8,128)S(1)} %collective-permute-done.17.s2, ...), custom_call_target="tpu_custom_call" | custom-call | tf_op jit(solution)/shard_map/link_2/pallas_call | solution.py:165
  89.3 0.9 collective-permute-start.24
  90.1 1.2 collective-permute-start.23
  91.3 3.2 %collective-permute-done.24.s3 = f32[128,256]{1,0:T(8,128)S(1)} collective-permute-done((f32[128,256]{1,0:T(8,128)S(1)}, f32[128,256]{1,0:T(8,128)S(1)}, u32[]{:S(2)}, u32[]{:S(2)}) %collective-permute-start.24) | collective-permute-done | bytes 131104 | tf_op jit(solution)/shard_map/ppermute | solution.py:67
  94.6 3.4 %collective-permute-done.23.s2 = f32[128,256]{1,0:T(8,128)S(1)} collective-permute-done((f32[128,256]{1,0:T(8,128)S(1)}, f32[128,256]{1,0:T(8,128)S(1)}, u32[]{:S(2)}, u32[]{:S(2)}) %collective-permute-start.23) | collective-permute-done | bytes 131104 | tf_op jit(solution)/shard_map/ppermute | solution.py:67
  97.9 1.1 link_3.1
  99.0 0.7 collective-permute-start.25
  99.7 0.7 collective-permute-start.26
  100.4 2.9 %collective-permute-start.27 = (f32[4,32,128]{2,1,0:T(8,128)S(1)}, f32[4,32,128]{2,1,0:T(8,128)S(1)}, u32[]{:S(2)}, u32[]{:S(2)}) collective-permute-start(f32[4,32,128]{2,1,0:T(8,128)S(1)} %get-tuple-element.76), channel_id=1, source_target_pairs={{0,8},{1,25},{2,10},{3,27},{4,12},{5,29},{6,14},{7,31},{8,0},{9,17... | collective-permute-start | bytes 196616 | tf_op jit(solution)/shard_map/ppermute | solution.py:67
  103.2 0.9 collective-permute-start.28
  104.2 1.4 %collective-permute-done.27 = f32[4,32,128]{2,1,0:T(8,128)S(1)} collective-permute-done((f32[4,32,128]{2,1,0:T(8,128)S(1)}, f32[4,32,128]{2,1,0:T(8,128)S(1)}, u32[]{:S(2)}, u32[]{:S(2)}) %collective-permute-start.27) | collective-permute-done | bytes 65568 | tf_op jit(solution)/shard_map/ppermute | solution.py:67
  105.5 5.7 %collective-permute-done.28 = f32[4,32,128]{2,1,0:T(8,128)S(1)} collective-permute-done((f32[4,32,128]{2,1,0:T(8,128)S(1)}, f32[4,32,128]{2,1,0:T(8,128)S(1)}, u32[]{:S(2)}, u32[]{:S(2)}) %collective-permute-start.28) | collective-permute-done | bytes 65568 | tf_op jit(solution)/shard_map/ppermute | solution.py:67
  111.3 0.7 collective-permute-start.30
  112.0 1.3 %collective-permute-start.29 = (f32[4,2,32,128]{3,2,1,0:T(8,128)S(1)}, f32[4,2,32,128]{3,2,1,0:T(8,128)S(1)}, u32[]{:S(2)}, u32[]{:S(2)}) collective-permute-start(f32[4,2,32,128]{3,2,1,0:T(8,128)S(1)} %get-tuple-element.79.near_ref), channel_id=1, source_target_pairs={{0,16},{1,17},{2,18},{3,19},{4,20},{5,21},{6,22},{7,23},{8,24},{9,... | collective-permute-start | bytes 393224 | tf_op jit(solution)/shard_map/ppermute | solution.py:67
  113.3 0.9 join_root.1
  114.1 3.3 %collective-permute-done.29.other_ref = f32[4,2,32,128]{3,2,1,0:T(8,128)S(1)} collective-permute-done((f32[4,2,32,128]{3,2,1,0:T(8,128)S(1)}, f32[4,2,32,128]{3,2,1,0:T(8,128)S(1)}, u32[]{:S(2)}, u32[]{:S(2)}) %collective-permute-start.29) | collective-permute-done | bytes 131104 | tf_op jit(solution)/shard_map/ppermute | solution.py:67
  117.4 0.9 join_leaf.1
  (54 shorter events, 1.7 us)
Async XLA Ops:
  0.6 0.7 copy-start
  3.4 5.9 %collective-permute-start = (f32[3,2,32,128]{3,2,1,0:T(8,128)S(1)}, f32[3,2,32,128]{3,2,1,0:T(8,128)S(1)}, u32[]{:S(2)}, u32[]{:S(2)}) collective-permute-start(f32[3,2,32,128]{3,2,1,0:T(8,128)S(1)} %get-tuple-element.45), channel_id=1, source_target_pairs={{0,4},{1,5},{2,6},{3,7},{4,0},{5,1},{6,2},{7,3},{8,12},{9,13},{10,... | collective-permute-start | bytes 294920 | tf_op jit(solution)/shard_map/ppermute | solution.py:67
  6.5 9.8 %collective-permute-start.2 = (f32[2,32,128]{2,1,0:T(8,128)S(1)}, f32[2,32,128]{2,1,0:T(8,128)S(1)}, u32[]{:S(2)}, u32[]{:S(2)}) collective-permute-start(f32[2,32,128]{2,1,0:T(8,128)S(1)} %slice_bitcast_fusion.1), channel_id=1, source_target_pairs={{0,12},{1,13},{2,14},{3,15},{4,8},{5,9},{6,10},{7,11},{8,4},{9,5},... | collective-permute-start | bytes 98312 | tf_op jit(solution)/shard_map/ppermute | solution.py:67
  9.0 7.3 %collective-permute-start.1 = (f32[3,2,32,128]{3,2,1,0:T(8,128)S(1)}, f32[3,2,32,128]{3,2,1,0:T(8,128)S(1)}, u32[]{:S(2)}, u32[]{:S(2)}) collective-permute-start(f32[3,2,32,128]{3,2,1,0:T(8,128)S(1)} %get-tuple-element.44), channel_id=1, source_target_pairs={{0,8},{1,9},{2,10},{3,11},{4,12},{5,13},{6,14},{7,15},{8,0},{9,1},... | collective-permute-start | bytes 294920 | tf_op jit(solution)/shard_map/ppermute | solution.py:67
  16.4 7.1 %collective-permute-start.6 = (f32[2,4,2,32,128]{4,3,2,1,0:T(8,128)S(1)}, f32[2,4,2,32,128]{4,3,2,1,0:T(8,128)S(1)}, u32[]{:S(2)}, u32[]{:S(2)}) collective-permute-start(f32[2,4,2,32,128]{4,3,2,1,0:T(8,128)S(1)} %pad_maximum_fusion.4), channel_id=1, source_target_pairs={{0,2},{1,17},{2,0},{3,19},{4,6},{5,21},{6,4},{7,23},{8,10},{9,25},... | collective-permute-start | bytes 786440 | tf_op jit(solution)/shard_map/ppermute | solution.py:67
  17.9 9.5 %collective-permute-start.3 = (f32[4,32,128]{2,1,0:T(8,128)S(1)}, f32[4,32,128]{2,1,0:T(8,128)S(1)}, u32[]{:S(2)}, u32[]{:S(2)}) collective-permute-start(f32[4,32,128]{2,1,0:T(8,128)S(1)} %get-tuple-element.47), channel_id=1, source_target_pairs={{0,2},{1,3},{2,0},{3,1},{4,6},{5,7},{6,4},{7,5},{8,10},{9,11},{10,... | collective-permute-start | bytes 196616 | tf_op jit(solution)/shard_map/ppermute | solution.py:67
  18.6 27.1 %collective-permute-start.11 = (f32[13,2,32,128]{3,2,1,0:T(8,128)S(1)}, f32[13,2,32,128]{3,2,1,0:T(8,128)S(1)}, u32[]{:S(2)}, u32[]{:S(2)}) collective-permute-start(f32[13,2,32,128]{3,2,1,0:T(8,128)S(1)} %get-tuple-element.80), channel_id=1, source_target_pairs={{0,2},{1,17},{2,0},{3,19},{4,6},{5,21},{6,4},{7,23},{8,10},{9,25},... | collective-permute-start | bytes 1277960 | tf_op jit(solution)/shard_map/ppermute | solution.py:67
  23.6 20.6 %collective-permute-start.7 = (f32[4,4,2,32,128]{4,3,2,1,0:T(8,128)S(1)}, f32[4,4,2,32,128]{4,3,2,1,0:T(8,128)S(1)}, u32[]{:S(2)}, u32[]{:S(2)}) collective-permute-start(f32[4,4,2,32,128]{4,3,2,1,0:T(8,128)S(1)} %pad_maximum_fusion.3.four), channel_id=1, source_target_pairs={{0,16},{1,3},{2,18},{3,1},{4,20},{5,7},{6,22},{7,5},{8,24},{9,11},... | collective-permute-start | bytes 1572872 | tf_op jit(solution)/shard_map/ppermute | solution.py:67
  24.5 19.7 %collective-permute-start.9 = (f32[9,2,32,128]{3,2,1,0:T(8,128)S(1)}, f32[9,2,32,128]{3,2,1,0:T(8,128)S(1)}, u32[]{:S(2)}, u32[]{:S(2)}) collective-permute-start(f32[9,2,32,128]{3,2,1,0:T(8,128)S(1)} %constant_dynamic-update-slice_fusion), channel_id=1, source_target_pairs={{0,8},{1,9},{2,10},{3,11},{4,12},{5,13},{6,14},{7,15},{8,0},{9,1},... | collective-permute-start | bytes 884744 | tf_op jit(solution)/shard_map/ppermute | solution.py:67
  24.5 18.2 %collective-permute-start.4 = (f32[4,32,128]{2,1,0:T(8,128)S(1)}, f32[4,32,128]{2,1,0:T(8,128)S(1)}, u32[]{:S(2)}, u32[]{:S(2)}) collective-permute-start(f32[4,32,128]{2,1,0:T(8,128)S(1)} %get-tuple-element.48), channel_id=1, source_target_pairs={{0,8},{1,9},{2,10},{3,11},{4,12},{5,13},{6,14},{7,15},{8,0},{9,1},... | collective-permute-start | bytes 196616 | tf_op jit(solution)/shard_map/ppermute | solution.py:67
  27.5 16.6 %collective-permute-start.5 = (f32[4,32,128]{2,1,0:T(8,128)S(1)}, f32[4,32,128]{2,1,0:T(8,128)S(1)}, u32[]{:S(2)}, u32[]{:S(2)}) collective-permute-start(f32[4,32,128]{2,1,0:T(8,128)S(1)} %get-tuple-element.49), channel_id=1, source_target_pairs={{0,10},{1,11},{2,8},{3,9},{4,14},{5,15},{6,12},{7,13},{8,2},{9,3},... | collective-permute-start | bytes 196616 | tf_op jit(solution)/shard_map/ppermute | solution.py:67
  44.1 8.3 %collective-permute-start.8 = (f32[4,4,32,128]{3,2,1,0:T(8,128)S(1)}, f32[4,4,32,128]{3,2,1,0:T(8,128)S(1)}, u32[]{:S(2)}, u32[]{:S(2)}) collective-permute-start(f32[4,4,32,128]{3,2,1,0:T(8,128)S(1)} %pad_maximum_fusion.5.near_ref), channel_id=1, source_target_pairs={{0,4},{1,5},{2,6},{3,7},{4,0},{5,1},{6,2},{7,3},{8,12},{9,13},{10,... | collective-permute-start | bytes 786440 | tf_op jit(solution)/shard_map/ppermute | solution.py:67
  44.2 15.1 %collective-permute-start.14 = (f32[9,2,32,128]{3,2,1,0:T(8,128)S(1)}, f32[9,2,32,128]{3,2,1,0:T(8,128)S(1)}, u32[]{:S(2)}, u32[]{:S(2)}) collective-permute-start(f32[9,2,32,128]{3,2,1,0:T(8,128)S(1)} %collective-permute-done.9), channel_id=1, source_target_pairs={{0,2},{1,17},{2,0},{3,19},{4,6},{5,21},{6,4},{7,23},{8,10},{9,25},... | collective-permute-start | bytes 884744 | tf_op jit(solution)/shard_map/ppermute | solution.py:67
  45.8 22.2 %collective-permute-start.13 = (f32[2,13,2,32,128]{4,3,2,1,0:T(8,128)S(1)}, f32[2,13,2,32,128]{4,3,2,1,0:T(8,128)S(1)}, u32[]{:S(2)}, u32[]{:S(2)}) collective-permute-start(f32[2,13,2,32,128]{4,3,2,1,0:T(8,128)S(1)} %pad_maximum_fusion.n0), channel_id=1, source_target_pairs={{0,16},{1,3},{2,18},{3,1},{4,20},{5,7},{6,22},{7,5},{8,24},{9,11},... | collective-permute-start | bytes 2555912 | tf_op jit(solution)/shard_map/ppermute | solution.py:67
  54.3 5.0 %collective-permute-start.12 = (f32[128,256]{1,0:T(8,128)S(1)}, f32[128,256]{1,0:T(8,128)S(1)}, u32[]{:S(2)}, u32[]{:S(2)}) collective-permute-start(f32[128,256]{1,0:T(8,128)S(1)} %get-tuple-element.63.own), channel_id=1, source_target_pairs={{0,4},{1,5},{2,6},{3,7},{4,0},{5,1},{6,2},{7,3},{8,12},{9,13},{10,... | collective-permute-start | bytes 393224 | tf_op jit(solution)/shard_map/ppermute | solution.py:67
  59.3 9.9 %collective-permute-start.15 = (f32[2,9,2,32,128]{4,3,2,1,0:T(8,128)S(1)}, f32[2,9,2,32,128]{4,3,2,1,0:T(8,128)S(1)}, u32[]{:S(2)}, u32[]{:S(2)}) collective-permute-start(f32[2,9,2,32,128]{4,3,2,1,0:T(8,128)S(1)} %pad_maximum_fusion.2.f0), channel_id=1, source_target_pairs={{0,16},{1,3},{2,18},{3,1},{4,20},{5,7},{6,22},{7,5},{8,24},{9,11},... | collective-permute-start | bytes 1769480 | tf_op jit(solution)/shard_map/ppermute | solution.py:67
  60.9 7.1 %collective-permute-start.10 = (f32[4,2,32,128]{3,2,1,0:T(8,128)S(1)}, f32[4,2,32,128]{3,2,1,0:T(8,128)S(1)}, u32[]{:S(2)}, u32[]{:S(2)}) collective-permute-start(f32[4,2,32,128]{3,2,1,0:T(8,128)S(1)} %get-tuple-element.59), channel_id=1, source_target_pairs={{0,8},{1,9},{2,10},{3,11},{4,12},{5,13},{6,14},{7,15},{8,0},{9,1},... | collective-permute-start | bytes 393224 | tf_op jit(solution)/shard_map/ppermute | solution.py:67
  71.7 14.2 %collective-permute-start.21 = (f32[8,3,2,32,128]{4,3,2,1,0:T(8,128)S(1)}, f32[8,3,2,32,128]{4,3,2,1,0:T(8,128)S(1)}, u32[]{:S(2)}, u32[]{:S(2)}) collective-permute-start(f32[8,3,2,32,128]{4,3,2,1,0:T(8,128)S(1)} %pad_maximum_fusion.1.root), channel_id=1, source_target_pairs={{0,1},{1,0},{2,3},{3,2},{4,5},{5,4},{6,7},{7,6},{8,9},{9,8},{10,11... | collective-permute-start | bytes 2359304 | tf_op jit(solution)/shard_map/ppermute | solution.py:67
  71.7 5.0 %collective-permute-start.19 = (f32[4,2,32,128]{3,2,1,0:T(8,128)S(1)}, f32[4,2,32,128]{3,2,1,0:T(8,128)S(1)}, u32[]{:S(2)}, u32[]{:S(2)}) collective-permute-start(f32[4,2,32,128]{3,2,1,0:T(8,128)S(1)} %collective-permute-done.10), channel_id=1, source_target_pairs={{0,2},{1,17},{2,0},{3,19},{4,6},{5,21},{6,4},{7,23},{8,10},{9,25},... | collective-permute-start | bytes 393224 | tf_op jit(solution)/shard_map/ppermute | solution.py:67
  76.8 9.1 %collective-permute-start.20 = (f32[2,4,2,32,128]{4,3,2,1,0:T(8,128)S(1)}, f32[2,4,2,32,128]{4,3,2,1,0:T(8,128)S(1)}, u32[]{:S(2)}, u32[]{:S(2)}) collective-permute-start(f32[2,4,2,32,128]{4,3,2,1,0:T(8,128)S(1)} %pad_maximum_fusion.6.f0), channel_id=1, source_target_pairs={{0,16},{1,3},{2,18},{3,1},{4,20},{5,7},{6,22},{7,5},{8,24},{9,11},... | collective-permute-start | bytes 786440 | tf_op jit(solution)/shard_map/ppermute | solution.py:67
  78.4 5.8 %collective-permute-start.18 = (f32[128,256]{1,0:T(8,128)S(1)}, f32[128,256]{1,0:T(8,128)S(1)}, u32[]{:S(2)}, u32[]{:S(2)}) collective-permute-start(f32[128,256]{1,0:T(8,128)S(1)} %get-tuple-element.68.s0), channel_id=1, source_target_pairs={{0,5},{1,4},{2,7},{3,6},{4,1},{5,0},{6,3},{7,2},{8,13},{9,12},{10,... | collective-permute-start | bytes 393224 | tf_op jit(solution)/shard_map/ppermute | solution.py:67
  78.4 7.5 %collective-permute-start.17 = (f32[128,256]{1,0:T(8,128)S(1)}, f32[128,256]{1,0:T(8,128)S(1)}, u32[]{:S(2)}, u32[]{:S(2)}) collective-permute-start(f32[128,256]{1,0:T(8,128)S(1)} %get-tuple-element.68.s0), channel_id=1, source_target_pairs={{0,4},{1,5},{2,6},{3,7},{4,0},{5,1},{6,2},{7,3},{8,12},{9,13},{10,... | collective-permute-start | bytes 393224 | tf_op jit(solution)/shard_map/ppermute | solution.py:67
  79.3 6.6 %collective-permute-start.16 = (f32[128,256]{1,0:T(8,128)S(1)}, f32[128,256]{1,0:T(8,128)S(1)}, u32[]{:S(2)}, u32[]{:S(2)}) collective-permute-start(f32[128,256]{1,0:T(8,128)S(1)} %get-tuple-element.68.s0), channel_id=1, source_target_pairs={{0,1},{1,0},{2,3},{3,2},{4,5},{5,4},{6,7},{7,6},{8,9},{9,8},{10,11... | collective-permute-start | bytes 393224 | tf_op jit(solution)/shard_map/ppermute | solution.py:67
  89.3 5.3 %collective-permute-start.24 = (f32[128,256]{1,0:T(8,128)S(1)}, f32[128,256]{1,0:T(8,128)S(1)}, u32[]{:S(2)}, u32[]{:S(2)}) collective-permute-start(f32[128,256]{1,0:T(8,128)S(1)} %get-tuple-element.72.s0), channel_id=1, source_target_pairs={{0,5},{1,4},{2,7},{3,6},{4,1},{5,0},{6,3},{7,2},{8,13},{9,12},{10,... | collective-permute-start | bytes 393224 | tf_op jit(solution)/shard_map/ppermute | solution.py:67
  90.1 7.8 %collective-permute-start.23 = (f32[128,256]{1,0:T(8,128)S(1)}, f32[128,256]{1,0:T(8,128)S(1)}, u32[]{:S(2)}, u32[]{:S(2)}) collective-permute-start(f32[128,256]{1,0:T(8,128)S(1)} %get-tuple-element.72.s0), channel_id=1, source_target_pairs={{0,4},{1,5},{2,6},{3,7},{4,0},{5,1},{6,2},{7,3},{8,12},{9,13},{10,... | collective-permute-start | bytes 393224 | tf_op jit(solution)/shard_map/ppermute | solution.py:67
  91.3 6.6 %collective-permute-start.22 = (f32[128,256]{1,0:T(8,128)S(1)}, f32[128,256]{1,0:T(8,128)S(1)}, u32[]{:S(2)}, u32[]{:S(2)}) collective-permute-start(f32[128,256]{1,0:T(8,128)S(1)} %get-tuple-element.72.s0), channel_id=1, source_target_pairs={{0,1},{1,0},{2,3},{3,2},{4,5},{5,4},{6,7},{7,6},{8,9},{9,8},{10,11... | collective-permute-start | bytes 393224 | tf_op jit(solution)/shard_map/ppermute | solution.py:67
  99.0 5.1 %collective-permute-start.25 = (f32[4,32,128]{2,1,0:T(8,128)S(1)}, f32[4,32,128]{2,1,0:T(8,128)S(1)}, u32[]{:S(2)}, u32[]{:S(2)}) collective-permute-start(f32[4,32,128]{2,1,0:T(8,128)S(1)} %get-tuple-element.74), channel_id=1, source_target_pairs={{0,0},{1,17},{2,2},{3,19},{4,4},{5,21},{6,6},{7,23},{8,8},{9,25},{... | collective-permute-start | bytes 196616 | tf_op jit(solution)/shard_map/ppermute | solution.py:67
  99.7 4.5 %collective-permute-start.26 = (f32[4,32,128]{2,1,0:T(8,128)S(1)}, f32[4,32,128]{2,1,0:T(8,128)S(1)}, u32[]{:S(2)}, u32[]{:S(2)}) collective-permute-start(f32[4,32,128]{2,1,0:T(8,128)S(1)} %get-tuple-element.75), channel_id=1, source_target_pairs={{0,2},{1,19},{2,0},{3,17},{4,6},{5,23},{6,4},{7,21},{8,10},{9,27},... | collective-permute-start | bytes 196616 | tf_op jit(solution)/shard_map/ppermute | solution.py:67
  100.4 5.2 %collective-permute-start.27 = (f32[4,32,128]{2,1,0:T(8,128)S(1)}, f32[4,32,128]{2,1,0:T(8,128)S(1)}, u32[]{:S(2)}, u32[]{:S(2)}) collective-permute-start(f32[4,32,128]{2,1,0:T(8,128)S(1)} %get-tuple-element.76), channel_id=1, source_target_pairs={{0,8},{1,25},{2,10},{3,27},{4,12},{5,29},{6,14},{7,31},{8,0},{9,17... | collective-permute-start | bytes 196616 | tf_op jit(solution)/shard_map/ppermute | solution.py:67
  103.2 8.0 %collective-permute-start.28 = (f32[4,32,128]{2,1,0:T(8,128)S(1)}, f32[4,32,128]{2,1,0:T(8,128)S(1)}, u32[]{:S(2)}, u32[]{:S(2)}) collective-permute-start(f32[4,32,128]{2,1,0:T(8,128)S(1)} %get-tuple-element.77), channel_id=1, source_target_pairs={{0,10},{1,27},{2,8},{3,25},{4,14},{5,31},{6,12},{7,29},{8,2},{9,19... | collective-permute-start | bytes 196616 | tf_op jit(solution)/shard_map/ppermute | solution.py:67
  111.3 2.0 %collective-permute-start.30 = (f32[4,2,32,128]{3,2,1,0:T(8,128)S(1)}, f32[4,2,32,128]{3,2,1,0:T(8,128)S(1)}, u32[]{:S(2)}, u32[]{:S(2)}) collective-permute-start(f32[4,2,32,128]{3,2,1,0:T(8,128)S(1)} %get-tuple-element.78.near_ref), channel_id=1, source_target_pairs={{0,1},{1,0},{2,3},{3,2},{4,5},{5,4},{6,7},{7,6},{8,9},{9,8},{10,11... | collective-permute-start | bytes 393224 | tf_op jit(solution)/shard_map/ppermute | solution.py:67
  112.0 5.5 %collective-permute-start.29 = (f32[4,2,32,128]{3,2,1,0:T(8,128)S(1)}, f32[4,2,32,128]{3,2,1,0:T(8,128)S(1)}, u32[]{:S(2)}, u32[]{:S(2)}) collective-permute-start(f32[4,2,32,128]{3,2,1,0:T(8,128)S(1)} %get-tuple-element.79.near_ref), channel_id=1, source_target_pairs={{0,16},{1,17},{2,18},{3,19},{4,20},{5,21},{6,22},{7,23},{8,24},{9,... | collective-permute-start | bytes 393224 | tf_op jit(solution)/shard_map/ppermute | solution.py:67

commit v6 on v5

--- a/solution.py
+++ b/solution.py
@@ -169,6 +169,7 @@
         out_specs=[vmem() for _ in outs],
         scratch_shapes=list(scratch),
         compiler_params=pltpu.CompilerParams(vmem_limit_bytes=VMEM_OF_A_KERNEL),
+
         name=name,
     )(*fixed)
 
@@ -247,6 +248,7 @@
         scratch_shapes=[pltpu.VMEM(a.shape, F32) for a in arrays]
         + [pltpu.VMEM((4, 4, 32, 128), F32), pltpu.SemaphoreType.DMA((6,))],
         compiler_params=pltpu.CompilerParams(vmem_limit_bytes=VMEM_OF_A_KERNEL),
+
         name="begin",
     )(tiles, *(pltpu.with_memory_space_constraint(a, pltpu.HBM) for a in arrays))
 
@@ -459,6 +461,7 @@
         out_specs=vmem(),
         scratch_shapes=[pltpu.VMEM((8, 2, 32, 128), F32)],
         compiler_params=pltpu.CompilerParams(vmem_limit_bytes=VMEM_OF_A_KERNEL),
+
         name=name,
     )(*(pltpu.with_memory_space_constraint(v, pltpu.VMEM) for v in (near, other)))
 
@@ -486,19 +489,19 @@
     def first_chunk(values, got):
         return jnp.concatenate([whole(values[0], got), values[1:]])
 
+    moved = to_groups(cuts)
     two_a = jnp.stack([first_chunk(first, pair[0]), first_chunk(first_far, first_far_pair)])
     second_a = send(two_a, to_second)
-
-    late = after(pair, two_a)
+    rhs_in = jnp.stack(after(moved, two_a))
+    rhs_pair = send(rhs_in, to_pair)
+
+    late = after(pair, rhs_in)
     own_units = jnp.concatenate(
         [whole(rest[0], late[1]), blocks[:4], whole(rest[1], late[2]), lower, blocks[4:]]
     )
     far_b = send(own_units[:9], to_far)
     second_own = send(own_units, to_second)
-    moved = to_groups(after(cuts, two_a))
-    rhs_in = jnp.stack(moved)
-    rhs_pair = send(rhs_in, to_pair)
-    four_a = jnp.concatenate([two_a, second_a])
+    four_a = jnp.concatenate([two_a, after(second_a, own_units)])
     third_a = send(four_a, to_third)
     near_0 = jnp.stack([own_units, after(second_own, third_a)])
     near_1 = send(near_0, to_third)
@@ -526,14 +529,16 @@
     got = send(own, to_pair)
     far_b_0 = jnp.stack([far_b, after(second_b, got)])
     far_b_1 = send(far_b_0, to_third)
-    far_c = after(far_c, got)
+    far_c = after(far_c, far_b_0)
     second_c = send(far_c, to_second)
+    far_c_0 = jnp.stack([far_c, second_c])
+    far_c_1 = send(far_c_0, to_third)
 
     own, y1 = call(
         "link_1",
         link_1_kernel,
         VECTOR,
-        after(b1, far_c),
+        after(b1, far_c_0),
         own,
         got,
         y0,
@@ -548,8 +553,6 @@
         [after(near_0[:, 6:9], own), near_1[:, 6:9], far_b_0[:, 6:9], far_b_1[:, 6:9]]
     )
     root_swapped = send(root_own, to_core)
-    far_c_0 = jnp.stack([far_c, after(second_c, own)])
-    far_c_1 = send(far_c_0, to_third)
 
     own, y2 = call(
         "link_2",

time: 118 us -> 110 us (0.932)
  waiting for transfers between devices: 69.3 us -> 61.4 us
    ppermute x31, waiting for transfers between devices: 69.3 us -> 61.4 us  [send(): return lax.ppermute(value, AXES, pairs(dest))]
  transfers between devices with their start and end apart: 31 -> 31, of which waited for: 17 -> 16; matrix products, arithmetic and copies ran while one was open for 0% -> 0% of each run, Pallas kernels for 2% -> 2%
where the time goes in v6:
time: 110 us; the launch traced here: 109 us
  waiting for transfers between devices  61.4 us (56%)
  starting transfers between devices  33.5 us (30%)
  Pallas kernels  12.4 us (11%)
    ppermute x31, waiting for transfers between devices, send(): return lax.ppermute(value, AXES, pairs(dest))  61.4 us
    ppermute x31, starting transfers between devices, send(): return lax.ppermute(value, AXES, pairs(dest))  33.5 us
    pallas_call x5, Pallas kernels, call(): pl.pallas_call(kernel, out_shape=[pltpu.VMEM(dims, F32) for dims in outs]...  8.59 us
  transfers between devices with their start and end apart: 31, of which 16 were waited for; matrix products, arithmetic and copies ran while one was open for 0% of the time, Pallas kernels for 2%

profile of v6, /device:TPU:0, one launch (start us, length us, event | category | flops | bytes accessed | tf_op | source)
XLA Modules:
  0.0 109.4 jit_solution(7301431174141482287)
XLA Ops:
  0.6 0.7 copy-done
  1.3 2.1 %begin.1 = (f32[3,2,32,128]{3,2,1,0:T(8,128)S(1)}, f32[3,2,32,128]{3,2,1,0:T(8,128)S(1)}, f32[2,2,32,128]{3,2,1,0:T(8,128)S(1)}, f32[8,2,32,128]{3,2,1,0:T(8,128...) custom-call(s32[1,2,1,5]{3,2,1,0:T(1,128)S(1)} %bitcast.33, ...), custom_call_target="tpu_custom_call" | custom-call | tf_op jit(solution)/shard_map/begin/pallas_call | solution.py:243
  3.4 3.1 %collective-permute-start.3 = (f32[3,2,32,128]{3,2,1,0:T(8,128)S(1)}, f32[3,2,32,128]{3,2,1,0:T(8,128)S(1)}, u32[]{:S(2)}, u32[]{:S(2)}) collective-permute-start(f32[3,2,32,128]{3,2,1,0:T(8,128)S(1)} %get-tuple-element.45), channel_id=1, source_target_pairs={{0,4},{1,5},{2,6},{3,7},{4,0},{5,1},{6,2},{7,3},{8,12},{9,13},{10,... | collective-permute-start | bytes 294920 | tf_op jit(solution)/shard_map/ppermute | solution.py:67
  6.5 2.5 %collective-permute-start.5 = (f32[2,32,128]{2,1,0:T(8,128)S(1)}, f32[2,32,128]{2,1,0:T(8,128)S(1)}, u32[]{:S(2)}, u32[]{:S(2)}) collective-permute-start(f32[2,32,128]{2,1,0:T(8,128)S(1)} %slice_bitcast_fusion.1), channel_id=1, source_target_pairs={{0,12},{1,13},{2,14},{3,15},{4,8},{5,9},{6,10},{7,11},{8,4},{9,5},... | collective-permute-start | bytes 98312 | tf_op jit(solution)/shard_map/ppermute | solution.py:67
  9.0 1.5 %collective-permute-start = (f32[4,32,128]{2,1,0:T(8,128)S(1)}, f32[4,32,128]{2,1,0:T(8,128)S(1)}, u32[]{:S(2)}, u32[]{:S(2)}) collective-permute-start(f32[4,32,128]{2,1,0:T(8,128)S(1)} %get-tuple-element.41), channel_id=1, source_target_pairs={{0,2},{1,3},{2,0},{3,1},{4,6},{5,7},{6,4},{7,5},{8,10},{9,11},{10,... | collective-permute-start | bytes 196616 | tf_op jit(solution)/shard_map/ppermute | solution.py:67
  10.5 0.1 collective-permute-start.1
  10.6 2.8 %collective-permute-start.4 = (f32[3,2,32,128]{3,2,1,0:T(8,128)S(1)}, f32[3,2,32,128]{3,2,1,0:T(8,128)S(1)}, u32[]{:S(2)}, u32[]{:S(2)}) collective-permute-start(f32[3,2,32,128]{3,2,1,0:T(8,128)S(1)} %get-tuple-element.44), channel_id=1, source_target_pairs={{0,8},{1,9},{2,10},{3,11},{4,12},{5,13},{6,14},{7,15},{8,0},{9,1},... | collective-permute-start | bytes 294920 | tf_op jit(solution)/shard_map/ppermute | solution.py:67
  13.4 0.2 collective-permute-start.2
  13.6 8.2 %collective-permute-done.4 = f32[3,2,32,128]{3,2,1,0:T(8,128)S(1)} collective-permute-done((f32[3,2,32,128]{3,2,1,0:T(8,128)S(1)}, f32[3,2,32,128]{3,2,1,0:T(8,128)S(1)}, u32[]{:S(2)}, u32[]{:S(2)}) %collective-permute-start.4) | collective-permute-done | bytes 98336 | tf_op jit(solution)/shard_map/ppermute | solution.py:67
  21.8 0.6 collective-permute-start.6
  22.4 0.5 collective-permute-done.2
  23.1 1.3 %collective-permute-start.12 = (f32[13,2,32,128]{3,2,1,0:T(8,128)S(1)}, f32[13,2,32,128]{3,2,1,0:T(8,128)S(1)}, u32[]{:S(2)}, u32[]{:S(2)}) collective-permute-start(f32[13,2,32,128]{3,2,1,0:T(8,128)S(1)} %get-tuple-element.81), channel_id=1, source_target_pairs={{0,2},{1,17},{2,0},{3,19},{4,6},{5,21},{6,4},{7,23},{8,10},{9,25},... | collective-permute-start | bytes 1277960 | tf_op jit(solution)/shard_map/ppermute | solution.py:67
  24.5 3.8 %collective-permute-done.6 = f32[2,4,2,32,128]{4,3,2,1,0:T(8,128)S(1)} collective-permute-done((f32[2,4,2,32,128]{4,3,2,1,0:T(8,128)S(1)}, f32[2,4,2,32,128]{4,3,2,1,0:T(8,128)S(1)}, u32[]{:S(2)}, u32[]{:S(2)}) %collective-permute-start.6) | collective-permute-done | bytes 262176 | tf_op jit(solution)/shard_map/ppermute | solution.py:67
  28.3 1.6 %collective-permute-start.7 = (f32[4,4,2,32,128]{4,3,2,1,0:T(8,128)S(1)}, f32[4,4,2,32,128]{4,3,2,1,0:T(8,128)S(1)}, u32[]{:S(2)}, u32[]{:S(2)}) collective-permute-start(f32[4,4,2,32,128]{4,3,2,1,0:T(8,128)S(1)} %pad_maximum_fusion.3.four), channel_id=1, source_target_pairs={{0,16},{1,3},{2,18},{3,1},{4,20},{5,7},{6,22},{7,5},{8,24},{9,11},... | collective-permute-start | bytes 1572872 | tf_op jit(solution)/shard_map/ppermute | solution.py:67
  30.0 2.5 %collective-permute-start.8 = (f32[4,4,32,128]{3,2,1,0:T(8,128)S(1)}, f32[4,4,32,128]{3,2,1,0:T(8,128)S(1)}, u32[]{:S(2)}, u32[]{:S(2)}) collective-permute-start(f32[4,4,32,128]{3,2,1,0:T(8,128)S(1)} %pad_maximum_fusion.5.near_ref), channel_id=1, source_target_pairs={{0,4},{1,5},{2,6},{3,7},{4,0},{5,1},{6,2},{7,3},{8,12},{9,13},{10,... | collective-permute-start | bytes 786440 | tf_op jit(solution)/shard_map/ppermute | solution.py:67
  32.5 10.2 %collective-permute-done.9 = f32[9,2,32,128]{3,2,1,0:T(8,128)S(1)} collective-permute-done((f32[9,2,32,128]{3,2,1,0:T(8,128)S(1)}, f32[9,2,32,128]{3,2,1,0:T(8,128)S(1)}, u32[]{:S(2)}, u32[]{:S(2)}) %collective-permute-start.9) | collective-permute-done | bytes 294944 | tf_op jit(solution)/shard_map/ppermute | solution.py:67
  42.7 0.8 collective-permute-start.11
  43.6 1.6 %collective-permute-start.15 = (f32[2,13,2,32,128]{4,3,2,1,0:T(8,128)S(1)}, f32[2,13,2,32,128]{4,3,2,1,0:T(8,128)S(1)}, u32[]{:S(2)}, u32[]{:S(2)}) collective-permute-start(f32[2,13,2,32,128]{4,3,2,1,0:T(8,128)S(1)} %pad_maximum_fusion.n0), channel_id=1, source_target_pairs={{0,16},{1,3},{2,18},{3,1},{4,20},{5,7},{6,22},{7,5},{8,24},{9,11},... | collective-permute-start | bytes 2555912 | tf_op jit(solution)/shard_map/ppermute | solution.py:67
  45.2 0.2 stand.1
  45.4 1.6 %link_0.1 = (f32[128,256]{1,0:T(8,128)S(1)}, f32[128,128]{1,0:T(8,128)S(1)}) custom-call(f32[128,256]{1,0:T(8,128)S(1)} %get-tuple-element.63.b_ref, f32[4,4,2,32,128]{4,3,2,1,0:T(8,128)S(1)} %pad_maximum_fusion.3.four, f32[4,4,2,32,128]{4,3,2,1,0:T(8,128)S(1)} %collective-permute-done.7.third), custom_call_target="tpu_custom_call" | custom-call | tf_op jit(solution)/shard_map/link_0/pallas_call | solution.py:165
  47.1 5.0 %collective-permute-done.13.got = f32[128,256]{1,0:T(8,128)S(1)} collective-permute-done((f32[128,256]{1,0:T(8,128)S(1)}, f32[128,256]{1,0:T(8,128)S(1)}, u32[]{:S(2)}, u32[]{:S(2)}) %collective-permute-start.13) | collective-permute-done | bytes 131104 | tf_op jit(solution)/shard_map/ppermute | solution.py:67
  52.1 0.1 collective-permute-done.11
  52.2 2.0 %collective-permute-start.16 = (f32[2,9,2,32,128]{4,3,2,1,0:T(8,128)S(1)}, f32[2,9,2,32,128]{4,3,2,1,0:T(8,128)S(1)}, u32[]{:S(2)}, u32[]{:S(2)}) collective-permute-start(f32[2,9,2,32,128]{4,3,2,1,0:T(8,128)S(1)} %pad_maximum_fusion.2.f0), channel_id=1, source_target_pairs={{0,16},{1,3},{2,18},{3,1},{4,20},{5,7},{6,22},{7,5},{8,24},{9,11},... | collective-permute-start | bytes 1769480 | tf_op jit(solution)/shard_map/ppermute | solution.py:67
  54.3 6.6 %collective-permute-done.10 = f32[4,2,32,128]{3,2,1,0:T(8,128)S(1)} collective-permute-done((f32[4,2,32,128]{3,2,1,0:T(8,128)S(1)}, f32[4,2,32,128]{3,2,1,0:T(8,128)S(1)}, u32[]{:S(2)}, u32[]{:S(2)}) %collective-permute-start.10) | collective-permute-done | bytes 131104 | tf_op jit(solution)/shard_map/ppermute | solution.py:67
  60.9 1.1 collective-permute-start.14
  62.0 4.3 %collective-permute-done.14 = f32[4,2,32,128]{3,2,1,0:T(8,128)S(1)} collective-permute-done((f32[4,2,32,128]{3,2,1,0:T(8,128)S(1)}, f32[4,2,32,128]{3,2,1,0:T(8,128)S(1)}, u32[]{:S(2)}, u32[]{:S(2)}) %collective-permute-start.14) | collective-permute-done | bytes 131104 | tf_op jit(solution)/shard_map/ppermute | solution.py:67
  66.4 2.3 %link_1.1 = (f32[128,256]{1,0:T(8,128)S(1)}, f32[128,128]{1,0:T(8,128)S(1)}) custom-call(f32[128,256]{1,0:T(8,128)S(1)} %get-tuple-element.67.b_ref, f32[128,256]{1,0:T(8,128)S(1)} %get-tuple-element.64.own, f32[128,256]{1,0:T(8,128)S(1)} %collective-permute-done.13.got, f32[128,128]{1,0:T(8,128)S(1)} %get-tuple-element.68.y0_ref, ...), custom_call_target="tpu_custom_call" | custom-call | tf_op jit(solution)/shard_map/link_1/pallas_call | solution.py:165
  68.9 0.8 collective-permute-start.20
  69.7 1.8 %collective-permute-start.18 = (f32[128,256]{1,0:T(8,128)S(1)}, f32[128,256]{1,0:T(8,128)S(1)}, u32[]{:S(2)}, u32[]{:S(2)}) collective-permute-start(f32[128,256]{1,0:T(8,128)S(1)} %get-tuple-element.69.s0), channel_id=1, source_target_pairs={{0,4},{1,5},{2,6},{3,7},{4,0},{5,1},{6,2},{7,3},{8,12},{9,13},{10,... | collective-permute-start | bytes 393224 | tf_op jit(solution)/shard_map/ppermute | solution.py:67
  71.5 3.8 %collective-permute-done.20.f1 = f32[2,4,2,32,128]{4,3,2,1,0:T(8,128)S(1)} collective-permute-done((f32[2,4,2,32,128]{4,3,2,1,0:T(8,128)S(1)}, f32[2,4,2,32,128]{4,3,2,1,0:T(8,128)S(1)}, u32[]{:S(2)}, u32[]{:S(2)}) %collective-permute-start.20) | collective-permute-done | bytes 262176 | tf_op jit(solution)/shard_map/ppermute | solution.py:67
  75.3 3.0 %collective-permute-done.18.s2 = f32[128,256]{1,0:T(8,128)S(1)} collective-permute-done((f32[128,256]{1,0:T(8,128)S(1)}, f32[128,256]{1,0:T(8,128)S(1)}, u32[]{:S(2)}, u32[]{:S(2)}) %collective-permute-start.18) | collective-permute-done | bytes 131104 | tf_op jit(solution)/shard_map/ppermute | solution.py:67
  78.3 3.3 %link_2.1 = (f32[128,256]{1,0:T(8,128)S(1)}, f32[128,128]{1,0:T(8,128)S(1)}) custom-call(f32[128,256]{1,0:T(8,128)S(1)} %get-tuple-element.57.b_ref, f32[128,256]{1,0:T(8,128)S(1)} %get-tuple-element.69.s0, f32[128,256]{1,0:T(8,128)S(1)} %collective-permute-done.17.s1, f32[128,256]{1,0:T(8,128)S(1)} %collective-permute-done.18.s2, ...), custom_call_target="tpu_custom_call" | custom-call | tf_op jit(solution)/shard_map/link_2/pallas_call | solution.py:165
  81.7 1.4 %collective-permute-start.23 = (f32[128,256]{1,0:T(8,128)S(1)}, f32[128,256]{1,0:T(8,128)S(1)}, u32[]{:S(2)}, u32[]{:S(2)}) collective-permute-start(f32[128,256]{1,0:T(8,128)S(1)} %get-tuple-element.72.s0), channel_id=1, source_target_pairs={{0,4},{1,5},{2,6},{3,7},{4,0},{5,1},{6,2},{7,3},{8,12},{9,13},{10,... | collective-permute-start | bytes 393224 | tf_op jit(solution)/shard_map/ppermute | solution.py:67
  83.0 0.5 collective-permute-start.22
  83.5 3.9 %collective-permute-done.24.s3 = f32[128,256]{1,0:T(8,128)S(1)} collective-permute-done((f32[128,256]{1,0:T(8,128)S(1)}, f32[128,256]{1,0:T(8,128)S(1)}, u32[]{:S(2)}, u32[]{:S(2)}) %collective-permute-start.24) | collective-permute-done | bytes 131104 | tf_op jit(solution)/shard_map/ppermute | solution.py:67
  87.5 2.6 %collective-permute-done.23.s2 = f32[128,256]{1,0:T(8,128)S(1)} collective-permute-done((f32[128,256]{1,0:T(8,128)S(1)}, f32[128,256]{1,0:T(8,128)S(1)}, u32[]{:S(2)}, u32[]{:S(2)}) %collective-permute-start.23) | collective-permute-done | bytes 131104 | tf_op jit(solution)/shard_map/ppermute | solution.py:67
  90.1 1.1 link_3.1
  91.2 0.7 collective-permute-start.25
  92.0 2.3 %collective-permute-start.27 = (f32[4,32,128]{2,1,0:T(8,128)S(1)}, f32[4,32,128]{2,1,0:T(8,128)S(1)}, u32[]{:S(2)}, u32[]{:S(2)}) collective-permute-start(f32[4,32,128]{2,1,0:T(8,128)S(1)} %get-tuple-element.76), channel_id=1, source_target_pairs={{0,8},{1,25},{2,10},{3,27},{4,12},{5,29},{6,14},{7,31},{8,0},{9,17... | collective-permute-start | bytes 196616 | tf_op jit(solution)/shard_map/ppermute | solution.py:67
  94.2 2.1 %collective-permute-start.28 = (f32[4,32,128]{2,1,0:T(8,128)S(1)}, f32[4,32,128]{2,1,0:T(8,128)S(1)}, u32[]{:S(2)}, u32[]{:S(2)}) collective-permute-start(f32[4,32,128]{2,1,0:T(8,128)S(1)} %get-tuple-element.77), channel_id=1, source_target_pairs={{0,10},{1,27},{2,8},{3,25},{4,14},{5,31},{6,12},{7,29},{8,2},{9,19... | collective-permute-start | bytes 196616 | tf_op jit(solution)/shard_map/ppermute | solution.py:67
  96.3 0.8 collective-permute-done.27
  97.2 4.7 %collective-permute-done.28 = f32[4,32,128]{2,1,0:T(8,128)S(1)} collective-permute-done((f32[4,32,128]{2,1,0:T(8,128)S(1)}, f32[4,32,128]{2,1,0:T(8,128)S(1)}, u32[]{:S(2)}, u32[]{:S(2)}) %collective-permute-start.28) | collective-permute-done | bytes 65568 | tf_op jit(solution)/shard_map/ppermute | solution.py:67
  101.9 1.2 %collective-permute-start.30 = (f32[4,2,32,128]{3,2,1,0:T(8,128)S(1)}, f32[4,2,32,128]{3,2,1,0:T(8,128)S(1)}, u32[]{:S(2)}, u32[]{:S(2)}) collective-permute-start(f32[4,2,32,128]{3,2,1,0:T(8,128)S(1)} %get-tuple-element.78.near_ref), channel_id=1, source_target_pairs={{0,1},{1,0},{2,3},{3,2},{4,5},{5,4},{6,7},{7,6},{8,9},{9,8},{10,11... | collective-permute-start | bytes 393224 | tf_op jit(solution)/shard_map/ppermute | solution.py:67
  103.1 0.8 collective-permute-start.29
  103.9 0.2 collective-permute-done.30.other_ref
  104.1 0.9 join_root.1
  104.9 3.6 %collective-permute-done.29.other_ref = f32[4,2,32,128]{3,2,1,0:T(8,128)S(1)} collective-permute-done((f32[4,2,32,128]{3,2,1,0:T(8,128)S(1)}, f32[4,2,32,128]{3,2,1,0:T(8,128)S(1)}, u32[]{:S(2)}, u32[]{:S(2)}) %collective-permute-start.29) | collective-permute-done | bytes 131104 | tf_op jit(solution)/shard_map/ppermute | solution.py:67
  108.6 0.9 join_leaf.1
  (54 shorter events, 1.0 us)
Async XLA Ops:
  0.6 0.7 copy-start
  3.4 10.0 %collective-permute-start.3 = (f32[3,2,32,128]{3,2,1,0:T(8,128)S(1)}, f32[3,2,32,128]{3,2,1,0:T(8,128)S(1)}, u32[]{:S(2)}, u32[]{:S(2)}) collective-permute-start(f32[3,2,32,128]{3,2,1,0:T(8,128)S(1)} %get-tuple-element.45), channel_id=1, source_target_pairs={{0,4},{1,5},{2,6},{3,7},{4,0},{5,1},{6,2},{7,3},{8,12},{9,13},{10,... | collective-permute-start | bytes 294920 | tf_op jit(solution)/shard_map/ppermute | solution.py:67
  6.5 15.3 %collective-permute-start.5 = (f32[2,32,128]{2,1,0:T(8,128)S(1)}, f32[2,32,128]{2,1,0:T(8,128)S(1)}, u32[]{:S(2)}, u32[]{:S(2)}) collective-permute-start(f32[2,32,128]{2,1,0:T(8,128)S(1)} %slice_bitcast_fusion.1), channel_id=1, source_target_pairs={{0,12},{1,13},{2,14},{3,15},{4,8},{5,9},{6,10},{7,11},{8,4},{9,5},... | collective-permute-start | bytes 98312 | tf_op jit(solution)/shard_map/ppermute | solution.py:67
  9.0 13.4 %collective-permute-start = (f32[4,32,128]{2,1,0:T(8,128)S(1)}, f32[4,32,128]{2,1,0:T(8,128)S(1)}, u32[]{:S(2)}, u32[]{:S(2)}) collective-permute-start(f32[4,32,128]{2,1,0:T(8,128)S(1)} %get-tuple-element.41), channel_id=1, source_target_pairs={{0,2},{1,3},{2,0},{3,1},{4,6},{5,7},{6,4},{7,5},{8,10},{9,11},{10,... | collective-permute-start | bytes 196616 | tf_op jit(solution)/shard_map/ppermute | solution.py:67
  10.5 12.0 %collective-permute-start.1 = (f32[4,32,128]{2,1,0:T(8,128)S(1)}, f32[4,32,128]{2,1,0:T(8,128)S(1)}, u32[]{:S(2)}, u32[]{:S(2)}) collective-permute-start(f32[4,32,128]{2,1,0:T(8,128)S(1)} %get-tuple-element.42), channel_id=1, source_target_pairs={{0,8},{1,9},{2,10},{3,11},{4,12},{5,13},{6,14},{7,15},{8,0},{9,1},... | collective-permute-start | bytes 196616 | tf_op jit(solution)/shard_map/ppermute | solution.py:67
  10.6 11.2 %collective-permute-start.4 = (f32[3,2,32,128]{3,2,1,0:T(8,128)S(1)}, f32[3,2,32,128]{3,2,1,0:T(8,128)S(1)}, u32[]{:S(2)}, u32[]{:S(2)}) collective-permute-start(f32[3,2,32,128]{3,2,1,0:T(8,128)S(1)} %get-tuple-element.44), channel_id=1, source_target_pairs={{0,8},{1,9},{2,10},{3,11},{4,12},{5,13},{6,14},{7,15},{8,0},{9,1},... | collective-permute-start | bytes 294920 | tf_op jit(solution)/shard_map/ppermute | solution.py:67
  13.4 9.6 %collective-permute-start.2 = (f32[4,32,128]{2,1,0:T(8,128)S(1)}, f32[4,32,128]{2,1,0:T(8,128)S(1)}, u32[]{:S(2)}, u32[]{:S(2)}) collective-permute-start(f32[4,32,128]{2,1,0:T(8,128)S(1)} %get-tuple-element.43), channel_id=1, source_target_pairs={{0,10},{1,11},{2,8},{3,9},{4,14},{5,15},{6,12},{7,13},{8,2},{9,3},... | collective-permute-start | bytes 196616 | tf_op jit(solution)/shard_map/ppermute | solution.py:67
  21.8 6.4 %collective-permute-start.6 = (f32[2,4,2,32,128]{4,3,2,1,0:T(8,128)S(1)}, f32[2,4,2,32,128]{4,3,2,1,0:T(8,128)S(1)}, u32[]{:S(2)}, u32[]{:S(2)}) collective-permute-start(f32[2,4,2,32,128]{4,3,2,1,0:T(8,128)S(1)} %pad_maximum_fusion.4), channel_id=1, source_target_pairs={{0,2},{1,17},{2,0},{3,19},{4,6},{5,21},{6,4},{7,23},{8,10},{9,25},... | collective-permute-start | bytes 786440 | tf_op jit(solution)/shard_map/ppermute | solution.py:67
  23.1 20.4 %collective-permute-start.12 = (f32[13,2,32,128]{3,2,1,0:T(8,128)S(1)}, f32[13,2,32,128]{3,2,1,0:T(8,128)S(1)}, u32[]{:S(2)}, u32[]{:S(2)}) collective-permute-start(f32[13,2,32,128]{3,2,1,0:T(8,128)S(1)} %get-tuple-element.81), channel_id=1, source_target_pairs={{0,2},{1,17},{2,0},{3,19},{4,6},{5,21},{6,4},{7,23},{8,10},{9,25},... | collective-permute-start | bytes 1277960 | tf_op jit(solution)/shard_map/ppermute | solution.py:67
  28.3 14.4 %collective-permute-start.7 = (f32[4,4,2,32,128]{4,3,2,1,0:T(8,128)S(1)}, f32[4,4,2,32,128]{4,3,2,1,0:T(8,128)S(1)}, u32[]{:S(2)}, u32[]{:S(2)}) collective-permute-start(f32[4,4,2,32,128]{4,3,2,1,0:T(8,128)S(1)} %pad_maximum_fusion.3.four), channel_id=1, source_target_pairs={{0,16},{1,3},{2,18},{3,1},{4,20},{5,7},{6,22},{7,5},{8,24},{9,11},... | collective-permute-start | bytes 1572872 | tf_op jit(solution)/shard_map/ppermute | solution.py:67
  29.9 12.8 %collective-permute-start.9 = (f32[9,2,32,128]{3,2,1,0:T(8,128)S(1)}, f32[9,2,32,128]{3,2,1,0:T(8,128)S(1)}, u32[]{:S(2)}, u32[]{:S(2)}) collective-permute-start(f32[9,2,32,128]{3,2,1,0:T(8,128)S(1)} %constant_dynamic-update-slice_fusion.6), channel_id=1, source_target_pairs={{0,8},{1,9},{2,10},{3,11},{4,12},{5,13},{6,14},{7,15},{8,0},{9,1},... | collective-permute-start | bytes 884744 | tf_op jit(solution)/shard_map/ppermute | solution.py:67
  30.0 15.2 %collective-permute-start.8 = (f32[4,4,32,128]{3,2,1,0:T(8,128)S(1)}, f32[4,4,32,128]{3,2,1,0:T(8,128)S(1)}, u32[]{:S(2)}, u32[]{:S(2)}) collective-permute-start(f32[4,4,32,128]{3,2,1,0:T(8,128)S(1)} %pad_maximum_fusion.5.near_ref), channel_id=1, source_target_pairs={{0,4},{1,5},{2,6},{3,7},{4,0},{5,1},{6,2},{7,3},{8,12},{9,13},{10,... | collective-permute-start | bytes 786440 | tf_op jit(solution)/shard_map/ppermute | solution.py:67
  42.7 9.4 %collective-permute-start.11 = (f32[9,2,32,128]{3,2,1,0:T(8,128)S(1)}, f32[9,2,32,128]{3,2,1,0:T(8,128)S(1)}, u32[]{:S(2)}, u32[]{:S(2)}) collective-permute-start(f32[9,2,32,128]{3,2,1,0:T(8,128)S(1)} %collective-permute-done.9), channel_id=1, source_target_pairs={{0,2},{1,17},{2,0},{3,19},{4,6},{5,21},{6,4},{7,23},{8,10},{9,25},... | collective-permute-start | bytes 884744 | tf_op jit(solution)/shard_map/ppermute | solution.py:67
  43.6 22.7 %collective-permute-start.15 = (f32[2,13,2,32,128]{4,3,2,1,0:T(8,128)S(1)}, f32[2,13,2,32,128]{4,3,2,1,0:T(8,128)S(1)}, u32[]{:S(2)}, u32[]{:S(2)}) collective-permute-start(f32[2,13,2,32,128]{4,3,2,1,0:T(8,128)S(1)} %pad_maximum_fusion.n0), channel_id=1, source_target_pairs={{0,16},{1,3},{2,18},{3,1},{4,20},{5,7},{6,22},{7,5},{8,24},{9,11},... | collective-permute-start | bytes 2555912 | tf_op jit(solution)/shard_map/ppermute | solution.py:67
  47.1 5.0 %collective-permute-start.13 = (f32[128,256]{1,0:T(8,128)S(1)}, f32[128,256]{1,0:T(8,128)S(1)}, u32[]{:S(2)}, u32[]{:S(2)}) collective-permute-start(f32[128,256]{1,0:T(8,128)S(1)} %get-tuple-element.64.own), channel_id=1, source_target_pairs={{0,4},{1,5},{2,6},{3,7},{4,0},{5,1},{6,2},{7,3},{8,12},{9,13},{10,... | collective-permute-start | bytes 393224 | tf_op jit(solution)/shard_map/ppermute | solution.py:67
  52.2 14.1 %collective-permute-start.16 = (f32[2,9,2,32,128]{4,3,2,1,0:T(8,128)S(1)}, f32[2,9,2,32,128]{4,3,2,1,0:T(8,128)S(1)}, u32[]{:S(2)}, u32[]{:S(2)}) collective-permute-start(f32[2,9,2,32,128]{4,3,2,1,0:T(8,128)S(1)} %pad_maximum_fusion.2.f0), channel_id=1, source_target_pairs={{0,16},{1,3},{2,18},{3,1},{4,20},{5,7},{6,22},{7,5},{8,24},{9,11},... | collective-permute-start | bytes 1769480 | tf_op jit(solution)/shard_map/ppermute | solution.py:67
  54.3 6.6 %collective-permute-start.10 = (f32[4,2,32,128]{3,2,1,0:T(8,128)S(1)}, f32[4,2,32,128]{3,2,1,0:T(8,128)S(1)}, u32[]{:S(2)}, u32[]{:S(2)}) collective-permute-start(f32[4,2,32,128]{3,2,1,0:T(8,128)S(1)} %get-tuple-element.60), channel_id=1, source_target_pairs={{0,8},{1,9},{2,10},{3,11},{4,12},{5,13},{6,14},{7,15},{8,0},{9,1},... | collective-permute-start | bytes 393224 | tf_op jit(solution)/shard_map/ppermute | solution.py:67
  60.9 5.5 %collective-permute-start.14 = (f32[4,2,32,128]{3,2,1,0:T(8,128)S(1)}, f32[4,2,32,128]{3,2,1,0:T(8,128)S(1)}, u32[]{:S(2)}, u32[]{:S(2)}) collective-permute-start(f32[4,2,32,128]{3,2,1,0:T(8,128)S(1)} %collective-permute-done.10), channel_id=1, source_target_pairs={{0,2},{1,17},{2,0},{3,19},{4,6},{5,21},{6,4},{7,23},{8,10},{9,25},... | collective-permute-start | bytes 393224 | tf_op jit(solution)/shard_map/ppermute | solution.py:67
  68.8 9.5 %collective-permute-start.21 = (f32[8,3,2,32,128]{4,3,2,1,0:T(8,128)S(1)}, f32[8,3,2,32,128]{4,3,2,1,0:T(8,128)S(1)}, u32[]{:S(2)}, u32[]{:S(2)}) collective-permute-start(f32[8,3,2,32,128]{4,3,2,1,0:T(8,128)S(1)} %pad_maximum_fusion.1.root), channel_id=1, source_target_pairs={{0,1},{1,0},{2,3},{3,2},{4,5},{5,4},{6,7},{7,6},{8,9},{9,8},{10,11... | collective-permute-start | bytes 2359304 | tf_op jit(solution)/shard_map/ppermute | solution.py:67
  68.9 6.4 %collective-permute-start.20 = (f32[2,4,2,32,128]{4,3,2,1,0:T(8,128)S(1)}, f32[2,4,2,32,128]{4,3,2,1,0:T(8,128)S(1)}, u32[]{:S(2)}, u32[]{:S(2)}) collective-permute-start(f32[2,4,2,32,128]{4,3,2,1,0:T(8,128)S(1)} %pad_maximum_fusion.6.f0), channel_id=1, source_target_pairs={{0,16},{1,3},{2,18},{3,1},{4,20},{5,7},{6,22},{7,5},{8,24},{9,11},... | collective-permute-start | bytes 786440 | tf_op jit(solution)/shard_map/ppermute | solution.py:67
  69.7 5.6 %collective-permute-start.19 = (f32[128,256]{1,0:T(8,128)S(1)}, f32[128,256]{1,0:T(8,128)S(1)}, u32[]{:S(2)}, u32[]{:S(2)}) collective-permute-start(f32[128,256]{1,0:T(8,128)S(1)} %get-tuple-element.69.s0), channel_id=1, source_target_pairs={{0,5},{1,4},{2,7},{3,6},{4,1},{5,0},{6,3},{7,2},{8,13},{9,12},{10,... | collective-permute-start | bytes 393224 | tf_op jit(solution)/shard_map/ppermute | solution.py:67
  69.7 8.6 %collective-permute-start.18 = (f32[128,256]{1,0:T(8,128)S(1)}, f32[128,256]{1,0:T(8,128)S(1)}, u32[]{:S(2)}, u32[]{:S(2)}) collective-permute-start(f32[128,256]{1,0:T(8,128)S(1)} %get-tuple-element.69.s0), channel_id=1, source_target_pairs={{0,4},{1,5},{2,6},{3,7},{4,0},{5,1},{6,2},{7,3},{8,12},{9,13},{10,... | collective-permute-start | bytes 393224 | tf_op jit(solution)/shard_map/ppermute | solution.py:67
  71.5 6.8 %collective-permute-start.17 = (f32[128,256]{1,0:T(8,128)S(1)}, f32[128,256]{1,0:T(8,128)S(1)}, u32[]{:S(2)}, u32[]{:S(2)}) collective-permute-start(f32[128,256]{1,0:T(8,128)S(1)} %get-tuple-element.69.s0), channel_id=1, source_target_pairs={{0,1},{1,0},{2,3},{3,2},{4,5},{5,4},{6,7},{7,6},{8,9},{9,8},{10,11... | collective-permute-start | bytes 393224 | tf_op jit(solution)/shard_map/ppermute | solution.py:67
  81.6 5.9 %collective-permute-start.24 = (f32[128,256]{1,0:T(8,128)S(1)}, f32[128,256]{1,0:T(8,128)S(1)}, u32[]{:S(2)}, u32[]{:S(2)}) collective-permute-start(f32[128,256]{1,0:T(8,128)S(1)} %get-tuple-element.72.s0), channel_id=1, source_target_pairs={{0,5},{1,4},{2,7},{3,6},{4,1},{5,0},{6,3},{7,2},{8,13},{9,12},{10,... | collective-permute-start | bytes 393224 | tf_op jit(solution)/shard_map/ppermute | solution.py:67
  81.7 8.4 %collective-permute-start.23 = (f32[128,256]{1,0:T(8,128)S(1)}, f32[128,256]{1,0:T(8,128)S(1)}, u32[]{:S(2)}, u32[]{:S(2)}) collective-permute-start(f32[128,256]{1,0:T(8,128)S(1)} %get-tuple-element.72.s0), channel_id=1, source_target_pairs={{0,4},{1,5},{2,6},{3,7},{4,0},{5,1},{6,2},{7,3},{8,12},{9,13},{10,... | collective-permute-start | bytes 393224 | tf_op jit(solution)/shard_map/ppermute | solution.py:67
  83.0 7.1 %collective-permute-start.22 = (f32[128,256]{1,0:T(8,128)S(1)}, f32[128,256]{1,0:T(8,128)S(1)}, u32[]{:S(2)}, u32[]{:S(2)}) collective-permute-start(f32[128,256]{1,0:T(8,128)S(1)} %get-tuple-element.72.s0), channel_id=1, source_target_pairs={{0,1},{1,0},{2,3},{3,2},{4,5},{5,4},{6,7},{7,6},{8,9},{9,8},{10,11... | collective-permute-start | bytes 393224 | tf_op jit(solution)/shard_map/ppermute | solution.py:67
  91.2 5.1 %collective-permute-start.25 = (f32[4,32,128]{2,1,0:T(8,128)S(1)}, f32[4,32,128]{2,1,0:T(8,128)S(1)}, u32[]{:S(2)}, u32[]{:S(2)}) collective-permute-start(f32[4,32,128]{2,1,0:T(8,128)S(1)} %get-tuple-element.74), channel_id=1, source_target_pairs={{0,0},{1,17},{2,2},{3,19},{4,4},{5,21},{6,6},{7,23},{8,8},{9,25},{... | collective-permute-start | bytes 196616 | tf_op jit(solution)/shard_map/ppermute | solution.py:67
  91.9 4.5 %collective-permute-start.26 = (f32[4,32,128]{2,1,0:T(8,128)S(1)}, f32[4,32,128]{2,1,0:T(8,128)S(1)}, u32[]{:S(2)}, u32[]{:S(2)}) collective-permute-start(f32[4,32,128]{2,1,0:T(8,128)S(1)} %get-tuple-element.75), channel_id=1, source_target_pairs={{0,2},{1,19},{2,0},{3,17},{4,6},{5,23},{6,4},{7,21},{8,10},{9,27},... | collective-permute-start | bytes 196616 | tf_op jit(solution)/shard_map/ppermute | solution.py:67
  92.0 5.2 %collective-permute-start.27 = (f32[4,32,128]{2,1,0:T(8,128)S(1)}, f32[4,32,128]{2,1,0:T(8,128)S(1)}, u32[]{:S(2)}, u32[]{:S(2)}) collective-permute-start(f32[4,32,128]{2,1,0:T(8,128)S(1)} %get-tuple-element.76), channel_id=1, source_target_pairs={{0,8},{1,25},{2,10},{3,27},{4,12},{5,29},{6,14},{7,31},{8,0},{9,17... | collective-permute-start | bytes 196616 | tf_op jit(solution)/shard_map/ppermute | solution.py:67
  94.2 7.6 %collective-permute-start.28 = (f32[4,32,128]{2,1,0:T(8,128)S(1)}, f32[4,32,128]{2,1,0:T(8,128)S(1)}, u32[]{:S(2)}, u32[]{:S(2)}) collective-permute-start(f32[4,32,128]{2,1,0:T(8,128)S(1)} %get-tuple-element.77), channel_id=1, source_target_pairs={{0,10},{1,27},{2,8},{3,25},{4,14},{5,31},{6,12},{7,29},{8,2},{9,19... | collective-permute-start | bytes 196616 | tf_op jit(solution)/shard_map/ppermute | solution.py:67
  101.9 2.2 %collective-permute-start.30 = (f32[4,2,32,128]{3,2,1,0:T(8,128)S(1)}, f32[4,2,32,128]{3,2,1,0:T(8,128)S(1)}, u32[]{:S(2)}, u32[]{:S(2)}) collective-permute-start(f32[4,2,32,128]{3,2,1,0:T(8,128)S(1)} %get-tuple-element.78.near_ref), channel_id=1, source_target_pairs={{0,1},{1,0},{2,3},{3,2},{4,5},{5,4},{6,7},{7,6},{8,9},{9,8},{10,11... | collective-permute-start | bytes 393224 | tf_op jit(solution)/shard_map/ppermute | solution.py:67
  103.1 5.5 %collective-permute-start.29 = (f32[4,2,32,128]{3,2,1,0:T(8,128)S(1)}, f32[4,2,32,128]{3,2,1,0:T(8,128)S(1)}, u32[]{:S(2)}, u32[]{:S(2)}) collective-permute-start(f32[4,2,32,128]{3,2,1,0:T(8,128)S(1)} %get-tuple-element.79.near_ref), channel_id=1, source_target_pairs={{0,16},{1,17},{2,18},{3,19},{4,20},{5,21},{6,22},{7,23},{8,24},{9,... | collective-permute-start | bytes 393224 | tf_op jit(solution)/shard_map/ppermute | solution.py:67

commit v7 on v6

--- a/solution.py
+++ b/solution.py
@@ -48,63 +48,62 @@
 
 
 def pairs(dest):
-    out = []
-    for r in range(2):
-        for zh in range(2):
-            for zl in range(2):
-                for x in range(2):
-                    for l in range(2):
-                        d = dest(r, zh, zl, x, l)
-                        if d is None:
-                            continue
-                        s = (r * 8 + zh * 4 + zl * 2 + x) * 2 + l
-                        e = (d[0] * 8 + d[1] * 4 + d[2] * 2 + d[3]) * 2 + d[4]
-                        out.append((s, e))
-    return out
+    def place(r, z, side, x, l):
+        return (r * 8 + side * 4 + z * 2 + x) * 2 + l
+
+    every = [
+        (r, z, side, x, l)
+        for r in range(2)
+        for z in range(2)
+        for side in range(2)
+        for x in range(2)
+        for l in range(2)
+    ]
+    return sorted((place(*d), place(*dest(*d))) for d in every)
 
 
 def send(value, dest):
     return lax.ppermute(value, AXES, pairs(dest))
 
 
-def to_far(r, zh, zl, x, l):
-    return r, zh ^ 1, zl, x, l
-
-
-def to_second(r, zh, zl, x, l):
-    return (r, zh, zl, x ^ 1, l) if l == 0 else (r ^ 1, zh, zl, x, l)
-
-
-def to_third(r, zh, zl, x, l):
-    return (r ^ 1, zh, zl, x, l) if l == 0 else (r, zh, zl, x ^ 1, l)
-
-
-def to_pair(r, zh, zl, x, l):
-    return r, zh, zl ^ 1, x, l
-
-
-def to_core(r, zh, zl, x, l):
-    return r, zh, zl, x, l ^ 1
-
-
-def to_pair_core(r, zh, zl, x, l):
-    return r, zh, zl ^ 1, x, l ^ 1
-
-
-def to_far_pair(r, zh, zl, x, l):
-    return r, zh ^ 1, zl ^ 1, x, l
-
-
-def to_row(r, zh, zl, x, l):
-    return r ^ 1, zh, zl, x, l
+def to_far(r, z, side, x, l):
+    return r, z ^ 1, side, x, l
+
+
+def to_second(r, z, side, x, l):
+    return (r, z, side, x ^ 1, l) if l == 0 else (r ^ 1, z, side, x, l)
+
+
+def to_third(r, z, side, x, l):
+    return (r ^ 1, z, side, x, l) if l == 0 else (r, z, side, x ^ 1, l)
+
+
+def to_pair(r, z, side, x, l):
+    return r, z, side ^ 1, x, l
+
+
+def to_core(r, z, side, x, l):
+    return r, z, side, x, l ^ 1
+
+
+def to_pair_core(r, z, side, x, l):
+    return r, z, side ^ 1, x, l ^ 1
+
+
+def to_far_pair(r, z, side, x, l):
+    return r, z ^ 1, side ^ 1, x, l
+
+
+def to_row(r, z, side, x, l):
+    return r ^ 1, z, side, x, l
 
 
 def to_group(b1, b2):
-    return lambda r, zh, zl, x, l: (r, zh ^ b1, zl, x ^ b2, l)
+    return lambda r, z, side, x, l: (r, z ^ b1, side, x ^ b2, l)
 
 
 def to_group_by_core(b1, b2):
-    return lambda r, zh, zl, x, l: (r ^ l, zh ^ b1, zl, x ^ b2, l)
+    return lambda r, z, side, x, l: (r ^ l, z ^ b1, side, x ^ b2, l)
 
 
 def after(value, *others):
@@ -153,7 +152,7 @@
 
 def spot():
     row, col, core = (lax.axis_index(name) for name in AXES)
-    return row, col // 4, (col // 2) % 2, col % 2, core
+    return row, (col // 2) % 2, col // 4, col % 2, core
 
 
 def call(name, kernel, outs, *operands, specs=None, scratch=()):
@@ -169,7 +168,6 @@
         out_specs=[vmem() for _ in outs],
         scratch_shapes=list(scratch),
         compiler_params=pltpu.CompilerParams(vmem_limit_bytes=VMEM_OF_A_KERNEL),
-
         name=name,
     )(*fixed)
 
@@ -187,16 +185,17 @@
 
 
 def part_rows(source, keep, out):
-    zl = spot()[2]
+    side = spot()[2]
+    mine = pl.multiple_of(side * 128, 128)
+    theirs = pl.multiple_of((1 - side) * 128, 128)
     for a in range(2):
-        even, odd = swap_lanes(source[a, :, :128], source[a, :, 128:])
-        keep[a] = jnp.where(zl == 0, even, odd)
-        out[a] = jnp.where(zl == 0, odd, even)
+        keep[a] = source[a, :, pl.ds(mine, 128)]
+        out[a] = source[a, :, pl.ds(theirs, 128)]
 
 
 def begin_kernel(tiles, *refs):
-    sources, outs, places = refs[:6], refs[6:15], refs[15:21]
-    cuts, sems = refs[21:]
+    sources, outs, places = refs[:6], refs[6:16], refs[16:22]
+    cuts, sems = refs[22:]
     copies = [
         pltpu.make_async_copy(source, place, sems.at[k])
         for k, (source, place) in enumerate(zip(sources, places))
@@ -204,7 +203,7 @@
     for copy in copies:
         copy.start()
     leaf_inv, blocks, leaf_rhs, root_rhs, root_inv, lower = places
-    away, first, rest, masked_out, lower_out = outs[:5]
+    away, first, rest_away, rest, masked_out, lower_out = outs[:6]
     core = spot()[4]
 
     def mask(m, dest, base):
@@ -215,20 +214,20 @@
                 dest[base + t, a] = blocks[0, m, a, :, lanes] * weight
 
     copies[0].wait()
-    part_rows(leaf_inv.at[0, 0], first.at[0], away.at[0])
+    part_rows(leaf_inv.at[0, 0], first.at[0], away)
     copies[1].wait()
     mask(0, first, 1)
     copies[2].wait()
     cut_columns(leaf_rhs.at[0], cuts, 0)
     copies[3].wait()
     cut_columns(root_rhs, cuts, 2)
-    _, zh, _, x, _ = spot()
+    _, z, _, x, _ = spot()
     for b1 in range(2):
         for b2 in range(2):
-            outs[5 + b1 * 2 + b2][...] = cuts[(zh ^ b1) * 2 + (x ^ b2)]
-    part_rows(leaf_inv.at[0, 1], rest.at[0], away.at[1])
+            outs[6 + b1 * 2 + b2][...] = cuts[(z ^ b1) * 2 + (x ^ b2)]
+    part_rows(leaf_inv.at[0, 1], rest.at[0], rest_away.at[0])
     copies[4].wait()
-    part_rows(root_inv.at[core], rest.at[1], away.at[2])
+    part_rows(root_inv.at[core], rest.at[1], rest_away.at[1])
     copies[5].wait()
     for a in range(2):
         start = pl.multiple_of(core * 128, 128)
@@ -239,7 +238,7 @@
 
 def begin(pattern, *arrays):
     tiles = pattern.transpose(0, 2, 3, 1)
-    outs = [(3, 2, 32, 128), (3, 2, 32, 128), (2, 2, 32, 128)] + [(8, 2, 32, 128), (1, 2, 32, 128)] + [(4, 32, 128)] * 4
+    outs = [(2, 32, 128), (3, 2, 32, 128), (2, 2, 32, 128), (2, 2, 32, 128)] + [(8, 2, 32, 128), (1, 2, 32, 128)] + [(4, 32, 128)] * 4
     return pl.pallas_call(
         begin_kernel,
         out_shape=[pltpu.VMEM(dims, F32) for dims in outs],
@@ -248,13 +247,12 @@
         scratch_shapes=[pltpu.VMEM(a.shape, F32) for a in arrays]
         + [pltpu.VMEM((4, 4, 32, 128), F32), pltpu.SemaphoreType.DMA((6,))],
         compiler_params=pltpu.CompilerParams(vmem_limit_bytes=VMEM_OF_A_KERNEL),
-
         name="begin",
     )(tiles, *(pltpu.with_memory_space_constraint(a, pltpu.HBM) for a in arrays))
 
 
 def fetch(pick, dest, sems, swapped=None, from_core=0):
-    r, zh, _, x, l = spot()
+    r, z, _, x, l = spot()
     copies = []
     for b3 in range(2):
         for b2 in range(2):
@@ -265,7 +263,7 @@
                     xx = x ^ jnp.where(core == 0, b2, b3)
                     return pltpu.make_async_copy(
                         source(b3, b2, b1),
-                        dest(rr, zh ^ b1, xx),
+                        dest(rr, z ^ b1, xx),
                         sems.at[b3 * 4 + b2 * 2 + b1],
                     )
 
@@ -304,10 +302,6 @@
     return jnp.concatenate(sums, axis=0)
 
 
-def sum_four(refs):
-    return (refs[0][...] + refs[2][...]) + (refs[1][...] + refs[3][...])
-
-
 def first_chunk_unit(four, third):
     return lambda unit: lambda b3, b2, b1: (four, third)[b3].at[b2 * 2 + b1, unit]
 
@@ -331,7 +325,7 @@
     for half in range(2):
         copies += fetch(
             unit(half),
-            lambda r, zh, x, half=half: inverse.at[r, :, zh, half, x],
+            lambda r, z, x, half=half: inverse.at[r, :, half, z, x],
             sems.at[half],
             swapped and swapped(half),
             from_core,
@@ -343,7 +337,7 @@
     copies = []
     for half in range(2):
         copies += fetch(
-            unit(half), lambda r, zh, x, half=half: held.at[t, r, half, :, zh, x], sems.at[half]
+            unit(half), lambda r, z, x, half=half: held.at[t, r, half, :, z, x], sems.at[half]
         )
     return copies
 
@@ -353,7 +347,7 @@
     for half in range(2):
         copies += fetch(
             root(2),
-            lambda r, zh, x, half=half: held.at[t, r, half, :, zh, x],
+            lambda r, z, x, half=half: held.at[t, r, half, :, z, x],
             sems.at[half],
             swapped(2),
             half,
@@ -386,7 +380,7 @@
     part_ref[...] = update(held, [y0_ref[...], solved], waits)
 
 
-def link_2_kernel(b_ref, s0, s1, s2, s3, y0_ref, y1_ref, n0, n1, f0, f1, root, swapped, *refs):
+def link_2_kernel(b_ref, s0, s1, y0_ref, y1_ref, n0, n1, f0, f1, root, swapped, *refs):
     part_ref, y_ref, inverse, held, sems = refs
     unit = chunk_unit((n0, n1), (f0, f1), 9, 0)
     root, swapped = root_unit(root), root_unit(swapped)
@@ -394,24 +388,24 @@
     copies = [fetch_block(shifted(unit, 2 * t), held, t, sems.at[t + 1]) for t in range(2)]
     copies.append(fetch_halves(root, swapped, held, 2, sems.at[3]))
     wait_all(first)
-    solved = solve(inverse, b_ref[...] - sum_four((s0, s1, s2, s3)))
+    solved = solve(inverse, b_ref[...] - (s0[...] + s1[...]))
     y_ref[...] = solved
     waits = [functools.partial(wait_all, c) for c in copies]
     last = jnp.where(spot()[4] == 0, solved, 0.0)
     part_ref[...] = update(held, [y0_ref[...], y1_ref[...], last], waits)
 
 
-def link_3_kernel(b_ref, s0, s1, s2, s3, y0_ref, y1_ref, y2_ref, root, swapped, *refs):
+def link_3_kernel(b_ref, s0, s1, y0_ref, y1_ref, y2_ref, root, swapped, *refs):
     outs, (pieces, inverse, sems) = refs[:4], refs[4:]
     first = fetch_inverse(root_unit(root), inverse, sems.at[0], root_unit(swapped), 1)
-    vector = b_ref[...] - sum_four((s0, s1, s2, s3))
+    vector = b_ref[...] - (s0[...] + s1[...])
     lay_values((y0_ref, y1_ref, y2_ref), pieces)
     wait_all(first)
     pieces[:, 3] = solve(inverse, vector).T.reshape(4, 32, 128)
-    _, zh, _, x, _ = spot()
+    _, z, _, x, _ = spot()
     for b1 in range(2):
         for b2 in range(2):
-            outs[b1 * 2 + b2][...] = pieces[(zh ^ b1) * 2 + (x ^ b2)]
+            outs[b1 * 2 + b2][...] = pieces[(z ^ b1) * 2 + (x ^ b2)]
 
 
 def link_scratch(nblocks, nsems):
@@ -421,28 +415,35 @@
     )
 
 
+def root_kernel(n0, n1, f0, f1, _, out):
+    for k, ref in enumerate((n0, n1, f0, f1)):
+        for b2 in range(2):
+            for unit in range(3):
+                out[2 * k + b2, unit] = ref[b2, 6 + unit]
+
+
 def lay_values(refs, held):
     for p, ref in enumerate(refs):
         held[:, p] = ref[...].T.reshape(4, 32, 128)
 
 
 def stand_kernel(near_ref, other_ref, *refs):
-    outs, held = refs[:4], refs[4]
-    _, zh, zl, x, _ = spot()
+    outs, held = refs[:2], refs[2]
+    _, z, side, x, _ = spot()
     for b1 in range(2):
         for b2 in range(2):
             for b, source in enumerate((near_ref, other_ref)):
-                held[((zh ^ b1) * 2 + (zl ^ b)) * 2 + (x ^ b2)] = source[b1 * 2 + b2]
+                held[((side ^ b) * 2 + (z ^ b1)) * 2 + (x ^ b2)] = source[b1 * 2 + b2]
     for p, out in enumerate(outs):
         out[...] = held[:, p].reshape(256, 128).T
 
 
 def join_kernel(near_ref, other_ref, out_ref, held):
-    r, zh, _, x, core = spot()
+    r, z, _, x, core = spot()
     near = r ^ core
     for b1 in range(2):
         for b2 in range(2):
-            place = (zh ^ b1) * 2 + (x ^ b2)
+            place = (z ^ b1) * 2 + (x ^ b2)
             held[near * 4 + place] = near_ref[b1 * 2 + b2]
             held[(near ^ 1) * 4 + place] = other_ref[b1 * 2 + b2]
     for p in range(2):
@@ -461,7 +462,6 @@
         out_specs=vmem(),
         scratch_shapes=[pltpu.VMEM((8, 2, 32, 128), F32)],
         compiler_params=pltpu.CompilerParams(vmem_limit_bytes=VMEM_OF_A_KERNEL),
-
         name=name,
     )(*(pltpu.with_memory_space_constraint(v, pltpu.VMEM) for v in (near, other)))
 
@@ -474,30 +474,32 @@
 
 
 def grouped(leaf_rhs, root_rhs, leaf_inverses, root_inverses, leaf_blocks, root_block, pattern):
-    zl = (lax.axis_index("col") // 2) % 2
+    side = lax.axis_index("col") // 4
+    standing = [pltpu.VMEM((8, 2, 32, 128), F32)]
 
     def whole(keep, got):
-        return jnp.stack([jnp.where(zl == 0, keep, got), jnp.where(zl == 0, got, keep)])
-
-    away, first, rest, blocks, lower, *cuts = begin(
-        pattern, leaf_inverses, leaf_blocks, leaf_rhs, root_rhs, root_inverses, root_block
-    )
-    pair = send(away, to_pair)
-    first_far = send(first, to_far)
-    first_far_pair = send(away[0], to_far_pair)
+        return jnp.stack([jnp.where(side == 0, keep, got), jnp.where(side == 0, got, keep)])
 
     def first_chunk(values, got):
         return jnp.concatenate([whole(values[0], got), values[1:]])
 
+    away, first, rest_away, rest, blocks, lower, *cuts = begin(
+        pattern, leaf_inverses, leaf_blocks, leaf_rhs, root_rhs, root_inverses, root_block
+    )
+    first_pair = send(away, to_pair)
+    first_far = send(first, to_far)
+    first_far_pair = send(away, to_far_pair)
+    rest_pair = send(rest_away, to_pair)
     moved = to_groups(cuts)
-    two_a = jnp.stack([first_chunk(first, pair[0]), first_chunk(first_far, first_far_pair)])
+
+    two_a = jnp.stack([first_chunk(first, first_pair), first_chunk(first_far, first_far_pair)])
     second_a = send(two_a, to_second)
     rhs_in = jnp.stack(after(moved, two_a))
-    rhs_pair = send(rhs_in, to_pair)
-
-    late = after(pair, rhs_in)
+    leaf_pair = send(rhs_in[:, :2], to_pair)
+
+    late = after(rest_pair, rhs_in)
     own_units = jnp.concatenate(
-        [whole(rest[0], late[1]), blocks[:4], whole(rest[1], late[2]), lower, blocks[4:]]
+        [whole(rest[0], late[0]), blocks[:4], whole(rest[1], late[1]), lower, blocks[4:]]
     )
     far_b = send(own_units[:9], to_far)
     second_own = send(own_units, to_second)
@@ -508,13 +510,13 @@
     far_b = after(far_b, third_a)
     second_b = send(far_b, to_second)
     far_c = send(after(own_units[9:], far_b), to_far)
-    b0, b1, r2, r3 = call(
-        "stand",
+    b0, b1 = call(
+        "stand_leaf",
         stand_kernel,
-        [(128, 256)] * 4,
-        after(rhs_in, third_a),
-        rhs_pair,
-        scratch=[pltpu.VMEM((8, 4, 32, 128), F32)],
+        [(128, 256)] * 2,
+        after(rhs_in[:, :2], third_a),
+        leaf_pair,
+        scratch=standing,
     )
 
     own, y0 = call(
@@ -531,6 +533,8 @@
     far_b_1 = send(far_b_0, to_third)
     far_c = after(far_c, far_b_0)
     second_c = send(far_c, to_second)
+    root_in = after(rhs_in[:, 2:], far_b_0)
+    root_pair = send(root_in, to_pair)
     far_c_0 = jnp.stack([far_c, second_c])
     far_c_1 = send(far_c_0, to_third)
 
@@ -548,18 +552,28 @@
         far_b_1,
         scratch=link_scratch(2, 3),
     )
-    sums = [own, send(own, to_core), send(own, to_pair), send(own, to_pair_core)]
-    root_own = jnp.concatenate(
-        [after(near_0[:, 6:9], own), near_1[:, 6:9], far_b_0[:, 6:9], far_b_1[:, 6:9]]
+    both = own + send(own, to_core)
+    got = send(both, to_pair)
+    (root_own,) = call(
+        "root_shards", root_kernel, [(8, 3, 2, 32, 128)], near_0, near_1, far_b_0, far_b_1, both
     )
     root_swapped = send(root_own, to_core)
+    r2, r3 = call(
+        "stand_root",
+        stand_kernel,
+        [(128, 256)] * 2,
+        after(root_in, both),
+        root_pair,
+        scratch=standing,
+    )
 
     own, y2 = call(
         "link_2",
         link_2_kernel,
         VECTOR,
         r2,
-        *sums,
+        both,
+        got,
         y0,
         y1,
         near_0,
@@ -570,13 +584,16 @@
         root_swapped,
         scratch=link_scratch(3, 4),
     )
-    sums = [own, send(own, to_core), send(own, to_pair), send(own, to_pair_core)]
+    both = own + send(own, to_core)
+    got = send(both, to_pair)
+
     parts = call(
         "link_3",
         link_3_kernel,
         [(4, 32, 128)] * 4,
         r3,
-        *sums,
+        both,
+        got,
         y0,
         y1,
         y2,

time: 110 us -> 115 us (1.045)
  waiting for transfers between devices: 61.4 us -> 65.8 us
  starting transfers between devices: 33.5 us -> 34.7 us
    ppermute x31, waiting for transfers between devices: 61.4 us -> 65.8 us  [send(): return lax.ppermute(value, AXES, pairs(dest))]
    ppermute x31, starting transfers between devices: 33.5 us -> 34.7 us  [send(): return lax.ppermute(value, AXES, pairs(dest))]
    pallas_call x5 -> x7, Pallas kernels: 8.59 us -> 8.68 us  [call(): pl.pallas_call(kernel, out_shape=[pltpu.VMEM(dims, F32) for dims in outs]...]
  transfers between devices with their start and end apart: 31 -> 31, of which waited for: 16 -> 19; matrix products, arithmetic and copies ran while one was open for 0% -> 0% of each run, Pallas kernels for 2% -> 2%
where the time goes in v7:
time: 115 us
  waiting for transfers between devices  65.8 us (57%)
  starting transfers between devices  34.7 us (30%)
  Pallas kernels  12.4 us (11%)
    ppermute x31, waiting for transfers between devices, send(): return lax.ppermute(value, AXES, pairs(dest))  65.8 us
    ppermute x31, starting transfers between devices, send(): return lax.ppermute(value, AXES, pairs(dest))  34.7 us
    pallas_call x7, Pallas kernels, call(): pl.pallas_call(kernel, out_shape=[pltpu.VMEM(dims, F32) for dims in outs]...  8.68 us
  transfers between devices with their start and end apart: 31, of which 19 were waited for; matrix products, arithmetic and copies ran while one was open for 0% of the time, Pallas kernels for 2%

profile of v7, /device:TPU:0, one launch (start us, length us, event | category | flops | bytes accessed | tf_op | source)
XLA Modules:
  0.0 114.9 jit_solution(12254675139194597465)
XLA Ops:
  0.6 0.7 copy-done
  1.3 2.0 %begin.1 = (f32[2,32,128]{2,1,0:T(8,128)S(1)}, f32[3,2,32,128]{3,2,1,0:T(8,128)S(1)}, f32[2,2,32,128]{3,2,1,0:T(8,128)S(1)}, f32[2,2,32,128]{3,2,1,0:T(8,128)S(1...) custom-call(s32[1,2,1,5]{3,2,1,0:T(1,128)S(1)} %bitcast.42, ...), custom_call_target="tpu_custom_call" | custom-call | tf_op jit(solution)/shard_map/begin/pallas_call | solution.py:242
  3.3 4.1 %collective-permute-start.3 = (f32[2,32,128]{2,1,0:T(8,128)S(1)}, f32[2,32,128]{2,1,0:T(8,128)S(1)}, u32[]{:S(2)}, u32[]{:S(2)}) collective-permute-start(f32[2,32,128]{2,1,0:T(8,128)S(1)} %get-tuple-element.47), channel_id=1, source_target_pairs={{0,8},{1,9},{2,10},{3,11},{4,12},{5,13},{6,14},{7,15},{8,0},{9,1},... | collective-permute-start | bytes 98312 | tf_op jit(solution)/shard_map/ppermute | solution.py:66
  7.4 1.3 %collective-permute-start.5 = (f32[2,32,128]{2,1,0:T(8,128)S(1)}, f32[2,32,128]{2,1,0:T(8,128)S(1)}, u32[]{:S(2)}, u32[]{:S(2)}) collective-permute-start(f32[2,32,128]{2,1,0:T(8,128)S(1)} %get-tuple-element.47), channel_id=1, source_target_pairs={{0,12},{1,13},{2,14},{3,15},{4,8},{5,9},{6,10},{7,11},{8,4},{9,5},... | collective-permute-start | bytes 98312 | tf_op jit(solution)/shard_map/ppermute | solution.py:66
  9.0 1.5 %collective-permute-start = (f32[4,32,128]{2,1,0:T(8,128)S(1)}, f32[4,32,128]{2,1,0:T(8,128)S(1)}, u32[]{:S(2)}, u32[]{:S(2)}) collective-permute-start(f32[4,32,128]{2,1,0:T(8,128)S(1)} %get-tuple-element.43), channel_id=1, source_target_pairs={{0,2},{1,3},{2,0},{3,1},{4,6},{5,7},{6,4},{7,5},{8,10},{9,11},{10,... | collective-permute-start | bytes 196616 | tf_op jit(solution)/shard_map/ppermute | solution.py:66
  10.5 1.8 %collective-permute-start.1 = (f32[4,32,128]{2,1,0:T(8,128)S(1)}, f32[4,32,128]{2,1,0:T(8,128)S(1)}, u32[]{:S(2)}, u32[]{:S(2)}) collective-permute-start(f32[4,32,128]{2,1,0:T(8,128)S(1)} %get-tuple-element.44), channel_id=1, source_target_pairs={{0,4},{1,5},{2,6},{3,7},{4,0},{5,1},{6,2},{7,3},{8,12},{9,13},{10,... | collective-permute-start | bytes 196616 | tf_op jit(solution)/shard_map/ppermute | solution.py:66
  12.6 2.2 %collective-permute-done.4 = f32[3,2,32,128]{3,2,1,0:T(8,128)S(1)} collective-permute-done((f32[3,2,32,128]{3,2,1,0:T(8,128)S(1)}, f32[3,2,32,128]{3,2,1,0:T(8,128)S(1)}, u32[]{:S(2)}, u32[]{:S(2)}) %collective-permute-start.4) | collective-permute-done | bytes 98336 | tf_op jit(solution)/shard_map/ppermute | solution.py:66
  14.8 0.8 collective-permute-start.6
  15.6 1.9 %collective-permute-start.8 = (f32[2,4,2,32,128]{4,3,2,1,0:T(8,128)S(1)}, f32[2,4,2,32,128]{4,3,2,1,0:T(8,128)S(1)}, u32[]{:S(2)}, u32[]{:S(2)}) collective-permute-start(f32[2,4,2,32,128]{4,3,2,1,0:T(8,128)S(1)} %pad_maximum_fusion.3), channel_id=1, source_target_pairs={{0,2},{1,17},{2,0},{3,19},{4,6},{5,21},{6,4},{7,23},{8,10},{9,25},... | collective-permute-start | bytes 786440 | tf_op jit(solution)/shard_map/ppermute | solution.py:66
  17.9 2.0 %collective-permute-done.6 = f32[2,2,32,128]{3,2,1,0:T(8,128)S(1)} collective-permute-done((f32[2,2,32,128]{3,2,1,0:T(8,128)S(1)}, f32[2,2,32,128]{3,2,1,0:T(8,128)S(1)}, u32[]{:S(2)}, u32[]{:S(2)}) %collective-permute-start.6) | collective-permute-done | bytes 65568 | tf_op jit(solution)/shard_map/ppermute | solution.py:66
  20.1 2.6 %collective-permute-done.8 = f32[2,4,2,32,128]{4,3,2,1,0:T(8,128)S(1)} collective-permute-done((f32[2,4,2,32,128]{4,3,2,1,0:T(8,128)S(1)}, f32[2,4,2,32,128]{4,3,2,1,0:T(8,128)S(1)}, u32[]{:S(2)}, u32[]{:S(2)}) %collective-permute-start.8) | collective-permute-done | bytes 262176 | tf_op jit(solution)/shard_map/ppermute | solution.py:66
  22.7 1.6 %collective-permute-start.9 = (f32[4,4,2,32,128]{4,3,2,1,0:T(8,128)S(1)}, f32[4,4,2,32,128]{4,3,2,1,0:T(8,128)S(1)}, u32[]{:S(2)}, u32[]{:S(2)}) collective-permute-start(f32[4,4,2,32,128]{4,3,2,1,0:T(8,128)S(1)} %pad_maximum_fusion.2.four), channel_id=1, source_target_pairs={{0,16},{1,3},{2,18},{3,1},{4,20},{5,7},{6,22},{7,5},{8,24},{9,11},... | collective-permute-start | bytes 1572872 | tf_op jit(solution)/shard_map/ppermute | solution.py:66
  24.3 1.7 %collective-permute-start.7 = (f32[9,2,32,128]{3,2,1,0:T(8,128)S(1)}, f32[9,2,32,128]{3,2,1,0:T(8,128)S(1)}, u32[]{:S(2)}, u32[]{:S(2)}) collective-permute-start(f32[9,2,32,128]{3,2,1,0:T(8,128)S(1)} %constant_dynamic-update-slice_fusion), channel_id=1, source_target_pairs={{0,4},{1,5},{2,6},{3,7},{4,0},{5,1},{6,2},{7,3},{8,12},{9,13},{10,... | collective-permute-start | bytes 884744 | tf_op jit(solution)/shard_map/ppermute | solution.py:66
  26.1 1.5 %collective-permute-start.12 = (f32[13,2,32,128]{3,2,1,0:T(8,128)S(1)}, f32[13,2,32,128]{3,2,1,0:T(8,128)S(1)}, u32[]{:S(2)}, u32[]{:S(2)}) collective-permute-start(f32[13,2,32,128]{3,2,1,0:T(8,128)S(1)} %get-tuple-element.85), channel_id=1, source_target_pairs={{0,2},{1,17},{2,0},{3,19},{4,6},{5,21},{6,4},{7,23},{8,10},{9,25},... | collective-permute-start | bytes 1277960 | tf_op jit(solution)/shard_map/ppermute | solution.py:66
  27.6 3.6 %collective-permute-done.7 = f32[9,2,32,128]{3,2,1,0:T(8,128)S(1)} collective-permute-done((f32[9,2,32,128]{3,2,1,0:T(8,128)S(1)}, f32[9,2,32,128]{3,2,1,0:T(8,128)S(1)}, u32[]{:S(2)}, u32[]{:S(2)}) %collective-permute-start.7) | collective-permute-done | bytes 294944 | tf_op jit(solution)/shard_map/ppermute | solution.py:66
  31.1 6.5 %collective-permute-done.9.third = f32[4,4,2,32,128]{4,3,2,1,0:T(8,128)S(1)} collective-permute-done((f32[4,4,2,32,128]{4,3,2,1,0:T(8,128)S(1)}, f32[4,4,2,32,128]{4,3,2,1,0:T(8,128)S(1)}, u32[]{:S(2)}, u32[]{:S(2)}) %collective-permute-start.9) | collective-permute-done | bytes 524320 | tf_op jit(solution)/shard_map/ppermute | solution.py:66
  37.6 0.9 collective-permute-start.10
  38.5 0.8 collective-permute-start.11
  39.4 1.6 %collective-permute-start.16 = (f32[2,13,2,32,128]{4,3,2,1,0:T(8,128)S(1)}, f32[2,13,2,32,128]{4,3,2,1,0:T(8,128)S(1)}, u32[]{:S(2)}, u32[]{:S(2)}) collective-permute-start(f32[2,13,2,32,128]{4,3,2,1,0:T(8,128)S(1)} %pad_maximum_fusion.n0), channel_id=1, source_target_pairs={{0,16},{1,3},{2,18},{3,1},{4,20},{5,7},{6,22},{7,5},{8,24},{9,11},... | collective-permute-start | bytes 2555912 | tf_op jit(solution)/shard_map/ppermute | solution.py:66
  41.0 4.2 %collective-permute-done.11.other_ref = f32[4,2,32,128]{3,2,1,0:T(8,128)S(1)} collective-permute-done((f32[4,2,32,128]{3,2,1,0:T(8,128)S(1)}, f32[4,2,32,128]{3,2,1,0:T(8,128)S(1)}, u32[]{:S(2)}, u32[]{:S(2)}) %collective-permute-start.11) | collective-permute-done | bytes 131104 | tf_op jit(solution)/shard_map/ppermute | solution.py:66
  45.4 1.6 %link_0.1 = (f32[128,256]{1,0:T(8,128)S(1)}, f32[128,128]{1,0:T(8,128)S(1)}) custom-call(f32[128,256]{1,0:T(8,128)S(1)} %get-tuple-element.62.b_ref, f32[4,4,2,32,128]{4,3,2,1,0:T(8,128)S(1)} %pad_maximum_fusion.2.four, f32[4,4,2,32,128]{4,3,2,1,0:T(8,128)S(1)} %collective-permute-done.9.third), custom_call_target="tpu_custom_call" | custom-call | tf_op jit(solution)/shard_map/link_0/pallas_call | solution.py:164
  47.1 7.1 %collective-permute-done.13.got = f32[128,256]{1,0:T(8,128)S(1)} collective-permute-done((f32[128,256]{1,0:T(8,128)S(1)}, f32[128,256]{1,0:T(8,128)S(1)}, u32[]{:S(2)}, u32[]{:S(2)}) %collective-permute-start.13) | collective-permute-done | bytes 131104 | tf_op jit(solution)/shard_map/ppermute | solution.py:66
  54.3 0.5 collective-permute-start.17
  54.8 5.0 %collective-permute-done.14 = f32[4,2,32,128]{3,2,1,0:T(8,128)S(1)} collective-permute-done((f32[4,2,32,128]{3,2,1,0:T(8,128)S(1)}, f32[4,2,32,128]{3,2,1,0:T(8,128)S(1)}, u32[]{:S(2)}, u32[]{:S(2)}) %collective-permute-start.14) | collective-permute-done | bytes 131104 | tf_op jit(solution)/shard_map/ppermute | solution.py:66
  59.8 1.5 %collective-permute-start.15 = (f32[4,2,32,128]{3,2,1,0:T(8,128)S(1)}, f32[4,2,32,128]{3,2,1,0:T(8,128)S(1)}, u32[]{:S(2)}, u32[]{:S(2)}) collective-permute-start(f32[4,2,32,128]{3,2,1,0:T(8,128)S(1)} %collective-permute-done.14), channel_id=1, source_target_pairs={{0,2},{1,17},{2,0},{3,19},{4,6},{5,21},{6,4},{7,23},{8,10},{9,25},... | collective-permute-start | bytes 393224 | tf_op jit(solution)/shard_map/ppermute | solution.py:66
  61.3 3.5 %collective-permute-done.15 = f32[4,2,32,128]{3,2,1,0:T(8,128)S(1)} collective-permute-done((f32[4,2,32,128]{3,2,1,0:T(8,128)S(1)}, f32[4,2,32,128]{3,2,1,0:T(8,128)S(1)}, u32[]{:S(2)}, u32[]{:S(2)}) %collective-permute-start.15) | collective-permute-done | bytes 131104 | tf_op jit(solution)/shard_map/ppermute | solution.py:66
  64.8 2.3 %link_1.1 = (f32[128,256]{1,0:T(8,128)S(1)}, f32[128,128]{1,0:T(8,128)S(1)}) custom-call(f32[128,256]{1,0:T(8,128)S(1)} %get-tuple-element.69.b_ref, f32[128,256]{1,0:T(8,128)S(1)} %get-tuple-element.63.own, f32[128,256]{1,0:T(8,128)S(1)} %collective-permute-done.13.got, f32[128,128]{1,0:T(8,128)S(1)} %get-tuple-element.70.y0_ref, ...), custom_call_target="tpu_custom_call" | custom-call | tf_op jit(solution)/shard_map/link_1/pallas_call | solution.py:164
  67.2 1.3 %collective-permute-done.18 = f32[128,256]{1,0:T(8,128)S(1)} collective-permute-done((f32[128,256]{1,0:T(8,128)S(1)}, f32[128,256]{1,0:T(8,128)S(1)}, u32[]{:S(2)}, u32[]{:S(2)}) %collective-permute-start.18) | collective-permute-done | bytes 131104 | tf_op jit(solution)/shard_map/ppermute | solution.py:66
  68.8 1.6 %collective-permute-start.21 = (f32[2,4,2,32,128]{4,3,2,1,0:T(8,128)S(1)}, f32[2,4,2,32,128]{4,3,2,1,0:T(8,128)S(1)}, u32[]{:S(2)}, u32[]{:S(2)}) collective-permute-start(f32[2,4,2,32,128]{4,3,2,1,0:T(8,128)S(1)} %pad_maximum_fusion.5.f0), channel_id=1, source_target_pairs={{0,16},{1,3},{2,18},{3,1},{4,20},{5,7},{6,22},{7,5},{8,24},{9,11},... | collective-permute-start | bytes 786440 | tf_op jit(solution)/shard_map/ppermute | solution.py:66
  70.4 0.5 collective-permute-start.19
  70.9 2.4 %collective-permute-start.20 = (f32[128,256]{1,0:T(8,128)S(1)}, f32[128,256]{1,0:T(8,128)S(1)}, u32[]{:S(2)}, u32[]{:S(2)}) collective-permute-start(f32[128,256]{1,0:T(8,128)S(1)} %add.7._.s0), channel_id=1, source_target_pairs={{0,8},{1,9},{2,10},{3,11},{4,12},{5,13},{6,14},{7,15},{8,0},{9,1},... | collective-permute-start | bytes 393224 | tf_op jit(solution)/shard_map/ppermute | solution.py:66
  73.3 8.6 %collective-permute-done.19.other_ref = f32[4,2,32,128]{3,2,1,0:T(8,128)S(1)} collective-permute-done((f32[4,2,32,128]{3,2,1,0:T(8,128)S(1)}, f32[4,2,32,128]{3,2,1,0:T(8,128)S(1)}, u32[]{:S(2)}, u32[]{:S(2)}) %collective-permute-start.19) | collective-permute-done | bytes 131104 | tf_op jit(solution)/shard_map/ppermute | solution.py:66
  82.1 2.5 %collective-permute-done.20.s1 = f32[128,256]{1,0:T(8,128)S(1)} collective-permute-done((f32[128,256]{1,0:T(8,128)S(1)}, f32[128,256]{1,0:T(8,128)S(1)}, u32[]{:S(2)}, u32[]{:S(2)}) %collective-permute-start.20) | collective-permute-done | bytes 131104 | tf_op jit(solution)/shard_map/ppermute | solution.py:66
  84.6 3.3 %link_2.1 = (f32[128,256]{1,0:T(8,128)S(1)}, f32[128,128]{1,0:T(8,128)S(1)}) custom-call(f32[128,256]{1,0:T(8,128)S(1)} %get-tuple-element.74.b_ref, f32[128,256]{1,0:T(8,128)S(1)} %add.7._.s0, f32[128,256]{1,0:T(8,128)S(1)} %collective-permute-done.20.s1, f32[128,128]{1,0:T(8,128)S(1)} %get-tuple-element.70.y0_ref, ...), custom_call_target="tpu_custom_call" | custom-call | tf_op jit(solution)/shard_map/link_2/pallas_call | solution.py:164
  88.0 1.3 %collective-permute-done.23 = f32[128,256]{1,0:T(8,128)S(1)} collective-permute-done((f32[128,256]{1,0:T(8,128)S(1)}, f32[128,256]{1,0:T(8,128)S(1)}, u32[]{:S(2)}, u32[]{:S(2)}) %collective-permute-start.23) | collective-permute-done | bytes 131104 | tf_op jit(solution)/shard_map/ppermute | solution.py:66
  89.4 8.7 %collective-permute-done.24.s1 = f32[128,256]{1,0:T(8,128)S(1)} collective-permute-done((f32[128,256]{1,0:T(8,128)S(1)}, f32[128,256]{1,0:T(8,128)S(1)}, u32[]{:S(2)}, u32[]{:S(2)}) %collective-permute-start.24) | collective-permute-done | bytes 131104 | tf_op jit(solution)/shard_map/ppermute | solution.py:66
  98.1 1.1 link_3.1
  99.2 0.7 collective-permute-start.25
  99.9 0.6 collective-permute-start.26
  100.5 2.9 %collective-permute-start.28 = (f32[4,32,128]{2,1,0:T(8,128)S(1)}, f32[4,32,128]{2,1,0:T(8,128)S(1)}, u32[]{:S(2)}, u32[]{:S(2)}) collective-permute-start(f32[4,32,128]{2,1,0:T(8,128)S(1)} %get-tuple-element.81), channel_id=1, source_target_pairs={{0,6},{1,23},{2,4},{3,21},{4,2},{5,19},{6,0},{7,17},{8,14},{9,31},... | collective-permute-start | bytes 196616 | tf_op jit(solution)/shard_map/ppermute | solution.py:66
  103.4 0.8 collective-permute-done.26
  104.2 0.5 collective-permute-done.27
  104.8 1.7 %collective-permute-done.28 = f32[4,32,128]{2,1,0:T(8,128)S(1)} collective-permute-done((f32[4,32,128]{2,1,0:T(8,128)S(1)}, f32[4,32,128]{2,1,0:T(8,128)S(1)}, u32[]{:S(2)}, u32[]{:S(2)}) %collective-permute-start.28) | collective-permute-done | bytes 65568 | tf_op jit(solution)/shard_map/ppermute | solution.py:66
  106.5 2.1 %collective-permute-start.30 = (f32[4,2,32,128]{3,2,1,0:T(8,128)S(1)}, f32[4,2,32,128]{3,2,1,0:T(8,128)S(1)}, u32[]{:S(2)}, u32[]{:S(2)}) collective-permute-start(f32[4,2,32,128]{3,2,1,0:T(8,128)S(1)} %get-tuple-element.82.near_ref), channel_id=1, source_target_pairs={{0,1},{1,0},{2,3},{3,2},{4,5},{5,4},{6,7},{7,6},{8,9},{9,8},{10,11... | collective-permute-start | bytes 393224 | tf_op jit(solution)/shard_map/ppermute | solution.py:66
  108.6 1.3 %collective-permute-start.29 = (f32[4,2,32,128]{3,2,1,0:T(8,128)S(1)}, f32[4,2,32,128]{3,2,1,0:T(8,128)S(1)}, u32[]{:S(2)}, u32[]{:S(2)}) collective-permute-start(f32[4,2,32,128]{3,2,1,0:T(8,128)S(1)} %get-tuple-element.83.near_ref), channel_id=1, source_target_pairs={{0,16},{1,17},{2,18},{3,19},{4,20},{5,21},{6,22},{7,23},{8,24},{9,... | collective-permute-start | bytes 393224 | tf_op jit(solution)/shard_map/ppermute | solution.py:66
  109.9 0.9 join_root.1
  110.7 3.3 %collective-permute-done.29.other_ref = f32[4,2,32,128]{3,2,1,0:T(8,128)S(1)} collective-permute-done((f32[4,2,32,128]{3,2,1,0:T(8,128)S(1)}, f32[4,2,32,128]{3,2,1,0:T(8,128)S(1)}, u32[]{:S(2)}, u32[]{:S(2)}) %collective-permute-start.29) | collective-permute-done | bytes 131104 | tf_op jit(solution)/shard_map/ppermute | solution.py:66
  114.1 0.9 join_leaf.1
  (53 shorter events, 2.3 us)
Async XLA Ops:
  0.6 0.7 copy-start
  3.3 9.0 %collective-permute-start.3 = (f32[2,32,128]{2,1,0:T(8,128)S(1)}, f32[2,32,128]{2,1,0:T(8,128)S(1)}, u32[]{:S(2)}, u32[]{:S(2)}) collective-permute-start(f32[2,32,128]{2,1,0:T(8,128)S(1)} %get-tuple-element.47), channel_id=1, source_target_pairs={{0,8},{1,9},{2,10},{3,11},{4,12},{5,13},{6,14},{7,15},{8,0},{9,1},... | collective-permute-start | bytes 98312 | tf_op jit(solution)/shard_map/ppermute | solution.py:66
  7.4 8.1 %collective-permute-start.5 = (f32[2,32,128]{2,1,0:T(8,128)S(1)}, f32[2,32,128]{2,1,0:T(8,128)S(1)}, u32[]{:S(2)}, u32[]{:S(2)}) collective-permute-start(f32[2,32,128]{2,1,0:T(8,128)S(1)} %get-tuple-element.47), channel_id=1, source_target_pairs={{0,12},{1,13},{2,14},{3,15},{4,8},{5,9},{6,10},{7,11},{8,4},{9,5},... | collective-permute-start | bytes 98312 | tf_op jit(solution)/shard_map/ppermute | solution.py:66
  8.8 6.0 %collective-permute-start.4 = (f32[3,2,32,128]{3,2,1,0:T(8,128)S(1)}, f32[3,2,32,128]{3,2,1,0:T(8,128)S(1)}, u32[]{:S(2)}, u32[]{:S(2)}) collective-permute-start(f32[3,2,32,128]{3,2,1,0:T(8,128)S(1)} %get-tuple-element.46), channel_id=1, source_target_pairs={{0,4},{1,5},{2,6},{3,7},{4,0},{5,1},{6,2},{7,3},{8,12},{9,13},{10,... | collective-permute-start | bytes 294920 | tf_op jit(solution)/shard_map/ppermute | solution.py:66
  9.0 8.6 %collective-permute-start = (f32[4,32,128]{2,1,0:T(8,128)S(1)}, f32[4,32,128]{2,1,0:T(8,128)S(1)}, u32[]{:S(2)}, u32[]{:S(2)}) collective-permute-start(f32[4,32,128]{2,1,0:T(8,128)S(1)} %get-tuple-element.43), channel_id=1, source_target_pairs={{0,2},{1,3},{2,0},{3,1},{4,6},{5,7},{6,4},{7,5},{8,10},{9,11},{10,... | collective-permute-start | bytes 196616 | tf_op jit(solution)/shard_map/ppermute | solution.py:66
  10.5 7.1 %collective-permute-start.1 = (f32[4,32,128]{2,1,0:T(8,128)S(1)}, f32[4,32,128]{2,1,0:T(8,128)S(1)}, u32[]{:S(2)}, u32[]{:S(2)}) collective-permute-start(f32[4,32,128]{2,1,0:T(8,128)S(1)} %get-tuple-element.44), channel_id=1, source_target_pairs={{0,4},{1,5},{2,6},{3,7},{4,0},{5,1},{6,2},{7,3},{8,12},{9,13},{10,... | collective-permute-start | bytes 196616 | tf_op jit(solution)/shard_map/ppermute | solution.py:66
  12.3 5.6 %collective-permute-start.2 = (f32[4,32,128]{2,1,0:T(8,128)S(1)}, f32[4,32,128]{2,1,0:T(8,128)S(1)}, u32[]{:S(2)}, u32[]{:S(2)}) collective-permute-start(f32[4,32,128]{2,1,0:T(8,128)S(1)} %get-tuple-element.45), channel_id=1, source_target_pairs={{0,6},{1,7},{2,4},{3,5},{4,2},{5,3},{6,0},{7,1},{8,14},{9,15},{10,... | collective-permute-start | bytes 196616 | tf_op jit(solution)/shard_map/ppermute | solution.py:66
  14.8 5.2 %collective-permute-start.6 = (f32[2,2,32,128]{3,2,1,0:T(8,128)S(1)}, f32[2,2,32,128]{3,2,1,0:T(8,128)S(1)}, u32[]{:S(2)}, u32[]{:S(2)}) collective-permute-start(f32[2,2,32,128]{3,2,1,0:T(8,128)S(1)} %get-tuple-element.53), channel_id=1, source_target_pairs={{0,8},{1,9},{2,10},{3,11},{4,12},{5,13},{6,14},{7,15},{8,0},{9,1},... | collective-permute-start | bytes 196616 | tf_op jit(solution)/shard_map/ppermute | solution.py:66
  15.6 7.1 %collective-permute-start.8 = (f32[2,4,2,32,128]{4,3,2,1,0:T(8,128)S(1)}, f32[2,4,2,32,128]{4,3,2,1,0:T(8,128)S(1)}, u32[]{:S(2)}, u32[]{:S(2)}) collective-permute-start(f32[2,4,2,32,128]{4,3,2,1,0:T(8,128)S(1)} %pad_maximum_fusion.3), channel_id=1, source_target_pairs={{0,2},{1,17},{2,0},{3,19},{4,6},{5,21},{6,4},{7,23},{8,10},{9,25},... | collective-permute-start | bytes 786440 | tf_op jit(solution)/shard_map/ppermute | solution.py:66
  22.7 14.9 %collective-permute-start.9 = (f32[4,4,2,32,128]{4,3,2,1,0:T(8,128)S(1)}, f32[4,4,2,32,128]{4,3,2,1,0:T(8,128)S(1)}, u32[]{:S(2)}, u32[]{:S(2)}) collective-permute-start(f32[4,4,2,32,128]{4,3,2,1,0:T(8,128)S(1)} %pad_maximum_fusion.2.four), channel_id=1, source_target_pairs={{0,16},{1,3},{2,18},{3,1},{4,20},{5,7},{6,22},{7,5},{8,24},{9,11},... | collective-permute-start | bytes 1572872 | tf_op jit(solution)/shard_map/ppermute | solution.py:66
  24.3 6.8 %collective-permute-start.7 = (f32[9,2,32,128]{3,2,1,0:T(8,128)S(1)}, f32[9,2,32,128]{3,2,1,0:T(8,128)S(1)}, u32[]{:S(2)}, u32[]{:S(2)}) collective-permute-start(f32[9,2,32,128]{3,2,1,0:T(8,128)S(1)} %constant_dynamic-update-slice_fusion), channel_id=1, source_target_pairs={{0,4},{1,5},{2,6},{3,7},{4,0},{5,1},{6,2},{7,3},{8,12},{9,13},{10,... | collective-permute-start | bytes 884744 | tf_op jit(solution)/shard_map/ppermute | solution.py:66
  26.1 13.2 %collective-permute-start.12 = (f32[13,2,32,128]{3,2,1,0:T(8,128)S(1)}, f32[13,2,32,128]{3,2,1,0:T(8,128)S(1)}, u32[]{:S(2)}, u32[]{:S(2)}) collective-permute-start(f32[13,2,32,128]{3,2,1,0:T(8,128)S(1)} %get-tuple-element.85), channel_id=1, source_target_pairs={{0,2},{1,17},{2,0},{3,19},{4,6},{5,21},{6,4},{7,23},{8,10},{9,25},... | collective-permute-start | bytes 1277960 | tf_op jit(solution)/shard_map/ppermute | solution.py:66
  37.6 16.6 %collective-permute-start.10 = (f32[9,2,32,128]{3,2,1,0:T(8,128)S(1)}, f32[9,2,32,128]{3,2,1,0:T(8,128)S(1)}, u32[]{:S(2)}, u32[]{:S(2)}) collective-permute-start(f32[9,2,32,128]{3,2,1,0:T(8,128)S(1)} %collective-permute-done.7), channel_id=1, source_target_pairs={{0,2},{1,17},{2,0},{3,19},{4,6},{5,21},{6,4},{7,23},{8,10},{9,25},... | collective-permute-start | bytes 884744 | tf_op jit(solution)/shard_map/ppermute | solution.py:66
  38.5 6.7 %collective-permute-start.11 = (f32[4,2,32,128]{3,2,1,0:T(8,128)S(1)}, f32[4,2,32,128]{3,2,1,0:T(8,128)S(1)}, u32[]{:S(2)}, u32[]{:S(2)}) collective-permute-start(f32[4,2,32,128]{3,2,1,0:T(8,128)S(1)} %get-tuple-element.59.near_ref), channel_id=1, source_target_pairs={{0,8},{1,9},{2,10},{3,11},{4,12},{5,13},{6,14},{7,15},{8,0},{9,1},... | collective-permute-start | bytes 393224 | tf_op jit(solution)/shard_map/ppermute | solution.py:66
  39.4 25.4 %collective-permute-start.16 = (f32[2,13,2,32,128]{4,3,2,1,0:T(8,128)S(1)}, f32[2,13,2,32,128]{4,3,2,1,0:T(8,128)S(1)}, u32[]{:S(2)}, u32[]{:S(2)}) collective-permute-start(f32[2,13,2,32,128]{4,3,2,1,0:T(8,128)S(1)} %pad_maximum_fusion.n0), channel_id=1, source_target_pairs={{0,16},{1,3},{2,18},{3,1},{4,20},{5,7},{6,22},{7,5},{8,24},{9,11},... | collective-permute-start | bytes 2555912 | tf_op jit(solution)/shard_map/ppermute | solution.py:66
  47.0 7.3 %collective-permute-start.13 = (f32[128,256]{1,0:T(8,128)S(1)}, f32[128,256]{1,0:T(8,128)S(1)}, u32[]{:S(2)}, u32[]{:S(2)}) collective-permute-start(f32[128,256]{1,0:T(8,128)S(1)} %get-tuple-element.63.own), channel_id=1, source_target_pairs={{0,8},{1,9},{2,10},{3,11},{4,12},{5,13},{6,14},{7,15},{8,0},{9,1},... | collective-permute-start | bytes 393224 | tf_op jit(solution)/shard_map/ppermute | solution.py:66
  54.3 10.5 %collective-permute-start.17 = (f32[2,9,2,32,128]{4,3,2,1,0:T(8,128)S(1)}, f32[2,9,2,32,128]{4,3,2,1,0:T(8,128)S(1)}, u32[]{:S(2)}, u32[]{:S(2)}) collective-permute-start(f32[2,9,2,32,128]{4,3,2,1,0:T(8,128)S(1)} %pad_maximum_fusion.1.f0), channel_id=1, source_target_pairs={{0,16},{1,3},{2,18},{3,1},{4,20},{5,7},{6,22},{7,5},{8,24},{9,11},... | collective-permute-start | bytes 1769480 | tf_op jit(solution)/shard_map/ppermute | solution.py:66
  54.8 5.0 %collective-permute-start.14 = (f32[4,2,32,128]{3,2,1,0:T(8,128)S(1)}, f32[4,2,32,128]{3,2,1,0:T(8,128)S(1)}, u32[]{:S(2)}, u32[]{:S(2)}) collective-permute-start(f32[4,2,32,128]{3,2,1,0:T(8,128)S(1)} %get-tuple-element.67), channel_id=1, source_target_pairs={{0,4},{1,5},{2,6},{3,7},{4,0},{5,1},{6,2},{7,3},{8,12},{9,13},{10,... | collective-permute-start | bytes 393224 | tf_op jit(solution)/shard_map/ppermute | solution.py:66
  59.8 5.0 %collective-permute-start.15 = (f32[4,2,32,128]{3,2,1,0:T(8,128)S(1)}, f32[4,2,32,128]{3,2,1,0:T(8,128)S(1)}, u32[]{:S(2)}, u32[]{:S(2)}) collective-permute-start(f32[4,2,32,128]{3,2,1,0:T(8,128)S(1)} %collective-permute-done.14), channel_id=1, source_target_pairs={{0,2},{1,17},{2,0},{3,19},{4,6},{5,21},{6,4},{7,23},{8,10},{9,25},... | collective-permute-start | bytes 393224 | tf_op jit(solution)/shard_map/ppermute | solution.py:66
  67.1 1.4 %collective-permute-start.18 = (f32[128,256]{1,0:T(8,128)S(1)}, f32[128,256]{1,0:T(8,128)S(1)}, u32[]{:S(2)}, u32[]{:S(2)}) collective-permute-start(f32[128,256]{1,0:T(8,128)S(1)} %get-tuple-element.71), channel_id=1, source_target_pairs={{0,1},{1,0},{2,3},{3,2},{4,5},{5,4},{6,7},{7,6},{8,9},{9,8},{10,11... | collective-permute-start | bytes 393224 | tf_op jit(solution)/shard_map/ppermute | solution.py:66
  68.6 16.0 %collective-permute-start.22 = (f32[8,3,2,32,128]{4,3,2,1,0:T(8,128)S(1)}, f32[8,3,2,32,128]{4,3,2,1,0:T(8,128)S(1)}, u32[]{:S(2)}, u32[]{:S(2)}) collective-permute-start(f32[8,3,2,32,128]{4,3,2,1,0:T(8,128)S(1)} %root_shards.1.root), channel_id=1, source_target_pairs={{0,1},{1,0},{2,3},{3,2},{4,5},{5,4},{6,7},{7,6},{8,9},{9,8},{10,11... | collective-permute-start | bytes 2359304 | tf_op jit(solution)/shard_map/ppermute | solution.py:66
  68.8 13.3 %collective-permute-start.21 = (f32[2,4,2,32,128]{4,3,2,1,0:T(8,128)S(1)}, f32[2,4,2,32,128]{4,3,2,1,0:T(8,128)S(1)}, u32[]{:S(2)}, u32[]{:S(2)}) collective-permute-start(f32[2,4,2,32,128]{4,3,2,1,0:T(8,128)S(1)} %pad_maximum_fusion.5.f0), channel_id=1, source_target_pairs={{0,16},{1,3},{2,18},{3,1},{4,20},{5,7},{6,22},{7,5},{8,24},{9,11},... | collective-permute-start | bytes 786440 | tf_op jit(solution)/shard_map/ppermute | solution.py:66
  70.4 11.5 %collective-permute-start.19 = (f32[4,2,32,128]{3,2,1,0:T(8,128)S(1)}, f32[4,2,32,128]{3,2,1,0:T(8,128)S(1)}, u32[]{:S(2)}, u32[]{:S(2)}) collective-permute-start(f32[4,2,32,128]{3,2,1,0:T(8,128)S(1)} %get-tuple-element.72.near_ref), channel_id=1, source_target_pairs={{0,8},{1,9},{2,10},{3,11},{4,12},{5,13},{6,14},{7,15},{8,0},{9,1},... | collective-permute-start | bytes 393224 | tf_op jit(solution)/shard_map/ppermute | solution.py:66
  70.9 13.7 %collective-permute-start.20 = (f32[128,256]{1,0:T(8,128)S(1)}, f32[128,256]{1,0:T(8,128)S(1)}, u32[]{:S(2)}, u32[]{:S(2)}) collective-permute-start(f32[128,256]{1,0:T(8,128)S(1)} %add.7._.s0), channel_id=1, source_target_pairs={{0,8},{1,9},{2,10},{3,11},{4,12},{5,13},{6,14},{7,15},{8,0},{9,1},... | collective-permute-start | bytes 393224 | tf_op jit(solution)/shard_map/ppermute | solution.py:66
  87.9 1.4 %collective-permute-start.23 = (f32[128,256]{1,0:T(8,128)S(1)}, f32[128,256]{1,0:T(8,128)S(1)}, u32[]{:S(2)}, u32[]{:S(2)}) collective-permute-start(f32[128,256]{1,0:T(8,128)S(1)} %get-tuple-element.76), channel_id=1, source_target_pairs={{0,1},{1,0},{2,3},{3,2},{4,5},{5,4},{6,7},{7,6},{8,9},{9,8},{10,11... | collective-permute-start | bytes 393224 | tf_op jit(solution)/shard_map/ppermute | solution.py:66
  89.4 8.8 %collective-permute-start.24 = (f32[128,256]{1,0:T(8,128)S(1)}, f32[128,256]{1,0:T(8,128)S(1)}, u32[]{:S(2)}, u32[]{:S(2)}) collective-permute-start(f32[128,256]{1,0:T(8,128)S(1)} %add.8.s0), channel_id=1, source_target_pairs={{0,8},{1,9},{2,10},{3,11},{4,12},{5,13},{6,14},{7,15},{8,0},{9,1},... | collective-permute-start | bytes 393224 | tf_op jit(solution)/shard_map/ppermute | solution.py:66
  99.2 4.2 %collective-permute-start.25 = (f32[4,32,128]{2,1,0:T(8,128)S(1)}, f32[4,32,128]{2,1,0:T(8,128)S(1)}, u32[]{:S(2)}, u32[]{:S(2)}) collective-permute-start(f32[4,32,128]{2,1,0:T(8,128)S(1)} %get-tuple-element.78), channel_id=1, source_target_pairs={{0,0},{1,17},{2,2},{3,19},{4,4},{5,21},{6,6},{7,23},{8,8},{9,25},{... | collective-permute-start | bytes 196616 | tf_op jit(solution)/shard_map/ppermute | solution.py:66
  99.9 4.3 %collective-permute-start.26 = (f32[4,32,128]{2,1,0:T(8,128)S(1)}, f32[4,32,128]{2,1,0:T(8,128)S(1)}, u32[]{:S(2)}, u32[]{:S(2)}) collective-permute-start(f32[4,32,128]{2,1,0:T(8,128)S(1)} %get-tuple-element.79), channel_id=1, source_target_pairs={{0,2},{1,19},{2,0},{3,17},{4,6},{5,23},{6,4},{7,21},{8,10},{9,27},... | collective-permute-start | bytes 196616 | tf_op jit(solution)/shard_map/ppermute | solution.py:66
  100.5 4.3 %collective-permute-start.27 = (f32[4,32,128]{2,1,0:T(8,128)S(1)}, f32[4,32,128]{2,1,0:T(8,128)S(1)}, u32[]{:S(2)}, u32[]{:S(2)}) collective-permute-start(f32[4,32,128]{2,1,0:T(8,128)S(1)} %get-tuple-element.80), channel_id=1, source_target_pairs={{0,4},{1,21},{2,6},{3,23},{4,0},{5,17},{6,2},{7,19},{8,12},{9,29},... | collective-permute-start | bytes 196616 | tf_op jit(solution)/shard_map/ppermute | solution.py:66
  100.5 5.9 %collective-permute-start.28 = (f32[4,32,128]{2,1,0:T(8,128)S(1)}, f32[4,32,128]{2,1,0:T(8,128)S(1)}, u32[]{:S(2)}, u32[]{:S(2)}) collective-permute-start(f32[4,32,128]{2,1,0:T(8,128)S(1)} %get-tuple-element.81), channel_id=1, source_target_pairs={{0,6},{1,23},{2,4},{3,21},{4,2},{5,19},{6,0},{7,17},{8,14},{9,31},... | collective-permute-start | bytes 196616 | tf_op jit(solution)/shard_map/ppermute | solution.py:66
  106.5 3.4 %collective-permute-start.30 = (f32[4,2,32,128]{3,2,1,0:T(8,128)S(1)}, f32[4,2,32,128]{3,2,1,0:T(8,128)S(1)}, u32[]{:S(2)}, u32[]{:S(2)}) collective-permute-start(f32[4,2,32,128]{3,2,1,0:T(8,128)S(1)} %get-tuple-element.82.near_ref), channel_id=1, source_target_pairs={{0,1},{1,0},{2,3},{3,2},{4,5},{5,4},{6,7},{7,6},{8,9},{9,8},{10,11... | collective-permute-start | bytes 393224 | tf_op jit(solution)/shard_map/ppermute | solution.py:66
  108.6 5.5 %collective-permute-start.29 = (f32[4,2,32,128]{3,2,1,0:T(8,128)S(1)}, f32[4,2,32,128]{3,2,1,0:T(8,128)S(1)}, u32[]{:S(2)}, u32[]{:S(2)}) collective-permute-start(f32[4,2,32,128]{3,2,1,0:T(8,128)S(1)} %get-tuple-element.83.near_ref), channel_id=1, source_target_pairs={{0,16},{1,17},{2,18},{3,19},{4,20},{5,21},{6,22},{7,23},{8,24},{9,... | collective-permute-start | bytes 393224 | tf_op jit(solution)/shard_map/ppermute | solution.py:66

commit v8 on v6

--- a/solution.py
+++ b/solution.py
@@ -195,8 +195,8 @@
 
 
 def begin_kernel(tiles, *refs):
-    sources, outs, places = refs[:6], refs[6:15], refs[15:21]
-    cuts, sems = refs[21:]
+    sources, outs, places = refs[:6], refs[6:13], refs[13:19]
+    cuts, sems = refs[19:]
     copies = [
         pltpu.make_async_copy(source, place, sems.at[k])
         for k, (source, place) in enumerate(zip(sources, places))
@@ -204,7 +204,7 @@
     for copy in copies:
         copy.start()
     leaf_inv, blocks, leaf_rhs, root_rhs, root_inv, lower = places
-    away, first, rest, masked_out, lower_out = outs[:5]
+    away, first, masked_out = outs[:3]
     core = spot()[4]
 
     def mask(m, dest, base):
@@ -225,21 +225,21 @@
     _, zh, _, x, _ = spot()
     for b1 in range(2):
         for b2 in range(2):
-            outs[5 + b1 * 2 + b2][...] = cuts[(zh ^ b1) * 2 + (x ^ b2)]
-    part_rows(leaf_inv.at[0, 1], rest.at[0], away.at[1])
+            outs[3 + b1 * 2 + b2][...] = cuts[(zh ^ b1) * 2 + (x ^ b2)]
+    part_rows(leaf_inv.at[0, 1], first.at[3], away.at[1])
     copies[4].wait()
-    part_rows(root_inv.at[core], rest.at[1], away.at[2])
+    part_rows(root_inv.at[core], first.at[4], away.at[2])
     copies[5].wait()
     for a in range(2):
         start = pl.multiple_of(core * 128, 128)
-        lower_out[0, a] = lower[a, :, pl.ds(start, 128)]
+        masked_out[8, a] = lower[a, :, pl.ds(start, 128)]
     for m in range(1, 5):
         mask(m, masked_out, 2 * (m - 1))
 
 
 def begin(pattern, *arrays):
     tiles = pattern.transpose(0, 2, 3, 1)
-    outs = [(3, 2, 32, 128), (3, 2, 32, 128), (2, 2, 32, 128)] + [(8, 2, 32, 128), (1, 2, 32, 128)] + [(4, 32, 128)] * 4
+    outs = [(3, 2, 32, 128), (5, 2, 32, 128), (9, 2, 32, 128)] + [(4, 32, 128)] * 4
     return pl.pallas_call(
         begin_kernel,
         out_shape=[pltpu.VMEM(dims, F32) for dims in outs],
@@ -312,14 +312,8 @@
     return lambda unit: lambda b3, b2, b1: (four, third)[b3].at[b2 * 2 + b1, unit]
 
 
-def chunk_unit(near, far, start, far_start):
-    def of(unit):
-        def pick(b3, b2, b1):
-            return (near, far)[b1][b3].at[b2, (start, far_start)[b1] + unit]
-
-        return pick
-
-    return of
+def block_unit(near, far):
+    return lambda unit: lambda b3, b2, b1: (near, far)[b1][b3].at[b2, unit]
 
 
 def root_unit(ref):
@@ -375,10 +369,11 @@
     part_ref[...] = update(held, [solved], [functools.partial(wait_all, second)])
 
 
-def link_1_kernel(b_ref, own, got, y0_ref, n0, n1, f0, f1, part_ref, y_ref, inverse, held, sems):
-    unit = chunk_unit((n0, n1), (f0, f1), 0, 0)
-    first = fetch_inverse(unit, inverse, sems.at[0])
-    copies = [fetch_block(shifted(unit, 2 * t + 2), held, t, sems.at[t + 1]) for t in range(2)]
+def link_1_kernel(b_ref, own, got, y0_ref, four, third, n0, n1, f0, f1, *refs):
+    part_ref, y_ref, inverse, held, sems = refs
+    first = fetch_inverse(shifted(first_chunk_unit(four, third), 4), inverse, sems.at[0])
+    unit = block_unit((n0, n1), (f0, f1))
+    copies = [fetch_block(shifted(unit, 2 * t), held, t, sems.at[t + 1]) for t in range(2)]
     wait_all(first)
     solved = solve(inverse, b_ref[...] - (own[...] + got[...]))
     y_ref[...] = solved
@@ -388,10 +383,10 @@
 
 def link_2_kernel(b_ref, s0, s1, s2, s3, y0_ref, y1_ref, n0, n1, f0, f1, root, swapped, *refs):
     part_ref, y_ref, inverse, held, sems = refs
-    unit = chunk_unit((n0, n1), (f0, f1), 9, 0)
+    unit = block_unit((n0, n1), (f0, f1))
     root, swapped = root_unit(root), root_unit(swapped)
     first = fetch_inverse(root, inverse, sems.at[0], swapped, 0)
-    copies = [fetch_block(shifted(unit, 2 * t), held, t, sems.at[t + 1]) for t in range(2)]
+    copies = [fetch_block(shifted(unit, 2 * t + 4), held, t, sems.at[t + 1]) for t in range(2)]
     copies.append(fetch_halves(root, swapped, held, 2, sems.at[3]))
     wait_all(first)
     solved = solve(inverse, b_ref[...] - sum_four((s0, s1, s2, s3)))
@@ -419,6 +414,16 @@
     return (
         [pltpu.VMEM((2, 2, 2, 2, 2, 32, 128), F32)] + blocks + [pltpu.SemaphoreType.DMA((nsems, 2, 8))]
     )
+
+
+def root_kernel(four, third, n0, n1, f0, f1, out):
+    for b1 in range(2):
+        for b3 in range(2):
+            for b2 in range(2):
+                place = b1 * 4 + b3 * 2 + b2
+                for unit in range(2):
+                    out[place, unit] = (four, third)[b3][b2 * 2 + b1, 6 + unit]
+                out[place, 2] = ((n0, n1), (f0, f1))[b1][b3][b2, 8]
 
 
 def lay_values(refs, held):
@@ -479,78 +484,81 @@
     def whole(keep, got):
         return jnp.stack([jnp.where(zl == 0, keep, got), jnp.where(zl == 0, got, keep)])
 
-    away, first, rest, blocks, lower, *cuts = begin(
+    def first_chunk(values, got):
+        return jnp.concatenate(
+            [whole(values[0], got[0]), values[1:3], whole(values[3], got[1]), whole(values[4], got[2])]
+        )
+
+    away, first, blocks, *cuts = begin(
         pattern, leaf_inverses, leaf_blocks, leaf_rhs, root_rhs, root_inverses, root_block
     )
+    first_far = send(first, to_far)
+    first_far_pair = send(away, to_far_pair)
     pair = send(away, to_pair)
-    first_far = send(first, to_far)
-    first_far_pair = send(away[0], to_far_pair)
-
-    def first_chunk(values, got):
-        return jnp.concatenate([whole(values[0], got), values[1:]])
-
+    second_own = send(blocks, to_second)
     moved = to_groups(cuts)
-    two_a = jnp.stack([first_chunk(first, pair[0]), first_chunk(first_far, first_far_pair)])
+
+    near_0 = jnp.stack([blocks, second_own])
+    near_1 = send(near_0, to_third)
+    first_far = after(first_far, near_0)
+    two_a = jnp.stack([first_chunk(first, pair), first_chunk(first_far, first_far_pair)])
     second_a = send(two_a, to_second)
+    far = send(after(blocks, two_a), to_far)
     rhs_in = jnp.stack(after(moved, two_a))
     rhs_pair = send(rhs_in, to_pair)
 
-    late = after(pair, rhs_in)
-    own_units = jnp.concatenate(
-        [whole(rest[0], late[1]), blocks[:4], whole(rest[1], late[2]), lower, blocks[4:]]
-    )
-    far_b = send(own_units[:9], to_far)
-    second_own = send(own_units, to_second)
-    four_a = jnp.concatenate([two_a, after(second_a, own_units)])
+    four_a = jnp.concatenate([two_a, after(second_a, near_1, rhs_in)])
     third_a = send(four_a, to_third)
-    near_0 = jnp.stack([own_units, after(second_own, third_a)])
-    near_1 = send(near_0, to_third)
-    far_b = after(far_b, third_a)
-    second_b = send(far_b, to_second)
-    far_c = send(after(own_units[9:], far_b), to_far)
     b0, b1, r2, r3 = call(
         "stand",
         stand_kernel,
         [(128, 256)] * 4,
-        after(rhs_in, third_a),
+        after(rhs_in, four_a),
         rhs_pair,
         scratch=[pltpu.VMEM((8, 4, 32, 128), F32)],
     )
+    far = after(far, b0)
+    far_0 = jnp.stack([far, send(far, to_second)])
+    far_1 = send(far_0, to_third)
 
     own, y0 = call(
         "link_0",
         link_0_kernel,
         VECTOR,
-        after(b0, near_0, far_b),
+        after(b0, far_0),
         four_a,
         third_a,
         scratch=link_scratch(1, 2),
     )
     got = send(own, to_pair)
-    far_b_0 = jnp.stack([far_b, after(second_b, got)])
-    far_b_1 = send(far_b_0, to_third)
-    far_c = after(far_c, far_b_0)
-    second_c = send(far_c, to_second)
-    far_c_0 = jnp.stack([far_c, second_c])
-    far_c_1 = send(far_c_0, to_third)
 
     own, y1 = call(
         "link_1",
         link_1_kernel,
         VECTOR,
-        after(b1, far_c_0),
+        b1,
         own,
         got,
         y0,
+        four_a,
+        third_a,
         near_0,
         near_1,
-        far_b_0,
-        far_b_1,
+        far_0,
+        far_1,
         scratch=link_scratch(2, 3),
     )
     sums = [own, send(own, to_core), send(own, to_pair), send(own, to_pair_core)]
-    root_own = jnp.concatenate(
-        [after(near_0[:, 6:9], own), near_1[:, 6:9], far_b_0[:, 6:9], far_b_1[:, 6:9]]
+    (root_own,) = call(
+        "root_shards",
+        root_kernel,
+        [(8, 3, 2, 32, 128)],
+        after(four_a, own),
+        third_a,
+        near_0,
+        near_1,
+        far_0,
+        far_1,
     )
     root_swapped = send(root_own, to_core)
 
@@ -564,8 +572,8 @@
         y1,
         near_0,
         near_1,
-        far_c_0,
-        far_c_1,
+        far_0,
+        far_1,
         root_own,
         root_swapped,
         scratch=link_scratch(3, 4),

time: 110 us -> 107 us (0.973)
  waiting for transfers between devices: 61.4 us -> 57.7 us
    ppermute x31 -> x28, waiting for transfers between devices: 61.4 us -> 57.7 us  [send(): return lax.ppermute(value, AXES, pairs(dest))]
    ppermute x31 -> x28, starting transfers between devices: 33.5 us -> 34.5 us  [send(): return lax.ppermute(value, AXES, pairs(dest))]
    pallas_call x5 -> x6, Pallas kernels: 8.59 us -> 8.66 us  [call(): pl.pallas_call(kernel, out_shape=[pltpu.VMEM(dims, F32) for dims in outs]...]
  transfers between devices with their start and end apart: 31 -> 28, of which waited for: 16 -> 14; matrix products, arithmetic and copies ran while one was open for 0% -> 0% of each run, Pallas kernels for 2% -> 3%
where the time goes in v8:
time: 107 us
  waiting for transfers between devices  57.7 us (54%)
  starting transfers between devices  34.5 us (32%)
  Pallas kernels  12.4 us (12%)
    ppermute x28, waiting for transfers between devices, send(): return lax.ppermute(value, AXES, pairs(dest))  57.7 us
    ppermute x28, starting transfers between devices, send(): return lax.ppermute(value, AXES, pairs(dest))  34.5 us
    pallas_call x6, Pallas kernels, call(): pl.pallas_call(kernel, out_shape=[pltpu.VMEM(dims, F32) for dims in outs]...  8.66 us
  transfers between devices with their start and end apart: 28, of which 14 were waited for; matrix products, arithmetic and copies ran while one was open for 0% of the time, Pallas kernels for 3%

profile of v8, /device:TPU:0, one launch (start us, length us, event | category | flops | bytes accessed | tf_op | source)
XLA Modules:
  0.0 106.6 jit_solution(18309715757282496631)
XLA Ops:
  0.6 0.7 copy-done
  1.3 2.1 %begin.1 = (f32[3,2,32,128]{3,2,1,0:T(8,128)S(1)}, f32[5,2,32,128]{3,2,1,0:T(8,128)S(1)}, f32[9,2,32,128]{3,2,1,0:T(8,128)S(1)}, f32[4,32,128]{2,1,0:T(8,128)S(1...) custom-call(s32[1,2,1,5]{3,2,1,0:T(1,128)S(1)} %bitcast.18, ...), custom_call_target="tpu_custom_call" | custom-call | tf_op jit(solution)/shard_map/begin/pallas_call | solution.py:243
  3.4 3.1 %collective-permute-start.3 = (f32[3,2,32,128]{3,2,1,0:T(8,128)S(1)}, f32[3,2,32,128]{3,2,1,0:T(8,128)S(1)}, u32[]{:S(2)}, u32[]{:S(2)}) collective-permute-start(f32[3,2,32,128]{3,2,1,0:T(8,128)S(1)} %get-tuple-element.39), channel_id=1, source_target_pairs={{0,4},{1,5},{2,6},{3,7},{4,0},{5,1},{6,2},{7,3},{8,12},{9,13},{10,... | collective-permute-start | bytes 294920 | tf_op jit(solution)/shard_map/ppermute | solution.py:67
  6.5 2.5 %collective-permute-start.6 = (f32[3,2,32,128]{3,2,1,0:T(8,128)S(1)}, f32[3,2,32,128]{3,2,1,0:T(8,128)S(1)}, u32[]{:S(2)}, u32[]{:S(2)}) collective-permute-start(f32[3,2,32,128]{3,2,1,0:T(8,128)S(1)} %get-tuple-element.39), channel_id=1, source_target_pairs={{0,12},{1,13},{2,14},{3,15},{4,8},{5,9},{6,10},{7,11},{8,4},{9,5},... | collective-permute-start | bytes 294920 | tf_op jit(solution)/shard_map/ppermute | solution.py:67
  9.0 0.1 collective-permute-start.4
  9.1 1.5 %collective-permute-start.5 = (f32[9,2,32,128]{3,2,1,0:T(8,128)S(1)}, f32[9,2,32,128]{3,2,1,0:T(8,128)S(1)}, u32[]{:S(2)}, u32[]{:S(2)}) collective-permute-start(f32[9,2,32,128]{3,2,1,0:T(8,128)S(1)} %get-tuple-element.52), channel_id=1, source_target_pairs={{0,2},{1,17},{2,0},{3,19},{4,6},{5,21},{6,4},{7,23},{8,10},{9,25},... | collective-permute-start | bytes 884744 | tf_op jit(solution)/shard_map/ppermute | solution.py:67
  10.7 5.1 %collective-permute-done.5 = f32[9,2,32,128]{3,2,1,0:T(8,128)S(1)} collective-permute-done((f32[9,2,32,128]{3,2,1,0:T(8,128)S(1)}, f32[9,2,32,128]{3,2,1,0:T(8,128)S(1)}, u32[]{:S(2)}, u32[]{:S(2)}) %collective-permute-start.5) | collective-permute-done | bytes 294944 | tf_op jit(solution)/shard_map/ppermute | solution.py:67
  15.9 1.6 %collective-permute-start.8 = (f32[2,9,2,32,128]{4,3,2,1,0:T(8,128)S(1)}, f32[2,9,2,32,128]{4,3,2,1,0:T(8,128)S(1)}, u32[]{:S(2)}, u32[]{:S(2)}) collective-permute-start(f32[2,9,2,32,128]{4,3,2,1,0:T(8,128)S(1)} %pad_maximum_fusion.1.n0), channel_id=1, source_target_pairs={{0,16},{1,3},{2,18},{3,1},{4,20},{5,7},{6,22},{7,5},{8,24},{9,11},... | collective-permute-start | bytes 1769480 | tf_op jit(solution)/shard_map/ppermute | solution.py:67
  17.4 3.3 %collective-permute-done.4 = f32[5,2,32,128]{3,2,1,0:T(8,128)S(1)} collective-permute-done((f32[5,2,32,128]{3,2,1,0:T(8,128)S(1)}, f32[5,2,32,128]{3,2,1,0:T(8,128)S(1)}, u32[]{:S(2)}, u32[]{:S(2)}) %collective-permute-start.4) | collective-permute-done | bytes 163872 | tf_op jit(solution)/shard_map/ppermute | solution.py:67
  20.9 1.6 %collective-permute-start.7 = (f32[2,8,2,32,128]{4,3,2,1,0:T(8,128)S(1)}, f32[2,8,2,32,128]{4,3,2,1,0:T(8,128)S(1)}, u32[]{:S(2)}, u32[]{:S(2)}) collective-permute-start(f32[2,8,2,32,128]{4,3,2,1,0:T(8,128)S(1)} %pad_maximum_fusion.3), channel_id=1, source_target_pairs={{0,2},{1,17},{2,0},{3,19},{4,6},{5,21},{6,4},{7,23},{8,10},{9,25},... | collective-permute-start | bytes 1572872 | tf_op jit(solution)/shard_map/ppermute | solution.py:67
  22.4 0.5 collective-permute-start
  23.0 3.8 %collective-permute-start.2 = (f32[4,32,128]{2,1,0:T(8,128)S(1)}, f32[4,32,128]{2,1,0:T(8,128)S(1)}, u32[]{:S(2)}, u32[]{:S(2)}) collective-permute-start(f32[4,32,128]{2,1,0:T(8,128)S(1)} %get-tuple-element.37), channel_id=1, source_target_pairs={{0,10},{1,11},{2,8},{3,9},{4,14},{5,15},{6,12},{7,13},{8,2},{9,3},... | collective-permute-start | bytes 196616 | tf_op jit(solution)/shard_map/ppermute | solution.py:67
  26.8 6.0 %collective-permute-done = f32[4,32,128]{2,1,0:T(8,128)S(1)} collective-permute-done((f32[4,32,128]{2,1,0:T(8,128)S(1)}, f32[4,32,128]{2,1,0:T(8,128)S(1)}, u32[]{:S(2)}, u32[]{:S(2)}) %collective-permute-start) | collective-permute-done | bytes 65568 | tf_op jit(solution)/shard_map/ppermute | solution.py:67
  32.8 0.5 collective-permute-start.9
  33.3 2.4 %collective-permute-start.10 = (f32[9,2,32,128]{3,2,1,0:T(8,128)S(1)}, f32[9,2,32,128]{3,2,1,0:T(8,128)S(1)}, u32[]{:S(2)}, u32[]{:S(2)}) collective-permute-start(f32[9,2,32,128]{3,2,1,0:T(8,128)S(1)} %get-tuple-element.52), channel_id=1, source_target_pairs={{0,8},{1,9},{2,10},{3,11},{4,12},{5,13},{6,14},{7,15},{8,0},{9,1},... | collective-permute-start | bytes 884744 | tf_op jit(solution)/shard_map/ppermute | solution.py:67
  35.7 0.1 pad_maximum_fusion.four
  35.8 1.4 %collective-permute-start.12 = (f32[4,8,2,32,128]{4,3,2,1,0:T(8,128)S(1)}, f32[4,8,2,32,128]{4,3,2,1,0:T(8,128)S(1)}, u32[]{:S(2)}, u32[]{:S(2)}) collective-permute-start(f32[4,8,2,32,128]{4,3,2,1,0:T(8,128)S(1)} %pad_maximum_fusion.four), channel_id=1, source_target_pairs={{0,16},{1,3},{2,18},{3,1},{4,20},{5,7},{6,22},{7,5},{8,24},{9,11},... | collective-permute-start | bytes 3145736 | tf_op jit(solution)/shard_map/ppermute | solution.py:67
  37.2 5.0 %collective-permute-done.9.other_ref = f32[4,4,32,128]{3,2,1,0:T(8,128)S(1)} collective-permute-done((f32[4,4,32,128]{3,2,1,0:T(8,128)S(1)}, f32[4,4,32,128]{3,2,1,0:T(8,128)S(1)}, u32[]{:S(2)}, u32[]{:S(2)}) %collective-permute-start.9) | collective-permute-done | bytes 262176 | tf_op jit(solution)/shard_map/ppermute | solution.py:67
  42.3 0.2 stand.1
  42.5 4.1 %collective-permute-done.10 = f32[9,2,32,128]{3,2,1,0:T(8,128)S(1)} collective-permute-done((f32[9,2,32,128]{3,2,1,0:T(8,128)S(1)}, f32[9,2,32,128]{3,2,1,0:T(8,128)S(1)}, u32[]{:S(2)}, u32[]{:S(2)}) %collective-permute-start.10) | collective-permute-done | bytes 294944 | tf_op jit(solution)/shard_map/ppermute | solution.py:67
  46.6 2.1 %collective-permute-start.11 = (f32[9,2,32,128]{3,2,1,0:T(8,128)S(1)}, f32[9,2,32,128]{3,2,1,0:T(8,128)S(1)}, u32[]{:S(2)}, u32[]{:S(2)}) collective-permute-start(f32[9,2,32,128]{3,2,1,0:T(8,128)S(1)} %collective-permute-done.10), channel_id=1, source_target_pairs={{0,2},{1,17},{2,0},{3,19},{4,6},{5,21},{6,4},{7,23},{8,10},{9,25},... | collective-permute-start | bytes 884744 | tf_op jit(solution)/shard_map/ppermute | solution.py:67
  48.7 4.7 %collective-permute-done.11 = f32[9,2,32,128]{3,2,1,0:T(8,128)S(1)} collective-permute-done((f32[9,2,32,128]{3,2,1,0:T(8,128)S(1)}, f32[9,2,32,128]{3,2,1,0:T(8,128)S(1)}, u32[]{:S(2)}, u32[]{:S(2)}) %collective-permute-start.11) | collective-permute-done | bytes 294944 | tf_op jit(solution)/shard_map/ppermute | solution.py:67
  53.4 1.0 collective-permute-start.14
  54.5 1.6 %link_0.1 = (f32[128,256]{1,0:T(8,128)S(1)}, f32[128,128]{1,0:T(8,128)S(1)}) custom-call(f32[128,256]{1,0:T(8,128)S(1)} %get-tuple-element.54.b_ref, f32[4,8,2,32,128]{4,3,2,1,0:T(8,128)S(1)} %pad_maximum_fusion.four, f32[4,8,2,32,128]{4,3,2,1,0:T(8,128)S(1)} %collective-permute-done.12.third), custom_call_target="tpu_custom_call" | custom-call | tf_op jit(solution)/shard_map/link_0/pallas_call | solution.py:165
  56.1 0.1 collective-permute-start.13
  56.1 7.2 %collective-permute-done.14.f1 = f32[2,9,2,32,128]{4,3,2,1,0:T(8,128)S(1)} collective-permute-done((f32[2,9,2,32,128]{4,3,2,1,0:T(8,128)S(1)}, f32[2,9,2,32,128]{4,3,2,1,0:T(8,128)S(1)}, u32[]{:S(2)}, u32[]{:S(2)}) %collective-permute-start.14) | collective-permute-done | bytes 589856 | tf_op jit(solution)/shard_map/ppermute | solution.py:67
  63.4 2.4 %link_1.1 = (f32[128,256]{1,0:T(8,128)S(1)}, f32[128,128]{1,0:T(8,128)S(1)}) custom-call(f32[128,256]{1,0:T(8,128)S(1)} %get-tuple-element.50.b_ref, f32[128,256]{1,0:T(8,128)S(1)} %get-tuple-element.55.own, f32[128,256]{1,0:T(8,128)S(1)} %collective-permute-done.13.got, f32[128,128]{1,0:T(8,128)S(1)} %get-tuple-element.56.y0_ref, ...), custom_call_target="tpu_custom_call" | custom-call | tf_op jit(solution)/shard_map/link_1/pallas_call | solution.py:165
  65.9 0.1 collective-permute-start.17
  66.0 2.0 %collective-permute-start.16 = (f32[128,256]{1,0:T(8,128)S(1)}, f32[128,256]{1,0:T(8,128)S(1)}, u32[]{:S(2)}, u32[]{:S(2)}) collective-permute-start(f32[128,256]{1,0:T(8,128)S(1)} %get-tuple-element.57.s0), channel_id=1, source_target_pairs={{0,4},{1,5},{2,6},{3,7},{4,0},{5,1},{6,2},{7,3},{8,12},{9,13},{10,... | collective-permute-start | bytes 393224 | tf_op jit(solution)/shard_map/ppermute | solution.py:67
  68.0 3.1 %collective-permute-done.17.s3 = f32[128,256]{1,0:T(8,128)S(1)} collective-permute-done((f32[128,256]{1,0:T(8,128)S(1)}, f32[128,256]{1,0:T(8,128)S(1)}, u32[]{:S(2)}, u32[]{:S(2)}) %collective-permute-start.17) | collective-permute-done | bytes 131104 | tf_op jit(solution)/shard_map/ppermute | solution.py:67
  71.1 3.4 %collective-permute-done.16.s2 = f32[128,256]{1,0:T(8,128)S(1)} collective-permute-done((f32[128,256]{1,0:T(8,128)S(1)}, f32[128,256]{1,0:T(8,128)S(1)}, u32[]{:S(2)}, u32[]{:S(2)}) %collective-permute-start.16) | collective-permute-done | bytes 131104 | tf_op jit(solution)/shard_map/ppermute | solution.py:67
  74.6 3.3 %link_2.1 = (f32[128,256]{1,0:T(8,128)S(1)}, f32[128,128]{1,0:T(8,128)S(1)}) custom-call(f32[128,256]{1,0:T(8,128)S(1)} %get-tuple-element.49.b_ref, f32[128,256]{1,0:T(8,128)S(1)} %get-tuple-element.57.s0, f32[128,256]{1,0:T(8,128)S(1)} %collective-permute-done.15.s1, f32[128,256]{1,0:T(8,128)S(1)} %collective-permute-done.16.s2, ...), custom_call_target="tpu_custom_call" | custom-call | tf_op jit(solution)/shard_map/link_2/pallas_call | solution.py:165
  77.9 0.1 collective-permute-start.21
  78.0 1.1 %collective-permute-start.20 = (f32[128,256]{1,0:T(8,128)S(1)}, f32[128,256]{1,0:T(8,128)S(1)}, u32[]{:S(2)}, u32[]{:S(2)}) collective-permute-start(f32[128,256]{1,0:T(8,128)S(1)} %get-tuple-element.60.s0), channel_id=1, source_target_pairs={{0,4},{1,5},{2,6},{3,7},{4,0},{5,1},{6,2},{7,3},{8,12},{9,13},{10,... | collective-permute-start | bytes 393224 | tf_op jit(solution)/shard_map/ppermute | solution.py:67
  79.1 0.7 collective-permute-start.19
  79.8 3.9 %collective-permute-done.21.s3 = f32[128,256]{1,0:T(8,128)S(1)} collective-permute-done((f32[128,256]{1,0:T(8,128)S(1)}, f32[128,256]{1,0:T(8,128)S(1)}, u32[]{:S(2)}, u32[]{:S(2)}) %collective-permute-start.21) | collective-permute-done | bytes 131104 | tf_op jit(solution)/shard_map/ppermute | solution.py:67
  83.8 2.2 %collective-permute-done.20.s2 = f32[128,256]{1,0:T(8,128)S(1)} collective-permute-done((f32[128,256]{1,0:T(8,128)S(1)}, f32[128,256]{1,0:T(8,128)S(1)}, u32[]{:S(2)}, u32[]{:S(2)}) %collective-permute-start.20) | collective-permute-done | bytes 131104 | tf_op jit(solution)/shard_map/ppermute | solution.py:67
  85.9 1.1 %link_3.1 = (f32[4,32,128]{2,1,0:T(8,128)S(1)}, f32[4,32,128]{2,1,0:T(8,128)S(1)}, f32[4,32,128]{2,1,0:T(8,128)S(1)}, f32[4,32,128]{2,1,0:T(8,128)S(1)}) custom-call(f32[128,256]{1,0:T(8,128)S(1)} %get-tuple-element.48.b_ref, f32[128,256]{1,0:T(8,128)S(1)} %get-tuple-element.60.s0, f32[128,256]{1,0:T(8,128)S(1)} %collective-permute-done.19.s1, ...), custom_call_target="tpu_custom_call" | custom-call | tf_op jit(solution)/shard_map/link_3/pallas_call | solution.py:165
  87.0 0.7 collective-permute-start.22
  87.7 2.1 %collective-permute-start.23 = (f32[4,32,128]{2,1,0:T(8,128)S(1)}, f32[4,32,128]{2,1,0:T(8,128)S(1)}, u32[]{:S(2)}, u32[]{:S(2)}) collective-permute-start(f32[4,32,128]{2,1,0:T(8,128)S(1)} %get-tuple-element.63), channel_id=1, source_target_pairs={{0,2},{1,19},{2,0},{3,17},{4,6},{5,23},{6,4},{7,21},{8,10},{9,27},... | collective-permute-start | bytes 196616 | tf_op jit(solution)/shard_map/ppermute | solution.py:67
  89.8 3.1 %collective-permute-start.24 = (f32[4,32,128]{2,1,0:T(8,128)S(1)}, f32[4,32,128]{2,1,0:T(8,128)S(1)}, u32[]{:S(2)}, u32[]{:S(2)}) collective-permute-start(f32[4,32,128]{2,1,0:T(8,128)S(1)} %get-tuple-element.64), channel_id=1, source_target_pairs={{0,8},{1,25},{2,10},{3,27},{4,12},{5,29},{6,14},{7,31},{8,0},{9,17... | collective-permute-start | bytes 196616 | tf_op jit(solution)/shard_map/ppermute | solution.py:67
  92.8 3.0 %collective-permute-done.24 = f32[4,32,128]{2,1,0:T(8,128)S(1)} collective-permute-done((f32[4,32,128]{2,1,0:T(8,128)S(1)}, f32[4,32,128]{2,1,0:T(8,128)S(1)}, u32[]{:S(2)}, u32[]{:S(2)}) %collective-permute-start.24) | collective-permute-done | bytes 65568 | tf_op jit(solution)/shard_map/ppermute | solution.py:67
  95.9 3.7 %collective-permute-done.25 = f32[4,32,128]{2,1,0:T(8,128)S(1)} collective-permute-done((f32[4,32,128]{2,1,0:T(8,128)S(1)}, f32[4,32,128]{2,1,0:T(8,128)S(1)}, u32[]{:S(2)}, u32[]{:S(2)}) %collective-permute-start.25) | collective-permute-done | bytes 65568 | tf_op jit(solution)/shard_map/ppermute | solution.py:67
  99.7 0.6 collective-permute-start.27
  100.2 1.7 %collective-permute-start.26 = (f32[4,2,32,128]{3,2,1,0:T(8,128)S(1)}, f32[4,2,32,128]{3,2,1,0:T(8,128)S(1)}, u32[]{:S(2)}, u32[]{:S(2)}) collective-permute-start(f32[4,2,32,128]{3,2,1,0:T(8,128)S(1)} %get-tuple-element.67.near_ref), channel_id=1, source_target_pairs={{0,16},{1,17},{2,18},{3,19},{4,20},{5,21},{6,22},{7,23},{8,24},{9,... | collective-permute-start | bytes 393224 | tf_op jit(solution)/shard_map/ppermute | solution.py:67
  102.0 0.9 join_root.1
  102.8 2.9 %collective-permute-done.26.other_ref = f32[4,2,32,128]{3,2,1,0:T(8,128)S(1)} collective-permute-done((f32[4,2,32,128]{3,2,1,0:T(8,128)S(1)}, f32[4,2,32,128]{3,2,1,0:T(8,128)S(1)}, u32[]{:S(2)}, u32[]{:S(2)}) %collective-permute-start.26) | collective-permute-done | bytes 131104 | tf_op jit(solution)/shard_map/ppermute | solution.py:67
  105.7 0.9 join_leaf.1
  (40 shorter events, 0.5 us)
Async XLA Ops:
  0.6 0.7 copy-start
  3.4 7.2 %collective-permute-start.3 = (f32[3,2,32,128]{3,2,1,0:T(8,128)S(1)}, f32[3,2,32,128]{3,2,1,0:T(8,128)S(1)}, u32[]{:S(2)}, u32[]{:S(2)}) collective-permute-start(f32[3,2,32,128]{3,2,1,0:T(8,128)S(1)} %get-tuple-element.39), channel_id=1, source_target_pairs={{0,4},{1,5},{2,6},{3,7},{4,0},{5,1},{6,2},{7,3},{8,12},{9,13},{10,... | collective-permute-start | bytes 294920 | tf_op jit(solution)/shard_map/ppermute | solution.py:67
  6.5 14.2 %collective-permute-start.6 = (f32[3,2,32,128]{3,2,1,0:T(8,128)S(1)}, f32[3,2,32,128]{3,2,1,0:T(8,128)S(1)}, u32[]{:S(2)}, u32[]{:S(2)}) collective-permute-start(f32[3,2,32,128]{3,2,1,0:T(8,128)S(1)} %get-tuple-element.39), channel_id=1, source_target_pairs={{0,12},{1,13},{2,14},{3,15},{4,8},{5,9},{6,10},{7,11},{8,4},{9,5},... | collective-permute-start | bytes 294920 | tf_op jit(solution)/shard_map/ppermute | solution.py:67
  9.0 11.8 %collective-permute-start.4 = (f32[5,2,32,128]{3,2,1,0:T(8,128)S(1)}, f32[5,2,32,128]{3,2,1,0:T(8,128)S(1)}, u32[]{:S(2)}, u32[]{:S(2)}) collective-permute-start(f32[5,2,32,128]{3,2,1,0:T(8,128)S(1)} %get-tuple-element.38), channel_id=1, source_target_pairs={{0,8},{1,9},{2,10},{3,11},{4,12},{5,13},{6,14},{7,15},{8,0},{9,1},... | collective-permute-start | bytes 491528 | tf_op jit(solution)/shard_map/ppermute | solution.py:67
  9.1 6.7 %collective-permute-start.5 = (f32[9,2,32,128]{3,2,1,0:T(8,128)S(1)}, f32[9,2,32,128]{3,2,1,0:T(8,128)S(1)}, u32[]{:S(2)}, u32[]{:S(2)}) collective-permute-start(f32[9,2,32,128]{3,2,1,0:T(8,128)S(1)} %get-tuple-element.52), channel_id=1, source_target_pairs={{0,2},{1,17},{2,0},{3,19},{4,6},{5,21},{6,4},{7,23},{8,10},{9,25},... | collective-permute-start | bytes 884744 | tf_op jit(solution)/shard_map/ppermute | solution.py:67
  15.9 19.9 %collective-permute-start.8 = (f32[2,9,2,32,128]{4,3,2,1,0:T(8,128)S(1)}, f32[2,9,2,32,128]{4,3,2,1,0:T(8,128)S(1)}, u32[]{:S(2)}, u32[]{:S(2)}) collective-permute-start(f32[2,9,2,32,128]{4,3,2,1,0:T(8,128)S(1)} %pad_maximum_fusion.1.n0), channel_id=1, source_target_pairs={{0,16},{1,3},{2,18},{3,1},{4,20},{5,7},{6,22},{7,5},{8,24},{9,11},... | collective-permute-start | bytes 1769480 | tf_op jit(solution)/shard_map/ppermute | solution.py:67
  20.9 14.9 %collective-permute-start.7 = (f32[2,8,2,32,128]{4,3,2,1,0:T(8,128)S(1)}, f32[2,8,2,32,128]{4,3,2,1,0:T(8,128)S(1)}, u32[]{:S(2)}, u32[]{:S(2)}) collective-permute-start(f32[2,8,2,32,128]{4,3,2,1,0:T(8,128)S(1)} %pad_maximum_fusion.3), channel_id=1, source_target_pairs={{0,2},{1,17},{2,0},{3,19},{4,6},{5,21},{6,4},{7,23},{8,10},{9,25},... | collective-permute-start | bytes 1572872 | tf_op jit(solution)/shard_map/ppermute | solution.py:67
  22.4 10.3 %collective-permute-start = (f32[4,32,128]{2,1,0:T(8,128)S(1)}, f32[4,32,128]{2,1,0:T(8,128)S(1)}, u32[]{:S(2)}, u32[]{:S(2)}) collective-permute-start(f32[4,32,128]{2,1,0:T(8,128)S(1)} %get-tuple-element.35), channel_id=1, source_target_pairs={{0,2},{1,3},{2,0},{3,1},{4,6},{5,7},{6,4},{7,5},{8,10},{9,11},{10,... | collective-permute-start | bytes 196616 | tf_op jit(solution)/shard_map/ppermute | solution.py:67
  23.0 9.8 %collective-permute-start.1 = (f32[4,32,128]{2,1,0:T(8,128)S(1)}, f32[4,32,128]{2,1,0:T(8,128)S(1)}, u32[]{:S(2)}, u32[]{:S(2)}) collective-permute-start(f32[4,32,128]{2,1,0:T(8,128)S(1)} %get-tuple-element.36), channel_id=1, source_target_pairs={{0,8},{1,9},{2,10},{3,11},{4,12},{5,13},{6,14},{7,15},{8,0},{9,1},... | collective-permute-start | bytes 196616 | tf_op jit(solution)/shard_map/ppermute | solution.py:67
  23.0 9.8 %collective-permute-start.2 = (f32[4,32,128]{2,1,0:T(8,128)S(1)}, f32[4,32,128]{2,1,0:T(8,128)S(1)}, u32[]{:S(2)}, u32[]{:S(2)}) collective-permute-start(f32[4,32,128]{2,1,0:T(8,128)S(1)} %get-tuple-element.37), channel_id=1, source_target_pairs={{0,10},{1,11},{2,8},{3,9},{4,14},{5,15},{6,12},{7,13},{8,2},{9,3},... | collective-permute-start | bytes 196616 | tf_op jit(solution)/shard_map/ppermute | solution.py:67
  32.8 9.5 %collective-permute-start.9 = (f32[4,4,32,128]{3,2,1,0:T(8,128)S(1)}, f32[4,4,32,128]{3,2,1,0:T(8,128)S(1)}, u32[]{:S(2)}, u32[]{:S(2)}) collective-permute-start(f32[4,4,32,128]{3,2,1,0:T(8,128)S(1)} %pad_maximum_fusion.4.near_ref), channel_id=1, source_target_pairs={{0,4},{1,5},{2,6},{3,7},{4,0},{5,1},{6,2},{7,3},{8,12},{9,13},{10,... | collective-permute-start | bytes 786440 | tf_op jit(solution)/shard_map/ppermute | solution.py:67
  33.3 13.3 %collective-permute-start.10 = (f32[9,2,32,128]{3,2,1,0:T(8,128)S(1)}, f32[9,2,32,128]{3,2,1,0:T(8,128)S(1)}, u32[]{:S(2)}, u32[]{:S(2)}) collective-permute-start(f32[9,2,32,128]{3,2,1,0:T(8,128)S(1)} %get-tuple-element.52), channel_id=1, source_target_pairs={{0,8},{1,9},{2,10},{3,11},{4,12},{5,13},{6,14},{7,15},{8,0},{9,1},... | collective-permute-start | bytes 884744 | tf_op jit(solution)/shard_map/ppermute | solution.py:67
  35.8 18.6 %collective-permute-start.12 = (f32[4,8,2,32,128]{4,3,2,1,0:T(8,128)S(1)}, f32[4,8,2,32,128]{4,3,2,1,0:T(8,128)S(1)}, u32[]{:S(2)}, u32[]{:S(2)}) collective-permute-start(f32[4,8,2,32,128]{4,3,2,1,0:T(8,128)S(1)} %pad_maximum_fusion.four), channel_id=1, source_target_pairs={{0,16},{1,3},{2,18},{3,1},{4,20},{5,7},{6,22},{7,5},{8,24},{9,11},... | collective-permute-start | bytes 3145736 | tf_op jit(solution)/shard_map/ppermute | solution.py:67
  46.6 6.8 %collective-permute-start.11 = (f32[9,2,32,128]{3,2,1,0:T(8,128)S(1)}, f32[9,2,32,128]{3,2,1,0:T(8,128)S(1)}, u32[]{:S(2)}, u32[]{:S(2)}) collective-permute-start(f32[9,2,32,128]{3,2,1,0:T(8,128)S(1)} %collective-permute-done.10), channel_id=1, source_target_pairs={{0,2},{1,17},{2,0},{3,19},{4,6},{5,21},{6,4},{7,23},{8,10},{9,25},... | collective-permute-start | bytes 884744 | tf_op jit(solution)/shard_map/ppermute | solution.py:67
  53.4 9.9 %collective-permute-start.14 = (f32[2,9,2,32,128]{4,3,2,1,0:T(8,128)S(1)}, f32[2,9,2,32,128]{4,3,2,1,0:T(8,128)S(1)}, u32[]{:S(2)}, u32[]{:S(2)}) collective-permute-start(f32[2,9,2,32,128]{4,3,2,1,0:T(8,128)S(1)} %pad_maximum_fusion.2.f0), channel_id=1, source_target_pairs={{0,16},{1,3},{2,18},{3,1},{4,20},{5,7},{6,22},{7,5},{8,24},{9,11},... | collective-permute-start | bytes 1769480 | tf_op jit(solution)/shard_map/ppermute | solution.py:67
  56.1 7.3 %collective-permute-start.13 = (f32[128,256]{1,0:T(8,128)S(1)}, f32[128,256]{1,0:T(8,128)S(1)}, u32[]{:S(2)}, u32[]{:S(2)}) collective-permute-start(f32[128,256]{1,0:T(8,128)S(1)} %get-tuple-element.55.own), channel_id=1, source_target_pairs={{0,4},{1,5},{2,6},{3,7},{4,0},{5,1},{6,2},{7,3},{8,12},{9,13},{10,... | collective-permute-start | bytes 393224 | tf_op jit(solution)/shard_map/ppermute | solution.py:67
  65.8 8.8 %collective-permute-start.18 = (f32[8,3,2,32,128]{4,3,2,1,0:T(8,128)S(1)}, f32[8,3,2,32,128]{4,3,2,1,0:T(8,128)S(1)}, u32[]{:S(2)}, u32[]{:S(2)}) collective-permute-start(f32[8,3,2,32,128]{4,3,2,1,0:T(8,128)S(1)} %root_shards.1.root), channel_id=1, source_target_pairs={{0,1},{1,0},{2,3},{3,2},{4,5},{5,4},{6,7},{7,6},{8,9},{9,8},{10,11... | collective-permute-start | bytes 2359304 | tf_op jit(solution)/shard_map/ppermute | solution.py:67
  65.9 5.2 %collective-permute-start.17 = (f32[128,256]{1,0:T(8,128)S(1)}, f32[128,256]{1,0:T(8,128)S(1)}, u32[]{:S(2)}, u32[]{:S(2)}) collective-permute-start(f32[128,256]{1,0:T(8,128)S(1)} %get-tuple-element.57.s0), channel_id=1, source_target_pairs={{0,5},{1,4},{2,7},{3,6},{4,1},{5,0},{6,3},{7,2},{8,13},{9,12},{10,... | collective-permute-start | bytes 393224 | tf_op jit(solution)/shard_map/ppermute | solution.py:67
  66.0 8.6 %collective-permute-start.16 = (f32[128,256]{1,0:T(8,128)S(1)}, f32[128,256]{1,0:T(8,128)S(1)}, u32[]{:S(2)}, u32[]{:S(2)}) collective-permute-start(f32[128,256]{1,0:T(8,128)S(1)} %get-tuple-element.57.s0), channel_id=1, source_target_pairs={{0,4},{1,5},{2,6},{3,7},{4,0},{5,1},{6,2},{7,3},{8,12},{9,13},{10,... | collective-permute-start | bytes 393224 | tf_op jit(solution)/shard_map/ppermute | solution.py:67
  68.0 6.5 %collective-permute-start.15 = (f32[128,256]{1,0:T(8,128)S(1)}, f32[128,256]{1,0:T(8,128)S(1)}, u32[]{:S(2)}, u32[]{:S(2)}) collective-permute-start(f32[128,256]{1,0:T(8,128)S(1)} %get-tuple-element.57.s0), channel_id=1, source_target_pairs={{0,1},{1,0},{2,3},{3,2},{4,5},{5,4},{6,7},{7,6},{8,9},{9,8},{10,11... | collective-permute-start | bytes 393224 | tf_op jit(solution)/shard_map/ppermute | solution.py:67
  77.9 5.9 %collective-permute-start.21 = (f32[128,256]{1,0:T(8,128)S(1)}, f32[128,256]{1,0:T(8,128)S(1)}, u32[]{:S(2)}, u32[]{:S(2)}) collective-permute-start(f32[128,256]{1,0:T(8,128)S(1)} %get-tuple-element.60.s0), channel_id=1, source_target_pairs={{0,5},{1,4},{2,7},{3,6},{4,1},{5,0},{6,3},{7,2},{8,13},{9,12},{10,... | collective-permute-start | bytes 393224 | tf_op jit(solution)/shard_map/ppermute | solution.py:67
  78.0 7.9 %collective-permute-start.20 = (f32[128,256]{1,0:T(8,128)S(1)}, f32[128,256]{1,0:T(8,128)S(1)}, u32[]{:S(2)}, u32[]{:S(2)}) collective-permute-start(f32[128,256]{1,0:T(8,128)S(1)} %get-tuple-element.60.s0), channel_id=1, source_target_pairs={{0,4},{1,5},{2,6},{3,7},{4,0},{5,1},{6,2},{7,3},{8,12},{9,13},{10,... | collective-permute-start | bytes 393224 | tf_op jit(solution)/shard_map/ppermute | solution.py:67
  79.1 6.8 %collective-permute-start.19 = (f32[128,256]{1,0:T(8,128)S(1)}, f32[128,256]{1,0:T(8,128)S(1)}, u32[]{:S(2)}, u32[]{:S(2)}) collective-permute-start(f32[128,256]{1,0:T(8,128)S(1)} %get-tuple-element.60.s0), channel_id=1, source_target_pairs={{0,1},{1,0},{2,3},{3,2},{4,5},{5,4},{6,7},{7,6},{8,9},{9,8},{10,11... | collective-permute-start | bytes 393224 | tf_op jit(solution)/shard_map/ppermute | solution.py:67
  87.0 5.8 %collective-permute-start.22 = (f32[4,32,128]{2,1,0:T(8,128)S(1)}, f32[4,32,128]{2,1,0:T(8,128)S(1)}, u32[]{:S(2)}, u32[]{:S(2)}) collective-permute-start(f32[4,32,128]{2,1,0:T(8,128)S(1)} %get-tuple-element.62), channel_id=1, source_target_pairs={{0,0},{1,17},{2,2},{3,19},{4,4},{5,21},{6,6},{7,23},{8,8},{9,25},{... | collective-permute-start | bytes 196616 | tf_op jit(solution)/shard_map/ppermute | solution.py:67
  87.7 5.2 %collective-permute-start.23 = (f32[4,32,128]{2,1,0:T(8,128)S(1)}, f32[4,32,128]{2,1,0:T(8,128)S(1)}, u32[]{:S(2)}, u32[]{:S(2)}) collective-permute-start(f32[4,32,128]{2,1,0:T(8,128)S(1)} %get-tuple-element.63), channel_id=1, source_target_pairs={{0,2},{1,19},{2,0},{3,17},{4,6},{5,23},{6,4},{7,21},{8,10},{9,27},... | collective-permute-start | bytes 196616 | tf_op jit(solution)/shard_map/ppermute | solution.py:67
  89.8 6.1 %collective-permute-start.24 = (f32[4,32,128]{2,1,0:T(8,128)S(1)}, f32[4,32,128]{2,1,0:T(8,128)S(1)}, u32[]{:S(2)}, u32[]{:S(2)}) collective-permute-start(f32[4,32,128]{2,1,0:T(8,128)S(1)} %get-tuple-element.64), channel_id=1, source_target_pairs={{0,8},{1,25},{2,10},{3,27},{4,12},{5,29},{6,14},{7,31},{8,0},{9,17... | collective-permute-start | bytes 196616 | tf_op jit(solution)/shard_map/ppermute | solution.py:67
  92.8 6.8 %collective-permute-start.25 = (f32[4,32,128]{2,1,0:T(8,128)S(1)}, f32[4,32,128]{2,1,0:T(8,128)S(1)}, u32[]{:S(2)}, u32[]{:S(2)}) collective-permute-start(f32[4,32,128]{2,1,0:T(8,128)S(1)} %get-tuple-element.65), channel_id=1, source_target_pairs={{0,10},{1,27},{2,8},{3,25},{4,14},{5,31},{6,12},{7,29},{8,2},{9,19... | collective-permute-start | bytes 196616 | tf_op jit(solution)/shard_map/ppermute | solution.py:67
  99.7 2.3 %collective-permute-start.27 = (f32[4,2,32,128]{3,2,1,0:T(8,128)S(1)}, f32[4,2,32,128]{3,2,1,0:T(8,128)S(1)}, u32[]{:S(2)}, u32[]{:S(2)}) collective-permute-start(f32[4,2,32,128]{3,2,1,0:T(8,128)S(1)} %get-tuple-element.66.near_ref), channel_id=1, source_target_pairs={{0,1},{1,0},{2,3},{3,2},{4,5},{5,4},{6,7},{7,6},{8,9},{9,8},{10,11... | collective-permute-start | bytes 393224 | tf_op jit(solution)/shard_map/ppermute | solution.py:67
  100.2 5.5 %collective-permute-start.26 = (f32[4,2,32,128]{3,2,1,0:T(8,128)S(1)}, f32[4,2,32,128]{3,2,1,0:T(8,128)S(1)}, u32[]{:S(2)}, u32[]{:S(2)}) collective-permute-start(f32[4,2,32,128]{3,2,1,0:T(8,128)S(1)} %get-tuple-element.67.near_ref), channel_id=1, source_target_pairs={{0,16},{1,17},{2,18},{3,19},{4,20},{5,21},{6,22},{7,23},{8,24},{9,... | collective-permute-start | bytes 393224 | tf_op jit(solution)/shard_map/ppermute | solution.py:67
